TPU v7x, 32 devices: a whole 2x2x4 slice. The times are simulated.
32 devices in a mesh: groups: 2 (over x), net: 8 (over z, y), tm: 2 (over core).
Axes of the slice: x: 2, y: 2, z: 4, core: 2. Of those that a mesh axis runs over, the one named last changes fastest.
Arguments:
- proposal: float32 [16384, 256], P(('groups', 'net'), 'tm'), parts along dimension 0, may hold values from -6 to 6
- flow_dual: float32 [8192, 256], P(('groups', 'net'), 'tm'), parts along dimension 0, may hold values from -4 to 4
- shift_factors: bfloat16 [4096, 8192], P('net'), may hold values from -0.09375 to 0.09375
- outage_line: int32 [4096], P('net'), may hold values from 0 to 511
- ratings: float32 [512], replicated, may hold values from 0.3 to 3
- ramp_limit: float32 [8192], P('net'), may hold values from 0.05 to 1
Outputs:
- dispatch: float32 [16384, 256], P(('groups', 'net'), 'tm'), parts along dimension 0
- new_dual: float32 [8192, 256], P(('groups', 'net'), 'tm'), parts along dimension 0
- residual_norms: float32 [4], P('groups'), parts along dimension 0
There are 2 independent parts, one for each index of `groups`. A program takes and returns all parts, laid end to end along the dimension named above; an argument that names none is the same for every part. Nothing has to cross between parts.
All inputs are finite; a program needn't handle non-finite values.
Results may differ from a plain program's by a relative error of at most 0.0024.
Values may be sent and summed in bfloat16 or wider, within the bound.
No kernel may reach another device: no remote copies, remote signals or barrier semaphores. Data moves between devices by JAX's collectives and lax.ppermute only.
A program may use at most 64 MiB of HBM per device.

v0:
```python
import jax
import jax.numpy as jnp
from jax import lax
from jax.sharding import PartitionSpec as P

relax_step = 0.1


def with_halo(block, sides, width):
    for axis, dim in sides:
        count = lax.axis_size(axis)
        forward = [(i, i + 1) for i in range(count - 1)]
        backward = [(target, source) for source, target in forward]
        low = lax.ppermute(
            lax.slice_in_dim(block, block.shape[dim] - width, None, axis=dim), axis, forward
        )
        high = lax.ppermute(lax.slice_in_dim(block, 0, width, axis=dim), axis, backward)
        block = jnp.concatenate([low, block, high], axis=dim)
    return block


def limits_of(outage_line, ratings):
    levels = lax.broadcasted_iota(jnp.int32, (outage_line.shape[0], ratings.shape[0]), 1)
    return jnp.sum(jnp.where(outage_line[:, None] == levels, ratings[None, :], 0.0), axis=1)


def project(flows, dual, limits):
    bound = limits[:, None]
    kept = jnp.clip(flows + dual, -bound, bound)
    misfit = flows - kept
    return (misfit, dual + misfit)


def forward(shift_factors, inject):
    return jnp.dot(
        shift_factors,
        lax.all_gather(inject.astype(jnp.bfloat16), "net", axis=0, tiled=True),
        preferred_element_type=jnp.float32,
    )


def backward(shift_factors, misfit, owned):
    narrow = misfit.astype(jnp.bfloat16)
    return lax.psum_scatter(
        lax.dot_general(
            shift_factors, narrow, (((0,), (0,)), ((), ())), preferred_element_type=jnp.float32
        ),
        "net",
        scatter_dimension=0,
        tiled=True,
    )


def body(proposal, flow_dual, shift_factors, outage_line, ratings, ramp_limit):
    limits = limits_of(outage_line, ratings)
    owned = proposal.shape[0]
    periods = proposal.shape[1]
    dual = flow_dual
    inject = proposal
    flows = forward(shift_factors, inject)
    first, dual = project(flows, dual, limits)
    inject = inject - relax_step * backward(shift_factors, first, owned)
    flows = forward(shift_factors, inject)
    misfit, dual = project(flows, dual, limits)
    inject = inject - relax_step * backward(shift_factors, misfit, owned)
    sums = lax.psum((jnp.sum(first * first), jnp.sum(misfit * misfit)), ("net", "tm"))
    count = jnp.float32(
        shift_factors.shape[0] * lax.axis_size("net") * periods * lax.axis_size("tm")
    )
    residual_norms = jnp.sqrt(jnp.stack([sums[0], sums[1]]) / count)
    padded = with_halo(inject, (("tm", 1),), 1)
    step = padded[:, 1:] - padded[:, :-1]
    bound = ramp_limit[:, None]
    moment = lax.axis_index("tm") * periods + lax.broadcasted_iota(jnp.int32, (1, periods + 1), 1)
    valid = (moment >= 1) & (moment <= periods * lax.axis_size("tm") - 1)
    excess = jnp.where(valid, step - jnp.clip(step, -bound, bound), 0.0)
    dispatch = inject - 0.5 * excess[:, :-1] + 0.5 * excess[:, 1:]
    return (dispatch, dual, residual_norms)


def solution(mesh):
    return jax.shard_map(
        body,
        mesh=mesh,
        in_specs=(
            P(("groups", "net"), "tm"),
            P(("groups", "net"), "tm"),
            P("net", None),
            P("net"),
            P(),
            P("net"),
        ),
        out_specs=(P(("groups", "net"), "tm"), P(("groups", "net"), "tm"), P("groups")),
        check_vma=False,
    )
```

profile of v0, /device:TPU:0, one launch (start us, length us, event | category | flops | bytes accessed | tf_op | source)
XLA Modules:
  0.0 328.7 jit_solution(8050252087186580614)
XLA Ops:
  7.2 0.0 copy-start.3
  7.2 0.0 all-gather.3.cloned.1.call-start
  7.2 1.8 convert_element_type.12
  9.0 0.0 all-gather.3.cloned.1.call-update
  9.0 0.0 reduce-scatter.3.cloned.1.call-start
  9.1 0.9 select_reduce_fusion
  10.1 52.5 %all-gather.3.cloned.1.call-done = bf16[8192,128]{1,0:T(8,128)(2,1)} async-done(((bf16[1024,128]{1,0:T(8,128)(2,1)}), bf16[8192,128]{1,0:T(8,128)(2,1)}) %all-gather.3.cloned.1.call-update) | async-done | bytes 2097168 | tf_op jit(solution)/shard_map/all_gather | solution.py:37
  62.5 0.0 copy-start
  62.5 6.5 %fusion.10 = f32[512,128]{1,0:T(8,128)S(1)} fusion(bf16[512,8192]{1,0:T(8,128)(2,1)} %param.8, bf16[8192,128]{1,0:T(8,128)(2,1)} %all-gather.3.cloned.1.call-done), kind=kOutput, calls=%fused_computation.27 | convolution fusion | flops 1073741824 | bytes 10747904 | tf_op jit(solution)/shard_map/dot_general | solution.py:35
  69.0 0.0 copy-done.3
  69.0 0.0 copy-done
  69.0 0.0 copy-start.1
  69.0 3.5 %convolution_bitcast_fusion.1 = f32[8192,128]{0,1:T(8,128)} fusion(bf16[512,8192]{1,0:T(8,128)(2,1)S(1)} %copy-done, f32[512,128]{1,0:T(8,128)S(1)} %fusion.10, f32[512,128]{1,0:T(8,128)S(1)} %copy-done.3, f32[512]{0:T(512)S(1)} %neg.13, f32[512]{0:T(512)S(1)} %select_reduce_fusion), kind=kOutput, calls=%fused_computation.1 | convolution fusion | flops 1074069504 | bytes 13111296 | tf_op jit(solution)/shard_map/dot_general | solution.py:45
  72.5 0.0 reduce-scatter.3.cloned.1.call-update
  72.6 0.0 all-gather.5.cloned.1.call-start
  72.6 0.0 copy-done.1
  72.6 0.2 copy.12
  72.8 87.1 %reduce-scatter.3.cloned.1.call-done = f32[1024,128]{0,1:T(8,128)} async-done(((f32[8192,128]{0,1:T(8,128)}), f32[1024,128]{0,1:T(8,128)}) %reduce-scatter.3.cloned.1.call-update) | async-done | bytes 524304 | tf_op jit(solution)/shard_map/reduce_scatter | solution.py:44
  160.0 1.8 fusion.2
  161.8 0.0 all-gather.5.cloned.1.call-update
  161.8 0.0 reduce-scatter.5.cloned.1.call-start
  161.9 49.6 %all-gather.5.cloned.1.call-done = bf16[8192,128]{0,1:T(8,128)(2,1)} async-done(((bf16[1024,128]{0,1:T(8,128)(2,1)}), bf16[8192,128]{0,1:T(8,128)(2,1)}) %all-gather.5.cloned.1.call-update) | async-done | bytes 2097168 | tf_op jit(solution)/shard_map/all_gather | solution.py:37
  211.5 7.7 %multiply_reduce_fusion.1 = (f32[]{:T(128)}, f32[512,128]{1,0:T(8,128)}, f32[]{:T(128)}, bf16[512,128]{1,0:T(8,128)(2,1)S(1)}) fusion(f32[512,128]{1,0:T(8,128)S(1)} %fusion.10, f32[512,128]{1,0:T(8,128)S(1)} %copy-done.3, f32[512]{0:T(512)S(1)} %neg.13, f32[512]{0:T(512)S(1)} %select_reduce_fusion, bf16[8192,128]{0,1:T(8,128)(2,1)} %all-gather.5.cloned.1.call-done, ...), kind=kOutput, calls=%fused_computation.14 | convolution fusion | flops 1074724864 | bytes 11407368 | tf_op jit(solution)/shard_map/dot_general | solution.py:35
  219.2 0.0 copy-start.4
  219.2 0.0 copy-start.2
  219.2 6.7 %convolution_bitcast_fusion = f32[8192,128]{0,1:T(8,128)} fusion(bf16[512,8192]{1,0:T(8,128)(2,1)} %param.8, bf16[512,128]{1,0:T(8,128)(2,1)S(1)} %get-tuple-element.16), kind=kOutput, calls=%fused_computation | convolution fusion | flops 1073741824 | bytes 12713984 | tf_op jit(solution)/shard_map/dot_general | solution.py:45
  225.9 0.0 reduce-scatter.5.cloned.1.call-update
  225.9 0.0 copy-done.4
  225.9 32.5 %all-reduce = (f32[1]{0:T(128)}, f32[1]{0:T(128)}) all-reduce(f32[1]{0:T(128)} %bitcast.4, f32[1]{0:T(128)} %bitcast.3), channel_id=1, replica_groups=mesh['groups'=2,'net'=8,'tm'=2] {'net','tm'}, use_global_device_ids=true, to_apply=%region_6.7 | all-reduce | flops 2 | bytes 16 | tf_op jit(solution)/shard_map/psum | solution.py:66
  258.4 55.1 %reduce-scatter.5.cloned.1.call-done = f32[1024,128]{0,1:T(8,128)} async-done(((f32[8192,128]{0,1:T(8,128)}), f32[1024,128]{0,1:T(8,128)}) %reduce-scatter.5.cloned.1.call-update) | async-done | bytes 524304 | tf_op jit(solution)/shard_map/reduce_scatter | solution.py:44
  313.5 0.0 copy-done.2
  313.5 1.2 multiply_subtract_fusion
  314.7 1.3 collective-permute-start
  316.0 3.0 collective-permute-start.1
  319.0 1.9 fusion.7
  320.9 0.0 collective-permute-done
  320.9 0.0 collective-permute-done.1
  320.9 0.2 subtract_select_fusion
  321.1 0.1 fusion
  321.2 1.0 copy.14
  (4 shorter events, 0.0 us)
Async XLA Ops:
  7.2 61.8 %copy-start.3 = (f32[512,128]{1,0:T(8,128)S(1)}, f32[512,128]{1,0:T(8,128)}, u32[]{:S(2)}) copy-start(f32[512,128]{1,0:T(8,128)} %param.7) | copy-start | bytes 786436
  7.2 55.3 %all-gather.3.cloned.1.call-start = ((), (), s32[]{:S(2)}) async-start(), calls=%async_computation.2 | async-start | bytes 2359296 | tf_op jit(solution)/shard_map/all_gather | solution.py:37
  9.0 150.9 %reduce-scatter.3.cloned.1.call-start = ((), (), s32[]{:S(2)}) async-start(), calls=%async_computation.3 | async-start | bytes 4718592 | tf_op jit(solution)/shard_map/reduce_scatter | solution.py:44
  62.5 6.5 %copy-start = (bf16[512,8192]{1,0:T(8,128)(2,1)S(1)}, bf16[512,8192]{1,0:T(8,128)(2,1)}, u32[]{:S(2)}) copy-start(bf16[512,8192]{1,0:T(8,128)(2,1)} %param.8) | copy-start | bytes 25165828
  69.0 3.6 %copy-start.1 = (f32[1024,128]{1,0:T(8,128)S(1)}, f32[1024,128]{1,0:T(8,128)}, u32[]{:S(2)}) copy-start(f32[1024,128]{1,0:T(8,128)} %param.6) | copy-start | bytes 1572868
  72.6 138.9 %all-gather.5.cloned.1.call-start = ((), (), s32[]{:S(2)}) async-start(), calls=%async_computation.4 | async-start | bytes 2359296 | tf_op jit(solution)/shard_map/all_gather | solution.py:37
  161.8 151.7 %reduce-scatter.5.cloned.1.call-start = ((), (), s32[]{:S(2)}) async-start(), calls=%async_computation.5 | async-start | bytes 4718592 | tf_op jit(solution)/shard_map/reduce_scatter | solution.py:44
  219.2 6.7 %copy-start.4 = (f32[1024]{0:T(1024)S(1)}, f32[1024]{0:T(1024)}, u32[]{:S(2)}) copy-start(f32[1024]{0:T(1024)} %param.11) | copy-start | bytes 12292
  219.2 94.4 %copy-start.2 = (f32[1024,128]{0,1:T(8,128)S(1)}, f32[1024,128]{0,1:T(8,128)}, u32[]{:S(2)}) copy-start(f32[1024,128]{0,1:T(8,128)} %reduce-scatter.3.cloned.1.call-done) | copy-start | bytes 1572868
  314.7 6.2 %collective-permute-start = (f32[1024,1]{0,1:T(1,128)S(1)}, f32[1024,1]{0,1:T(1,128)S(1)}, u32[]{:S(2)}, u32[]{:S(2)}) collective-permute-start(f32[1024,1]{0,1:T(1,128)S(1)} %get-tuple-element.13), channel_id=1, source_target_pairs={{1,0},{3,2},{5,4},{7,6},{9,8},{11,10},{13,12},{15,14},{17,16},{19,... | collective-permute-start | bytes 12296 | tf_op jit(solution)/shard_map/ppermute | solution.py:17
  316.0 4.9 %collective-permute-start.1 = (f32[1024,1]{0,1:T(1,128)S(1)}, f32[1024,1]{0,1:T(1,128)S(1)}, u32[]{:S(2)}, u32[]{:S(2)}) collective-permute-start(f32[1024,1]{0,1:T(1,128)S(1)} %get-tuple-element.14), channel_id=1, source_target_pairs={{0,1},{2,3},{4,5},{6,7},{8,9},{10,11},{12,13},{14,15},{16,17},{18,... | collective-permute-start | bytes 12296 | tf_op jit(solution)/shard_map/ppermute | solution.py:14
Sparse Core Ops, SparseCore 0:
  10.7 51.7 all-gather.2
  72.7 87.2 reduce-scatter.2
  162.7 48.7 all-gather.4
  226.0 87.4 reduce-scatter.4
where the time goes:
time: 329 us
  waiting for transfers between devices  244 us (74%)
  blocking collectives  32.5 us (10%)
  matrix products  24.3 us (7%)
  between operations  13.9 us (4%)
  other arithmetic  7.86 us (2%)
  starting transfers between devices  4.48 us (1%)
    reduce_scatter x2, waiting for transfers between devices, backward(): lax.psum_scatter(lax.dot_general(shift_factors, narrow, (((0,), (0,)), ((...  142 us
    all_gather x2, waiting for transfers between devices, forward(): lax.all_gather(inject.astype(jnp.bfloat16), 'net', axis=0, tiled=True)  102 us
    psum x1, blocking collectives, body(): lax.psum((jnp.sum(first * first), jnp.sum(misfit * misfit)), ('net', 'tm'))  32.5 us
    dot_general x2, matrix products, forward(): jnp.dot(shift_factors, lax.all_gather(inject.astype(jnp.bfloat16), 'net',...  14.1 us
    dot_general x2, matrix products, backward(): lax.dot_general(shift_factors, narrow, (((0,), (0,)), ((), ())), preferre...  10.2 us
  transfers between devices with their start and end apart: 6, of which 4 were waited for; matrix products, arithmetic and copies ran while one was open for 1% of the time, Pallas kernels for 0%

commit v1 on v0

v1 whole, which is shorter than its diff:
```python
import jax
import jax.numpy as jnp
from jax import lax
from jax.experimental import pallas as pl
from jax.experimental.pallas import tpu as pltpu
from jax.sharding import PartitionSpec as P

relax_step = 0.1
chunks = 2
passes = 2
longest_ring = 8


def ring_order(count):
    return list(range(0, count, 2)) + list(range(count - 1 - count % 2, 0, -2))


def hop_counts(count, chunk):
    far, near = count // 2, (count - 1) // 2
    return (near, far) if chunk % 2 else (far, near)


def gather_sends(count):
    sends = []
    for hop in range(1, count // 2 + 1):
        for flip in (0, 1):
            for chunk in range(chunks):
                for way in (1, -1):
                    limit = hop_counts(count, chunk)[0 if way == 1 else 1]
                    if hop <= limit and (chunk % 2 == (way == -1)) == (flip == 0):
                        sends.append((chunk, way, hop))
    return sends


def hop_to(block, send, order):
    count = len(order)
    pairs = [(order[i], order[(i + send[1]) % count]) for i in range(count)]
    return lax.ppermute(block, "net", pairs)


def by_distance(count):
    out = [0]
    for hop in range(1, count // 2 + 1):
        out += [count - hop] if 2 * hop == count else [count - hop, hop]
    return out


def ring_gather(pieces, order):
    count = len(order)
    got = [{0: p} for p in pieces]
    held = {}
    for send in gather_sends(count):
        chunk, way, hop = send
        block = hop_to(held.get((chunk, way), pieces[chunk]), send, order)
        held[chunk, way] = block
        got[chunk][(-way * hop) % count] = block
    return got


def ring_scatter(part, order):
    count = len(order)
    held = {}
    for send in reversed(gather_sends(count)):
        chunk, way, hop = send
        mine = part[chunk][(way * hop) % count]
        if (chunk, way) in held:
            mine = mine + held[chunk, way].astype(jnp.float32)
        held[chunk, way] = hop_to(mine.astype(jnp.bfloat16), send, order)
    totals = []
    for chunk in range(chunks):
        total = part[chunk][0]
        for way in (1, -1):
            if (chunk, way) in held:
                total = total + held[chunk, way].astype(jnp.float32)
        totals.append(total)
    return totals


def reorder_kernel(at_ref, factors_ref, out_ref, sems):
    width = out_ref.shape[1] // sems.shape[0]
    copies = [
        pltpu.make_async_copy(
            factors_ref.at[:, pl.ds(pl.multiple_of(at_ref[j] * width, width), width)],
            out_ref.at[:, pl.ds(j * width, width)],
            sems.at[j],
        )
        for j in range(sems.shape[0])
    ]
    for copy in copies:
        copy.start()
    for copy in copies:
        copy.wait()


def reorder(factors, at):
    return pl.pallas_call(
        reorder_kernel,
        out_shape=jax.ShapeDtypeStruct(factors.shape, factors.dtype),
        in_specs=[pl.BlockSpec(memory_space=pltpu.SMEM), pl.BlockSpec(memory_space=pl.ANY)],
        out_specs=pl.BlockSpec(memory_space=pltpu.VMEM),
        scratch_shapes=[pltpu.SemaphoreType.DMA((at.shape[0],))],
        compiler_params=pltpu.CompilerParams(vmem_limit_bytes=20 << 20),
        cost_estimate=pl.CostEstimate(flops=0, transcendentals=0, bytes_accessed=2 * factors.size * factors.dtype.itemsize),
    )(at, factors)


def limits_of(outage_line, ratings):
    levels = lax.broadcasted_iota(jnp.int32, (outage_line.shape[0], ratings.shape[0]), 1)
    return jnp.sum(jnp.where(outage_line[:, None] == levels, ratings[None, :], 0.0), axis=1)


def project(flows, dual, limits):
    bound = limits[:, None]
    kept = jnp.clip(flows + dual, -bound, bound)
    misfit = flows - kept
    return (misfit, dual + misfit)


def total_over(value, axis):
    count = lax.axis_size(axis)
    if count & (count - 1):
        return lax.psum(value, axis)
    bit = 1
    while bit < count:
        value = value + lax.ppermute(value, axis, [(i, i ^ bit) for i in range(count)])
        bit *= 2
    return value


def beside(block, axis):
    count = lax.axis_size(axis)
    first, last = block[:, :1], block[:, -1:]
    zeros = jnp.zeros_like(first)
    if count == 1:
        return zeros, zeros
    if count == 2:
        at = lax.axis_index(axis)
        other = lax.ppermute(jnp.where(at == 0, last, first), axis, [(0, 1), (1, 0)])
        return jnp.where(at == 0, zeros, other), jnp.where(at == 0, other, zeros)
    low = lax.ppermute(last, axis, [(i, i + 1) for i in range(count - 1)])
    high = lax.ppermute(first, axis, [(i + 1, i) for i in range(count - 1)])
    return low, high


def body(proposal, flow_dual, shift_factors, outage_line, ratings, ramp_limit):
    limits = limits_of(outage_line, ratings)
    owned, periods = proposal.shape
    count = lax.axis_size("net")
    ring = count <= longest_ring and count % 2 == 0
    height = owned // chunks
    if ring:
        order = ring_order(count)
        ahead = by_distance(count)
        near = count - 3 if count > 4 else count // 2
        mine = jnp.array([order.index(i) for i in range(count)], jnp.int32)[lax.axis_index("net")]
        at = jnp.array(order, jnp.int32)[(mine + jnp.array(ahead, jnp.int32)) % count]
        factors = reorder(shift_factors, at)
        cut = near * owned

    def forward(pieces):
        pieces = [p.astype(jnp.bfloat16) for p in pieces]
        if not ring:
            whole = lax.all_gather(jnp.concatenate(pieces, axis=0), "net", axis=0, tiled=True)
            return jnp.dot(shift_factors, whole, preferred_element_type=jnp.float32)
        got = ring_gather(pieces, order)
        flows = 0.0
        for group, cols in ((ahead[:near], slice(0, cut)), (ahead[near:], slice(cut, None))):
            blocks = jnp.concatenate([got[c][d] for d in group for c in range(chunks)], axis=0)
            flows = flows + jnp.dot(factors[:, cols], blocks, preferred_element_type=jnp.float32)
        return flows

    def backward(misfit):
        narrow = misfit.astype(jnp.bfloat16)

        def share(cols):
            return lax.dot_general(cols, narrow, (((0,), (0,)), ((), ())), preferred_element_type=jnp.float32)

        if not ring:
            spread = lax.psum_scatter(share(shift_factors), "net", scatter_dimension=0, tiled=True)
            return [spread[c * height : (c + 1) * height] for c in range(chunks)]
        part = [{} for _ in range(chunks)]
        for group, cols in ((ahead[near:], slice(cut, None)), (ahead[:near], slice(0, cut))):
            spread = share(factors[:, cols])
            for j, d in enumerate(group):
                for c in range(chunks):
                    low = j * owned + c * height
                    part[c][d] = spread[low : low + height]
        return ring_scatter(part, order)

    pieces = [proposal[c * height : (c + 1) * height] for c in range(chunks)]
    dual = flow_dual
    sums = []
    for _ in range(passes):
        misfit, dual = project(forward(pieces), dual, limits)
        sums.append(jnp.sum(misfit * misfit))
        pieces = [p - relax_step * s for p, s in zip(pieces, backward(misfit))]
    inject = jnp.concatenate(pieces, axis=0)
    sums = total_over(total_over(jnp.stack(sums), "tm"), "net")
    entries = jnp.float32(shift_factors.shape[0] * count * periods * lax.axis_size("tm"))
    residual_norms = jnp.sqrt(sums / entries)
    low, high = beside(inject, "tm")
    padded = jnp.concatenate([low, inject, high], axis=1)
    step = padded[:, 1:] - padded[:, :-1]
    bound = ramp_limit[:, None]
    moment = lax.axis_index("tm") * periods + lax.broadcasted_iota(jnp.int32, (1, periods + 1), 1)
    valid = (moment >= 1) & (moment <= periods * lax.axis_size("tm") - 1)
    excess = jnp.where(valid, step - jnp.clip(step, -bound, bound), 0.0)
    dispatch = inject - 0.5 * excess[:, :-1] + 0.5 * excess[:, 1:]
    return (dispatch, dual, residual_norms)


def solution(mesh):
    return jax.shard_map(
        body,
        mesh=mesh,
        in_specs=(
            P(("groups", "net"), "tm"),
            P(("groups", "net"), "tm"),
            P("net", None),
            P("net"),
            P(),
            P("net"),
        ),
        out_specs=(P(("groups", "net"), "tm"), P(("groups", "net"), "tm"), P("groups")),
        check_vma=False,
    )
```

time: 329 us -> 152 us (0.46)
  waiting for transfers between devices: 244 us -> 45.2 us
  starting transfers between devices: 4.48 us -> 64.2 us
  blocking collectives: 32.5 us -> 0 us
  between operations: 13.9 us -> 1.11 us
  matrix products: 24.3 us -> 15.6 us
  local copies, waits for them, and re-layouts: 1.22 us -> 8.52 us
  other arithmetic: 7.86 us -> 14.2 us
    reduce_scatter x2 -> x0, waiting for transfers between devices: 142 us -> none  [backward(): lax.psum_scatter(lax.dot_general(shift_factors, narrow, (((0,), (0,)), ((...]
    all_gather x2 -> x0, waiting for transfers between devices: 102 us -> none  [forward(): lax.all_gather(inject.astype(jnp.bfloat16), 'net', axis=0, tiled=True)]
    ppermute x2 -> x61, starting transfers between devices: 4.32 us -> 64.2 us  [the longest x56 60.5 us: hop_to(): return lax.ppermute(block, 'net', pairs)]
    ppermute x2 -> x61, waiting for transfers between devices: 0.01 us -> 45.2 us  [the longest x56 41 us: hop_to(): return lax.ppermute(block, 'net', pairs)]
    psum x1 -> x0, blocking collectives: 32.5 us -> none  [body(): lax.psum((jnp.sum(first * first), jnp.sum(misfit * misfit)), ('net', 'tm'))]
    dot_general x4 -> x8, matrix products: 24.3 us -> 15.6 us  [the longest x4 9.13 us: share(): lax.dot_general(cols, narrow, (((0,), (0,)), ((), ())), preferred_element...]
    unnamed x12 -> x38, local copies, waits for them, and re-layouts: 1.21 us -> 5.83 us
  transfers between devices with their start and end apart: 6 -> 61, of which waited for: 4 -> 31; matrix products, arithmetic and copies ran while one was open for 1% -> 17% of each run, Pallas kernels for 0% -> 2%
where the time goes in v1:
time: 152 us; the launch traced here: 151 us
  starting transfers between devices  64.2 us (42%)
  waiting for transfers between devices  45.2 us (30%)
  matrix products  15.6 us (10%)
  other arithmetic  14.2 us (9%)
  local copies, waits for them, and re-layouts  8.52 us (6%)
  Pallas kernels  2.64 us (2%)
    ppermute x56, starting transfers between devices, hop_to(): return lax.ppermute(block, 'net', pairs)  60.5 us
    ppermute x56, waiting for transfers between devices, hop_to(): return lax.ppermute(block, 'net', pairs)  41 us
    dot_general x4, matrix products, share(): lax.dot_general(cols, narrow, (((0,), (0,)), ((), ())), preferred_element...  9.13 us
    dot_general x4, matrix products, forward(): jnp.dot(factors[:, cols], blocks, preferred_element_type=jnp.float32)  6.43 us
    unnamed x38, local copies, waits for them, and re-layouts  5.83 us
    ppermute x4, waiting for transfers between devices, total_over(): lax.ppermute(value, axis, [(i, i ^ bit) for i in range(count)])  4.25 us
    convert_element_type x8, other arithmetic, ring_scatter(): held[chunk, way] = hop_to(mine.astype(jnp.bfloat16), send, order)  3.79 us
    ppermute x4, starting transfers between devices, total_over(): lax.ppermute(value, axis, [(i, i ^ bit) for i in range(count)])  3.68 us
  transfers between devices with their start and end apart: 61, of which 31 were waited for; matrix products, arithmetic and copies ran while one was open for 17% of the time, Pallas kernels for 2%

profile of v1, /device:TPU:0, one launch (start us, length us, event | category | flops | bytes accessed | tf_op | source)
XLA Modules:
  0.0 151.5 jit_solution(18192508195327140640)
XLA Ops:
  1.6 3.1 %collective-permute-start = (bf16[512,128]{1,0:T(8,128)(2,1)S(1)}, bf16[512,128]{1,0:T(8,128)(2,1)S(1)}, u32[]{:S(2)}, u32[]{:S(2)}) collective-permute-start(bf16[512,128]{1,0:T(8,128)(2,1)S(1)} %get-tuple-element.10), channel_id=1, source_target_pairs={{0,4},{4,8},{8,12},{12,14},{14,10},{10,6},{6,2},{2,0},{1,5},{5,9},... | collective-permute-start | bytes 393224 | tf_op jit(solution)/shard_map/ppermute | solution.py:38
  5.7 2.1 %collective-permute-start.1 = (bf16[512,128]{1,0:T(8,128)(2,1)S(1)}, bf16[512,128]{1,0:T(8,128)(2,1)S(1)}, u32[]{:S(2)}, u32[]{:S(2)}) collective-permute-start(bf16[512,128]{1,0:T(8,128)(2,1)S(1)} %get-tuple-element.8), channel_id=1, source_target_pairs={{0,4},{4,8},{8,12},{12,14},{14,10},{10,6},{6,2},{2,0},{1,5},{5,9},... | collective-permute-start | bytes 393224 | tf_op jit(solution)/shard_map/ppermute | solution.py:38
  9.1 1.3 compare_select_fusion
  11.3 1.3 gather_fusion
  12.6 3.4 %copy-done.1 = bf16[512,8192]{1,0:T(8,128)(2,1)S(1)} copy-done((bf16[512,8192]{1,0:T(8,128)(2,1)S(1)}, bf16[512,8192]{1,0:T(8,128)(2,1)}, u32[]{:S(2)}) %copy-start.1) | copy-done | bytes 8388632
  16.0 2.6 %shard_map.112 = bf16[512,8192]{1,0:T(8,128)(2,1)S(1)} custom-call(s32[8]{0:T(128)S(1)} %gather_fusion, bf16[512,8192]{1,0:T(8,128)(2,1)S(1)} %copy-done.1), custom_call_target="tpu_custom_call" | custom-call | bytes 16777216 | tf_op jit(solution)/shard_map/pallas_call | solution.py:96
  18.7 1.8 %collective-permute-start.4 = (bf16[512,128]{1,0:T(8,128)(2,1)S(1)}, bf16[512,128]{1,0:T(8,128)(2,1)S(1)}, u32[]{:S(2)}, u32[]{:S(2)}) collective-permute-start(bf16[512,128]{1,0:T(8,128)(2,1)S(1)} %collective-permute-done), channel_id=1, source_target_pairs={{0,4},{4,8},{8,12},{12,14},{14,10},{10,6},{6,2},{2,0},{1,5},{5,9},... | collective-permute-start | bytes 393224 | tf_op jit(solution)/shard_map/ppermute | solution.py:38
  20.6 1.4 collective-permute-start.5
  23.1 1.9 %collective-permute-done.4 = bf16[512,128]{1,0:T(8,128)(2,1)S(1)} collective-permute-done((bf16[512,128]{1,0:T(8,128)(2,1)S(1)}, bf16[512,128]{1,0:T(8,128)(2,1)S(1)}, u32[]{:S(2)}, u32[]{:S(2)}) %collective-permute-start.4) | collective-permute-done | bytes 131104 | tf_op jit(solution)/shard_map/ppermute | solution.py:38
  24.9 1.5 collective-permute-start.8
  27.7 1.5 collective-permute-start.9
  29.9 1.5 %fusion.6 = f32[512,128]{1,0:T(8,128)S(1)} fusion(bf16[5120,128]{1,0:T(8,128)(2,1)S(1)} %constant_dynamic-update-slice_fusion, bf16[512,8192]{1,0:T(8,128)(2,1)S(1)} %shard_map.112), kind=kOutput, calls=%fused_computation.7 | convolution fusion | flops 671088640 | bytes 6815744 | tf_op jit(solution)/shard_map/dot_general | solution.py:169
  31.4 1.5 collective-permute-start.10
  33.6 1.8 %collective-permute-done.11 = bf16[512,128]{1,0:T(8,128)(2,1)S(1)} collective-permute-done((bf16[512,128]{1,0:T(8,128)(2,1)S(1)}, bf16[512,128]{1,0:T(8,128)(2,1)S(1)}, u32[]{:S(2)}, u32[]{:S(2)}) %collective-permute-start.11) | collective-permute-done | bytes 131104 | tf_op jit(solution)/shard_map/ppermute | solution.py:38
  38.0 2.3 %collective-permute-done.13 = bf16[512,128]{1,0:T(8,128)(2,1)S(1)} collective-permute-done((bf16[512,128]{1,0:T(8,128)(2,1)S(1)}, bf16[512,128]{1,0:T(8,128)(2,1)S(1)}, u32[]{:S(2)}, u32[]{:S(2)}) %collective-permute-start.13) | collective-permute-done | bytes 131104 | tf_op jit(solution)/shard_map/ppermute | solution.py:38
  42.5 1.4 collective-permute-start.14
  44.5 1.6 %fusion.4 = f32[5120,128]{1,0:T(8,128)S(1)} fusion(bf16[512,8192]{1,0:T(8,128)(2,1)S(1)} %shard_map.112, f32[512,128]{1,0:T(8,128)S(1)} %minimum_subtract_fusion.1), kind=kOutput, calls=%fused_computation.5 | convolution fusion | flops 671154176 | bytes 8126464 | tf_op jit(solution)/shard_map/dot_general | solution.py:176
  46.1 1.4 collective-permute-start.21
  48.9 1.7 %collective-permute-start.15 = (bf16[512,128]{1,0:T(8,128)(2,1)S(1)}, bf16[512,128]{1,0:T(8,128)(2,1)S(1)}, u32[]{:S(2)}, u32[]{:S(2)}) collective-permute-start(bf16[512,128]{1,0:T(8,128)(2,1)S(1)} %get-tuple-element.30), channel_id=1, source_target_pairs={{0,4},{4,8},{8,12},{12,14},{14,10},{10,6},{6,2},{2,0},{1,5},{5,9},... | collective-permute-start | bytes 393224 | tf_op jit(solution)/shard_map/ppermute | solution.py:38
  51.2 1.5 %collective-permute-start.22 = (bf16[512,128]{1,0:T(8,128)(2,1)S(1)}, bf16[512,128]{1,0:T(8,128)(2,1)S(1)}, u32[]{:S(2)}, u32[]{:S(2)}) collective-permute-start(bf16[512,128]{1,0:T(8,128)(2,1)S(1)} %fusion.46), channel_id=1, source_target_pairs={{0,4},{4,8},{8,12},{12,14},{14,10},{10,6},{6,2},{2,0},{1,5},{5,9},... | collective-permute-start | bytes 393224 | tf_op jit(solution)/shard_map/ppermute | solution.py:38
  52.7 1.9 %collective-permute-done.15 = bf16[512,128]{1,0:T(8,128)(2,1)S(1)} collective-permute-done((bf16[512,128]{1,0:T(8,128)(2,1)S(1)}, bf16[512,128]{1,0:T(8,128)(2,1)S(1)}, u32[]{:S(2)}, u32[]{:S(2)}) %collective-permute-start.15) | collective-permute-done | bytes 131104 | tf_op jit(solution)/shard_map/ppermute | solution.py:38
  54.6 2.4 %collective-permute-done.25 = bf16[512,128]{1,0:T(8,128)(2,1)S(1)} collective-permute-done((bf16[512,128]{1,0:T(8,128)(2,1)S(1)}, bf16[512,128]{1,0:T(8,128)(2,1)S(1)}, u32[]{:S(2)}, u32[]{:S(2)}) %collective-permute-start.25) | collective-permute-done | bytes 131104 | tf_op jit(solution)/shard_map/ppermute | solution.py:38
  59.5 4.0 %collective-permute-done.16 = bf16[512,128]{1,0:T(8,128)(2,1)S(1)} collective-permute-done((bf16[512,128]{1,0:T(8,128)(2,1)S(1)}, bf16[512,128]{1,0:T(8,128)(2,1)S(1)}, u32[]{:S(2)}, u32[]{:S(2)}) %collective-permute-start.16) | collective-permute-done | bytes 131104 | tf_op jit(solution)/shard_map/ppermute | solution.py:38
  64.5 1.8 %collective-permute-done.26 = bf16[512,128]{1,0:T(8,128)(2,1)S(1)} collective-permute-done((bf16[512,128]{1,0:T(8,128)(2,1)S(1)}, bf16[512,128]{1,0:T(8,128)(2,1)S(1)}, u32[]{:S(2)}, u32[]{:S(2)}) %collective-permute-start.26) | collective-permute-done | bytes 131104 | tf_op jit(solution)/shard_map/ppermute | solution.py:38
  70.5 2.3 %collective-permute-done.17 = bf16[512,128]{1,0:T(8,128)(2,1)S(1)} collective-permute-done((bf16[512,128]{1,0:T(8,128)(2,1)S(1)}, bf16[512,128]{1,0:T(8,128)(2,1)S(1)}, u32[]{:S(2)}, u32[]{:S(2)}) %collective-permute-start.17) | collective-permute-done | bytes 131104 | tf_op jit(solution)/shard_map/ppermute | solution.py:38
  73.4 2.1 %collective-permute-done.23 = bf16[512,128]{1,0:T(8,128)(2,1)S(1)} collective-permute-done((bf16[512,128]{1,0:T(8,128)(2,1)S(1)}, bf16[512,128]{1,0:T(8,128)(2,1)S(1)}, u32[]{:S(2)}, u32[]{:S(2)}) %collective-permute-start.23) | collective-permute-done | bytes 131104 | tf_op jit(solution)/shard_map/ppermute | solution.py:38
  77.2 1.4 collective-permute-start.30
  79.8 2.0 %collective-permute-done.29 = bf16[512,128]{1,0:T(8,128)(2,1)S(1)} collective-permute-done((bf16[512,128]{1,0:T(8,128)(2,1)S(1)}, bf16[512,128]{1,0:T(8,128)(2,1)S(1)}, u32[]{:S(2)}, u32[]{:S(2)}) %collective-permute-start.29) | collective-permute-done | bytes 131104 | tf_op jit(solution)/shard_map/ppermute | solution.py:38
  86.1 1.6 %collective-permute-start.35 = (bf16[512,128]{1,0:T(8,128)(2,1)S(1)}, bf16[512,128]{1,0:T(8,128)(2,1)S(1)}, u32[]{:S(2)}, u32[]{:S(2)}) collective-permute-start(bf16[512,128]{1,0:T(8,128)(2,1)S(1)} %collective-permute-done.31), channel_id=1, source_target_pairs={{0,2},{4,0},{8,4},{12,8},{14,12},{10,14},{6,10},{2,6},{1,3},{5,1},... | collective-permute-start | bytes 393224 | tf_op jit(solution)/shard_map/ppermute | solution.py:38
  89.4 1.6 %collective-permute-done.35 = bf16[512,128]{1,0:T(8,128)(2,1)S(1)} collective-permute-done((bf16[512,128]{1,0:T(8,128)(2,1)S(1)}, bf16[512,128]{1,0:T(8,128)(2,1)S(1)}, u32[]{:S(2)}, u32[]{:S(2)}) %collective-permute-start.35) | collective-permute-done | bytes 131104 | tf_op jit(solution)/shard_map/ppermute | solution.py:38
  91.1 1.6 %collective-permute-start.39 = (bf16[512,128]{1,0:T(8,128)(2,1)S(1)}, bf16[512,128]{1,0:T(8,128)(2,1)S(1)}, u32[]{:S(2)}, u32[]{:S(2)}) collective-permute-start(bf16[512,128]{1,0:T(8,128)(2,1)S(1)} %collective-permute-done.35), channel_id=1, source_target_pairs={{0,2},{4,0},{8,4},{12,8},{14,12},{10,14},{6,10},{2,6},{1,3},{5,1},... | collective-permute-start | bytes 393224 | tf_op jit(solution)/shard_map/ppermute | solution.py:38
  92.8 1.5 %fusion.2 = f32[512,128]{1,0:T(8,128)S(1)} fusion(bf16[5120,128]{1,0:T(8,128)(2,1)S(1)} %constant_dynamic-update-slice_fusion.16, bf16[512,8192]{1,0:T(8,128)(2,1)S(1)} %shard_map.112), kind=kOutput, calls=%fused_computation.3 | convolution fusion | flops 671088640 | bytes 6815744 | tf_op jit(solution)/shard_map/dot_general | solution.py:169
  96.5 1.6 %collective-permute-start.41 = (bf16[512,128]{1,0:T(8,128)(2,1)S(1)}, bf16[512,128]{1,0:T(8,128)(2,1)S(1)}, u32[]{:S(2)}, u32[]{:S(2)}) collective-permute-start(bf16[512,128]{1,0:T(8,128)(2,1)S(1)} %collective-permute-done.39), channel_id=1, source_target_pairs={{0,2},{4,0},{8,4},{12,8},{14,12},{10,14},{6,10},{2,6},{1,3},{5,1},... | collective-permute-start | bytes 393224 | tf_op jit(solution)/shard_map/ppermute | solution.py:38
  99.4 1.9 %collective-permute-done.40 = bf16[512,128]{1,0:T(8,128)(2,1)S(1)} collective-permute-done((bf16[512,128]{1,0:T(8,128)(2,1)S(1)}, bf16[512,128]{1,0:T(8,128)(2,1)S(1)}, u32[]{:S(2)}, u32[]{:S(2)}) %collective-permute-start.40) | collective-permute-done | bytes 131104 | tf_op jit(solution)/shard_map/ppermute | solution.py:38
  101.5 2.3 %multiply_reduce_fusion.1 = (f32[]{:T(128)}, f32[512,128]{1,0:T(8,128)}, f32[]{:T(128)}, bf16[512,128]{1,0:T(8,128)(2,1)S(1)}) fusion(f32[512,128]{1,0:T(8,128)S(1)} %minimum_subtract_fusion.1, f32[512,128]{1,0:T(8,128)S(1)} %copy-done.5, f32[512]{0:T(512)S(1)} %neg.13, f32[512]{0:T(512)S(1)} %select_reduce_fusion, f32[512,128]{1,0:T(8,128)S(1)} %fusion.2, ...), kind=kOutput, calls=%fused_computation.92 | convolution fusion | flops 403439616 | bytes 5115912 | tf_op jit(solution)/shard_map/dot_general | solution.py:169
  106.9 3.8 %collective-permute-done.42 = bf16[512,128]{1,0:T(8,128)(2,1)S(1)} collective-permute-done((bf16[512,128]{1,0:T(8,128)(2,1)S(1)}, bf16[512,128]{1,0:T(8,128)(2,1)S(1)}, u32[]{:S(2)}, u32[]{:S(2)}) %collective-permute-start.42) | collective-permute-done | bytes 131104 | tf_op jit(solution)/shard_map/ppermute | solution.py:38
  111.9 5.5 %fusion = f32[5120,128]{1,0:T(8,128)} fusion(bf16[512,8192]{1,0:T(8,128)(2,1)} %copy-done, bf16[512,128]{1,0:T(8,128)(2,1)S(1)} %get-tuple-element.48), kind=kOutput, calls=%fused_computation.1 | convolution fusion | flops 671088640 | bytes 7995392 | tf_op jit(solution)/shard_map/dot_general | solution.py:176
  122.5 1.4 pad_maximum_fusion.1
  124.4 2.0 %collective-permute-done.44 = bf16[512,128]{1,0:T(8,128)(2,1)S(1)} collective-permute-done((bf16[512,128]{1,0:T(8,128)(2,1)S(1)}, bf16[512,128]{1,0:T(8,128)(2,1)S(1)}, u32[]{:S(2)}, u32[]{:S(2)}) %collective-permute-start.44) | collective-permute-done | bytes 131104 | tf_op jit(solution)/shard_map/ppermute | solution.py:38
  126.5 1.3 fusion.39
  127.8 1.6 %collective-permute-start.47 = (bf16[512,128]{1,0:T(8,128)(2,1)S(1)}, bf16[512,128]{1,0:T(8,128)(2,1)S(1)}, u32[]{:S(2)}, u32[]{:S(2)}) collective-permute-start(bf16[512,128]{1,0:T(8,128)(2,1)S(1)} %get-tuple-element.16), channel_id=1, source_target_pairs={{0,2},{4,0},{8,4},{12,8},{14,12},{10,14},{6,10},{2,6},{1,3},{5,1},... | collective-permute-start | bytes 393224 | tf_op jit(solution)/shard_map/ppermute | solution.py:38
  129.8 1.6 %collective-permute-start.54 = (bf16[512,128]{1,0:T(8,128)(2,1)S(1)}, bf16[512,128]{1,0:T(8,128)(2,1)S(1)}, u32[]{:S(2)}, u32[]{:S(2)}) collective-permute-start(bf16[512,128]{1,0:T(8,128)(2,1)S(1)} %get-tuple-element.14), channel_id=1, source_target_pairs={{0,2},{4,0},{8,4},{12,8},{14,12},{10,14},{6,10},{2,6},{1,3},{5,1},... | collective-permute-start | bytes 393224 | tf_op jit(solution)/shard_map/ppermute | solution.py:38
  131.4 1.4 fusion.82
  132.8 1.6 %collective-permute-start.58 = (f32[2]{0:T(128)S(1)}, f32[2]{0:T(128)S(1)}, u32[]{:S(2)}, u32[]{:S(2)}) collective-permute-start(f32[2]{0:T(128)S(1)} %fusion.82), channel_id=1, source_target_pairs={{0,2},{2,0},{4,6},{6,4},{8,10},{10,8},{12,14},{14,12},{1,3},{3,1},... | collective-permute-start | bytes 32 | tf_op jit(solution)/shard_map/ppermute | solution.py:125
  139.8 1.4 fusion.83
  142.1 2.6 %collective-permute-done.59 = f32[2]{0:T(128)S(1)} collective-permute-done((f32[2]{0:T(128)S(1)}, f32[2]{0:T(128)S(1)}, u32[]{:S(2)}, u32[]{:S(2)}) %collective-permute-start.59) | collective-permute-done | bytes 40 | tf_op jit(solution)/shard_map/ppermute | solution.py:125
  145.9 1.4 fusion.42
  147.6 1.6 %collective-permute-done.60 = f32[2]{0:T(128)S(1)} collective-permute-done((f32[2]{0:T(128)S(1)}, f32[2]{0:T(128)S(1)}, u32[]{:S(2)}, u32[]{:S(2)}) %collective-permute-start.60) | collective-permute-done | bytes 40 | tf_op jit(solution)/shard_map/ppermute | solution.py:125
  (155 shorter events, 56.4 us)
Async XLA Ops:
  1.6 17.1 %collective-permute-start = (bf16[512,128]{1,0:T(8,128)(2,1)S(1)}, bf16[512,128]{1,0:T(8,128)(2,1)S(1)}, u32[]{:S(2)}, u32[]{:S(2)}) collective-permute-start(bf16[512,128]{1,0:T(8,128)(2,1)S(1)} %get-tuple-element.10), channel_id=1, source_target_pairs={{0,4},{4,8},{8,12},{12,14},{14,10},{10,6},{6,2},{2,0},{1,5},{5,9},... | collective-permute-start | bytes 393224 | tf_op jit(solution)/shard_map/ppermute | solution.py:38
  4.7 17.3 %collective-permute-start.2 = (bf16[512,128]{1,0:T(8,128)(2,1)S(1)}, bf16[512,128]{1,0:T(8,128)(2,1)S(1)}, u32[]{:S(2)}, u32[]{:S(2)}) collective-permute-start(bf16[512,128]{1,0:T(8,128)(2,1)S(1)} %get-tuple-element.10), channel_id=1, source_target_pairs={{0,2},{4,0},{8,4},{12,8},{14,12},{10,14},{6,10},{2,6},{1,3},{5,1},... | collective-permute-start | bytes 393224 | tf_op jit(solution)/shard_map/ppermute | solution.py:38
  5.7 14.8 %collective-permute-start.1 = (bf16[512,128]{1,0:T(8,128)(2,1)S(1)}, bf16[512,128]{1,0:T(8,128)(2,1)S(1)}, u32[]{:S(2)}, u32[]{:S(2)}) collective-permute-start(bf16[512,128]{1,0:T(8,128)(2,1)S(1)} %get-tuple-element.8), channel_id=1, source_target_pairs={{0,4},{4,8},{8,12},{12,14},{14,10},{10,6},{6,2},{2,0},{1,5},{5,9},... | collective-permute-start | bytes 393224 | tf_op jit(solution)/shard_map/ppermute | solution.py:38
  7.8 14.9 %collective-permute-start.3 = (bf16[512,128]{1,0:T(8,128)(2,1)S(1)}, bf16[512,128]{1,0:T(8,128)(2,1)S(1)}, u32[]{:S(2)}, u32[]{:S(2)}) collective-permute-start(bf16[512,128]{1,0:T(8,128)(2,1)S(1)} %get-tuple-element.8), channel_id=1, source_target_pairs={{0,2},{4,0},{8,4},{12,8},{14,12},{10,14},{6,10},{2,6},{1,3},{5,1},... | collective-permute-start | bytes 393224 | tf_op jit(solution)/shard_map/ppermute | solution.py:38
  18.7 6.2 %collective-permute-start.4 = (bf16[512,128]{1,0:T(8,128)(2,1)S(1)}, bf16[512,128]{1,0:T(8,128)(2,1)S(1)}, u32[]{:S(2)}, u32[]{:S(2)}) collective-permute-start(bf16[512,128]{1,0:T(8,128)(2,1)S(1)} %collective-permute-done), channel_id=1, source_target_pairs={{0,4},{4,8},{8,12},{12,14},{14,10},{10,6},{6,2},{2,0},{1,5},{5,9},... | collective-permute-start | bytes 393224 | tf_op jit(solution)/shard_map/ppermute | solution.py:38
  20.6 7.2 %collective-permute-start.5 = (bf16[512,128]{1,0:T(8,128)(2,1)S(1)}, bf16[512,128]{1,0:T(8,128)(2,1)S(1)}, u32[]{:S(2)}, u32[]{:S(2)}) collective-permute-start(bf16[512,128]{1,0:T(8,128)(2,1)S(1)} %collective-permute-done.1), channel_id=1, source_target_pairs={{0,4},{4,8},{8,12},{12,14},{14,10},{10,6},{6,2},{2,0},{1,5},{5,9},... | collective-permute-start | bytes 393224 | tf_op jit(solution)/shard_map/ppermute | solution.py:38
  22.0 7.8 %collective-permute-start.6 = (bf16[512,128]{1,0:T(8,128)(2,1)S(1)}, bf16[512,128]{1,0:T(8,128)(2,1)S(1)}, u32[]{:S(2)}, u32[]{:S(2)}) collective-permute-start(bf16[512,128]{1,0:T(8,128)(2,1)S(1)} %collective-permute-done.2), channel_id=1, source_target_pairs={{0,2},{4,0},{8,4},{12,8},{14,12},{10,14},{6,10},{2,6},{1,3},{5,1},... | collective-permute-start | bytes 393224 | tf_op jit(solution)/shard_map/ppermute | solution.py:38
  22.8 6.5 %collective-permute-start.7 = (bf16[512,128]{1,0:T(8,128)(2,1)S(1)}, bf16[512,128]{1,0:T(8,128)(2,1)S(1)}, u32[]{:S(2)}, u32[]{:S(2)}) collective-permute-start(bf16[512,128]{1,0:T(8,128)(2,1)S(1)} %collective-permute-done.3), channel_id=1, source_target_pairs={{0,2},{4,0},{8,4},{12,8},{14,12},{10,14},{6,10},{2,6},{1,3},{5,1},... | collective-permute-start | bytes 393224 | tf_op jit(solution)/shard_map/ppermute | solution.py:38
  24.9 8.0 %collective-permute-start.8 = (bf16[512,128]{1,0:T(8,128)(2,1)S(1)}, bf16[512,128]{1,0:T(8,128)(2,1)S(1)}, u32[]{:S(2)}, u32[]{:S(2)}) collective-permute-start(bf16[512,128]{1,0:T(8,128)(2,1)S(1)} %collective-permute-done.4), channel_id=1, source_target_pairs={{0,4},{4,8},{8,12},{12,14},{14,10},{10,6},{6,2},{2,0},{1,5},{5,9},... | collective-permute-start | bytes 393224 | tf_op jit(solution)/shard_map/ppermute | solution.py:38
  27.7 8.3 %collective-permute-start.9 = (bf16[512,128]{1,0:T(8,128)(2,1)S(1)}, bf16[512,128]{1,0:T(8,128)(2,1)S(1)}, u32[]{:S(2)}, u32[]{:S(2)}) collective-permute-start(bf16[512,128]{1,0:T(8,128)(2,1)S(1)} %collective-permute-done.5), channel_id=1, source_target_pairs={{0,4},{4,8},{8,12},{12,14},{14,10},{10,6},{6,2},{2,0},{1,5},{5,9},... | collective-permute-start | bytes 393224 | tf_op jit(solution)/shard_map/ppermute | solution.py:38
  29.3 6.1 %collective-permute-start.11 = (bf16[512,128]{1,0:T(8,128)(2,1)S(1)}, bf16[512,128]{1,0:T(8,128)(2,1)S(1)}, u32[]{:S(2)}, u32[]{:S(2)}) collective-permute-start(bf16[512,128]{1,0:T(8,128)(2,1)S(1)} %collective-permute-done.7), channel_id=1, source_target_pairs={{0,2},{4,0},{8,4},{12,8},{14,12},{10,14},{6,10},{2,6},{1,3},{5,1},... | collective-permute-start | bytes 393224 | tf_op jit(solution)/shard_map/ppermute | solution.py:38
  31.4 5.3 %collective-permute-start.10 = (bf16[512,128]{1,0:T(8,128)(2,1)S(1)}, bf16[512,128]{1,0:T(8,128)(2,1)S(1)}, u32[]{:S(2)}, u32[]{:S(2)}) collective-permute-start(bf16[512,128]{1,0:T(8,128)(2,1)S(1)} %collective-permute-done.6), channel_id=1, source_target_pairs={{0,2},{4,0},{8,4},{12,8},{14,12},{10,14},{6,10},{2,6},{1,3},{5,1},... | collective-permute-start | bytes 393224 | tf_op jit(solution)/shard_map/ppermute | solution.py:38
  42.5 6.1 %collective-permute-start.14 = (bf16[512,128]{1,0:T(8,128)(2,1)S(1)}, bf16[512,128]{1,0:T(8,128)(2,1)S(1)}, u32[]{:S(2)}, u32[]{:S(2)}) collective-permute-start(bf16[512,128]{1,0:T(8,128)(2,1)S(1)} %get-tuple-element.38), channel_id=1, source_target_pairs={{0,4},{4,8},{8,12},{12,14},{14,10},{10,6},{6,2},{2,0},{1,5},{5,9},... | collective-permute-start | bytes 393224 | tf_op jit(solution)/shard_map/ppermute | solution.py:38
  47.5 5.2 %collective-permute-start.18 = (bf16[512,128]{1,0:T(8,128)(2,1)S(1)}, bf16[512,128]{1,0:T(8,128)(2,1)S(1)}, u32[]{:S(2)}, u32[]{:S(2)}) collective-permute-start(bf16[512,128]{1,0:T(8,128)(2,1)S(1)} %get-tuple-element.37), channel_id=1, source_target_pairs={{0,2},{4,0},{8,4},{12,8},{14,12},{10,14},{6,10},{2,6},{1,3},{5,1},... | collective-permute-start | bytes 393224 | tf_op jit(solution)/shard_map/ppermute | solution.py:38
  48.9 5.7 %collective-permute-start.15 = (bf16[512,128]{1,0:T(8,128)(2,1)S(1)}, bf16[512,128]{1,0:T(8,128)(2,1)S(1)}, u32[]{:S(2)}, u32[]{:S(2)}) collective-permute-start(bf16[512,128]{1,0:T(8,128)(2,1)S(1)} %get-tuple-element.30), channel_id=1, source_target_pairs={{0,4},{4,8},{8,12},{12,14},{14,10},{10,6},{6,2},{2,0},{1,5},{5,9},... | collective-permute-start | bytes 393224 | tf_op jit(solution)/shard_map/ppermute | solution.py:38
  50.6 6.4 %collective-permute-start.25 = (bf16[512,128]{1,0:T(8,128)(2,1)S(1)}, bf16[512,128]{1,0:T(8,128)(2,1)S(1)}, u32[]{:S(2)}, u32[]{:S(2)}) collective-permute-start(bf16[512,128]{1,0:T(8,128)(2,1)S(1)} %get-tuple-element.29), channel_id=1, source_target_pairs={{0,2},{4,0},{8,4},{12,8},{14,12},{10,14},{6,10},{2,6},{1,3},{5,1},... | collective-permute-start | bytes 393224 | tf_op jit(solution)/shard_map/ppermute | solution.py:38
  51.2 5.8 %collective-permute-start.22 = (bf16[512,128]{1,0:T(8,128)(2,1)S(1)}, bf16[512,128]{1,0:T(8,128)(2,1)S(1)}, u32[]{:S(2)}, u32[]{:S(2)}) collective-permute-start(bf16[512,128]{1,0:T(8,128)(2,1)S(1)} %fusion.46), channel_id=1, source_target_pairs={{0,4},{4,8},{8,12},{12,14},{14,10},{10,6},{6,2},{2,0},{1,5},{5,9},... | collective-permute-start | bytes 393224 | tf_op jit(solution)/shard_map/ppermute | solution.py:38
  57.1 6.4 %collective-permute-start.16 = (bf16[512,128]{1,0:T(8,128)(2,1)S(1)}, bf16[512,128]{1,0:T(8,128)(2,1)S(1)}, u32[]{:S(2)}, u32[]{:S(2)}) collective-permute-start(bf16[512,128]{1,0:T(8,128)(2,1)S(1)} %get-tuple-element.23), channel_id=1, source_target_pairs={{0,4},{4,8},{8,12},{12,14},{14,10},{10,6},{6,2},{2,0},{1,5},{5,9},... | collective-permute-start | bytes 393224 | tf_op jit(solution)/shard_map/ppermute | solution.py:38
  58.1 6.4 %collective-permute-start.19 = (bf16[512,128]{1,0:T(8,128)(2,1)S(1)}, bf16[512,128]{1,0:T(8,128)(2,1)S(1)}, u32[]{:S(2)}, u32[]{:S(2)}) collective-permute-start(bf16[512,128]{1,0:T(8,128)(2,1)S(1)} %get-tuple-element.22), channel_id=1, source_target_pairs={{0,2},{4,0},{8,4},{12,8},{14,12},{10,14},{6,10},{2,6},{1,3},{5,1},... | collective-permute-start | bytes 393224 | tf_op jit(solution)/shard_map/ppermute | solution.py:38
  59.2 7.1 %collective-permute-start.26 = (bf16[512,128]{1,0:T(8,128)(2,1)S(1)}, bf16[512,128]{1,0:T(8,128)(2,1)S(1)}, u32[]{:S(2)}, u32[]{:S(2)}) collective-permute-start(bf16[512,128]{1,0:T(8,128)(2,1)S(1)} %get-tuple-element.21), channel_id=1, source_target_pairs={{0,2},{4,0},{8,4},{12,8},{14,12},{10,14},{6,10},{2,6},{1,3},{5,1},... | collective-permute-start | bytes 393224 | tf_op jit(solution)/shard_map/ppermute | solution.py:38
  66.4 6.4 %collective-permute-start.17 = (bf16[512,128]{1,0:T(8,128)(2,1)S(1)}, bf16[512,128]{1,0:T(8,128)(2,1)S(1)}, u32[]{:S(2)}, u32[]{:S(2)}) collective-permute-start(bf16[512,128]{1,0:T(8,128)(2,1)S(1)} %get-tuple-element.26), channel_id=1, source_target_pairs={{0,4},{4,8},{8,12},{12,14},{14,10},{10,6},{6,2},{2,0},{1,5},{5,9},... | collective-permute-start | bytes 393224 | tf_op jit(solution)/shard_map/ppermute | solution.py:38
  67.6 5.8 %collective-permute-start.20 = (bf16[512,128]{1,0:T(8,128)(2,1)S(1)}, bf16[512,128]{1,0:T(8,128)(2,1)S(1)}, u32[]{:S(2)}, u32[]{:S(2)}) collective-permute-start(bf16[512,128]{1,0:T(8,128)(2,1)S(1)} %get-tuple-element.25), channel_id=1, source_target_pairs={{0,2},{4,0},{8,4},{12,8},{14,12},{10,14},{6,10},{2,6},{1,3},{5,1},... | collective-permute-start | bytes 393224 | tf_op jit(solution)/shard_map/ppermute | solution.py:38
  68.5 7.1 %collective-permute-start.23 = (bf16[512,128]{1,0:T(8,128)(2,1)S(1)}, bf16[512,128]{1,0:T(8,128)(2,1)S(1)}, u32[]{:S(2)}, u32[]{:S(2)}) collective-permute-start(bf16[512,128]{1,0:T(8,128)(2,1)S(1)} %get-tuple-element.20), channel_id=1, source_target_pairs={{0,4},{4,8},{8,12},{12,14},{14,10},{10,6},{6,2},{2,0},{1,5},{5,9},... | collective-permute-start | bytes 393224 | tf_op jit(solution)/shard_map/ppermute | solution.py:38
  69.6 6.0 %collective-permute-start.27 = (bf16[512,128]{1,0:T(8,128)(2,1)S(1)}, bf16[512,128]{1,0:T(8,128)(2,1)S(1)}, u32[]{:S(2)}, u32[]{:S(2)}) collective-permute-start(bf16[512,128]{1,0:T(8,128)(2,1)S(1)} %get-tuple-element.24), channel_id=1, source_target_pairs={{0,2},{4,0},{8,4},{12,8},{14,12},{10,14},{6,10},{2,6},{1,3},{5,1},... | collective-permute-start | bytes 393224 | tf_op jit(solution)/shard_map/ppermute | solution.py:38
  75.7 6.1 %collective-permute-start.29 = (bf16[512,128]{1,0:T(8,128)(2,1)S(1)}, bf16[512,128]{1,0:T(8,128)(2,1)S(1)}, u32[]{:S(2)}, u32[]{:S(2)}) collective-permute-start(bf16[512,128]{1,0:T(8,128)(2,1)S(1)} %get-tuple-element.4), channel_id=1, source_target_pairs={{0,4},{4,8},{8,12},{12,14},{14,10},{10,6},{6,2},{2,0},{1,5},{5,9},... | collective-permute-start | bytes 393224 | tf_op jit(solution)/shard_map/ppermute | solution.py:38
  76.7 6.5 %collective-permute-start.28 = (bf16[512,128]{1,0:T(8,128)(2,1)S(1)}, bf16[512,128]{1,0:T(8,128)(2,1)S(1)}, u32[]{:S(2)}, u32[]{:S(2)}) collective-permute-start(bf16[512,128]{1,0:T(8,128)(2,1)S(1)} %get-tuple-element.6), channel_id=1, source_target_pairs={{0,4},{4,8},{8,12},{12,14},{14,10},{10,6},{6,2},{2,0},{1,5},{5,9},... | collective-permute-start | bytes 393224 | tf_op jit(solution)/shard_map/ppermute | solution.py:38
  77.2 6.9 %collective-permute-start.30 = (bf16[512,128]{1,0:T(8,128)(2,1)S(1)}, bf16[512,128]{1,0:T(8,128)(2,1)S(1)}, u32[]{:S(2)}, u32[]{:S(2)}) collective-permute-start(bf16[512,128]{1,0:T(8,128)(2,1)S(1)} %get-tuple-element.6), channel_id=1, source_target_pairs={{0,2},{4,0},{8,4},{12,8},{14,12},{10,14},{6,10},{2,6},{1,3},{5,1},... | collective-permute-start | bytes 393224 | tf_op jit(solution)/shard_map/ppermute | solution.py:38
  78.7 7.4 %collective-permute-start.31 = (bf16[512,128]{1,0:T(8,128)(2,1)S(1)}, bf16[512,128]{1,0:T(8,128)(2,1)S(1)}, u32[]{:S(2)}, u32[]{:S(2)}) collective-permute-start(bf16[512,128]{1,0:T(8,128)(2,1)S(1)} %get-tuple-element.4), channel_id=1, source_target_pairs={{0,2},{4,0},{8,4},{12,8},{14,12},{10,14},{6,10},{2,6},{1,3},{5,1},... | collective-permute-start | bytes 393224 | tf_op jit(solution)/shard_map/ppermute | solution.py:38
  81.8 6.0 %collective-permute-start.33 = (bf16[512,128]{1,0:T(8,128)(2,1)S(1)}, bf16[512,128]{1,0:T(8,128)(2,1)S(1)}, u32[]{:S(2)}, u32[]{:S(2)}) collective-permute-start(bf16[512,128]{1,0:T(8,128)(2,1)S(1)} %collective-permute-done.29), channel_id=1, source_target_pairs={{0,4},{4,8},{8,12},{12,14},{14,10},{10,6},{6,2},{2,0},{1,5},{5,9},... | collective-permute-start | bytes 393224 | tf_op jit(solution)/shard_map/ppermute | solution.py:38
  83.2 5.3 %collective-permute-start.32 = (bf16[512,128]{1,0:T(8,128)(2,1)S(1)}, bf16[512,128]{1,0:T(8,128)(2,1)S(1)}, u32[]{:S(2)}, u32[]{:S(2)}) collective-permute-start(bf16[512,128]{1,0:T(8,128)(2,1)S(1)} %collective-permute-done.28), channel_id=1, source_target_pairs={{0,4},{4,8},{8,12},{12,14},{14,10},{10,6},{6,2},{2,0},{1,5},{5,9},... | collective-permute-start | bytes 393224 | tf_op jit(solution)/shard_map/ppermute | solution.py:38
  84.2 8.5 %collective-permute-start.34 = (bf16[512,128]{1,0:T(8,128)(2,1)S(1)}, bf16[512,128]{1,0:T(8,128)(2,1)S(1)}, u32[]{:S(2)}, u32[]{:S(2)}) collective-permute-start(bf16[512,128]{1,0:T(8,128)(2,1)S(1)} %collective-permute-done.30), channel_id=1, source_target_pairs={{0,2},{4,0},{8,4},{12,8},{14,12},{10,14},{6,10},{2,6},{1,3},{5,1},... | collective-permute-start | bytes 393224 | tf_op jit(solution)/shard_map/ppermute | solution.py:38
  87.8 10.3 %collective-permute-start.37 = (bf16[512,128]{1,0:T(8,128)(2,1)S(1)}, bf16[512,128]{1,0:T(8,128)(2,1)S(1)}, u32[]{:S(2)}, u32[]{:S(2)}) collective-permute-start(bf16[512,128]{1,0:T(8,128)(2,1)S(1)} %collective-permute-done.33), channel_id=1, source_target_pairs={{0,4},{4,8},{8,12},{12,14},{14,10},{10,6},{6,2},{2,0},{1,5},{5,9},... | collective-permute-start | bytes 393224 | tf_op jit(solution)/shard_map/ppermute | solution.py:38
  88.5 6.8 %collective-permute-start.36 = (bf16[512,128]{1,0:T(8,128)(2,1)S(1)}, bf16[512,128]{1,0:T(8,128)(2,1)S(1)}, u32[]{:S(2)}, u32[]{:S(2)}) collective-permute-start(bf16[512,128]{1,0:T(8,128)(2,1)S(1)} %collective-permute-done.32), channel_id=1, source_target_pairs={{0,4},{4,8},{8,12},{12,14},{14,10},{10,6},{6,2},{2,0},{1,5},{5,9},... | collective-permute-start | bytes 393224 | tf_op jit(solution)/shard_map/ppermute | solution.py:38
  91.1 5.4 %collective-permute-start.39 = (bf16[512,128]{1,0:T(8,128)(2,1)S(1)}, bf16[512,128]{1,0:T(8,128)(2,1)S(1)}, u32[]{:S(2)}, u32[]{:S(2)}) collective-permute-start(bf16[512,128]{1,0:T(8,128)(2,1)S(1)} %collective-permute-done.35), channel_id=1, source_target_pairs={{0,2},{4,0},{8,4},{12,8},{14,12},{10,14},{6,10},{2,6},{1,3},{5,1},... | collective-permute-start | bytes 393224 | tf_op jit(solution)/shard_map/ppermute | solution.py:38
  95.3 6.0 %collective-permute-start.40 = (bf16[512,128]{1,0:T(8,128)(2,1)S(1)}, bf16[512,128]{1,0:T(8,128)(2,1)S(1)}, u32[]{:S(2)}, u32[]{:S(2)}) collective-permute-start(bf16[512,128]{1,0:T(8,128)(2,1)S(1)} %collective-permute-done.36), channel_id=1, source_target_pairs={{0,4},{4,8},{8,12},{12,14},{14,10},{10,6},{6,2},{2,0},{1,5},{5,9},... | collective-permute-start | bytes 393224 | tf_op jit(solution)/shard_map/ppermute | solution.py:38
  104.9 5.9 %collective-permute-start.42 = (bf16[512,128]{1,0:T(8,128)(2,1)S(1)}, bf16[512,128]{1,0:T(8,128)(2,1)S(1)}, u32[]{:S(2)}, u32[]{:S(2)}) collective-permute-start(bf16[512,128]{1,0:T(8,128)(2,1)S(1)} %get-tuple-element.31), channel_id=1, source_target_pairs={{0,4},{4,8},{8,12},{12,14},{14,10},{10,6},{6,2},{2,0},{1,5},{5,9},... | collective-permute-start | bytes 393224 | tf_op jit(solution)/shard_map/ppermute | solution.py:38
  110.8 9.6 %collective-permute-start.43 = (bf16[512,128]{1,0:T(8,128)(2,1)S(1)}, bf16[512,128]{1,0:T(8,128)(2,1)S(1)}, u32[]{:S(2)}, u32[]{:S(2)}) collective-permute-start(bf16[512,128]{1,0:T(8,128)(2,1)S(1)} %get-tuple-element.27), channel_id=1, source_target_pairs={{0,4},{4,8},{8,12},{12,14},{14,10},{10,6},{6,2},{2,0},{1,5},{5,9},... | collective-permute-start | bytes 393224 | tf_op jit(solution)/shard_map/ppermute | solution.py:38
  117.4 6.5 %collective-permute-start.46 = (bf16[512,128]{1,0:T(8,128)(2,1)S(1)}, bf16[512,128]{1,0:T(8,128)(2,1)S(1)}, u32[]{:S(2)}, u32[]{:S(2)}) collective-permute-start(bf16[512,128]{1,0:T(8,128)(2,1)S(1)} %get-tuple-element.34), channel_id=1, source_target_pairs={{0,2},{4,0},{8,4},{12,8},{14,12},{10,14},{6,10},{2,6},{1,3},{5,1},... | collective-permute-start | bytes 393224 | tf_op jit(solution)/shard_map/ppermute | solution.py:38
  118.4 5.5 %collective-permute-start.49 = (bf16[512,128]{1,0:T(8,128)(2,1)S(1)}, bf16[512,128]{1,0:T(8,128)(2,1)S(1)}, u32[]{:S(2)}, u32[]{:S(2)}) collective-permute-start(bf16[512,128]{1,0:T(8,128)(2,1)S(1)} %get-tuple-element.33), channel_id=1, source_target_pairs={{0,4},{4,8},{8,12},{12,14},{14,10},{10,6},{6,2},{2,0},{1,5},{5,9},... | collective-permute-start | bytes 393224 | tf_op jit(solution)/shard_map/ppermute | solution.py:38
  123.9 7.5 %collective-permute-start.57 = (f32[2]{0:T(128)S(1)}, f32[2]{0:T(128)S(1)}, u32[]{:S(2)}, u32[]{:S(2)}) collective-permute-start(f32[2]{0:T(128)S(1)} %pad_maximum_fusion.1), channel_id=1, source_target_pairs={{0,1},{1,0},{2,3},{3,2},{4,5},{5,4},{6,7},{7,6},{8,9},{9,8},{10,11... | collective-permute-start | bytes 32 | tf_op jit(solution)/shard_map/ppermute | solution.py:125
  127.8 7.5 %collective-permute-start.47 = (bf16[512,128]{1,0:T(8,128)(2,1)S(1)}, bf16[512,128]{1,0:T(8,128)(2,1)S(1)}, u32[]{:S(2)}, u32[]{:S(2)}) collective-permute-start(bf16[512,128]{1,0:T(8,128)(2,1)S(1)} %get-tuple-element.16), channel_id=1, source_target_pairs={{0,2},{4,0},{8,4},{12,8},{14,12},{10,14},{6,10},{2,6},{1,3},{5,1},... | collective-permute-start | bytes 393224 | tf_op jit(solution)/shard_map/ppermute | solution.py:38
  129.4 6.1 %collective-permute-start.50 = (bf16[512,128]{1,0:T(8,128)(2,1)S(1)}, bf16[512,128]{1,0:T(8,128)(2,1)S(1)}, u32[]{:S(2)}, u32[]{:S(2)}) collective-permute-start(bf16[512,128]{1,0:T(8,128)(2,1)S(1)} %get-tuple-element.15), channel_id=1, source_target_pairs={{0,4},{4,8},{8,12},{12,14},{14,10},{10,6},{6,2},{2,0},{1,5},{5,9},... | collective-permute-start | bytes 393224 | tf_op jit(solution)/shard_map/ppermute | solution.py:38
  129.8 5.6 %collective-permute-start.54 = (bf16[512,128]{1,0:T(8,128)(2,1)S(1)}, bf16[512,128]{1,0:T(8,128)(2,1)S(1)}, u32[]{:S(2)}, u32[]{:S(2)}) collective-permute-start(bf16[512,128]{1,0:T(8,128)(2,1)S(1)} %get-tuple-element.14), channel_id=1, source_target_pairs={{0,2},{4,0},{8,4},{12,8},{14,12},{10,14},{6,10},{2,6},{1,3},{5,1},... | collective-permute-start | bytes 393224 | tf_op jit(solution)/shard_map/ppermute | solution.py:38
  132.8 7.0 %collective-permute-start.58 = (f32[2]{0:T(128)S(1)}, f32[2]{0:T(128)S(1)}, u32[]{:S(2)}, u32[]{:S(2)}) collective-permute-start(f32[2]{0:T(128)S(1)} %fusion.82), channel_id=1, source_target_pairs={{0,2},{2,0},{4,6},{6,4},{8,10},{10,8},{12,14},{14,12},{1,3},{3,1},... | collective-permute-start | bytes 32 | tf_op jit(solution)/shard_map/ppermute | solution.py:125
  134.4 11.5 %collective-permute-start.45 = (bf16[512,128]{1,0:T(8,128)(2,1)S(1)}, bf16[512,128]{1,0:T(8,128)(2,1)S(1)}, u32[]{:S(2)}, u32[]{:S(2)}) collective-permute-start(bf16[512,128]{1,0:T(8,128)(2,1)S(1)} %get-tuple-element.13), channel_id=1, source_target_pairs={{0,4},{4,8},{8,12},{12,14},{14,10},{10,6},{6,2},{2,0},{1,5},{5,9},... | collective-permute-start | bytes 393224 | tf_op jit(solution)/shard_map/ppermute | solution.py:38
  136.6 9.2 %collective-permute-start.48 = (bf16[512,128]{1,0:T(8,128)(2,1)S(1)}, bf16[512,128]{1,0:T(8,128)(2,1)S(1)}, u32[]{:S(2)}, u32[]{:S(2)}) collective-permute-start(bf16[512,128]{1,0:T(8,128)(2,1)S(1)} %get-tuple-element.17), channel_id=1, source_target_pairs={{0,2},{4,0},{8,4},{12,8},{14,12},{10,14},{6,10},{2,6},{1,3},{5,1},... | collective-permute-start | bytes 393224 | tf_op jit(solution)/shard_map/ppermute | solution.py:38
  137.8 8.1 %collective-permute-start.51 = (bf16[512,128]{1,0:T(8,128)(2,1)S(1)}, bf16[512,128]{1,0:T(8,128)(2,1)S(1)}, u32[]{:S(2)}, u32[]{:S(2)}) collective-permute-start(bf16[512,128]{1,0:T(8,128)(2,1)S(1)} %get-tuple-element.19), channel_id=1, source_target_pairs={{0,4},{4,8},{8,12},{12,14},{14,10},{10,6},{6,2},{2,0},{1,5},{5,9},... | collective-permute-start | bytes 393224 | tf_op jit(solution)/shard_map/ppermute | solution.py:38
  138.7 7.2 %collective-permute-start.55 = (bf16[512,128]{1,0:T(8,128)(2,1)S(1)}, bf16[512,128]{1,0:T(8,128)(2,1)S(1)}, u32[]{:S(2)}, u32[]{:S(2)}) collective-permute-start(bf16[512,128]{1,0:T(8,128)(2,1)S(1)} %get-tuple-element.18), channel_id=1, source_target_pairs={{0,2},{4,0},{8,4},{12,8},{14,12},{10,14},{6,10},{2,6},{1,3},{5,1},... | collective-permute-start | bytes 393224 | tf_op jit(solution)/shard_map/ppermute | solution.py:38
  (19 other events, 215.1 us)

commit v2 on v1

--- a/solution.py
+++ b/solution.py
@@ -1,3 +1,5 @@
+import functools
+
 import jax
 import jax.numpy as jnp
 from jax import lax
@@ -32,6 +34,10 @@
     return sends
 
 
+def scatter_sends(count):
+    return gather_sends(count)[::-1]
+
+
 def hop_to(block, send, order):
     count = len(order)
     pairs = [(order[i], order[(i + send[1]) % count]) for i in range(count)]
@@ -57,51 +63,89 @@
     return got
 
 
-def ring_scatter(part, order):
+def whole_in_vmem(count):
+    return [pl.BlockSpec(memory_space=pltpu.VMEM)] * count
+
+
+def small_call(kernel, out_shape, *operands):
+    touched = sum(x.size * x.dtype.itemsize for x in jax.tree.leaves(out_shape)) * 3
+    return pl.pallas_call(
+        kernel,
+        out_shape=out_shape,
+        in_specs=whole_in_vmem(len(operands)),
+        out_specs=jax.tree.map(lambda _: pl.BlockSpec(memory_space=pltpu.VMEM), out_shape),
+        compiler_params=pltpu.CompilerParams(vmem_limit_bytes=16 << 20),
+        cost_estimate=pl.CostEstimate(flops=0, transcendentals=0, bytes_accessed=touched),
+    )(*operands)
+
+
+def sum_kernel(low, spread_ref, arrived_ref, out_ref):
+    mine = spread_ref[pl.ds(low, out_ref.shape[0]), :]
+    out_ref[...] = (mine + arrived_ref[...].astype(jnp.float32)).astype(out_ref.dtype)
+
+
+def update_kernel(low, spread_ref, ahead_ref, behind_ref, inject_ref, *out_refs):
+    total = spread_ref[pl.ds(low, inject_ref.shape[0]), :]
+    total = total + ahead_ref[...].astype(jnp.float32) + behind_ref[...].astype(jnp.float32)
+    inject = inject_ref[...] - relax_step * total
+    for ref in out_refs:
+        ref[...] = inject.astype(ref.dtype)
+
+
+def ring_scatter(part, order, height):
     count = len(order)
     held = {}
-    for send in reversed(gather_sends(count)):
+    for send in scatter_sends(count):
         chunk, way, hop = send
-        mine = part[chunk][(way * hop) % count]
+        spread, low = part(chunk, (way * hop) % count)
         if (chunk, way) in held:
-            mine = mine + held[chunk, way].astype(jnp.float32)
-        held[chunk, way] = hop_to(mine.astype(jnp.bfloat16), send, order)
-    totals = []
-    for chunk in range(chunks):
-        total = part[chunk][0]
-        for way in (1, -1):
-            if (chunk, way) in held:
-                total = total + held[chunk, way].astype(jnp.float32)
-        totals.append(total)
-    return totals
-
-
-def reorder_kernel(at_ref, factors_ref, out_ref, sems):
-    width = out_ref.shape[1] // sems.shape[0]
-    copies = [
-        pltpu.make_async_copy(
-            factors_ref.at[:, pl.ds(pl.multiple_of(at_ref[j] * width, width), width)],
-            out_ref.at[:, pl.ds(j * width, width)],
-            sems.at[j],
+            arrived = held[chunk, way]
+            shape = jax.ShapeDtypeStruct(arrived.shape, arrived.dtype)
+            mine = small_call(functools.partial(sum_kernel, low), shape, spread, arrived)
+        else:
+            mine = spread[low : low + height].astype(jnp.bfloat16)
+        held[chunk, way] = hop_to(mine, send, order)
+    return held
+
+
+def place_of(position, count):
+    return jnp.where(position % 2 == 0, position // 2, count - 1 - position // 2)
+
+
+def at_place(place, count):
+    return jnp.where(place < count // 2, 2 * place, 2 * (count - place) - 1)
+
+
+def reorder_kernel(ahead, here_ref, factors_ref, out_ref, sems):
+    count = len(ahead)
+    width = out_ref.shape[1] // count
+    mine = place_of(here_ref[0], count)
+    copies = []
+    for j, distance in enumerate(ahead):
+        source = at_place((mine + distance) % count, count) * width
+        copies.append(
+            pltpu.make_async_copy(
+                factors_ref.at[:, pl.ds(pl.multiple_of(source, width), width)],
+                out_ref.at[:, pl.ds(j * width, width)],
+                sems.at[j],
+            )
         )
-        for j in range(sems.shape[0])
-    ]
     for copy in copies:
         copy.start()
     for copy in copies:
         copy.wait()
 
 
-def reorder(factors, at):
+def reorder(factors, ahead):
     return pl.pallas_call(
-        reorder_kernel,
+        functools.partial(reorder_kernel, tuple(ahead)),
         out_shape=jax.ShapeDtypeStruct(factors.shape, factors.dtype),
-        in_specs=[pl.BlockSpec(memory_space=pltpu.SMEM), pl.BlockSpec(memory_space=pl.ANY)],
+        in_specs=[pl.BlockSpec(memory_space=pltpu.SMEM), pl.BlockSpec(memory_space=pltpu.HBM)],
         out_specs=pl.BlockSpec(memory_space=pltpu.VMEM),
-        scratch_shapes=[pltpu.SemaphoreType.DMA((at.shape[0],))],
+        scratch_shapes=[pltpu.SemaphoreType.DMA((len(ahead),))],
         compiler_params=pltpu.CompilerParams(vmem_limit_bytes=20 << 20),
-        cost_estimate=pl.CostEstimate(flops=0, transcendentals=0, bytes_accessed=2 * factors.size * factors.dtype.itemsize),
-    )(at, factors)
+        cost_estimate=pl.CostEstimate(flops=0, transcendentals=0, bytes_accessed=factors.size * factors.dtype.itemsize),
+    )(lax.axis_index("net").reshape(1), factors)
 
 
 def limits_of(outage_line, ratings):
@@ -116,14 +160,21 @@
     return (misfit, dual + misfit)
 
 
-def total_over(value, axis):
-    count = lax.axis_size(axis)
-    if count & (count - 1):
-        return lax.psum(value, axis)
-    bit = 1
-    while bit < count:
-        value = value + lax.ppermute(value, axis, [(i, i ^ bit) for i in range(count)])
-        bit *= 2
+def exchanges(axes):
+    out = []
+    for axis, count in axes:
+        if count & (count - 1):
+            return None
+        out += [(axis, 1 << k) for k in range(count.bit_length() - 1)]
+    return out
+
+
+def total_over(value, axes):
+    steps = exchanges([(axis, lax.axis_size(axis)) for axis in axes])
+    if steps is None:
+        return lax.psum(value, axes)
+    for axis, bit in steps:
+        value = value + lax.ppermute(value, axis, [(i, i ^ bit) for i in range(lax.axis_size(axis))])
     return value
 
 
@@ -152,13 +203,10 @@
         order = ring_order(count)
         ahead = by_distance(count)
         near = count - 3 if count > 4 else count // 2
-        mine = jnp.array([order.index(i) for i in range(count)], jnp.int32)[lax.axis_index("net")]
-        at = jnp.array(order, jnp.int32)[(mine + jnp.array(ahead, jnp.int32)) % count]
-        factors = reorder(shift_factors, at)
+        factors = reorder(shift_factors, ahead)
         cut = near * owned
 
     def forward(pieces):
-        pieces = [p.astype(jnp.bfloat16) for p in pieces]
         if not ring:
             whole = lax.all_gather(jnp.concatenate(pieces, axis=0), "net", axis=0, tiled=True)
             return jnp.dot(shift_factors, whole, preferred_element_type=jnp.float32)
@@ -169,7 +217,7 @@
             flows = flows + jnp.dot(factors[:, cols], blocks, preferred_element_type=jnp.float32)
         return flows
 
-    def backward(misfit):
+    def backward(stage, misfit, pieces):
         narrow = misfit.astype(jnp.bfloat16)
 
         def share(cols):
@@ -177,25 +225,38 @@
 
         if not ring:
             spread = lax.psum_scatter(share(shift_factors), "net", scatter_dimension=0, tiled=True)
-            return [spread[c * height : (c + 1) * height] for c in range(chunks)]
-        part = [{} for _ in range(chunks)]
-        for group, cols in ((ahead[near:], slice(cut, None)), (ahead[:near], slice(0, cut))):
-            spread = share(factors[:, cols])
-            for j, d in enumerate(group):
-                for c in range(chunks):
-                    low = j * owned + c * height
-                    part[c][d] = spread[low : low + height]
-        return ring_scatter(part, order)
+            pieces = [p - relax_step * spread[c * height : (c + 1) * height] for c, p in enumerate(pieces)]
+            return pieces, [p.astype(jnp.bfloat16) for p in pieces]
+        far, close = share(factors[:, cut:]), share(factors[:, :cut])
+
+        def part(chunk, distance):
+            j = ahead.index(distance)
+            spread, first = (close, 0) if j < near else (far, near)
+            return spread, (j - first) * owned + chunk * height
+
+        held = ring_scatter(part, order, height)
+        wide, slim = [], []
+        for c, p in enumerate(pieces):
+            shapes = [jax.ShapeDtypeStruct(p.shape, jnp.float32)]
+            if stage + 1 < passes:
+                shapes.append(jax.ShapeDtypeStruct(p.shape, jnp.bfloat16))
+            spread, low = part(c, 0)
+            new = small_call(functools.partial(update_kernel, low), shapes, spread, held[c, 1], held[c, -1], p)
+            wide.append(new[0])
+            slim.append(new[-1])
+        return wide, slim
 
     pieces = [proposal[c * height : (c + 1) * height] for c in range(chunks)]
+    slim = [p.astype(jnp.bfloat16) for p in pieces]
     dual = flow_dual
     sums = []
-    for _ in range(passes):
-        misfit, dual = project(forward(pieces), dual, limits)
-        sums.append(jnp.sum(misfit * misfit))
-        pieces = [p - relax_step * s for p, s in zip(pieces, backward(misfit))]
+    for stage in range(passes):
+        misfit, dual = project(forward(slim), dual, limits)
+        sums.append(jnp.sum((misfit * misfit).reshape(-1, 8, periods), axis=0))
+        pieces, slim = backward(stage, misfit, pieces)
     inject = jnp.concatenate(pieces, axis=0)
-    sums = total_over(total_over(jnp.stack(sums), "tm"), "net")
+    sums = total_over(jnp.concatenate(sums, axis=0), ("tm", "net"))
+    sums = jnp.sum(sums.reshape(passes, -1), axis=1)
     entries = jnp.float32(shift_factors.shape[0] * count * periods * lax.axis_size("tm"))
     residual_norms = jnp.sqrt(sums / entries)
     low, high = beside(inject, "tm")

time: 152 us -> 138 us (0.908)
  other arithmetic: 14.2 us -> 6.12 us
  waiting for transfers between devices: 45.2 us -> 37.5 us
  Pallas kernels: 2.64 us -> 9.49 us
  matrix products: 15.6 us -> 11 us
  local copies, waits for them, and re-layouts: 8.52 us -> 6.77 us
    ppermute x56, waiting for transfers between devices: 41 us -> 31 us  [hop_to(): return lax.ppermute(block, 'net', pairs)]
    pallas_call x1 -> x25, Pallas kernels: 2.64 us -> 9.49 us  [the longest x24 7.4 us: small_call(): pl.pallas_call(kernel, out_shape=out_shape, in_specs=whole_in_vmem(len(op...]
    dot_general x4, matrix products: 9.13 us -> 5.15 us  [share(): lax.dot_general(cols, narrow, (((0,), (0,)), ((), ())), preferred_element...]
    convert_element_type x8 -> x0, other arithmetic: 3.79 us -> none  [ring_scatter(): held[chunk, way] = hop_to(mine.astype(jnp.bfloat16), send, order)]
    add x3, other arithmetic: 2.74 us -> 0.71 us  [total_over(): value + lax.ppermute(value, axis, [(i, i ^ bit) for i in range(lax.axis_s...]
  transfers between devices with their start and end apart: 61 -> 61, of which waited for: 31 -> 25; matrix products, arithmetic and copies ran while one was open for 17% -> 9% of each run, Pallas kernels for 2% -> 6%
where the time goes in v2:
time: 138 us
  starting transfers between devices  65.7 us (48%)
  waiting for transfers between devices  37.5 us (27%)
  matrix products  11 us (8%)
  Pallas kernels  9.49 us (7%)
  local copies, waits for them, and re-layouts  6.77 us (5%)
  other arithmetic  6.12 us (4%)
    ppermute x56, starting transfers between devices, hop_to(): return lax.ppermute(block, 'net', pairs)  61.4 us
    ppermute x56, waiting for transfers between devices, hop_to(): return lax.ppermute(block, 'net', pairs)  31 us
    pallas_call x24, Pallas kernels, small_call(): pl.pallas_call(kernel, out_shape=out_shape, in_specs=whole_in_vmem(len(op...  7.4 us
    unnamed x38, local copies, waits for them, and re-layouts  5.85 us
    dot_general x4, matrix products, forward(): jnp.dot(factors[:, cols], blocks, preferred_element_type=jnp.float32)  5.8 us
    dot_general x4, matrix products, share(): lax.dot_general(cols, narrow, (((0,), (0,)), ((), ())), preferred_element...  5.15 us
    ppermute x4, waiting for transfers between devices, total_over(): lax.ppermute(value, axis, [(i, i ^ bit) for i in range(lax.axis_size(axis...  5.12 us
    ppermute x4, starting transfers between devices, total_over(): lax.ppermute(value, axis, [(i, i ^ bit) for i in range(lax.axis_size(axis...  4.18 us
  transfers between devices with their start and end apart: 61, of which 25 were waited for; matrix products, arithmetic and copies ran while one was open for 9% of the time, Pallas kernels for 6%

profile of v2, /device:TPU:0, one launch (start us, length us, event | category | flops | bytes accessed | tf_op | source)
XLA Modules:
  0.0 137.6 jit_solution(7469099143259871345)
XLA Ops:
  1.6 3.1 %collective-permute-start = (bf16[512,128]{1,0:T(8,128)(2,1)S(1)}, bf16[512,128]{1,0:T(8,128)(2,1)S(1)}, u32[]{:S(2)}, u32[]{:S(2)}) collective-permute-start(bf16[512,128]{1,0:T(8,128)(2,1)S(1)} %get-tuple-element.14), channel_id=1, source_target_pairs={{0,4},{4,8},{8,12},{12,14},{14,10},{10,6},{6,2},{2,0},{1,5},{5,9},... | collective-permute-start | bytes 393224 | tf_op jit(solution)/shard_map/ppermute | solution.py:44
  5.7 2.1 %collective-permute-start.1 = (bf16[512,128]{1,0:T(8,128)(2,1)S(1)}, bf16[512,128]{1,0:T(8,128)(2,1)S(1)}, u32[]{:S(2)}, u32[]{:S(2)}) collective-permute-start(bf16[512,128]{1,0:T(8,128)(2,1)S(1)} %get-tuple-element.12), channel_id=1, source_target_pairs={{0,4},{4,8},{8,12},{12,14},{14,10},{10,6},{6,2},{2,0},{1,5},{5,9},... | collective-permute-start | bytes 393224 | tf_op jit(solution)/shard_map/ppermute | solution.py:44
  8.8 3.4 %copy-done = bf16[512,8192]{1,0:T(8,128)(2,1)S(1)} copy-done((bf16[512,8192]{1,0:T(8,128)(2,1)S(1)}, bf16[512,8192]{1,0:T(8,128)(2,1)}, u32[]{:S(2)}) %copy-start) | copy-done | bytes 8388632
  12.2 2.1 %shard_map.85 = bf16[512,8192]{1,0:T(8,128)(2,1)S(1)} custom-call(s32[1]{0:T(128)} %bitcast.here_ref, bf16[512,8192]{1,0:T(8,128)(2,1)S(1)} %copy-done), custom_call_target="tpu_custom_call" | custom-call | bytes 8388608 | tf_op jit(solution)/shard_map/pallas_call | solution.py:140
  14.3 1.8 %collective-permute-start.4 = (bf16[512,128]{1,0:T(8,128)(2,1)S(1)}, bf16[512,128]{1,0:T(8,128)(2,1)S(1)}, u32[]{:S(2)}, u32[]{:S(2)}) collective-permute-start(bf16[512,128]{1,0:T(8,128)(2,1)S(1)} %collective-permute-done), channel_id=1, source_target_pairs={{0,4},{4,8},{8,12},{12,14},{14,10},{10,6},{6,2},{2,0},{1,5},{5,9},... | collective-permute-start | bytes 393224 | tf_op jit(solution)/shard_map/ppermute | solution.py:44
  16.2 1.4 %collective-permute-start.5 = (bf16[512,128]{1,0:T(8,128)(2,1)S(1)}, bf16[512,128]{1,0:T(8,128)(2,1)S(1)}, u32[]{:S(2)}, u32[]{:S(2)}) collective-permute-start(bf16[512,128]{1,0:T(8,128)(2,1)S(1)} %collective-permute-done.1), channel_id=1, source_target_pairs={{0,4},{4,8},{8,12},{12,14},{14,10},{10,6},{6,2},{2,0},{1,5},{5,9},... | collective-permute-start | bytes 393224 | tf_op jit(solution)/shard_map/ppermute | solution.py:44
  18.7 1.9 %collective-permute-done.4 = bf16[512,128]{1,0:T(8,128)(2,1)S(1)} collective-permute-done((bf16[512,128]{1,0:T(8,128)(2,1)S(1)}, bf16[512,128]{1,0:T(8,128)(2,1)S(1)}, u32[]{:S(2)}, u32[]{:S(2)}) %collective-permute-start.4) | collective-permute-done | bytes 131104 | tf_op jit(solution)/shard_map/ppermute | solution.py:44
  20.5 1.5 %collective-permute-start.8 = (bf16[512,128]{1,0:T(8,128)(2,1)S(1)}, bf16[512,128]{1,0:T(8,128)(2,1)S(1)}, u32[]{:S(2)}, u32[]{:S(2)}) collective-permute-start(bf16[512,128]{1,0:T(8,128)(2,1)S(1)} %collective-permute-done.4), channel_id=1, source_target_pairs={{0,4},{4,8},{8,12},{12,14},{14,10},{10,6},{6,2},{2,0},{1,5},{5,9},... | collective-permute-start | bytes 393224 | tf_op jit(solution)/shard_map/ppermute | solution.py:44
  22.1 1.3 collective-permute-done.5
  23.3 1.5 %collective-permute-start.9 = (bf16[512,128]{1,0:T(8,128)(2,1)S(1)}, bf16[512,128]{1,0:T(8,128)(2,1)S(1)}, u32[]{:S(2)}, u32[]{:S(2)}) collective-permute-start(bf16[512,128]{1,0:T(8,128)(2,1)S(1)} %collective-permute-done.5), channel_id=1, source_target_pairs={{0,4},{4,8},{8,12},{12,14},{14,10},{10,6},{6,2},{2,0},{1,5},{5,9},... | collective-permute-start | bytes 393224 | tf_op jit(solution)/shard_map/ppermute | solution.py:44
  25.4 1.5 %fusion.6 = f32[512,128]{1,0:T(8,128)S(1)} fusion(bf16[5120,128]{1,0:T(8,128)(2,1)S(1)} %constant_dynamic-update-slice_fusion, bf16[512,8192]{1,0:T(8,128)(2,1)S(1)} %shard_map.85), kind=kOutput, calls=%fused_computation.6 | convolution fusion | flops 671088640 | bytes 6815744 | tf_op jit(solution)/shard_map/dot_general | solution.py:217
  27.0 1.5 %collective-permute-start.10 = (bf16[512,128]{1,0:T(8,128)(2,1)S(1)}, bf16[512,128]{1,0:T(8,128)(2,1)S(1)}, u32[]{:S(2)}, u32[]{:S(2)}) collective-permute-start(bf16[512,128]{1,0:T(8,128)(2,1)S(1)} %collective-permute-done.6), channel_id=1, source_target_pairs={{0,2},{4,0},{8,4},{12,8},{14,12},{10,14},{6,10},{2,6},{1,3},{5,1},... | collective-permute-start | bytes 393224 | tf_op jit(solution)/shard_map/ppermute | solution.py:44
  29.2 1.8 %collective-permute-done.11 = bf16[512,128]{1,0:T(8,128)(2,1)S(1)} collective-permute-done((bf16[512,128]{1,0:T(8,128)(2,1)S(1)}, bf16[512,128]{1,0:T(8,128)(2,1)S(1)}, u32[]{:S(2)}, u32[]{:S(2)}) %collective-permute-start.11) | collective-permute-done | bytes 131104 | tf_op jit(solution)/shard_map/ppermute | solution.py:44
  33.6 2.7 %collective-permute-done.13 = bf16[512,128]{1,0:T(8,128)(2,1)S(1)} collective-permute-done((bf16[512,128]{1,0:T(8,128)(2,1)S(1)}, bf16[512,128]{1,0:T(8,128)(2,1)S(1)}, u32[]{:S(2)}, u32[]{:S(2)}) %collective-permute-start.13) | collective-permute-done | bytes 131104 | tf_op jit(solution)/shard_map/ppermute | solution.py:44
  39.0 1.5 %collective-permute-start.14 = (bf16[512,128]{1,0:T(8,128)(2,1)S(1)}, bf16[512,128]{1,0:T(8,128)(2,1)S(1)}, u32[]{:S(2)}, u32[]{:S(2)}) collective-permute-start(bf16[512,128]{1,0:T(8,128)(2,1)S(1)} %get-tuple-element.22), channel_id=1, source_target_pairs={{0,4},{4,8},{8,12},{12,14},{14,10},{10,6},{6,2},{2,0},{1,5},{5,9},... | collective-permute-start | bytes 393224 | tf_op jit(solution)/shard_map/ppermute | solution.py:44
  40.5 1.3 collective-permute-start.21
  44.9 1.7 %collective-permute-start.15 = (bf16[512,128]{1,0:T(8,128)(2,1)S(1)}, bf16[512,128]{1,0:T(8,128)(2,1)S(1)}, u32[]{:S(2)}, u32[]{:S(2)}) collective-permute-start(bf16[512,128]{1,0:T(8,128)(2,1)S(1)} %shard_map.86), channel_id=1, source_target_pairs={{0,4},{4,8},{8,12},{12,14},{14,10},{10,6},{6,2},{2,0},{1,5},{5,9},... | collective-permute-start | bytes 393224 | tf_op jit(solution)/shard_map/ppermute | solution.py:44
  46.6 1.6 %fusion.4.spread_ref = f32[5120,128]{1,0:T(8,128)S(1)} fusion(bf16[512,8192]{1,0:T(8,128)(2,1)S(1)} %shard_map.85, f32[512,128]{1,0:T(8,128)S(1)} %get-tuple-element.34), kind=kOutput, calls=%fused_computation.4 | convolution fusion | flops 671154176 | bytes 8126464 | tf_op jit(solution)/shard_map/dot_general | solution.py:224
  48.2 1.5 %collective-permute-start.22 = (bf16[512,128]{1,0:T(8,128)(2,1)S(1)}, bf16[512,128]{1,0:T(8,128)(2,1)S(1)}, u32[]{:S(2)}, u32[]{:S(2)}) collective-permute-start(bf16[512,128]{1,0:T(8,128)(2,1)S(1)} %shard_map.92), channel_id=1, source_target_pairs={{0,4},{4,8},{8,12},{12,14},{14,10},{10,6},{6,2},{2,0},{1,5},{5,9},... | collective-permute-start | bytes 393224 | tf_op jit(solution)/shard_map/ppermute | solution.py:44
  51.5 1.4 collective-permute-start.16
  52.9 1.7 %collective-permute-done.22.arrived_ref = bf16[512,128]{1,0:T(8,128)(2,1)S(1)} collective-permute-done((bf16[512,128]{1,0:T(8,128)(2,1)S(1)}, bf16[512,128]{1,0:T(8,128)(2,1)S(1)}, u32[]{:S(2)}, u32[]{:S(2)}) %collective-permute-start.22) | collective-permute-done | bytes 131104 | tf_op jit(solution)/shard_map/ppermute | solution.py:44
  54.6 1.5 %collective-permute-start.23 = (bf16[512,128]{1,0:T(8,128)(2,1)S(1)}, bf16[512,128]{1,0:T(8,128)(2,1)S(1)}, u32[]{:S(2)}, u32[]{:S(2)}) collective-permute-start(bf16[512,128]{1,0:T(8,128)(2,1)S(1)} %shard_map.93), channel_id=1, source_target_pairs={{0,4},{4,8},{8,12},{12,14},{14,10},{10,6},{6,2},{2,0},{1,5},{5,9},... | collective-permute-start | bytes 393224 | tf_op jit(solution)/shard_map/ppermute | solution.py:44
  59.0 3.5 %collective-permute-done.20.behind_ref = bf16[512,128]{1,0:T(8,128)(2,1)S(1)} collective-permute-done((bf16[512,128]{1,0:T(8,128)(2,1)S(1)}, bf16[512,128]{1,0:T(8,128)(2,1)S(1)}, u32[]{:S(2)}, u32[]{:S(2)}) %collective-permute-start.20) | collective-permute-done | bytes 131104 | tf_op jit(solution)/shard_map/ppermute | solution.py:44
  63.2 1.5 %collective-permute-start.28 = (bf16[512,128]{1,0:T(8,128)(2,1)S(1)}, bf16[512,128]{1,0:T(8,128)(2,1)S(1)}, u32[]{:S(2)}, u32[]{:S(2)}) collective-permute-start(bf16[512,128]{1,0:T(8,128)(2,1)S(1)} %get-tuple-element.7), channel_id=1, source_target_pairs={{0,4},{4,8},{8,12},{12,14},{14,10},{10,6},{6,2},{2,0},{1,5},{5,9},... | collective-permute-start | bytes 393224 | tf_op jit(solution)/shard_map/ppermute | solution.py:44
  65.3 1.5 %collective-permute-start.29 = (bf16[512,128]{1,0:T(8,128)(2,1)S(1)}, bf16[512,128]{1,0:T(8,128)(2,1)S(1)}, u32[]{:S(2)}, u32[]{:S(2)}) collective-permute-start(bf16[512,128]{1,0:T(8,128)(2,1)S(1)} %get-tuple-element.8), channel_id=1, source_target_pairs={{0,4},{4,8},{8,12},{12,14},{14,10},{10,6},{6,2},{2,0},{1,5},{5,9},... | collective-permute-start | bytes 393224 | tf_op jit(solution)/shard_map/ppermute | solution.py:44
  67.4 4.7 %collective-permute-done.29 = bf16[512,128]{1,0:T(8,128)(2,1)S(1)} collective-permute-done((bf16[512,128]{1,0:T(8,128)(2,1)S(1)}, bf16[512,128]{1,0:T(8,128)(2,1)S(1)}, u32[]{:S(2)}, u32[]{:S(2)}) %collective-permute-start.29) | collective-permute-done | bytes 131104 | tf_op jit(solution)/shard_map/ppermute | solution.py:44
  72.1 1.6 %collective-permute-start.33 = (bf16[512,128]{1,0:T(8,128)(2,1)S(1)}, bf16[512,128]{1,0:T(8,128)(2,1)S(1)}, u32[]{:S(2)}, u32[]{:S(2)}) collective-permute-start(bf16[512,128]{1,0:T(8,128)(2,1)S(1)} %collective-permute-done.29), channel_id=1, source_target_pairs={{0,4},{4,8},{8,12},{12,14},{14,10},{10,6},{6,2},{2,0},{1,5},{5,9},... | collective-permute-start | bytes 393224 | tf_op jit(solution)/shard_map/ppermute | solution.py:44
  74.4 1.4 collective-permute-start.34
  76.3 1.2 collective-permute-done.33
  77.6 1.5 %collective-permute-start.37 = (bf16[512,128]{1,0:T(8,128)(2,1)S(1)}, bf16[512,128]{1,0:T(8,128)(2,1)S(1)}, u32[]{:S(2)}, u32[]{:S(2)}) collective-permute-start(bf16[512,128]{1,0:T(8,128)(2,1)S(1)} %collective-permute-done.33), channel_id=1, source_target_pairs={{0,4},{4,8},{8,12},{12,14},{14,10},{10,6},{6,2},{2,0},{1,5},{5,9},... | collective-permute-start | bytes 393224 | tf_op jit(solution)/shard_map/ppermute | solution.py:44
  79.9 1.6 %collective-permute-start.36 = (bf16[512,128]{1,0:T(8,128)(2,1)S(1)}, bf16[512,128]{1,0:T(8,128)(2,1)S(1)}, u32[]{:S(2)}, u32[]{:S(2)}) collective-permute-start(bf16[512,128]{1,0:T(8,128)(2,1)S(1)} %collective-permute-done.32), channel_id=1, source_target_pairs={{0,4},{4,8},{8,12},{12,14},{14,10},{10,6},{6,2},{2,0},{1,5},{5,9},... | collective-permute-start | bytes 393224 | tf_op jit(solution)/shard_map/ppermute | solution.py:44
  82.2 1.3 collective-permute-start.39
  83.6 1.5 %fusion.2 = f32[512,128]{1,0:T(8,128)S(1)} fusion(bf16[5120,128]{1,0:T(8,128)(2,1)S(1)} %constant_dynamic-update-slice_fusion.16, bf16[512,8192]{1,0:T(8,128)(2,1)S(1)} %shard_map.85), kind=kOutput, calls=%fused_computation.2 | convolution fusion | flops 671088640 | bytes 6815744 | tf_op jit(solution)/shard_map/dot_general | solution.py:217
  85.5 1.8 %collective-permute-start.40 = (bf16[512,128]{1,0:T(8,128)(2,1)S(1)}, bf16[512,128]{1,0:T(8,128)(2,1)S(1)}, u32[]{:S(2)}, u32[]{:S(2)}) collective-permute-start(bf16[512,128]{1,0:T(8,128)(2,1)S(1)} %collective-permute-done.36), channel_id=1, source_target_pairs={{0,4},{4,8},{8,12},{12,14},{14,10},{10,6},{6,2},{2,0},{1,5},{5,9},... | collective-permute-start | bytes 393224 | tf_op jit(solution)/shard_map/ppermute | solution.py:44
  88.7 1.5 %collective-permute-done.38 = bf16[512,128]{1,0:T(8,128)(2,1)S(1)} collective-permute-done((bf16[512,128]{1,0:T(8,128)(2,1)S(1)}, bf16[512,128]{1,0:T(8,128)(2,1)S(1)}, u32[]{:S(2)}, u32[]{:S(2)}) %collective-permute-start.38) | collective-permute-done | bytes 131104 | tf_op jit(solution)/shard_map/ppermute | solution.py:44
  90.5 2.2 %collective-permute-done.41 = bf16[512,128]{1,0:T(8,128)(2,1)S(1)} collective-permute-done((bf16[512,128]{1,0:T(8,128)(2,1)S(1)}, bf16[512,128]{1,0:T(8,128)(2,1)S(1)}, u32[]{:S(2)}, u32[]{:S(2)}) %collective-permute-start.41) | collective-permute-done | bytes 131104 | tf_op jit(solution)/shard_map/ppermute | solution.py:44
  92.8 1.7 %add_add_fusion = (f32[512,128]{1,0:T(8,128)}, f32[512,128]{1,0:T(8,128)S(1)}) fusion(f32[512,128]{1,0:T(8,128)S(1)} %copy-done.4, f32[512,128]{1,0:T(8,128)S(1)} %get-tuple-element.34, f32[512]{0:T(512)S(1)} %neg.13, f32[512]{0:T(512)S(1)} %select_reduce_fusion, f32[512,128]{1,0:T(8,128)S(1)} %fusion.2, ...), kind=kOutput, calls=%fused_computation.40 | convolution fusion | flops 403111936 | bytes 5246976 | tf_op jit(solution)/shard_map/dot_general | solution.py:217
  102.3 1.2 collective-permute-start.53
  103.5 1.6 %fusion.spread_ref = f32[5120,128]{1,0:T(8,128)S(1)} fusion(bf16[512,8192]{1,0:T(8,128)(2,1)S(1)} %shard_map.85, f32[512,128]{1,0:T(8,128)S(1)} %get-tuple-element.32), kind=kOutput, calls=%fused_computation | convolution fusion | flops 671154176 | bytes 8126464 | tf_op jit(solution)/shard_map/dot_general | solution.py:224
  105.2 1.4 %collective-permute-start.47 = (bf16[512,128]{1,0:T(8,128)(2,1)S(1)}, bf16[512,128]{1,0:T(8,128)(2,1)S(1)}, u32[]{:S(2)}, u32[]{:S(2)}) collective-permute-start(bf16[512,128]{1,0:T(8,128)(2,1)S(1)} %shard_map.101), channel_id=1, source_target_pairs={{0,2},{4,0},{8,4},{12,8},{14,12},{10,14},{6,10},{2,6},{1,3},{5,1},... | collective-permute-start | bytes 393224 | tf_op jit(solution)/shard_map/ppermute | solution.py:44
  110.7 1.4 %collective-permute-start.58 = (f32[16,128]{1,0:T(8,128)S(1)}, f32[16,128]{1,0:T(8,128)S(1)}, u32[]{:S(2)}, u32[]{:S(2)}) collective-permute-start(f32[16,128]{1,0:T(8,128)S(1)} %fusion.35), channel_id=1, source_target_pairs={{0,2},{2,0},{4,6},{6,4},{8,10},{10,8},{12,14},{14,12},{1,3},{3,1},... | collective-permute-start | bytes 24584 | tf_op jit(solution)/shard_map/ppermute | solution.py:177
  112.1 2.3 %collective-permute-done.58 = f32[16,128]{1,0:T(8,128)S(1)} collective-permute-done((f32[16,128]{1,0:T(8,128)S(1)}, f32[16,128]{1,0:T(8,128)S(1)}, u32[]{:S(2)}, u32[]{:S(2)}) %collective-permute-start.58) | collective-permute-done | bytes 8224 | tf_op jit(solution)/shard_map/ppermute | solution.py:177
  115.3 2.8 %collective-permute-done.59 = f32[16,128]{1,0:T(8,128)} collective-permute-done((f32[16,128]{1,0:T(8,128)S(1)}, f32[16,128]{1,0:T(8,128)}, u32[]{:S(2)}, u32[]{:S(2)}) %collective-permute-start.59) | collective-permute-done | bytes 8224 | tf_op jit(solution)/shard_map/ppermute | solution.py:177
  118.8 1.8 %collective-permute-start.60 = (f32[16,128]{1,0:T(8,128)S(1)}, f32[16,128]{1,0:T(8,128)}, u32[]{:S(2)}, u32[]{:S(2)}) collective-permute-start(f32[16,128]{1,0:T(8,128)S(1)} %add.55), channel_id=1, source_target_pairs={{0,8},{2,10},{4,12},{6,14},{8,0},{10,2},{12,4},{14,6},{1,9},{3,11}... | collective-permute-start | bytes 24584 | tf_op jit(solution)/shard_map/ppermute | solution.py:177
  122.3 2.1 %collective-permute-start.51 = (bf16[512,128]{1,0:T(8,128)(2,1)S(1)}, bf16[512,128]{1,0:T(8,128)(2,1)}, u32[]{:S(2)}, u32[]{:S(2)}) collective-permute-start(bf16[512,128]{1,0:T(8,128)(2,1)S(1)} %shard_map.105), channel_id=1, source_target_pairs={{0,4},{4,8},{8,12},{12,14},{14,10},{10,6},{6,2},{2,0},{1,5},{5,9},... | collective-permute-start | bytes 393224 | tf_op jit(solution)/shard_map/ppermute | solution.py:44
  125.3 1.3 collective-permute-start.45
  128.9 1.3 add_reduce_fusion
  134.5 1.4 collective-permute-done.56
  (169 shorter events, 49.6 us)
Async XLA Ops:
  1.6 12.6 %collective-permute-start = (bf16[512,128]{1,0:T(8,128)(2,1)S(1)}, bf16[512,128]{1,0:T(8,128)(2,1)S(1)}, u32[]{:S(2)}, u32[]{:S(2)}) collective-permute-start(bf16[512,128]{1,0:T(8,128)(2,1)S(1)} %get-tuple-element.14), channel_id=1, source_target_pairs={{0,4},{4,8},{8,12},{12,14},{14,10},{10,6},{6,2},{2,0},{1,5},{5,9},... | collective-permute-start | bytes 393224 | tf_op jit(solution)/shard_map/ppermute | solution.py:44
  4.7 12.9 %collective-permute-start.2 = (bf16[512,128]{1,0:T(8,128)(2,1)S(1)}, bf16[512,128]{1,0:T(8,128)(2,1)S(1)}, u32[]{:S(2)}, u32[]{:S(2)}) collective-permute-start(bf16[512,128]{1,0:T(8,128)(2,1)S(1)} %get-tuple-element.14), channel_id=1, source_target_pairs={{0,2},{4,0},{8,4},{12,8},{14,12},{10,14},{6,10},{2,6},{1,3},{5,1},... | collective-permute-start | bytes 393224 | tf_op jit(solution)/shard_map/ppermute | solution.py:44
  5.7 10.4 %collective-permute-start.1 = (bf16[512,128]{1,0:T(8,128)(2,1)S(1)}, bf16[512,128]{1,0:T(8,128)(2,1)S(1)}, u32[]{:S(2)}, u32[]{:S(2)}) collective-permute-start(bf16[512,128]{1,0:T(8,128)(2,1)S(1)} %get-tuple-element.12), channel_id=1, source_target_pairs={{0,4},{4,8},{8,12},{12,14},{14,10},{10,6},{6,2},{2,0},{1,5},{5,9},... | collective-permute-start | bytes 393224 | tf_op jit(solution)/shard_map/ppermute | solution.py:44
  7.8 10.5 %collective-permute-start.3 = (bf16[512,128]{1,0:T(8,128)(2,1)S(1)}, bf16[512,128]{1,0:T(8,128)(2,1)S(1)}, u32[]{:S(2)}, u32[]{:S(2)}) collective-permute-start(bf16[512,128]{1,0:T(8,128)(2,1)S(1)} %get-tuple-element.12), channel_id=1, source_target_pairs={{0,2},{4,0},{8,4},{12,8},{14,12},{10,14},{6,10},{2,6},{1,3},{5,1},... | collective-permute-start | bytes 393224 | tf_op jit(solution)/shard_map/ppermute | solution.py:44
  14.3 6.2 %collective-permute-start.4 = (bf16[512,128]{1,0:T(8,128)(2,1)S(1)}, bf16[512,128]{1,0:T(8,128)(2,1)S(1)}, u32[]{:S(2)}, u32[]{:S(2)}) collective-permute-start(bf16[512,128]{1,0:T(8,128)(2,1)S(1)} %collective-permute-done), channel_id=1, source_target_pairs={{0,4},{4,8},{8,12},{12,14},{14,10},{10,6},{6,2},{2,0},{1,5},{5,9},... | collective-permute-start | bytes 393224 | tf_op jit(solution)/shard_map/ppermute | solution.py:44
  16.2 7.2 %collective-permute-start.5 = (bf16[512,128]{1,0:T(8,128)(2,1)S(1)}, bf16[512,128]{1,0:T(8,128)(2,1)S(1)}, u32[]{:S(2)}, u32[]{:S(2)}) collective-permute-start(bf16[512,128]{1,0:T(8,128)(2,1)S(1)} %collective-permute-done.1), channel_id=1, source_target_pairs={{0,4},{4,8},{8,12},{12,14},{14,10},{10,6},{6,2},{2,0},{1,5},{5,9},... | collective-permute-start | bytes 393224 | tf_op jit(solution)/shard_map/ppermute | solution.py:44
  17.6 7.8 %collective-permute-start.6 = (bf16[512,128]{1,0:T(8,128)(2,1)S(1)}, bf16[512,128]{1,0:T(8,128)(2,1)S(1)}, u32[]{:S(2)}, u32[]{:S(2)}) collective-permute-start(bf16[512,128]{1,0:T(8,128)(2,1)S(1)} %collective-permute-done.2), channel_id=1, source_target_pairs={{0,2},{4,0},{8,4},{12,8},{14,12},{10,14},{6,10},{2,6},{1,3},{5,1},... | collective-permute-start | bytes 393224 | tf_op jit(solution)/shard_map/ppermute | solution.py:44
  18.3 6.5 %collective-permute-start.7 = (bf16[512,128]{1,0:T(8,128)(2,1)S(1)}, bf16[512,128]{1,0:T(8,128)(2,1)S(1)}, u32[]{:S(2)}, u32[]{:S(2)}) collective-permute-start(bf16[512,128]{1,0:T(8,128)(2,1)S(1)} %collective-permute-done.3), channel_id=1, source_target_pairs={{0,2},{4,0},{8,4},{12,8},{14,12},{10,14},{6,10},{2,6},{1,3},{5,1},... | collective-permute-start | bytes 393224 | tf_op jit(solution)/shard_map/ppermute | solution.py:44
  20.5 8.0 %collective-permute-start.8 = (bf16[512,128]{1,0:T(8,128)(2,1)S(1)}, bf16[512,128]{1,0:T(8,128)(2,1)S(1)}, u32[]{:S(2)}, u32[]{:S(2)}) collective-permute-start(bf16[512,128]{1,0:T(8,128)(2,1)S(1)} %collective-permute-done.4), channel_id=1, source_target_pairs={{0,4},{4,8},{8,12},{12,14},{14,10},{10,6},{6,2},{2,0},{1,5},{5,9},... | collective-permute-start | bytes 393224 | tf_op jit(solution)/shard_map/ppermute | solution.py:44
  23.3 8.3 %collective-permute-start.9 = (bf16[512,128]{1,0:T(8,128)(2,1)S(1)}, bf16[512,128]{1,0:T(8,128)(2,1)S(1)}, u32[]{:S(2)}, u32[]{:S(2)}) collective-permute-start(bf16[512,128]{1,0:T(8,128)(2,1)S(1)} %collective-permute-done.5), channel_id=1, source_target_pairs={{0,4},{4,8},{8,12},{12,14},{14,10},{10,6},{6,2},{2,0},{1,5},{5,9},... | collective-permute-start | bytes 393224 | tf_op jit(solution)/shard_map/ppermute | solution.py:44
  24.8 6.1 %collective-permute-start.11 = (bf16[512,128]{1,0:T(8,128)(2,1)S(1)}, bf16[512,128]{1,0:T(8,128)(2,1)S(1)}, u32[]{:S(2)}, u32[]{:S(2)}) collective-permute-start(bf16[512,128]{1,0:T(8,128)(2,1)S(1)} %collective-permute-done.7), channel_id=1, source_target_pairs={{0,2},{4,0},{8,4},{12,8},{14,12},{10,14},{6,10},{2,6},{1,3},{5,1},... | collective-permute-start | bytes 393224 | tf_op jit(solution)/shard_map/ppermute | solution.py:44
  39.0 5.9 %collective-permute-start.14 = (bf16[512,128]{1,0:T(8,128)(2,1)S(1)}, bf16[512,128]{1,0:T(8,128)(2,1)S(1)}, u32[]{:S(2)}, u32[]{:S(2)}) collective-permute-start(bf16[512,128]{1,0:T(8,128)(2,1)S(1)} %get-tuple-element.22), channel_id=1, source_target_pairs={{0,4},{4,8},{8,12},{12,14},{14,10},{10,6},{6,2},{2,0},{1,5},{5,9},... | collective-permute-start | bytes 393224 | tf_op jit(solution)/shard_map/ppermute | solution.py:44
  40.5 7.7 %collective-permute-start.21 = (bf16[512,128]{1,0:T(8,128)(2,1)S(1)}, bf16[512,128]{1,0:T(8,128)(2,1)S(1)}, u32[]{:S(2)}, u32[]{:S(2)}) collective-permute-start(bf16[512,128]{1,0:T(8,128)(2,1)S(1)} %get-tuple-element.20), channel_id=1, source_target_pairs={{0,4},{4,8},{8,12},{12,14},{14,10},{10,6},{6,2},{2,0},{1,5},{5,9},... | collective-permute-start | bytes 393224 | tf_op jit(solution)/shard_map/ppermute | solution.py:44
  41.8 7.8 %collective-permute-start.18 = (bf16[512,128]{1,0:T(8,128)(2,1)S(1)}, bf16[512,128]{1,0:T(8,128)(2,1)S(1)}, u32[]{:S(2)}, u32[]{:S(2)}) collective-permute-start(bf16[512,128]{1,0:T(8,128)(2,1)S(1)} %get-tuple-element.21), channel_id=1, source_target_pairs={{0,2},{4,0},{8,4},{12,8},{14,12},{10,14},{6,10},{2,6},{1,3},{5,1},... | collective-permute-start | bytes 393224 | tf_op jit(solution)/shard_map/ppermute | solution.py:44
  43.4 6.9 %collective-permute-start.25 = (bf16[512,128]{1,0:T(8,128)(2,1)S(1)}, bf16[512,128]{1,0:T(8,128)(2,1)S(1)}, u32[]{:S(2)}, u32[]{:S(2)}) collective-permute-start(bf16[512,128]{1,0:T(8,128)(2,1)S(1)} %shard_map.94), channel_id=1, source_target_pairs={{0,2},{4,0},{8,4},{12,8},{14,12},{10,14},{6,10},{2,6},{1,3},{5,1},... | collective-permute-start | bytes 393224 | tf_op jit(solution)/shard_map/ppermute | solution.py:44
  44.9 6.6 %collective-permute-start.15 = (bf16[512,128]{1,0:T(8,128)(2,1)S(1)}, bf16[512,128]{1,0:T(8,128)(2,1)S(1)}, u32[]{:S(2)}, u32[]{:S(2)}) collective-permute-start(bf16[512,128]{1,0:T(8,128)(2,1)S(1)} %shard_map.86), channel_id=1, source_target_pairs={{0,4},{4,8},{8,12},{12,14},{14,10},{10,6},{6,2},{2,0},{1,5},{5,9},... | collective-permute-start | bytes 393224 | tf_op jit(solution)/shard_map/ppermute | solution.py:44
  48.2 6.4 %collective-permute-start.22 = (bf16[512,128]{1,0:T(8,128)(2,1)S(1)}, bf16[512,128]{1,0:T(8,128)(2,1)S(1)}, u32[]{:S(2)}, u32[]{:S(2)}) collective-permute-start(bf16[512,128]{1,0:T(8,128)(2,1)S(1)} %shard_map.92), channel_id=1, source_target_pairs={{0,4},{4,8},{8,12},{12,14},{14,10},{10,6},{6,2},{2,0},{1,5},{5,9},... | collective-permute-start | bytes 393224 | tf_op jit(solution)/shard_map/ppermute | solution.py:44
  49.7 6.4 %collective-permute-start.19 = (bf16[512,128]{1,0:T(8,128)(2,1)S(1)}, bf16[512,128]{1,0:T(8,128)(2,1)S(1)}, u32[]{:S(2)}, u32[]{:S(2)}) collective-permute-start(bf16[512,128]{1,0:T(8,128)(2,1)S(1)} %shard_map.89), channel_id=1, source_target_pairs={{0,2},{4,0},{8,4},{12,8},{14,12},{10,14},{6,10},{2,6},{1,3},{5,1},... | collective-permute-start | bytes 393224 | tf_op jit(solution)/shard_map/ppermute | solution.py:44
  50.4 6.4 %collective-permute-start.26 = (bf16[512,128]{1,0:T(8,128)(2,1)S(1)}, bf16[512,128]{1,0:T(8,128)(2,1)S(1)}, u32[]{:S(2)}, u32[]{:S(2)}) collective-permute-start(bf16[512,128]{1,0:T(8,128)(2,1)S(1)} %shard_map.95), channel_id=1, source_target_pairs={{0,2},{4,0},{8,4},{12,8},{14,12},{10,14},{6,10},{2,6},{1,3},{5,1},... | collective-permute-start | bytes 393224 | tf_op jit(solution)/shard_map/ppermute | solution.py:44
  51.5 6.3 %collective-permute-start.16 = (bf16[512,128]{1,0:T(8,128)(2,1)S(1)}, bf16[512,128]{1,0:T(8,128)(2,1)S(1)}, u32[]{:S(2)}, u32[]{:S(2)}) collective-permute-start(bf16[512,128]{1,0:T(8,128)(2,1)S(1)} %shard_map.87), channel_id=1, source_target_pairs={{0,4},{4,8},{8,12},{12,14},{14,10},{10,6},{6,2},{2,0},{1,5},{5,9},... | collective-permute-start | bytes 393224 | tf_op jit(solution)/shard_map/ppermute | solution.py:44
  54.6 10.7 %collective-permute-start.23 = (bf16[512,128]{1,0:T(8,128)(2,1)S(1)}, bf16[512,128]{1,0:T(8,128)(2,1)S(1)}, u32[]{:S(2)}, u32[]{:S(2)}) collective-permute-start(bf16[512,128]{1,0:T(8,128)(2,1)S(1)} %shard_map.93), channel_id=1, source_target_pairs={{0,4},{4,8},{8,12},{12,14},{14,10},{10,6},{6,2},{2,0},{1,5},{5,9},... | collective-permute-start | bytes 393224 | tf_op jit(solution)/shard_map/ppermute | solution.py:44
  56.1 6.4 %collective-permute-start.20 = (bf16[512,128]{1,0:T(8,128)(2,1)S(1)}, bf16[512,128]{1,0:T(8,128)(2,1)S(1)}, u32[]{:S(2)}, u32[]{:S(2)}) collective-permute-start(bf16[512,128]{1,0:T(8,128)(2,1)S(1)} %shard_map.90), channel_id=1, source_target_pairs={{0,2},{4,0},{8,4},{12,8},{14,12},{10,14},{6,10},{2,6},{1,3},{5,1},... | collective-permute-start | bytes 393224 | tf_op jit(solution)/shard_map/ppermute | solution.py:44
  56.8 8.4 %collective-permute-start.27 = (bf16[512,128]{1,0:T(8,128)(2,1)S(1)}, bf16[512,128]{1,0:T(8,128)(2,1)S(1)}, u32[]{:S(2)}, u32[]{:S(2)}) collective-permute-start(bf16[512,128]{1,0:T(8,128)(2,1)S(1)} %shard_map.96), channel_id=1, source_target_pairs={{0,2},{4,0},{8,4},{12,8},{14,12},{10,14},{6,10},{2,6},{1,3},{5,1},... | collective-permute-start | bytes 393224 | tf_op jit(solution)/shard_map/ppermute | solution.py:44
  63.2 10.6 %collective-permute-start.28 = (bf16[512,128]{1,0:T(8,128)(2,1)S(1)}, bf16[512,128]{1,0:T(8,128)(2,1)S(1)}, u32[]{:S(2)}, u32[]{:S(2)}) collective-permute-start(bf16[512,128]{1,0:T(8,128)(2,1)S(1)} %get-tuple-element.7), channel_id=1, source_target_pairs={{0,4},{4,8},{8,12},{12,14},{14,10},{10,6},{6,2},{2,0},{1,5},{5,9},... | collective-permute-start | bytes 393224 | tf_op jit(solution)/shard_map/ppermute | solution.py:44
  64.6 9.8 %collective-permute-start.30 = (bf16[512,128]{1,0:T(8,128)(2,1)S(1)}, bf16[512,128]{1,0:T(8,128)(2,1)S(1)}, u32[]{:S(2)}, u32[]{:S(2)}) collective-permute-start(bf16[512,128]{1,0:T(8,128)(2,1)S(1)} %get-tuple-element.7), channel_id=1, source_target_pairs={{0,2},{4,0},{8,4},{12,8},{14,12},{10,14},{6,10},{2,6},{1,3},{5,1},... | collective-permute-start | bytes 393224 | tf_op jit(solution)/shard_map/ppermute | solution.py:44
  65.3 6.8 %collective-permute-start.29 = (bf16[512,128]{1,0:T(8,128)(2,1)S(1)}, bf16[512,128]{1,0:T(8,128)(2,1)S(1)}, u32[]{:S(2)}, u32[]{:S(2)}) collective-permute-start(bf16[512,128]{1,0:T(8,128)(2,1)S(1)} %get-tuple-element.8), channel_id=1, source_target_pairs={{0,4},{4,8},{8,12},{12,14},{14,10},{10,6},{6,2},{2,0},{1,5},{5,9},... | collective-permute-start | bytes 393224 | tf_op jit(solution)/shard_map/ppermute | solution.py:44
  66.8 9.0 %collective-permute-start.31 = (bf16[512,128]{1,0:T(8,128)(2,1)S(1)}, bf16[512,128]{1,0:T(8,128)(2,1)S(1)}, u32[]{:S(2)}, u32[]{:S(2)}) collective-permute-start(bf16[512,128]{1,0:T(8,128)(2,1)S(1)} %get-tuple-element.8), channel_id=1, source_target_pairs={{0,2},{4,0},{8,4},{12,8},{14,12},{10,14},{6,10},{2,6},{1,3},{5,1},... | collective-permute-start | bytes 393224 | tf_op jit(solution)/shard_map/ppermute | solution.py:44
  72.1 5.4 %collective-permute-start.33 = (bf16[512,128]{1,0:T(8,128)(2,1)S(1)}, bf16[512,128]{1,0:T(8,128)(2,1)S(1)}, u32[]{:S(2)}, u32[]{:S(2)}) collective-permute-start(bf16[512,128]{1,0:T(8,128)(2,1)S(1)} %collective-permute-done.29), channel_id=1, source_target_pairs={{0,4},{4,8},{8,12},{12,14},{14,10},{10,6},{6,2},{2,0},{1,5},{5,9},... | collective-permute-start | bytes 393224 | tf_op jit(solution)/shard_map/ppermute | solution.py:44
  73.8 6.2 %collective-permute-start.32 = (bf16[512,128]{1,0:T(8,128)(2,1)S(1)}, bf16[512,128]{1,0:T(8,128)(2,1)S(1)}, u32[]{:S(2)}, u32[]{:S(2)}) collective-permute-start(bf16[512,128]{1,0:T(8,128)(2,1)S(1)} %collective-permute-done.28), channel_id=1, source_target_pairs={{0,4},{4,8},{8,12},{12,14},{14,10},{10,6},{6,2},{2,0},{1,5},{5,9},... | collective-permute-start | bytes 393224 | tf_op jit(solution)/shard_map/ppermute | solution.py:44
  74.4 9.1 %collective-permute-start.34 = (bf16[512,128]{1,0:T(8,128)(2,1)S(1)}, bf16[512,128]{1,0:T(8,128)(2,1)S(1)}, u32[]{:S(2)}, u32[]{:S(2)}) collective-permute-start(bf16[512,128]{1,0:T(8,128)(2,1)S(1)} %collective-permute-done.30), channel_id=1, source_target_pairs={{0,2},{4,0},{8,4},{12,8},{14,12},{10,14},{6,10},{2,6},{1,3},{5,1},... | collective-permute-start | bytes 393224 | tf_op jit(solution)/shard_map/ppermute | solution.py:44
  75.8 6.4 %collective-permute-start.35 = (bf16[512,128]{1,0:T(8,128)(2,1)S(1)}, bf16[512,128]{1,0:T(8,128)(2,1)S(1)}, u32[]{:S(2)}, u32[]{:S(2)}) collective-permute-start(bf16[512,128]{1,0:T(8,128)(2,1)S(1)} %collective-permute-done.31), channel_id=1, source_target_pairs={{0,2},{4,0},{8,4},{12,8},{14,12},{10,14},{6,10},{2,6},{1,3},{5,1},... | collective-permute-start | bytes 393224 | tf_op jit(solution)/shard_map/ppermute | solution.py:44
  77.6 11.1 %collective-permute-start.37 = (bf16[512,128]{1,0:T(8,128)(2,1)S(1)}, bf16[512,128]{1,0:T(8,128)(2,1)S(1)}, u32[]{:S(2)}, u32[]{:S(2)}) collective-permute-start(bf16[512,128]{1,0:T(8,128)(2,1)S(1)} %collective-permute-done.33), channel_id=1, source_target_pairs={{0,4},{4,8},{8,12},{12,14},{14,10},{10,6},{6,2},{2,0},{1,5},{5,9},... | collective-permute-start | bytes 393224 | tf_op jit(solution)/shard_map/ppermute | solution.py:44
  79.9 5.5 %collective-permute-start.36 = (bf16[512,128]{1,0:T(8,128)(2,1)S(1)}, bf16[512,128]{1,0:T(8,128)(2,1)S(1)}, u32[]{:S(2)}, u32[]{:S(2)}) collective-permute-start(bf16[512,128]{1,0:T(8,128)(2,1)S(1)} %collective-permute-done.32), channel_id=1, source_target_pairs={{0,4},{4,8},{8,12},{12,14},{14,10},{10,6},{6,2},{2,0},{1,5},{5,9},... | collective-permute-start | bytes 393224 | tf_op jit(solution)/shard_map/ppermute | solution.py:44
  82.2 5.6 %collective-permute-start.39 = (bf16[512,128]{1,0:T(8,128)(2,1)S(1)}, bf16[512,128]{1,0:T(8,128)(2,1)S(1)}, u32[]{:S(2)}, u32[]{:S(2)}) collective-permute-start(bf16[512,128]{1,0:T(8,128)(2,1)S(1)} %collective-permute-done.35), channel_id=1, source_target_pairs={{0,2},{4,0},{8,4},{12,8},{14,12},{10,14},{6,10},{2,6},{1,3},{5,1},... | collective-permute-start | bytes 393224 | tf_op jit(solution)/shard_map/ppermute | solution.py:44
  96.6 5.7 %collective-permute-start.52 = (bf16[512,128]{1,0:T(8,128)(2,1)S(1)}, bf16[512,128]{1,0:T(8,128)(2,1)S(1)}, u32[]{:S(2)}, u32[]{:S(2)}) collective-permute-start(bf16[512,128]{1,0:T(8,128)(2,1)S(1)} %get-tuple-element.16), channel_id=1, source_target_pairs={{0,2},{4,0},{8,4},{12,8},{14,12},{10,14},{6,10},{2,6},{1,3},{5,1},... | collective-permute-start | bytes 393224 | tf_op jit(solution)/shard_map/ppermute | solution.py:44
  97.7 13.0 %collective-permute-start.57 = (f32[16,128]{1,0:T(8,128)S(1)}, f32[16,128]{1,0:T(8,128)S(1)}, u32[]{:S(2)}, u32[]{:S(2)}) collective-permute-start(f32[16,128]{1,0:T(8,128)S(1)} %pad_maximum_fusion.1), channel_id=1, source_target_pairs={{0,1},{1,0},{2,3},{3,2},{4,5},{5,4},{6,7},{7,6},{8,9},{9,8},{10,11... | collective-permute-start | bytes 24584 | tf_op jit(solution)/shard_map/ppermute | solution.py:177
  97.8 7.3 %collective-permute-start.46 = (bf16[512,128]{1,0:T(8,128)(2,1)S(1)}, bf16[512,128]{1,0:T(8,128)(2,1)S(1)}, u32[]{:S(2)}, u32[]{:S(2)}) collective-permute-start(bf16[512,128]{1,0:T(8,128)(2,1)S(1)} %get-tuple-element.15), channel_id=1, source_target_pairs={{0,2},{4,0},{8,4},{12,8},{14,12},{10,14},{6,10},{2,6},{1,3},{5,1},... | collective-permute-start | bytes 393224 | tf_op jit(solution)/shard_map/ppermute | solution.py:44
  98.7 7.9 %collective-permute-start.49 = (bf16[512,128]{1,0:T(8,128)(2,1)S(1)}, bf16[512,128]{1,0:T(8,128)(2,1)S(1)}, u32[]{:S(2)}, u32[]{:S(2)}) collective-permute-start(bf16[512,128]{1,0:T(8,128)(2,1)S(1)} %get-tuple-element.17), channel_id=1, source_target_pairs={{0,4},{4,8},{8,12},{12,14},{14,10},{10,6},{6,2},{2,0},{1,5},{5,9},... | collective-permute-start | bytes 393224 | tf_op jit(solution)/shard_map/ppermute | solution.py:44
  100.6 6.7 %collective-permute-start.43 = (bf16[512,128]{1,0:T(8,128)(2,1)S(1)}, bf16[512,128]{1,0:T(8,128)(2,1)S(1)}, u32[]{:S(2)}, u32[]{:S(2)}) collective-permute-start(bf16[512,128]{1,0:T(8,128)(2,1)S(1)} %shard_map.98), channel_id=1, source_target_pairs={{0,4},{4,8},{8,12},{12,14},{14,10},{10,6},{6,2},{2,0},{1,5},{5,9},... | collective-permute-start | bytes 393224 | tf_op jit(solution)/shard_map/ppermute | solution.py:44
  102.3 6.6 %collective-permute-start.53 = (bf16[512,128]{1,0:T(8,128)(2,1)S(1)}, bf16[512,128]{1,0:T(8,128)(2,1)S(1)}, u32[]{:S(2)}, u32[]{:S(2)}) collective-permute-start(bf16[512,128]{1,0:T(8,128)(2,1)S(1)} %shard_map.106), channel_id=1, source_target_pairs={{0,2},{4,0},{8,4},{12,8},{14,12},{10,14},{6,10},{2,6},{1,3},{5,1},... | collective-permute-start | bytes 393224 | tf_op jit(solution)/shard_map/ppermute | solution.py:44
  105.2 15.5 %collective-permute-start.47 = (bf16[512,128]{1,0:T(8,128)(2,1)S(1)}, bf16[512,128]{1,0:T(8,128)(2,1)S(1)}, u32[]{:S(2)}, u32[]{:S(2)}) collective-permute-start(bf16[512,128]{1,0:T(8,128)(2,1)S(1)} %shard_map.101), channel_id=1, source_target_pairs={{0,2},{4,0},{8,4},{12,8},{14,12},{10,14},{6,10},{2,6},{1,3},{5,1},... | collective-permute-start | bytes 393224 | tf_op jit(solution)/shard_map/ppermute | solution.py:44
  106.6 14.7 %collective-permute-start.50 = (bf16[512,128]{1,0:T(8,128)(2,1)S(1)}, bf16[512,128]{1,0:T(8,128)(2,1)}, u32[]{:S(2)}, u32[]{:S(2)}) collective-permute-start(bf16[512,128]{1,0:T(8,128)(2,1)S(1)} %shard_map.104), channel_id=1, source_target_pairs={{0,4},{4,8},{8,12},{12,14},{14,10},{10,6},{6,2},{2,0},{1,5},{5,9},... | collective-permute-start | bytes 393224 | tf_op jit(solution)/shard_map/ppermute | solution.py:44
  108.0 16.3 %collective-permute-start.44 = (bf16[512,128]{1,0:T(8,128)(2,1)}, bf16[512,128]{1,0:T(8,128)(2,1)}, u32[]{:S(2)}, u32[]{:S(2)}) collective-permute-start(bf16[512,128]{1,0:T(8,128)(2,1)} %shard_map.99), channel_id=1, source_target_pairs={{0,4},{4,8},{8,12},{12,14},{14,10},{10,6},{6,2},{2,0},{1,5},{5,9},... | collective-permute-start | bytes 393224 | tf_op jit(solution)/shard_map/ppermute | solution.py:44
  109.6 17.0 %collective-permute-start.54 = (bf16[512,128]{1,0:T(8,128)(2,1)}, bf16[512,128]{1,0:T(8,128)(2,1)}, u32[]{:S(2)}, u32[]{:S(2)}) collective-permute-start(bf16[512,128]{1,0:T(8,128)(2,1)} %shard_map.107), channel_id=1, source_target_pairs={{0,2},{4,0},{8,4},{12,8},{14,12},{10,14},{6,10},{2,6},{1,3},{5,1},... | collective-permute-start | bytes 393224 | tf_op jit(solution)/shard_map/ppermute | solution.py:44
  118.8 10.0 %collective-permute-start.60 = (f32[16,128]{1,0:T(8,128)S(1)}, f32[16,128]{1,0:T(8,128)}, u32[]{:S(2)}, u32[]{:S(2)}) collective-permute-start(f32[16,128]{1,0:T(8,128)S(1)} %add.55), channel_id=1, source_target_pairs={{0,8},{2,10},{4,12},{6,14},{8,0},{10,2},{12,4},{14,6},{1,9},{3,11}... | collective-permute-start | bytes 24584 | tf_op jit(solution)/shard_map/ppermute | solution.py:177
  121.3 9.7 %collective-permute-start.48 = (bf16[512,128]{1,0:T(8,128)(2,1)}, bf16[512,128]{1,0:T(8,128)(2,1)}, u32[]{:S(2)}, u32[]{:S(2)}) collective-permute-start(bf16[512,128]{1,0:T(8,128)(2,1)} %shard_map.102), channel_id=1, source_target_pairs={{0,2},{4,0},{8,4},{12,8},{14,12},{10,14},{6,10},{2,6},{1,3},{5,1},... | collective-permute-start | bytes 393224 | tf_op jit(solution)/shard_map/ppermute | solution.py:44
  122.3 9.8 %collective-permute-start.51 = (bf16[512,128]{1,0:T(8,128)(2,1)S(1)}, bf16[512,128]{1,0:T(8,128)(2,1)}, u32[]{:S(2)}, u32[]{:S(2)}) collective-permute-start(bf16[512,128]{1,0:T(8,128)(2,1)S(1)} %shard_map.105), channel_id=1, source_target_pairs={{0,4},{4,8},{8,12},{12,14},{14,10},{10,6},{6,2},{2,0},{1,5},{5,9},... | collective-permute-start | bytes 393224 | tf_op jit(solution)/shard_map/ppermute | solution.py:44
  125.3 5.8 %collective-permute-start.45 = (bf16[512,128]{1,0:T(8,128)(2,1)S(1)}, bf16[512,128]{1,0:T(8,128)(2,1)}, u32[]{:S(2)}, u32[]{:S(2)}) collective-permute-start(bf16[512,128]{1,0:T(8,128)(2,1)S(1)} %shard_map.100), channel_id=1, source_target_pairs={{0,4},{4,8},{8,12},{12,14},{14,10},{10,6},{6,2},{2,0},{1,5},{5,9},... | collective-permute-start | bytes 393224 | tf_op jit(solution)/shard_map/ppermute | solution.py:44
  (18 other events, 81.3 us)

commit v3 on v2

--- a/solution.py
+++ b/solution.py
@@ -11,6 +11,10 @@
 chunks = 2
 passes = 2
 longest_ring = 8
+
+
+def is_ring(count, split):
+    return 4 <= count <= longest_ring and count % 2 == 0 and split == 2
 
 
 def ring_order(count):
@@ -51,6 +55,12 @@
     return out
 
 
+def ring_groups(count):
+    order = by_distance(count)
+    cuts = sorted({0, min(3, count), max(count - 3, min(3, count)), count - 1, count})
+    return [order[a:b] for a, b in zip(cuts, cuts[1:])]
+
+
 def ring_gather(pieces, order):
     count = len(order)
     got = [{0: p} for p in pieces]
@@ -63,16 +73,12 @@
     return got
 
 
-def whole_in_vmem(count):
-    return [pl.BlockSpec(memory_space=pltpu.VMEM)] * count
-
-
 def small_call(kernel, out_shape, *operands):
     touched = sum(x.size * x.dtype.itemsize for x in jax.tree.leaves(out_shape)) * 3
     return pl.pallas_call(
         kernel,
         out_shape=out_shape,
-        in_specs=whole_in_vmem(len(operands)),
+        in_specs=[pl.BlockSpec(memory_space=pltpu.SMEM if x.dtype == jnp.int32 else pltpu.VMEM) for x in operands],
         out_specs=jax.tree.map(lambda _: pl.BlockSpec(memory_space=pltpu.VMEM), out_shape),
         compiler_params=pltpu.CompilerParams(vmem_limit_bytes=16 << 20),
         cost_estimate=pl.CostEstimate(flops=0, transcendentals=0, bytes_accessed=touched),
@@ -84,12 +90,16 @@
     out_ref[...] = (mine + arrived_ref[...].astype(jnp.float32)).astype(out_ref.dtype)
 
 
-def update_kernel(low, spread_ref, ahead_ref, behind_ref, inject_ref, *out_refs):
-    total = spread_ref[pl.ds(low, inject_ref.shape[0]), :]
-    total = total + ahead_ref[...].astype(jnp.float32) + behind_ref[...].astype(jnp.float32)
-    inject = inject_ref[...] - relax_step * total
-    for ref in out_refs:
-        ref[...] = inject.astype(ref.dtype)
+def update_kernel(lows, spread_ref, *refs):
+    ahead, behind, inject_ref, out_ref, slim = refs[:chunks], refs[chunks : 2 * chunks], refs[2 * chunks], refs[2 * chunks + 1], refs[2 * chunks + 2 :]
+    height = ahead[0].shape[0]
+    for c, low in enumerate(lows):
+        rows = pl.ds(c * height, height)
+        total = spread_ref[pl.ds(low, height), :]
+        total = total + ahead[c][...].astype(jnp.float32) + behind[c][...].astype(jnp.float32)
+        inject = inject_ref[rows, :] - relax_step * total
+        out_ref[rows, :] = inject
+        slim[c][...] = inject.astype(slim[c].dtype)
 
 
 def ring_scatter(part, order, height):
@@ -116,12 +126,11 @@
     return jnp.where(place < count // 2, 2 * place, 2 * (count - place) - 1)
 
 
-def reorder_kernel(ahead, here_ref, factors_ref, out_ref, sems):
-    count = len(ahead)
-    width = out_ref.shape[1] // count
+def reorder_kernel(distances, count, here_ref, factors_ref, out_ref, sems):
+    width = factors_ref.shape[1] // count
     mine = place_of(here_ref[0], count)
     copies = []
-    for j, distance in enumerate(ahead):
+    for j, distance in enumerate(distances):
         source = at_place((mine + distance) % count, count) * width
         copies.append(
             pltpu.make_async_copy(
@@ -136,16 +145,61 @@
         copy.wait()
 
 
-def reorder(factors, ahead):
+def reorder(here, factors, distances, count):
+    rows, width = factors.shape[0], factors.shape[1] // count * len(distances)
     return pl.pallas_call(
-        functools.partial(reorder_kernel, tuple(ahead)),
-        out_shape=jax.ShapeDtypeStruct(factors.shape, factors.dtype),
+        functools.partial(reorder_kernel, tuple(distances), count),
+        out_shape=jax.ShapeDtypeStruct((rows, width), factors.dtype),
         in_specs=[pl.BlockSpec(memory_space=pltpu.SMEM), pl.BlockSpec(memory_space=pltpu.HBM)],
         out_specs=pl.BlockSpec(memory_space=pltpu.VMEM),
-        scratch_shapes=[pltpu.SemaphoreType.DMA((len(ahead),))],
-        compiler_params=pltpu.CompilerParams(vmem_limit_bytes=20 << 20),
-        cost_estimate=pl.CostEstimate(flops=0, transcendentals=0, bytes_accessed=factors.size * factors.dtype.itemsize),
-    )(lax.axis_index("net").reshape(1), factors)
+        scratch_shapes=[pltpu.SemaphoreType.DMA((len(distances),))],
+        compiler_params=pltpu.CompilerParams(vmem_limit_bytes=50 << 20),
+        cost_estimate=pl.CostEstimate(flops=0, transcendentals=0, bytes_accessed=rows * width * factors.dtype.itemsize),
+    )(here, factors)
+
+
+def narrow_kernel(wide_ref, *out_refs):
+    height = out_refs[0].shape[0]
+    for c, ref in enumerate(out_refs):
+        ref[...] = wide_ref[pl.ds(c * height, height), :].astype(ref.dtype)
+
+
+def last_update_kernel(lows, here_ref, *refs):
+    spread_ref, ahead, behind = refs[0], refs[1 : chunks + 1], refs[chunks + 1 : 2 * chunks + 1]
+    inject_ref, out_ref, edge_ref = refs[2 * chunks + 1 :]
+    height = ahead[0].shape[0]
+    first = here_ref[1] == 0
+    for c, low in enumerate(lows):
+        rows = pl.ds(c * height, height)
+        total = spread_ref[pl.ds(low, height), :]
+        total = total + ahead[c][...].astype(jnp.float32) + behind[c][...].astype(jnp.float32)
+        inject = inject_ref[rows, :] - relax_step * total
+        out_ref[rows, :] = inject
+        edge_ref[rows, :] = jnp.where(first, inject[:, -1:], inject[:, :1])
+
+
+def ramp_kernel(here_ref, inject_ref, edge_ref, bound_ref, out_ref):
+    first = here_ref[1] == 0
+    inject, edge, bound = inject_ref[...], edge_ref[...], bound_ref[...]
+    periods = inject.shape[1]
+    lane = lax.broadcasted_iota(jnp.int32, inject.shape, 1)
+
+    def excess(step):
+        return step - jnp.clip(step, -bound, bound)
+
+    before = jnp.where(lane == 0, edge, pltpu.roll(inject, 1, 1))
+    after = jnp.where(lane == periods - 1, edge, pltpu.roll(inject, periods - 1, 1))
+    low = jnp.where((lane == 0) & first, 0.0, excess(inject - before))
+    high = jnp.where((lane == periods - 1) & jnp.logical_not(first), 0.0, excess(after - inject))
+    out_ref[...] = inject - 0.5 * low + 0.5 * high
+
+
+def norms_kernel(entries, sums_ref, out_ref):
+    lane = lax.broadcasted_iota(jnp.int32, out_ref.shape, 1)
+    out = jnp.zeros(out_ref.shape, jnp.float32)
+    for k in range(passes):
+        out = jnp.where(lane == k, jnp.sum(sums_ref[pl.ds(8 * k, 8), :]), out)
+    out_ref[...] = jnp.sqrt(out / entries)
 
 
 def limits_of(outage_line, ratings):
@@ -197,68 +251,95 @@
     limits = limits_of(outage_line, ratings)
     owned, periods = proposal.shape
     count = lax.axis_size("net")
-    ring = count <= longest_ring and count % 2 == 0
+    ring = is_ring(count, lax.axis_size("tm"))
     height = owned // chunks
+    here = jnp.stack([lax.axis_index("net"), lax.axis_index("tm")]).astype(jnp.int32)
     if ring:
         order = ring_order(count)
-        ahead = by_distance(count)
-        near = count - 3 if count > 4 else count // 2
-        factors = reorder(shift_factors, ahead)
-        cut = near * owned
+        groups = ring_groups(count)
+        factors = []
+        for group in groups:
+            factors.append(reorder(here, shift_factors, group, count))
 
     def forward(pieces):
         if not ring:
             whole = lax.all_gather(jnp.concatenate(pieces, axis=0), "net", axis=0, tiled=True)
             return jnp.dot(shift_factors, whole, preferred_element_type=jnp.float32)
         got = ring_gather(pieces, order)
-        flows = 0.0
-        for group, cols in ((ahead[:near], slice(0, cut)), (ahead[near:], slice(cut, None))):
+        flows = None
+        for group, cols in zip(groups, factors):
             blocks = jnp.concatenate([got[c][d] for d in group for c in range(chunks)], axis=0)
-            flows = flows + jnp.dot(factors[:, cols], blocks, preferred_element_type=jnp.float32)
+            share = jnp.dot(cols, blocks, preferred_element_type=jnp.float32)
+            flows = share if flows is None else flows + share
         return flows
 
-    def backward(stage, misfit, pieces):
+    def backward(misfit):
         narrow = misfit.astype(jnp.bfloat16)
-
-        def share(cols):
-            return lax.dot_general(cols, narrow, (((0,), (0,)), ((), ())), preferred_element_type=jnp.float32)
-
-        if not ring:
-            spread = lax.psum_scatter(share(shift_factors), "net", scatter_dimension=0, tiled=True)
-            pieces = [p - relax_step * spread[c * height : (c + 1) * height] for c, p in enumerate(pieces)]
-            return pieces, [p.astype(jnp.bfloat16) for p in pieces]
-        far, close = share(factors[:, cut:]), share(factors[:, :cut])
-
-        def part(chunk, distance):
-            j = ahead.index(distance)
-            spread, first = (close, 0) if j < near else (far, near)
-            return spread, (j - first) * owned + chunk * height
-
-        held = ring_scatter(part, order, height)
-        wide, slim = [], []
-        for c, p in enumerate(pieces):
-            shapes = [jax.ShapeDtypeStruct(p.shape, jnp.float32)]
-            if stage + 1 < passes:
-                shapes.append(jax.ShapeDtypeStruct(p.shape, jnp.bfloat16))
-            spread, low = part(c, 0)
-            new = small_call(functools.partial(update_kernel, low), shapes, spread, held[c, 1], held[c, -1], p)
-            wide.append(new[0])
-            slim.append(new[-1])
-        return wide, slim
-
-    pieces = [proposal[c * height : (c + 1) * height] for c in range(chunks)]
-    slim = [p.astype(jnp.bfloat16) for p in pieces]
+        shares = {}
+        for group, cols in reversed(list(zip(groups, factors))):
+            spread = lax.dot_general(cols, narrow, (((0,), (0,)), ((), ())), preferred_element_type=jnp.float32)
+            for j, d in enumerate(group):
+                for c in range(chunks):
+                    shares[c, d] = (spread, j * owned + c * height)
+        held = ring_scatter(lambda c, d: shares[c, d], order, height)
+        return [shares[c, 0] for c in range(chunks)], held
+
     dual = flow_dual
     sums = []
+    entries = float(shift_factors.shape[0] * count * periods * lax.axis_size("tm"))
+    if not ring:
+        inject = proposal
+        for _ in range(passes):
+            misfit, dual = project(forward([inject.astype(jnp.bfloat16)]), dual, limits)
+            sums.append(jnp.sum(misfit * misfit))
+            share = lax.dot_general(
+                shift_factors,
+                misfit.astype(jnp.bfloat16),
+                (((0,), (0,)), ((), ())),
+                preferred_element_type=jnp.float32,
+            )
+            inject = inject - relax_step * lax.psum_scatter(share, "net", scatter_dimension=0, tiled=True)
+        norms = jnp.sqrt(total_over(jnp.stack(sums), ("tm", "net")) / entries)
+        return (ramp(inject, ramp_limit), dual, norms)
+
+    chunk_shape = jax.ShapeDtypeStruct((height, periods), jnp.bfloat16)
+    whole_shape = jax.ShapeDtypeStruct((owned, periods), jnp.float32)
+    slim = small_call(narrow_kernel, [chunk_shape] * chunks, proposal)
+    bound = jnp.broadcast_to(ramp_limit[:, None], (owned, periods))
+    inject = proposal
     for stage in range(passes):
         misfit, dual = project(forward(slim), dual, limits)
         sums.append(jnp.sum((misfit * misfit).reshape(-1, 8, periods), axis=0))
-        pieces, slim = backward(stage, misfit, pieces)
-    inject = jnp.concatenate(pieces, axis=0)
+        own, held = backward(misfit)
+        lows = tuple(low for _, low in own)
+        arrived = [held[c, way] for way in (1, -1) for c in range(chunks)]
+        if stage + 1 < passes:
+            inject, *slim = small_call(
+                functools.partial(update_kernel, lows),
+                [whole_shape] + [chunk_shape] * chunks,
+                own[0][0],
+                *arrived,
+                inject,
+            )
+        else:
+            inject, edge = small_call(
+                functools.partial(last_update_kernel, lows),
+                [whole_shape, jax.ShapeDtypeStruct((owned, 1), jnp.float32)],
+                here,
+                own[0][0],
+                *arrived,
+                inject,
+            )
     sums = total_over(jnp.concatenate(sums, axis=0), ("tm", "net"))
-    sums = jnp.sum(sums.reshape(passes, -1), axis=1)
-    entries = jnp.float32(shift_factors.shape[0] * count * periods * lax.axis_size("tm"))
-    residual_norms = jnp.sqrt(sums / entries)
+    tile = jax.ShapeDtypeStruct((8, periods), jnp.float32)
+    norms = small_call(functools.partial(norms_kernel, entries), tile, sums)[0, :passes]
+    edge = lax.ppermute(edge, "tm", [(0, 1), (1, 0)])
+    dispatch = small_call(ramp_kernel, whole_shape, here, inject, edge, bound)
+    return (dispatch, dual, norms)
+
+
+def ramp(inject, ramp_limit):
+    periods = inject.shape[1]
     low, high = beside(inject, "tm")
     padded = jnp.concatenate([low, inject, high], axis=1)
     step = padded[:, 1:] - padded[:, :-1]
@@ -266,8 +347,7 @@
     moment = lax.axis_index("tm") * periods + lax.broadcasted_iota(jnp.int32, (1, periods + 1), 1)
     valid = (moment >= 1) & (moment <= periods * lax.axis_size("tm") - 1)
     excess = jnp.where(valid, step - jnp.clip(step, -bound, bound), 0.0)
-    dispatch = inject - 0.5 * excess[:, :-1] + 0.5 * excess[:, 1:]
-    return (dispatch, dual, residual_norms)
+    return inject - 0.5 * excess[:, :-1] + 0.5 * excess[:, 1:]
 
 
 def solution(mesh):

time: 138 us -> 139 us (level)
  waiting for transfers between devices: 37.5 us -> 44.2 us
  other arithmetic: 6.12 us -> 1.18 us
  local copies, waits for them, and re-layouts: 6.77 us -> 2.03 us
  Pallas kernels: 9.49 us -> 12.2 us
  matrix products: 11 us -> 12.5 us
    ppermute x56, waiting for transfers between devices: 31 us -> 36.4 us  [hop_to(): return lax.ppermute(block, 'net', pairs)]
    unnamed x38 -> x18, local copies, waits for them, and re-layouts: 5.85 us -> 1.22 us
    pallas_call x25 -> x29, Pallas kernels: 9.49 us -> 12.2 us  [the longest x4 8.49 us: reorder(): pl.pallas_call(functools.partial(reorder_kernel, tuple(distances), count)...]
    ppermute x56, starting transfers between devices: 61.4 us -> 59.6 us  [hop_to(): return lax.ppermute(block, 'net', pairs)]
    dot_general x8 -> x16, matrix products: 11 us -> 12.5 us  [the longest x8 6.48 us: forward(): share = jnp.dot(cols, blocks, preferred_element_type=jnp.float32)]
    reduce_sum x2 -> x0, other arithmetic: 1.44 us -> none  [body(): sums = jnp.sum(sums.reshape(passes, -1), axis=1)]
  transfers between devices with their start and end apart: 61 -> 61, of which waited for: 25 -> 25; matrix products, arithmetic and copies ran while one was open for 9% -> 7% of each run, Pallas kernels for 6% -> 7%
where the time goes in v3:
time: 139 us; the launch traced here: 138 us
  starting transfers between devices  65.1 us (47%)
  waiting for transfers between devices  44.2 us (32%)
  matrix products  12.5 us (9%)
  Pallas kernels  12.2 us (9%)
  local copies, waits for them, and re-layouts  2.03 us (1%)
    ppermute x56, starting transfers between devices, hop_to(): return lax.ppermute(block, 'net', pairs)  59.6 us
    ppermute x56, waiting for transfers between devices, hop_to(): return lax.ppermute(block, 'net', pairs)  36.4 us
    pallas_call x4, Pallas kernels, reorder(): pl.pallas_call(functools.partial(reorder_kernel, tuple(distances), count)...  8.49 us
    dot_general x8, matrix products, forward(): share = jnp.dot(cols, blocks, preferred_element_type=jnp.float32)  6.48 us
    ppermute x4, waiting for transfers between devices, total_over(): lax.ppermute(value, axis, [(i, i ^ bit) for i in range(lax.axis_size(axis...  6.44 us
    dot_general x8, matrix products, backward(): lax.dot_general(cols, narrow, (((0,), (0,)), ((), ())), preferred_element...  5.98 us
    ppermute x4, starting transfers between devices, total_over(): lax.ppermute(value, axis, [(i, i ^ bit) for i in range(lax.axis_size(axis...  5.48 us
    pallas_call x25, Pallas kernels, small_call(): pl.pallas_call(kernel, out_shape=out_shape, in_specs=[pl.BlockSpec(memory...  3.75 us
  transfers between devices with their start and end apart: 61, of which 25 were waited for; matrix products, arithmetic and copies ran while one was open for 7% of the time, Pallas kernels for 7%

profile of v3, /device:TPU:0, one launch (start us, length us, event | category | flops | bytes accessed | tf_op | source)
XLA Modules:
  0.0 138.4 jit_solution(5747886631211549931)
XLA Ops:
  1.7 3.1 %collective-permute-start = (bf16[512,128]{1,0:T(8,128)(2,1)S(1)}, bf16[512,128]{1,0:T(8,128)(2,1)S(1)}, u32[]{:S(2)}, u32[]{:S(2)}) collective-permute-start(bf16[512,128]{1,0:T(8,128)(2,1)S(1)} %get-tuple-element.10), channel_id=1, source_target_pairs={{0,4},{4,8},{8,12},{12,14},{14,10},{10,6},{6,2},{2,0},{1,5},{5,9},... | collective-permute-start | bytes 393224 | tf_op jit(solution)/shard_map/ppermute | solution.py:48
  4.8 2.0 %collective-permute-start.1 = (bf16[512,128]{1,0:T(8,128)(2,1)S(1)}, bf16[512,128]{1,0:T(8,128)(2,1)S(1)}, u32[]{:S(2)}, u32[]{:S(2)}) collective-permute-start(bf16[512,128]{1,0:T(8,128)(2,1)S(1)} %get-tuple-element.11), channel_id=1, source_target_pairs={{0,4},{4,8},{8,12},{12,14},{14,10},{10,6},{6,2},{2,0},{1,5},{5,9},... | collective-permute-start | bytes 393224 | tf_op jit(solution)/shard_map/ppermute | solution.py:48
  7.9 2.5 %shard_map.85 = bf16[512,3072]{1,0:T(8,128)(2,1)S(1)} custom-call(s32[2]{0:T(128)S(1)} %pad_add_fusion.here_ref, bf16[512,8192]{1,0:T(8,128)(2,1)} %factors_ref.7), custom_call_target="tpu_custom_call" | custom-call | bytes 3145728 | tf_op jit(solution)/shard_map/pallas_call | solution.py:150
  10.4 2.1 %shard_map.87 = bf16[512,2048]{1,0:T(8,128)(2,1)S(1)} custom-call(s32[2]{0:T(128)S(1)} %pad_add_fusion.here_ref, bf16[512,8192]{1,0:T(8,128)(2,1)} %factors_ref.7), custom_call_target="tpu_custom_call" | custom-call | bytes 2097152 | tf_op jit(solution)/shard_map/pallas_call | solution.py:150
  12.5 2.1 %shard_map.88 = bf16[512,2048]{1,0:T(8,128)(2,1)S(1)} custom-call(s32[2]{0:T(128)S(1)} %pad_add_fusion.here_ref, bf16[512,8192]{1,0:T(8,128)(2,1)} %factors_ref.7), custom_call_target="tpu_custom_call" | custom-call | bytes 2097152 | tf_op jit(solution)/shard_map/pallas_call | solution.py:150
  14.6 1.8 %shard_map.89 = bf16[512,1024]{1,0:T(8,128)(2,1)S(1)} custom-call(s32[2]{0:T(128)S(1)} %pad_add_fusion.here_ref, bf16[512,8192]{1,0:T(8,128)(2,1)} %factors_ref.7), custom_call_target="tpu_custom_call" | custom-call | bytes 1048576 | tf_op jit(solution)/shard_map/pallas_call | solution.py:150
  16.5 2.1 %collective-permute-start.4 = (bf16[512,128]{1,0:T(8,128)(2,1)S(1)}, bf16[512,128]{1,0:T(8,128)(2,1)S(1)}, u32[]{:S(2)}, u32[]{:S(2)}) collective-permute-start(bf16[512,128]{1,0:T(8,128)(2,1)S(1)} %collective-permute-done), channel_id=1, source_target_pairs={{0,4},{4,8},{8,12},{12,14},{14,10},{10,6},{6,2},{2,0},{1,5},{5,9},... | collective-permute-start | bytes 393224 | tf_op jit(solution)/shard_map/ppermute | solution.py:48
  18.6 1.6 %collective-permute-start.5 = (bf16[512,128]{1,0:T(8,128)(2,1)S(1)}, bf16[512,128]{1,0:T(8,128)(2,1)S(1)}, u32[]{:S(2)}, u32[]{:S(2)}) collective-permute-start(bf16[512,128]{1,0:T(8,128)(2,1)S(1)} %collective-permute-done.1), channel_id=1, source_target_pairs={{0,4},{4,8},{8,12},{12,14},{14,10},{10,6},{6,2},{2,0},{1,5},{5,9},... | collective-permute-start | bytes 393224 | tf_op jit(solution)/shard_map/ppermute | solution.py:48
  21.8 4.9 %collective-permute-done.7 = bf16[512,128]{1,0:T(8,128)(2,1)S(1)} collective-permute-done((bf16[512,128]{1,0:T(8,128)(2,1)S(1)}, bf16[512,128]{1,0:T(8,128)(2,1)S(1)}, u32[]{:S(2)}, u32[]{:S(2)}) %collective-permute-start.7) | collective-permute-done | bytes 131104 | tf_op jit(solution)/shard_map/ppermute | solution.py:48
  27.8 1.4 %collective-permute-start.9 = (bf16[512,128]{1,0:T(8,128)(2,1)S(1)}, bf16[512,128]{1,0:T(8,128)(2,1)S(1)}, u32[]{:S(2)}, u32[]{:S(2)}) collective-permute-start(bf16[512,128]{1,0:T(8,128)(2,1)S(1)} %collective-permute-done.5), channel_id=1, source_target_pairs={{0,4},{4,8},{8,12},{12,14},{14,10},{10,6},{6,2},{2,0},{1,5},{5,9},... | collective-permute-start | bytes 393224 | tf_op jit(solution)/shard_map/ppermute | solution.py:48
  29.2 1.6 %collective-permute-start.8 = (bf16[512,128]{1,0:T(8,128)(2,1)S(1)}, bf16[512,128]{1,0:T(8,128)(2,1)S(1)}, u32[]{:S(2)}, u32[]{:S(2)}) collective-permute-start(bf16[512,128]{1,0:T(8,128)(2,1)S(1)} %collective-permute-done.4), channel_id=1, source_target_pairs={{0,4},{4,8},{8,12},{12,14},{14,10},{10,6},{6,2},{2,0},{1,5},{5,9},... | collective-permute-start | bytes 393224 | tf_op jit(solution)/shard_map/ppermute | solution.py:48
  31.5 1.4 %collective-permute-done.11 = bf16[512,128]{1,0:T(8,128)(2,1)S(1)} collective-permute-done((bf16[512,128]{1,0:T(8,128)(2,1)S(1)}, bf16[512,128]{1,0:T(8,128)(2,1)S(1)}, u32[]{:S(2)}, u32[]{:S(2)}) %collective-permute-start.11) | collective-permute-done | bytes 131104 | tf_op jit(solution)/shard_map/ppermute | solution.py:48
  33.4 2.1 %collective-permute-done.8 = bf16[512,128]{1,0:T(8,128)(2,1)S(1)} collective-permute-done((bf16[512,128]{1,0:T(8,128)(2,1)S(1)}, bf16[512,128]{1,0:T(8,128)(2,1)S(1)}, u32[]{:S(2)}, u32[]{:S(2)}) %collective-permute-start.8) | collective-permute-done | bytes 131104 | tf_op jit(solution)/shard_map/ppermute | solution.py:48
  35.6 1.4 %collective-permute-start.12 = (bf16[512,128]{1,0:T(8,128)(2,1)S(1)}, bf16[512,128]{1,0:T(8,128)(2,1)S(1)}, u32[]{:S(2)}, u32[]{:S(2)}) collective-permute-start(bf16[512,128]{1,0:T(8,128)(2,1)S(1)} %collective-permute-done.8), channel_id=1, source_target_pairs={{0,4},{4,8},{8,12},{12,14},{14,10},{10,6},{6,2},{2,0},{1,5},{5,9},... | collective-permute-start | bytes 393224 | tf_op jit(solution)/shard_map/ppermute | solution.py:48
  37.9 3.4 %collective-permute-done.12 = bf16[512,128]{1,0:T(8,128)(2,1)S(1)} collective-permute-done((bf16[512,128]{1,0:T(8,128)(2,1)S(1)}, bf16[512,128]{1,0:T(8,128)(2,1)S(1)}, u32[]{:S(2)}, u32[]{:S(2)}) %collective-permute-start.12) | collective-permute-done | bytes 131104 | tf_op jit(solution)/shard_map/ppermute | solution.py:48
  43.1 1.6 %collective-permute-start.14 = (bf16[512,128]{1,0:T(8,128)(2,1)S(1)}, bf16[512,128]{1,0:T(8,128)(2,1)S(1)}, u32[]{:S(2)}, u32[]{:S(2)}) collective-permute-start(bf16[512,128]{1,0:T(8,128)(2,1)S(1)} %get-tuple-element.26), channel_id=1, source_target_pairs={{0,4},{4,8},{8,12},{12,14},{14,10},{10,6},{6,2},{2,0},{1,5},{5,9},... | collective-permute-start | bytes 393224 | tf_op jit(solution)/shard_map/ppermute | solution.py:48
  45.5 1.3 collective-permute-start.18
  47.6 2.0 %collective-permute-done.14.arrived_ref = bf16[512,128]{1,0:T(8,128)(2,1)S(1)} collective-permute-done((bf16[512,128]{1,0:T(8,128)(2,1)S(1)}, bf16[512,128]{1,0:T(8,128)(2,1)S(1)}, u32[]{:S(2)}, u32[]{:S(2)}) %collective-permute-start.14) | collective-permute-done | bytes 131104 | tf_op jit(solution)/shard_map/ppermute | solution.py:48
  49.7 1.5 %collective-permute-start.15 = (bf16[512,128]{1,0:T(8,128)(2,1)S(1)}, bf16[512,128]{1,0:T(8,128)(2,1)S(1)}, u32[]{:S(2)}, u32[]{:S(2)}) collective-permute-start(bf16[512,128]{1,0:T(8,128)(2,1)S(1)} %shard_map.90), channel_id=1, source_target_pairs={{0,4},{4,8},{8,12},{12,14},{14,10},{10,6},{6,2},{2,0},{1,5},{5,9},... | collective-permute-start | bytes 393224 | tf_op jit(solution)/shard_map/ppermute | solution.py:48
  52.8 1.4 collective-permute-start.19
  63.4 2.0 %collective-permute-done.20.refs_1_ = bf16[512,128]{1,0:T(8,128)(2,1)S(1)} collective-permute-done((bf16[512,128]{1,0:T(8,128)(2,1)S(1)}, bf16[512,128]{1,0:T(8,128)(2,1)S(1)}, u32[]{:S(2)}, u32[]{:S(2)}) %collective-permute-start.20) | collective-permute-done | bytes 131104 | tf_op jit(solution)/shard_map/ppermute | solution.py:48
  65.3 1.2 collective-permute-done.23.refs_2_
  66.5 1.6 %collective-permute-done.17.refs_0_ = bf16[512,128]{1,0:T(8,128)(2,1)S(1)} collective-permute-done((bf16[512,128]{1,0:T(8,128)(2,1)S(1)}, bf16[512,128]{1,0:T(8,128)(2,1)S(1)}, u32[]{:S(2)}, u32[]{:S(2)}) %collective-permute-start.17) | collective-permute-done | bytes 131104 | tf_op jit(solution)/shard_map/ppermute | solution.py:48
  68.3 1.8 %collective-permute-start.28 = (bf16[512,128]{1,0:T(8,128)(2,1)S(1)}, bf16[512,128]{1,0:T(8,128)(2,1)S(1)}, u32[]{:S(2)}, u32[]{:S(2)}) collective-permute-start(bf16[512,128]{1,0:T(8,128)(2,1)S(1)} %get-tuple-element.12), channel_id=1, source_target_pairs={{0,4},{4,8},{8,12},{12,14},{14,10},{10,6},{6,2},{2,0},{1,5},{5,9},... | collective-permute-start | bytes 393224 | tf_op jit(solution)/shard_map/ppermute | solution.py:48
  70.4 1.7 %collective-permute-start.29 = (bf16[512,128]{1,0:T(8,128)(2,1)S(1)}, bf16[512,128]{1,0:T(8,128)(2,1)S(1)}, u32[]{:S(2)}, u32[]{:S(2)}) collective-permute-start(bf16[512,128]{1,0:T(8,128)(2,1)S(1)} %get-tuple-element.13), channel_id=1, source_target_pairs={{0,4},{4,8},{8,12},{12,14},{14,10},{10,6},{6,2},{2,0},{1,5},{5,9},... | collective-permute-start | bytes 393224 | tf_op jit(solution)/shard_map/ppermute | solution.py:48
  73.3 1.7 %collective-permute-start.32 = (bf16[512,128]{1,0:T(8,128)(2,1)S(1)}, bf16[512,128]{1,0:T(8,128)(2,1)S(1)}, u32[]{:S(2)}, u32[]{:S(2)}) collective-permute-start(bf16[512,128]{1,0:T(8,128)(2,1)S(1)} %collective-permute-done.28), channel_id=1, source_target_pairs={{0,4},{4,8},{8,12},{12,14},{14,10},{10,6},{6,2},{2,0},{1,5},{5,9},... | collective-permute-start | bytes 393224 | tf_op jit(solution)/shard_map/ppermute | solution.py:48
  75.4 1.7 %collective-permute-start.33 = (bf16[512,128]{1,0:T(8,128)(2,1)S(1)}, bf16[512,128]{1,0:T(8,128)(2,1)S(1)}, u32[]{:S(2)}, u32[]{:S(2)}) collective-permute-start(bf16[512,128]{1,0:T(8,128)(2,1)S(1)} %collective-permute-done.29), channel_id=1, source_target_pairs={{0,4},{4,8},{8,12},{12,14},{14,10},{10,6},{6,2},{2,0},{1,5},{5,9},... | collective-permute-start | bytes 393224 | tf_op jit(solution)/shard_map/ppermute | solution.py:48
  80.3 4.8 %collective-permute-done.35 = bf16[512,128]{1,0:T(8,128)(2,1)S(1)} collective-permute-done((bf16[512,128]{1,0:T(8,128)(2,1)S(1)}, bf16[512,128]{1,0:T(8,128)(2,1)S(1)}, u32[]{:S(2)}, u32[]{:S(2)}) %collective-permute-start.35) | collective-permute-done | bytes 131104 | tf_op jit(solution)/shard_map/ppermute | solution.py:48
  86.0 1.4 collective-permute-start.37
  87.3 1.7 %collective-permute-start.36 = (bf16[512,128]{1,0:T(8,128)(2,1)S(1)}, bf16[512,128]{1,0:T(8,128)(2,1)S(1)}, u32[]{:S(2)}, u32[]{:S(2)}) collective-permute-start(bf16[512,128]{1,0:T(8,128)(2,1)S(1)} %collective-permute-done.32), channel_id=1, source_target_pairs={{0,4},{4,8},{8,12},{12,14},{14,10},{10,6},{6,2},{2,0},{1,5},{5,9},... | collective-permute-start | bytes 393224 | tf_op jit(solution)/shard_map/ppermute | solution.py:48
  90.3 4.0 %collective-permute-done.36 = bf16[512,128]{1,0:T(8,128)(2,1)S(1)} collective-permute-done((bf16[512,128]{1,0:T(8,128)(2,1)S(1)}, bf16[512,128]{1,0:T(8,128)(2,1)S(1)}, u32[]{:S(2)}, u32[]{:S(2)}) %collective-permute-start.36) | collective-permute-done | bytes 131104 | tf_op jit(solution)/shard_map/ppermute | solution.py:48
  96.2 3.1 %collective-permute-done.40 = bf16[512,128]{1,0:T(8,128)(2,1)S(1)} collective-permute-done((bf16[512,128]{1,0:T(8,128)(2,1)S(1)}, bf16[512,128]{1,0:T(8,128)(2,1)S(1)}, u32[]{:S(2)}, u32[]{:S(2)}) %collective-permute-start.40) | collective-permute-done | bytes 131104 | tf_op jit(solution)/shard_map/ppermute | solution.py:48
  99.3 1.2 add_add_fusion
  102.5 1.2 collective-permute-start.42
  104.6 1.2 collective-permute-start.46
  107.5 1.2 collective-permute-start.43
  109.9 1.2 collective-permute-start.47
  112.6 1.2 collective-permute-start.44
  116.3 1.2 collective-permute-start.48
  119.2 1.2 collective-permute-start.45
  121.3 1.5 %collective-permute-start.58 = (f32[16,128]{1,0:T(8,128)S(1)}, f32[16,128]{1,0:T(8,128)S(1)}, u32[]{:S(2)}, u32[]{:S(2)}) collective-permute-start(f32[16,128]{1,0:T(8,128)S(1)} %fusion.44), channel_id=1, source_target_pairs={{0,2},{2,0},{4,6},{6,4},{8,10},{10,8},{12,14},{14,12},{1,3},{3,1},... | collective-permute-start | bytes 24584 | tf_op jit(solution)/shard_map/ppermute | solution.py:231
  122.9 2.1 %collective-permute-done.58 = f32[16,128]{1,0:T(8,128)S(1)} collective-permute-done((f32[16,128]{1,0:T(8,128)S(1)}, f32[16,128]{1,0:T(8,128)S(1)}, u32[]{:S(2)}, u32[]{:S(2)}) %collective-permute-start.58) | collective-permute-done | bytes 8224 | tf_op jit(solution)/shard_map/ppermute | solution.py:231
  125.0 1.2 collective-permute-start.59
  126.2 2.5 %collective-permute-done.59 = f32[16,128]{1,0:T(8,128)S(1)} collective-permute-done((f32[16,128]{1,0:T(8,128)S(1)}, f32[16,128]{1,0:T(8,128)S(1)}, u32[]{:S(2)}, u32[]{:S(2)}) %collective-permute-start.59) | collective-permute-done | bytes 8224 | tf_op jit(solution)/shard_map/ppermute | solution.py:231
  128.7 2.7 %collective-permute-start.60 = (f32[16,128]{1,0:T(8,128)S(1)}, f32[16,128]{1,0:T(8,128)S(1)}, u32[]{:S(2)}, u32[]{:S(2)}) collective-permute-start(f32[16,128]{1,0:T(8,128)S(1)} %add.54), channel_id=1, source_target_pairs={{0,8},{2,10},{4,12},{6,14},{8,0},{10,2},{12,4},{14,6},{1,9},{3,11}... | collective-permute-start | bytes 24584 | tf_op jit(solution)/shard_map/ppermute | solution.py:231
  131.4 1.8 %collective-permute-done.60 = f32[16,128]{1,0:T(8,128)S(1)} collective-permute-done((f32[16,128]{1,0:T(8,128)S(1)}, f32[16,128]{1,0:T(8,128)S(1)}, u32[]{:S(2)}, u32[]{:S(2)}) %collective-permute-start.60) | collective-permute-done | bytes 8224 | tf_op jit(solution)/shard_map/ppermute | solution.py:231
  134.9 1.4 collective-permute-done.56.edge_ref
  136.5 1.9 %shard_map.112 = f32[1024,128]{1,0:T(8,128)} custom-call(s32[2]{0:T(128)S(1)} %pad_add_fusion.here_ref, f32[1024,128]{1,0:T(8,128)S(1)} %get-tuple-element.15.inject_ref, f32[1024,1]{1,0:T(8,128)S(1)} %collective-permute-done.56.edge_ref, f32[1024,128]{1,0:T(8,128)S(1)} %broadcast_in_dim.24.bound_ref), custom_call_target="tpu_custom_call" | custom-call | bytes 1572864 | tf_op jit(solution)/shard_map/pallas_call | solution.py:78
  (155 shorter events, 44.2 us)
Async XLA Ops:
  1.7 14.7 %collective-permute-start = (bf16[512,128]{1,0:T(8,128)(2,1)S(1)}, bf16[512,128]{1,0:T(8,128)(2,1)S(1)}, u32[]{:S(2)}, u32[]{:S(2)}) collective-permute-start(bf16[512,128]{1,0:T(8,128)(2,1)S(1)} %get-tuple-element.10), channel_id=1, source_target_pairs={{0,4},{4,8},{8,12},{12,14},{14,10},{10,6},{6,2},{2,0},{1,5},{5,9},... | collective-permute-start | bytes 393224 | tf_op jit(solution)/shard_map/ppermute | solution.py:48
  4.8 15.4 %collective-permute-start.2 = (bf16[512,128]{1,0:T(8,128)(2,1)S(1)}, bf16[512,128]{1,0:T(8,128)(2,1)S(1)}, u32[]{:S(2)}, u32[]{:S(2)}) collective-permute-start(bf16[512,128]{1,0:T(8,128)(2,1)S(1)} %get-tuple-element.10), channel_id=1, source_target_pairs={{0,2},{4,0},{8,4},{12,8},{14,12},{10,14},{6,10},{2,6},{1,3},{5,1},... | collective-permute-start | bytes 393224 | tf_op jit(solution)/shard_map/ppermute | solution.py:48
  4.8 13.7 %collective-permute-start.1 = (bf16[512,128]{1,0:T(8,128)(2,1)S(1)}, bf16[512,128]{1,0:T(8,128)(2,1)S(1)}, u32[]{:S(2)}, u32[]{:S(2)}) collective-permute-start(bf16[512,128]{1,0:T(8,128)(2,1)S(1)} %get-tuple-element.11), channel_id=1, source_target_pairs={{0,4},{4,8},{8,12},{12,14},{14,10},{10,6},{6,2},{2,0},{1,5},{5,9},... | collective-permute-start | bytes 393224 | tf_op jit(solution)/shard_map/ppermute | solution.py:48
  6.8 13.9 %collective-permute-start.3 = (bf16[512,128]{1,0:T(8,128)(2,1)S(1)}, bf16[512,128]{1,0:T(8,128)(2,1)S(1)}, u32[]{:S(2)}, u32[]{:S(2)}) collective-permute-start(bf16[512,128]{1,0:T(8,128)(2,1)S(1)} %get-tuple-element.11), channel_id=1, source_target_pairs={{0,2},{4,0},{8,4},{12,8},{14,12},{10,14},{6,10},{2,6},{1,3},{5,1},... | collective-permute-start | bytes 393224 | tf_op jit(solution)/shard_map/ppermute | solution.py:48
  16.5 12.8 %collective-permute-start.4 = (bf16[512,128]{1,0:T(8,128)(2,1)S(1)}, bf16[512,128]{1,0:T(8,128)(2,1)S(1)}, u32[]{:S(2)}, u32[]{:S(2)}) collective-permute-start(bf16[512,128]{1,0:T(8,128)(2,1)S(1)} %collective-permute-done), channel_id=1, source_target_pairs={{0,4},{4,8},{8,12},{12,14},{14,10},{10,6},{6,2},{2,0},{1,5},{5,9},... | collective-permute-start | bytes 393224 | tf_op jit(solution)/shard_map/ppermute | solution.py:48
  18.6 9.2 %collective-permute-start.5 = (bf16[512,128]{1,0:T(8,128)(2,1)S(1)}, bf16[512,128]{1,0:T(8,128)(2,1)S(1)}, u32[]{:S(2)}, u32[]{:S(2)}) collective-permute-start(bf16[512,128]{1,0:T(8,128)(2,1)S(1)} %collective-permute-done.1), channel_id=1, source_target_pairs={{0,4},{4,8},{8,12},{12,14},{14,10},{10,6},{6,2},{2,0},{1,5},{5,9},... | collective-permute-start | bytes 393224 | tf_op jit(solution)/shard_map/ppermute | solution.py:48
  20.2 7.0 %collective-permute-start.6 = (bf16[512,128]{1,0:T(8,128)(2,1)S(1)}, bf16[512,128]{1,0:T(8,128)(2,1)S(1)}, u32[]{:S(2)}, u32[]{:S(2)}) collective-permute-start(bf16[512,128]{1,0:T(8,128)(2,1)S(1)} %collective-permute-done.2), channel_id=1, source_target_pairs={{0,2},{4,0},{8,4},{12,8},{14,12},{10,14},{6,10},{2,6},{1,3},{5,1},... | collective-permute-start | bytes 393224 | tf_op jit(solution)/shard_map/ppermute | solution.py:48
  20.8 6.0 %collective-permute-start.7 = (bf16[512,128]{1,0:T(8,128)(2,1)S(1)}, bf16[512,128]{1,0:T(8,128)(2,1)S(1)}, u32[]{:S(2)}, u32[]{:S(2)}) collective-permute-start(bf16[512,128]{1,0:T(8,128)(2,1)S(1)} %collective-permute-done.3), channel_id=1, source_target_pairs={{0,2},{4,0},{8,4},{12,8},{14,12},{10,14},{6,10},{2,6},{1,3},{5,1},... | collective-permute-start | bytes 393224 | tf_op jit(solution)/shard_map/ppermute | solution.py:48
  26.7 6.2 %collective-permute-start.11 = (bf16[512,128]{1,0:T(8,128)(2,1)S(1)}, bf16[512,128]{1,0:T(8,128)(2,1)S(1)}, u32[]{:S(2)}, u32[]{:S(2)}) collective-permute-start(bf16[512,128]{1,0:T(8,128)(2,1)S(1)} %collective-permute-done.7), channel_id=1, source_target_pairs={{0,2},{4,0},{8,4},{12,8},{14,12},{10,14},{6,10},{2,6},{1,3},{5,1},... | collective-permute-start | bytes 393224 | tf_op jit(solution)/shard_map/ppermute | solution.py:48
  27.2 9.8 %collective-permute-start.10 = (bf16[512,128]{1,0:T(8,128)(2,1)S(1)}, bf16[512,128]{1,0:T(8,128)(2,1)S(1)}, u32[]{:S(2)}, u32[]{:S(2)}) collective-permute-start(bf16[512,128]{1,0:T(8,128)(2,1)S(1)} %collective-permute-done.6), channel_id=1, source_target_pairs={{0,2},{4,0},{8,4},{12,8},{14,12},{10,14},{6,10},{2,6},{1,3},{5,1},... | collective-permute-start | bytes 393224 | tf_op jit(solution)/shard_map/ppermute | solution.py:48
  27.8 9.2 %collective-permute-start.9 = (bf16[512,128]{1,0:T(8,128)(2,1)S(1)}, bf16[512,128]{1,0:T(8,128)(2,1)S(1)}, u32[]{:S(2)}, u32[]{:S(2)}) collective-permute-start(bf16[512,128]{1,0:T(8,128)(2,1)S(1)} %collective-permute-done.5), channel_id=1, source_target_pairs={{0,4},{4,8},{8,12},{12,14},{14,10},{10,6},{6,2},{2,0},{1,5},{5,9},... | collective-permute-start | bytes 393224 | tf_op jit(solution)/shard_map/ppermute | solution.py:48
  29.2 6.3 %collective-permute-start.8 = (bf16[512,128]{1,0:T(8,128)(2,1)S(1)}, bf16[512,128]{1,0:T(8,128)(2,1)S(1)}, u32[]{:S(2)}, u32[]{:S(2)}) collective-permute-start(bf16[512,128]{1,0:T(8,128)(2,1)S(1)} %collective-permute-done.4), channel_id=1, source_target_pairs={{0,4},{4,8},{8,12},{12,14},{14,10},{10,6},{6,2},{2,0},{1,5},{5,9},... | collective-permute-start | bytes 393224 | tf_op jit(solution)/shard_map/ppermute | solution.py:48
  35.6 5.8 %collective-permute-start.12 = (bf16[512,128]{1,0:T(8,128)(2,1)S(1)}, bf16[512,128]{1,0:T(8,128)(2,1)S(1)}, u32[]{:S(2)}, u32[]{:S(2)}) collective-permute-start(bf16[512,128]{1,0:T(8,128)(2,1)S(1)} %collective-permute-done.8), channel_id=1, source_target_pairs={{0,4},{4,8},{8,12},{12,14},{14,10},{10,6},{6,2},{2,0},{1,5},{5,9},... | collective-permute-start | bytes 393224 | tf_op jit(solution)/shard_map/ppermute | solution.py:48
  43.1 6.5 %collective-permute-start.14 = (bf16[512,128]{1,0:T(8,128)(2,1)S(1)}, bf16[512,128]{1,0:T(8,128)(2,1)S(1)}, u32[]{:S(2)}, u32[]{:S(2)}) collective-permute-start(bf16[512,128]{1,0:T(8,128)(2,1)S(1)} %get-tuple-element.26), channel_id=1, source_target_pairs={{0,4},{4,8},{8,12},{12,14},{14,10},{10,6},{6,2},{2,0},{1,5},{5,9},... | collective-permute-start | bytes 393224 | tf_op jit(solution)/shard_map/ppermute | solution.py:48
  44.7 6.5 %collective-permute-start.24 = (bf16[512,128]{1,0:T(8,128)(2,1)S(1)}, bf16[512,128]{1,0:T(8,128)(2,1)S(1)}, u32[]{:S(2)}, u32[]{:S(2)}) collective-permute-start(bf16[512,128]{1,0:T(8,128)(2,1)S(1)} %get-tuple-element.25), channel_id=1, source_target_pairs={{0,2},{4,0},{8,4},{12,8},{14,12},{10,14},{6,10},{2,6},{1,3},{5,1},... | collective-permute-start | bytes 393224 | tf_op jit(solution)/shard_map/ppermute | solution.py:48
  45.5 7.2 %collective-permute-start.18 = (bf16[512,128]{1,0:T(8,128)(2,1)S(1)}, bf16[512,128]{1,0:T(8,128)(2,1)S(1)}, u32[]{:S(2)}, u32[]{:S(2)}) collective-permute-start(bf16[512,128]{1,0:T(8,128)(2,1)S(1)} %get-tuple-element.20), channel_id=1, source_target_pairs={{0,4},{4,8},{8,12},{12,14},{14,10},{10,6},{6,2},{2,0},{1,5},{5,9},... | collective-permute-start | bytes 393224 | tf_op jit(solution)/shard_map/ppermute | solution.py:48
  46.8 7.3 %collective-permute-start.21 = (bf16[512,128]{1,0:T(8,128)(2,1)S(1)}, bf16[512,128]{1,0:T(8,128)(2,1)S(1)}, u32[]{:S(2)}, u32[]{:S(2)}) collective-permute-start(bf16[512,128]{1,0:T(8,128)(2,1)S(1)} %get-tuple-element.19), channel_id=1, source_target_pairs={{0,2},{4,0},{8,4},{12,8},{14,12},{10,14},{6,10},{2,6},{1,3},{5,1},... | collective-permute-start | bytes 393224 | tf_op jit(solution)/shard_map/ppermute | solution.py:48
  49.7 6.0 %collective-permute-start.15 = (bf16[512,128]{1,0:T(8,128)(2,1)S(1)}, bf16[512,128]{1,0:T(8,128)(2,1)S(1)}, u32[]{:S(2)}, u32[]{:S(2)}) collective-permute-start(bf16[512,128]{1,0:T(8,128)(2,1)S(1)} %shard_map.90), channel_id=1, source_target_pairs={{0,4},{4,8},{8,12},{12,14},{14,10},{10,6},{6,2},{2,0},{1,5},{5,9},... | collective-permute-start | bytes 393224 | tf_op jit(solution)/shard_map/ppermute | solution.py:48
  51.2 5.6 %collective-permute-start.25 = (bf16[512,128]{1,0:T(8,128)(2,1)S(1)}, bf16[512,128]{1,0:T(8,128)(2,1)S(1)}, u32[]{:S(2)}, u32[]{:S(2)}) collective-permute-start(bf16[512,128]{1,0:T(8,128)(2,1)S(1)} %shard_map.97), channel_id=1, source_target_pairs={{0,2},{4,0},{8,4},{12,8},{14,12},{10,14},{6,10},{2,6},{1,3},{5,1},... | collective-permute-start | bytes 393224 | tf_op jit(solution)/shard_map/ppermute | solution.py:48
  52.8 6.1 %collective-permute-start.19 = (bf16[512,128]{1,0:T(8,128)(2,1)S(1)}, bf16[512,128]{1,0:T(8,128)(2,1)S(1)}, u32[]{:S(2)}, u32[]{:S(2)}) collective-permute-start(bf16[512,128]{1,0:T(8,128)(2,1)S(1)} %shard_map.93), channel_id=1, source_target_pairs={{0,4},{4,8},{8,12},{12,14},{14,10},{10,6},{6,2},{2,0},{1,5},{5,9},... | collective-permute-start | bytes 393224 | tf_op jit(solution)/shard_map/ppermute | solution.py:48
  54.2 5.9 %collective-permute-start.22 = (bf16[512,128]{1,0:T(8,128)(2,1)S(1)}, bf16[512,128]{1,0:T(8,128)(2,1)S(1)}, u32[]{:S(2)}, u32[]{:S(2)}) collective-permute-start(bf16[512,128]{1,0:T(8,128)(2,1)S(1)} %shard_map.95), channel_id=1, source_target_pairs={{0,2},{4,0},{8,4},{12,8},{14,12},{10,14},{6,10},{2,6},{1,3},{5,1},... | collective-permute-start | bytes 393224 | tf_op jit(solution)/shard_map/ppermute | solution.py:48
  55.7 5.4 %collective-permute-start.16 = (bf16[512,128]{1,0:T(8,128)(2,1)S(1)}, bf16[512,128]{1,0:T(8,128)(2,1)S(1)}, u32[]{:S(2)}, u32[]{:S(2)}) collective-permute-start(bf16[512,128]{1,0:T(8,128)(2,1)S(1)} %shard_map.91), channel_id=1, source_target_pairs={{0,4},{4,8},{8,12},{12,14},{14,10},{10,6},{6,2},{2,0},{1,5},{5,9},... | collective-permute-start | bytes 393224 | tf_op jit(solution)/shard_map/ppermute | solution.py:48
  56.9 5.4 %collective-permute-start.26 = (bf16[512,128]{1,0:T(8,128)(2,1)S(1)}, bf16[512,128]{1,0:T(8,128)(2,1)S(1)}, u32[]{:S(2)}, u32[]{:S(2)}) collective-permute-start(bf16[512,128]{1,0:T(8,128)(2,1)S(1)} %shard_map.98), channel_id=1, source_target_pairs={{0,2},{4,0},{8,4},{12,8},{14,12},{10,14},{6,10},{2,6},{1,3},{5,1},... | collective-permute-start | bytes 393224 | tf_op jit(solution)/shard_map/ppermute | solution.py:48
  58.9 6.4 %collective-permute-start.20 = (bf16[512,128]{1,0:T(8,128)(2,1)S(1)}, bf16[512,128]{1,0:T(8,128)(2,1)S(1)}, u32[]{:S(2)}, u32[]{:S(2)}) collective-permute-start(bf16[512,128]{1,0:T(8,128)(2,1)S(1)} %shard_map.94), channel_id=1, source_target_pairs={{0,4},{4,8},{8,12},{12,14},{14,10},{10,6},{6,2},{2,0},{1,5},{5,9},... | collective-permute-start | bytes 393224 | tf_op jit(solution)/shard_map/ppermute | solution.py:48
  60.1 6.4 %collective-permute-start.23 = (bf16[512,128]{1,0:T(8,128)(2,1)S(1)}, bf16[512,128]{1,0:T(8,128)(2,1)S(1)}, u32[]{:S(2)}, u32[]{:S(2)}) collective-permute-start(bf16[512,128]{1,0:T(8,128)(2,1)S(1)} %shard_map.96), channel_id=1, source_target_pairs={{0,2},{4,0},{8,4},{12,8},{14,12},{10,14},{6,10},{2,6},{1,3},{5,1},... | collective-permute-start | bytes 393224 | tf_op jit(solution)/shard_map/ppermute | solution.py:48
  61.1 7.0 %collective-permute-start.17 = (bf16[512,128]{1,0:T(8,128)(2,1)S(1)}, bf16[512,128]{1,0:T(8,128)(2,1)S(1)}, u32[]{:S(2)}, u32[]{:S(2)}) collective-permute-start(bf16[512,128]{1,0:T(8,128)(2,1)S(1)} %shard_map.92), channel_id=1, source_target_pairs={{0,4},{4,8},{8,12},{12,14},{14,10},{10,6},{6,2},{2,0},{1,5},{5,9},... | collective-permute-start | bytes 393224 | tf_op jit(solution)/shard_map/ppermute | solution.py:48
  62.3 5.9 %collective-permute-start.27 = (bf16[512,128]{1,0:T(8,128)(2,1)S(1)}, bf16[512,128]{1,0:T(8,128)(2,1)S(1)}, u32[]{:S(2)}, u32[]{:S(2)}) collective-permute-start(bf16[512,128]{1,0:T(8,128)(2,1)S(1)} %shard_map.99), channel_id=1, source_target_pairs={{0,2},{4,0},{8,4},{12,8},{14,12},{10,14},{6,10},{2,6},{1,3},{5,1},... | collective-permute-start | bytes 393224 | tf_op jit(solution)/shard_map/ppermute | solution.py:48
  70.1 7.1 %collective-permute-start.30 = (bf16[512,128]{1,0:T(8,128)(2,1)S(1)}, bf16[512,128]{1,0:T(8,128)(2,1)S(1)}, u32[]{:S(2)}, u32[]{:S(2)}) collective-permute-start(bf16[512,128]{1,0:T(8,128)(2,1)S(1)} %get-tuple-element.12), channel_id=1, source_target_pairs={{0,2},{4,0},{8,4},{12,8},{14,12},{10,14},{6,10},{2,6},{1,3},{5,1},... | collective-permute-start | bytes 393224 | tf_op jit(solution)/shard_map/ppermute | solution.py:48
  72.2 6.4 %collective-permute-start.31 = (bf16[512,128]{1,0:T(8,128)(2,1)S(1)}, bf16[512,128]{1,0:T(8,128)(2,1)S(1)}, u32[]{:S(2)}, u32[]{:S(2)}) collective-permute-start(bf16[512,128]{1,0:T(8,128)(2,1)S(1)} %get-tuple-element.13), channel_id=1, source_target_pairs={{0,2},{4,0},{8,4},{12,8},{14,12},{10,14},{6,10},{2,6},{1,3},{5,1},... | collective-permute-start | bytes 393224 | tf_op jit(solution)/shard_map/ppermute | solution.py:48
  73.3 14.0 %collective-permute-start.32 = (bf16[512,128]{1,0:T(8,128)(2,1)S(1)}, bf16[512,128]{1,0:T(8,128)(2,1)S(1)}, u32[]{:S(2)}, u32[]{:S(2)}) collective-permute-start(bf16[512,128]{1,0:T(8,128)(2,1)S(1)} %collective-permute-done.28), channel_id=1, source_target_pairs={{0,4},{4,8},{8,12},{12,14},{14,10},{10,6},{6,2},{2,0},{1,5},{5,9},... | collective-permute-start | bytes 393224 | tf_op jit(solution)/shard_map/ppermute | solution.py:48
  75.4 10.5 %collective-permute-start.33 = (bf16[512,128]{1,0:T(8,128)(2,1)S(1)}, bf16[512,128]{1,0:T(8,128)(2,1)S(1)}, u32[]{:S(2)}, u32[]{:S(2)}) collective-permute-start(bf16[512,128]{1,0:T(8,128)(2,1)S(1)} %collective-permute-done.29), channel_id=1, source_target_pairs={{0,4},{4,8},{8,12},{12,14},{14,10},{10,6},{6,2},{2,0},{1,5},{5,9},... | collective-permute-start | bytes 393224 | tf_op jit(solution)/shard_map/ppermute | solution.py:48
  77.2 8.1 %collective-permute-start.34 = (bf16[512,128]{1,0:T(8,128)(2,1)S(1)}, bf16[512,128]{1,0:T(8,128)(2,1)S(1)}, u32[]{:S(2)}, u32[]{:S(2)}) collective-permute-start(bf16[512,128]{1,0:T(8,128)(2,1)S(1)} %collective-permute-done.30), channel_id=1, source_target_pairs={{0,2},{4,0},{8,4},{12,8},{14,12},{10,14},{6,10},{2,6},{1,3},{5,1},... | collective-permute-start | bytes 393224 | tf_op jit(solution)/shard_map/ppermute | solution.py:48
  78.6 6.5 %collective-permute-start.35 = (bf16[512,128]{1,0:T(8,128)(2,1)S(1)}, bf16[512,128]{1,0:T(8,128)(2,1)S(1)}, u32[]{:S(2)}, u32[]{:S(2)}) collective-permute-start(bf16[512,128]{1,0:T(8,128)(2,1)S(1)} %collective-permute-done.31), channel_id=1, source_target_pairs={{0,2},{4,0},{8,4},{12,8},{14,12},{10,14},{6,10},{2,6},{1,3},{5,1},... | collective-permute-start | bytes 393224 | tf_op jit(solution)/shard_map/ppermute | solution.py:48
  85.3 10.2 %collective-permute-start.38 = (bf16[512,128]{1,0:T(8,128)(2,1)S(1)}, bf16[512,128]{1,0:T(8,128)(2,1)S(1)}, u32[]{:S(2)}, u32[]{:S(2)}) collective-permute-start(bf16[512,128]{1,0:T(8,128)(2,1)S(1)} %collective-permute-done.34), channel_id=1, source_target_pairs={{0,2},{4,0},{8,4},{12,8},{14,12},{10,14},{6,10},{2,6},{1,3},{5,1},... | collective-permute-start | bytes 393224 | tf_op jit(solution)/shard_map/ppermute | solution.py:48
  86.0 9.5 %collective-permute-start.37 = (bf16[512,128]{1,0:T(8,128)(2,1)S(1)}, bf16[512,128]{1,0:T(8,128)(2,1)S(1)}, u32[]{:S(2)}, u32[]{:S(2)}) collective-permute-start(bf16[512,128]{1,0:T(8,128)(2,1)S(1)} %collective-permute-done.33), channel_id=1, source_target_pairs={{0,4},{4,8},{8,12},{12,14},{14,10},{10,6},{6,2},{2,0},{1,5},{5,9},... | collective-permute-start | bytes 393224 | tf_op jit(solution)/shard_map/ppermute | solution.py:48
  87.3 7.0 %collective-permute-start.36 = (bf16[512,128]{1,0:T(8,128)(2,1)S(1)}, bf16[512,128]{1,0:T(8,128)(2,1)S(1)}, u32[]{:S(2)}, u32[]{:S(2)}) collective-permute-start(bf16[512,128]{1,0:T(8,128)(2,1)S(1)} %collective-permute-done.32), channel_id=1, source_target_pairs={{0,4},{4,8},{8,12},{12,14},{14,10},{10,6},{6,2},{2,0},{1,5},{5,9},... | collective-permute-start | bytes 393224 | tf_op jit(solution)/shard_map/ppermute | solution.py:48
  90.0 6.2 %collective-permute-start.41 = (bf16[512,128]{1,0:T(8,128)(2,1)S(1)}, bf16[512,128]{1,0:T(8,128)(2,1)S(1)}, u32[]{:S(2)}, u32[]{:S(2)}) collective-permute-start(bf16[512,128]{1,0:T(8,128)(2,1)S(1)} %collective-permute-done.39), channel_id=1, source_target_pairs={{0,2},{4,0},{8,4},{12,8},{14,12},{10,14},{6,10},{2,6},{1,3},{5,1},... | collective-permute-start | bytes 393224 | tf_op jit(solution)/shard_map/ppermute | solution.py:48
  104.6 5.3 %collective-permute-start.46 = (bf16[512,128]{1,0:T(8,128)(2,1)S(1)}, bf16[512,128]{1,0:T(8,128)(2,1)S(1)}, u32[]{:S(2)}, u32[]{:S(2)}) collective-permute-start(bf16[512,128]{1,0:T(8,128)(2,1)S(1)} %get-tuple-element.18), channel_id=1, source_target_pairs={{0,4},{4,8},{8,12},{12,14},{14,10},{10,6},{6,2},{2,0},{1,5},{5,9},... | collective-permute-start | bytes 393224 | tf_op jit(solution)/shard_map/ppermute | solution.py:48
  105.8 5.3 %collective-permute-start.49 = (bf16[512,128]{1,0:T(8,128)(2,1)S(1)}, bf16[512,128]{1,0:T(8,128)(2,1)S(1)}, u32[]{:S(2)}, u32[]{:S(2)}) collective-permute-start(bf16[512,128]{1,0:T(8,128)(2,1)S(1)} %get-tuple-element.17), channel_id=1, source_target_pairs={{0,2},{4,0},{8,4},{12,8},{14,12},{10,14},{6,10},{2,6},{1,3},{5,1},... | collective-permute-start | bytes 393224 | tf_op jit(solution)/shard_map/ppermute | solution.py:48
  109.8 11.6 %collective-permute-start.57 = (f32[16,128]{1,0:T(8,128)S(1)}, f32[16,128]{1,0:T(8,128)S(1)}, u32[]{:S(2)}, u32[]{:S(2)}) collective-permute-start(f32[16,128]{1,0:T(8,128)S(1)} %pad_maximum_fusion), channel_id=1, source_target_pairs={{0,1},{1,0},{2,3},{3,2},{4,5},{5,4},{6,7},{7,6},{8,9},{9,8},{10,11... | collective-permute-start | bytes 24584 | tf_op jit(solution)/shard_map/ppermute | solution.py:231
  109.9 6.4 %collective-permute-start.47 = (bf16[512,128]{1,0:T(8,128)(2,1)S(1)}, bf16[512,128]{1,0:T(8,128)(2,1)S(1)}, u32[]{:S(2)}, u32[]{:S(2)}) collective-permute-start(bf16[512,128]{1,0:T(8,128)(2,1)S(1)} %shard_map.104), channel_id=1, source_target_pairs={{0,4},{4,8},{8,12},{12,14},{14,10},{10,6},{6,2},{2,0},{1,5},{5,9},... | collective-permute-start | bytes 393224 | tf_op jit(solution)/shard_map/ppermute | solution.py:48
  111.1 6.4 %collective-permute-start.50 = (bf16[512,128]{1,0:T(8,128)(2,1)S(1)}, bf16[512,128]{1,0:T(8,128)(2,1)S(1)}, u32[]{:S(2)}, u32[]{:S(2)}) collective-permute-start(bf16[512,128]{1,0:T(8,128)(2,1)S(1)} %shard_map.106), channel_id=1, source_target_pairs={{0,2},{4,0},{8,4},{12,8},{14,12},{10,14},{6,10},{2,6},{1,3},{5,1},... | collective-permute-start | bytes 393224 | tf_op jit(solution)/shard_map/ppermute | solution.py:48
  112.6 6.5 %collective-permute-start.44 = (bf16[512,128]{1,0:T(8,128)(2,1)S(1)}, bf16[512,128]{1,0:T(8,128)(2,1)S(1)}, u32[]{:S(2)}, u32[]{:S(2)}) collective-permute-start(bf16[512,128]{1,0:T(8,128)(2,1)S(1)} %shard_map.102), channel_id=1, source_target_pairs={{0,4},{4,8},{8,12},{12,14},{14,10},{10,6},{6,2},{2,0},{1,5},{5,9},... | collective-permute-start | bytes 393224 | tf_op jit(solution)/shard_map/ppermute | solution.py:48
  113.8 6.6 %collective-permute-start.54 = (bf16[512,128]{1,0:T(8,128)(2,1)S(1)}, bf16[512,128]{1,0:T(8,128)(2,1)S(1)}, u32[]{:S(2)}, u32[]{:S(2)}) collective-permute-start(bf16[512,128]{1,0:T(8,128)(2,1)S(1)} %shard_map.109), channel_id=1, source_target_pairs={{0,2},{4,0},{8,4},{12,8},{14,12},{10,14},{6,10},{2,6},{1,3},{5,1},... | collective-permute-start | bytes 393224 | tf_op jit(solution)/shard_map/ppermute | solution.py:48
  116.3 17.0 %collective-permute-start.48 = (bf16[512,128]{1,0:T(8,128)(2,1)S(1)}, bf16[512,128]{1,0:T(8,128)(2,1)S(1)}, u32[]{:S(2)}, u32[]{:S(2)}) collective-permute-start(bf16[512,128]{1,0:T(8,128)(2,1)S(1)} %shard_map.105), channel_id=1, source_target_pairs={{0,4},{4,8},{8,12},{12,14},{14,10},{10,6},{6,2},{2,0},{1,5},{5,9},... | collective-permute-start | bytes 393224 | tf_op jit(solution)/shard_map/ppermute | solution.py:48
  117.6 15.8 %collective-permute-start.51 = (bf16[512,128]{1,0:T(8,128)(2,1)S(1)}, bf16[512,128]{1,0:T(8,128)(2,1)S(1)}, u32[]{:S(2)}, u32[]{:S(2)}) collective-permute-start(bf16[512,128]{1,0:T(8,128)(2,1)S(1)} %shard_map.107), channel_id=1, source_target_pairs={{0,2},{4,0},{8,4},{12,8},{14,12},{10,14},{6,10},{2,6},{1,3},{5,1},... | collective-permute-start | bytes 393224 | tf_op jit(solution)/shard_map/ppermute | solution.py:48
  119.2 14.2 %collective-permute-start.45 = (bf16[512,128]{1,0:T(8,128)(2,1)S(1)}, bf16[512,128]{1,0:T(8,128)(2,1)S(1)}, u32[]{:S(2)}, u32[]{:S(2)}) collective-permute-start(bf16[512,128]{1,0:T(8,128)(2,1)S(1)} %shard_map.103), channel_id=1, source_target_pairs={{0,4},{4,8},{8,12},{12,14},{14,10},{10,6},{6,2},{2,0},{1,5},{5,9},... | collective-permute-start | bytes 393224 | tf_op jit(solution)/shard_map/ppermute | solution.py:48
  120.4 13.0 %collective-permute-start.55 = (bf16[512,128]{1,0:T(8,128)(2,1)S(1)}, bf16[512,128]{1,0:T(8,128)(2,1)S(1)}, u32[]{:S(2)}, u32[]{:S(2)}) collective-permute-start(bf16[512,128]{1,0:T(8,128)(2,1)S(1)} %shard_map.110), channel_id=1, source_target_pairs={{0,2},{4,0},{8,4},{12,8},{14,12},{10,14},{6,10},{2,6},{1,3},{5,1},... | collective-permute-start | bytes 393224 | tf_op jit(solution)/shard_map/ppermute | solution.py:48
  (17 other events, 94.9 us)

commit v4 on v3

--- a/solution.py
+++ b/solution.py
@@ -61,6 +61,10 @@
     return [order[a:b] for a, b in zip(cuts, cuts[1:])]
 
 
+def reorder_parts(groups):
+    return [[g] for g in groups[:-2]] + [groups[-2:]]
+
+
 def ring_gather(pieces, order):
     count = len(order)
     got = [{0: p} for p in pieces]
@@ -79,15 +83,29 @@
         kernel,
         out_shape=out_shape,
         in_specs=[pl.BlockSpec(memory_space=pltpu.SMEM if x.dtype == jnp.int32 else pltpu.VMEM) for x in operands],
-        out_specs=jax.tree.map(lambda _: pl.BlockSpec(memory_space=pltpu.VMEM), out_shape),
+        out_specs=jax.tree.map(lambda x: pl.BlockSpec(memory_space=pltpu.VMEM if x.ndim > 1 else pltpu.SMEM), out_shape),
         compiler_params=pltpu.CompilerParams(vmem_limit_bytes=16 << 20),
         cost_estimate=pl.CostEstimate(flops=0, transcendentals=0, bytes_accessed=touched),
     )(*operands)
 
 
-def sum_kernel(low, spread_ref, arrived_ref, out_ref):
-    mine = spread_ref[pl.ds(low, out_ref.shape[0]), :]
-    out_ref[...] = (mine + arrived_ref[...].astype(jnp.float32)).astype(out_ref.dtype)
+def first_kernel(low, height, spread_ref, *refs):
+    out_ref = refs[-1]
+    out_ref[pl.ds(0, height), :] = spread_ref[pl.ds(low, height), :].astype(out_ref.dtype)
+    if len(refs) > 1:
+        out_ref[pl.ds(height, refs[0].shape[0]), :] = refs[0][...]
+
+
+def add_kernel(left_ref, right_ref, out_ref):
+    out_ref[...] = left_ref[...] + right_ref[...]
+
+
+def sum_kernel(low, height, spread_ref, arrived_ref, out_ref):
+    mine = spread_ref[pl.ds(low, height), :]
+    top, rest = pl.ds(0, height), out_ref.shape[0] - height
+    out_ref[top, :] = (mine + arrived_ref[top, :].astype(jnp.float32)).astype(out_ref.dtype)
+    if rest:
+        out_ref[pl.ds(height, rest), :] = arrived_ref[pl.ds(height, rest), :]
 
 
 def update_kernel(lows, spread_ref, *refs):
@@ -102,20 +120,24 @@
         slim[c][...] = inject.astype(slim[c].dtype)
 
 
-def ring_scatter(part, order, height):
+def ring_scatter(part, order, height, extra=None):
     count = len(order)
-    held = {}
+    held, tiles = {}, []
     for send in scatter_sends(count):
         chunk, way, hop = send
         spread, low = part(chunk, (way * hop) % count)
+        more = extra is not None and chunk == 0
+        rows = height + (extra.shape[0] if more else 0)
+        shape = jax.ShapeDtypeStruct((rows, spread.shape[1]), jnp.bfloat16)
         if (chunk, way) in held:
-            arrived = held[chunk, way]
-            shape = jax.ShapeDtypeStruct(arrived.shape, arrived.dtype)
-            mine = small_call(functools.partial(sum_kernel, low), shape, spread, arrived)
+            kernel, tail = sum_kernel, [held[chunk, way]]
         else:
-            mine = spread[low : low + height].astype(jnp.bfloat16)
+            kernel, tail = first_kernel, [extra] if more else []
+        mine = small_call(functools.partial(kernel, low, height), shape, spread, *tail)
         held[chunk, way] = hop_to(mine, send, order)
-    return held
+        if more:
+            tiles.append(held[chunk, way])
+    return held, tiles
 
 
 def place_of(position, count):
@@ -167,39 +189,99 @@
 def last_update_kernel(lows, here_ref, *refs):
     spread_ref, ahead, behind = refs[0], refs[1 : chunks + 1], refs[chunks + 1 : 2 * chunks + 1]
     inject_ref, out_ref, edge_ref = refs[2 * chunks + 1 :]
-    height = ahead[0].shape[0]
+    height, top = inject_ref.shape[0] // chunks, pl.ds(0, inject_ref.shape[0] // chunks)
     first = here_ref[1] == 0
     for c, low in enumerate(lows):
         rows = pl.ds(c * height, height)
         total = spread_ref[pl.ds(low, height), :]
-        total = total + ahead[c][...].astype(jnp.float32) + behind[c][...].astype(jnp.float32)
+        total = total + ahead[c][top, :].astype(jnp.float32) + behind[c][top, :].astype(jnp.float32)
         inject = inject_ref[rows, :] - relax_step * total
         out_ref[rows, :] = inject
         edge_ref[rows, :] = jnp.where(first, inject[:, -1:], inject[:, :1])
 
 
-def ramp_kernel(here_ref, inject_ref, edge_ref, bound_ref, out_ref):
-    first = here_ref[1] == 0
-    inject, edge, bound = inject_ref[...], edge_ref[...], bound_ref[...]
+def excess_of(step, bound):
+    return step - jnp.clip(step, -bound, bound)
+
+
+def inner_ramp_kernel(inject_ref, bound_ref, out_ref):
+    inject, bound = inject_ref[...], bound_ref[...]
     periods = inject.shape[1]
     lane = lax.broadcasted_iota(jnp.int32, inject.shape, 1)
-
-    def excess(step):
-        return step - jnp.clip(step, -bound, bound)
-
-    before = jnp.where(lane == 0, edge, pltpu.roll(inject, 1, 1))
-    after = jnp.where(lane == periods - 1, edge, pltpu.roll(inject, periods - 1, 1))
-    low = jnp.where((lane == 0) & first, 0.0, excess(inject - before))
-    high = jnp.where((lane == periods - 1) & jnp.logical_not(first), 0.0, excess(after - inject))
+    low = jnp.where(lane == 0, 0.0, excess_of(inject - pltpu.roll(inject, 1, 1), bound))
+    high = jnp.where(lane == periods - 1, 0.0, pltpu.roll(low, periods - 1, 1))
     out_ref[...] = inject - 0.5 * low + 0.5 * high
 
 
-def norms_kernel(entries, sums_ref, out_ref):
-    lane = lax.broadcasted_iota(jnp.int32, out_ref.shape, 1)
+def edge_ramp_kernel(here_ref, inner_ref, mine_ref, other_ref, bound_ref, out_ref, whole, sems):
+    first = here_ref[1] == 0
+    parts = sems.shape[0]
+    rows, periods = whole.shape[0] // parts, whole.shape[1]
+    edge = jnp.where(first, periods - 1, 0)
+    copies = []
+    for p in range(parts):
+        at = pl.ds(p * rows, rows)
+        mine, other, inner = mine_ref[at, :], other_ref[at, :], inner_ref[at, :]
+        excess = excess_of(jnp.where(first, other - mine, mine - other), bound_ref[at, :1])
+        share = jnp.where(first, 0.5 * excess, -0.5 * excess)
+        lane = lax.broadcasted_iota(jnp.int32, inner.shape, 1)
+        whole[at, :] = jnp.where(lane == edge, inner + share, inner)
+        copy = pltpu.make_async_copy(whole.at[at, :], out_ref.at[at, :], sems.at[p])
+        copy.start()
+        copies.append(copy)
+    for copy in copies:
+        copy.wait()
+
+
+def edge_ramp(here, inner, mine, other, bound):
+    parts = 4
+    return pl.pallas_call(
+        edge_ramp_kernel,
+        out_shape=jax.ShapeDtypeStruct(inner.shape, inner.dtype),
+        in_specs=[pl.BlockSpec(memory_space=pltpu.SMEM)] + [pl.BlockSpec(memory_space=pltpu.VMEM)] * 4,
+        out_specs=pl.BlockSpec(memory_space=pltpu.HBM),
+        scratch_shapes=[pltpu.VMEM(inner.shape, inner.dtype), pltpu.SemaphoreType.DMA((parts,))],
+        compiler_params=pltpu.CompilerParams(vmem_limit_bytes=16 << 20),
+        cost_estimate=pl.CostEstimate(flops=0, transcendentals=0, bytes_accessed=2 * inner.size * inner.dtype.itemsize),
+    )(here, inner, mine, other, bound)
+
+
+def squares_kernel(misfit_ref, out_ref):
+    misfit = misfit_ref[...]
+    out_ref[...] = jnp.sum((misfit * misfit).reshape(-1, 8, misfit.shape[1]), axis=0)
+
+
+def pack_kernel(*refs):
+    *earlier, misfit_ref, out_ref = refs
+    misfit = misfit_ref[...]
+    sums = [ref[...] for ref in earlier] + [(misfit * misfit).reshape(-1, 8, misfit.shape[1])]
+    row = lax.broadcasted_iota(jnp.int32, out_ref.shape, 0)
     out = jnp.zeros(out_ref.shape, jnp.float32)
+    for k, value in enumerate(sums):
+        left = jnp.sum(value.reshape(-1, misfit.shape[1]), axis=0, keepdims=True)
+        for j in range(3):
+            piece = left.astype(jnp.bfloat16).astype(jnp.float32)
+            out = jnp.where(row == 3 * k + j, piece, out)
+            left = left - piece
+    out_ref[...] = out.astype(out_ref.dtype)
+
+
+def unpack_kernel(own_ref, *refs):
+    *tiles, out_ref = refs
+    tall = own_ref.shape[0]
+    total = own_ref[...].astype(jnp.float32)
+    for ref in tiles:
+        total = total + ref[pl.ds(ref.shape[0] - tall, tall), :].astype(jnp.float32)
+    out_ref[...] = total
+
+
+def norms_kernel(entries, left_ref, right_ref, out_ref):
+    total = left_ref[...] + right_ref[...]
+    row = lax.broadcasted_iota(jnp.int32, total.shape, 0)
     for k in range(passes):
-        out = jnp.where(lane == k, jnp.sum(sums_ref[pl.ds(8 * k, 8), :]), out)
-    out_ref[...] = jnp.sqrt(out / entries)
+        square = jnp.sum(jnp.where((row >= 3 * k) & (row < 3 * k + 3), total, 0.0), axis=0, keepdims=True)
+        norm = jnp.sqrt(jnp.sum(square, axis=1, keepdims=True) / entries)
+        out_ref[k] = jnp.sum(norm)
 
 
 def limits_of(outage_line, ratings):
@@ -258,8 +340,12 @@
         order = ring_order(count)
         groups = ring_groups(count)
         factors = []
-        for group in groups:
-            factors.append(reorder(here, shift_factors, group, count))
+        for part in reorder_parts(groups):
+            side = reorder(here, shift_factors, [d for g in part for d in g], count)
+            low = 0
+            for g in part:
+                factors.append(side[:, low : low + len(g) * owned])
+                low += len(g) * owned
 
     def forward(pieces):
         if not ring:
@@ -273,16 +359,17 @@
             flows = share if flows is None else flows + share
         return flows
 
-    def backward(misfit):
+    def backward(misfit, extra):
         narrow = misfit.astype(jnp.bfloat16)
         shares = {}
-        for group, cols in reversed(list(zip(groups, factors))):
+        for g in reversed(range(len(groups))):
+            group, cols = groups[g], factors[g]
             spread = lax.dot_general(cols, narrow, (((0,), (0,)), ((), ())), preferred_element_type=jnp.float32)
             for j, d in enumerate(group):
                 for c in range(chunks):
                     shares[c, d] = (spread, j * owned + c * height)
-        held = ring_scatter(lambda c, d: shares[c, d], order, height)
-        return [shares[c, 0] for c in range(chunks)], held
+        held, tiles = ring_scatter(lambda c, d: shares[c, d], order, height, extra)
+        return [shares[c, 0] for c in range(chunks)], held, tiles
 
     dual = flow_dual
     sums = []
@@ -308,9 +395,16 @@
     bound = jnp.broadcast_to(ramp_limit[:, None], (owned, periods))
     inject = proposal
     for stage in range(passes):
-        misfit, dual = project(forward(slim), dual, limits)
-        sums.append(jnp.sum((misfit * misfit).reshape(-1, 8, periods), axis=0))
-        own, held = backward(misfit)
+        misfit, _ = project(forward(slim), dual, limits)
+        dual = small_call(add_kernel, jax.ShapeDtypeStruct(dual.shape, dual.dtype), dual, misfit)
+        if stage + 1 < passes:
+            tile = jax.ShapeDtypeStruct((8, periods), jnp.float32)
+            sums.append(small_call(squares_kernel, tile, misfit))
+            extra = None
+        else:
+            tile = jax.ShapeDtypeStruct((16, periods), jnp.bfloat16)
+            extra = small_call(pack_kernel, tile, *sums, misfit)
+        own, held, tiles = backward(misfit, extra)
         lows = tuple(low for _, low in own)
         arrived = [held[c, way] for way in (1, -1) for c in range(chunks)]
         if stage + 1 < passes:
@@ -330,11 +424,15 @@
                 *arrived,
                 inject,
             )
-    sums = total_over(jnp.concatenate(sums, axis=0), ("tm", "net"))
-    tile = jax.ShapeDtypeStruct((8, periods), jnp.float32)
-    norms = small_call(functools.partial(norms_kernel, entries), tile, sums)[0, :passes]
-    edge = lax.ppermute(edge, "tm", [(0, 1), (1, 0)])
-    dispatch = small_call(ramp_kernel, whole_shape, here, inject, edge, bound)
+    other = lax.ppermute(edge, "tm", [(0, 1), (1, 0)])
+    inner = small_call(inner_ramp_kernel, whole_shape, inject, bound)
+    wide = jax.ShapeDtypeStruct(extra.shape, jnp.float32)
+    sums = small_call(unpack_kernel, wide, extra, *tiles)
+    others = lax.ppermute(sums, "tm", [(0, 1), (1, 0)])
+    norms = small_call(
+        functools.partial(norms_kernel, entries), jax.ShapeDtypeStruct((passes,), jnp.float32), sums, others
+    )
+    dispatch = edge_ramp(here, inner, edge, other, bound)
     return (dispatch, dual, norms)
 
 

time: 139 us -> 120 us (0.86)
  waiting for transfers between devices: 44.2 us -> 32.5 us
  starting transfers between devices: 65.1 us -> 59.5 us
    ppermute x5 -> x2, waiting for transfers between devices: 7.82 us -> 0.57 us  [the longest x1 0.57 us: body(): other = lax.ppermute(edge, 'tm', [(0, 1), (1, 0)])]
    ppermute x5 -> x2, starting transfers between devices: 5.55 us -> 0.14 us  [the longest x1 0.07 us: body(): others = lax.ppermute(sums, 'tm', [(0, 1), (1, 0)])]
    ppermute x56, waiting for transfers between devices: 36.4 us -> 32 us  [hop_to(): return lax.ppermute(block, 'net', pairs)]
    pallas_call x0 -> x1, Pallas kernels: none -> 1.5 us  [edge_ramp(): pl.pallas_call(edge_ramp_kernel, out_shape=jax.ShapeDtypeStruct(inner.sha...]
    pallas_call x4 -> x3, Pallas kernels: 8.49 us -> 7.03 us  [reorder(): pl.pallas_call(functools.partial(reorder_kernel, tuple(distances), count)...]
    pallas_call x25 -> x38, Pallas kernels: 3.75 us -> 3.7 us  [small_call(): pl.pallas_call(kernel, out_shape=out_shape, in_specs=[pl.BlockSpec(memory...]
  transfers between devices with their start and end apart: 61 -> 58, of which waited for: 25 -> 31; matrix products, arithmetic and copies ran while one was open for 7% -> 9% of each run, Pallas kernels for 7% -> 9%
where the time goes in v4:
time: 120 us
  starting transfers between devices  59.5 us (50%)
  waiting for transfers between devices  32.5 us (27%)
  Pallas kernels  12.2 us (10%)
  matrix products  11.8 us (10%)
  local copies, waits for them, and re-layouts  1.45 us (1%)
  between operations  1.25 us (1%)
    ppermute x56, starting transfers between devices, hop_to(): return lax.ppermute(block, 'net', pairs)  59.4 us
    ppermute x56, waiting for transfers between devices, hop_to(): return lax.ppermute(block, 'net', pairs)  32 us
    pallas_call x3, Pallas kernels, reorder(): pl.pallas_call(functools.partial(reorder_kernel, tuple(distances), count)...  7.03 us
    dot_general x8, matrix products, backward(): lax.dot_general(cols, narrow, (((0,), (0,)), ((), ())), preferred_element...  5.93 us
    dot_general x8, matrix products, forward(): share = jnp.dot(cols, blocks, preferred_element_type=jnp.float32)  5.83 us
    pallas_call x38, Pallas kernels, small_call(): pl.pallas_call(kernel, out_shape=out_shape, in_specs=[pl.BlockSpec(memory...  3.7 us
  transfers between devices with their start and end apart: 58, of which 31 were waited for; matrix products, arithmetic and copies ran while one was open for 9% of the time, Pallas kernels for 9%

profile of v4, /device:TPU:0, one launch (start us, length us, event | category | flops | bytes accessed | tf_op | source)
XLA Modules:
  0.0 119.8 jit_solution(10618586369001392984)
XLA Ops:
  0.6 1.0 copy-done
  1.7 3.0 %collective-permute-start.2 = (bf16[512,128]{1,0:T(8,128)(2,1)S(1)}, bf16[512,128]{1,0:T(8,128)(2,1)S(1)}, u32[]{:S(2)}, u32[]{:S(2)}) collective-permute-start(bf16[512,128]{1,0:T(8,128)(2,1)S(1)} %get-tuple-element.10), channel_id=1, source_target_pairs={{0,2},{4,0},{8,4},{12,8},{14,12},{10,14},{6,10},{2,6},{1,3},{5,1},... | collective-permute-start | bytes 393224 | tf_op jit(solution)/shard_map/ppermute | solution.py:48
  4.9 1.9 %collective-permute-start.3 = (bf16[512,128]{1,0:T(8,128)(2,1)S(1)}, bf16[512,128]{1,0:T(8,128)(2,1)S(1)}, u32[]{:S(2)}, u32[]{:S(2)}) collective-permute-start(bf16[512,128]{1,0:T(8,128)(2,1)S(1)} %get-tuple-element.11), channel_id=1, source_target_pairs={{0,2},{4,0},{8,4},{12,8},{14,12},{10,14},{6,10},{2,6},{1,3},{5,1},... | collective-permute-start | bytes 393224 | tf_op jit(solution)/shard_map/ppermute | solution.py:48
  7.9 2.1 %shard_map.87 = bf16[512,2048]{1,0:T(8,128)(2,1)S(1)} custom-call(s32[2]{0:T(128)S(1)} %pad_add_fusion.here_ref, bf16[512,8192]{1,0:T(8,128)(2,1)} %factors_ref.5), custom_call_target="tpu_custom_call" | custom-call | bytes 2097152 | tf_op jit(solution)/shard_map/pallas_call | solution.py:172
  10.1 2.5 %shard_map.88 = bf16[512,3072]{1,0:T(8,128)(2,1)S(1)} custom-call(s32[2]{0:T(128)S(1)} %pad_add_fusion.here_ref, bf16[512,8192]{1,0:T(8,128)(2,1)} %factors_ref.5), custom_call_target="tpu_custom_call" | custom-call | bytes 3145728 | tf_op jit(solution)/shard_map/pallas_call | solution.py:172
  12.5 2.5 %shard_map.85 = bf16[512,3072]{1,0:T(8,128)(2,1)S(1)} custom-call(s32[2]{0:T(128)S(1)} %pad_add_fusion.here_ref, bf16[512,8192]{1,0:T(8,128)(2,1)} %factors_ref.5), custom_call_target="tpu_custom_call" | custom-call | bytes 3145728 | tf_op jit(solution)/shard_map/pallas_call | solution.py:172
  15.0 2.0 %collective-permute-start.6 = (bf16[512,128]{1,0:T(8,128)(2,1)S(1)}, bf16[512,128]{1,0:T(8,128)(2,1)S(1)}, u32[]{:S(2)}, u32[]{:S(2)}) collective-permute-start(bf16[512,128]{1,0:T(8,128)(2,1)S(1)} %collective-permute-done.2), channel_id=1, source_target_pairs={{0,2},{4,0},{8,4},{12,8},{14,12},{10,14},{6,10},{2,6},{1,3},{5,1},... | collective-permute-start | bytes 393224 | tf_op jit(solution)/shard_map/ppermute | solution.py:48
  17.1 1.9 %collective-permute-start.7 = (bf16[512,128]{1,0:T(8,128)(2,1)S(1)}, bf16[512,128]{1,0:T(8,128)(2,1)S(1)}, u32[]{:S(2)}, u32[]{:S(2)}) collective-permute-start(bf16[512,128]{1,0:T(8,128)(2,1)S(1)} %collective-permute-done.3), channel_id=1, source_target_pairs={{0,2},{4,0},{8,4},{12,8},{14,12},{10,14},{6,10},{2,6},{1,3},{5,1},... | collective-permute-start | bytes 393224 | tf_op jit(solution)/shard_map/ppermute | solution.py:48
  21.1 1.6 %collective-permute-start.10 = (bf16[512,128]{1,0:T(8,128)(2,1)S(1)}, bf16[512,128]{1,0:T(8,128)(2,1)S(1)}, u32[]{:S(2)}, u32[]{:S(2)}) collective-permute-start(bf16[512,128]{1,0:T(8,128)(2,1)S(1)} %collective-permute-done.6), channel_id=1, source_target_pairs={{0,2},{4,0},{8,4},{12,8},{14,12},{10,14},{6,10},{2,6},{1,3},{5,1},... | collective-permute-start | bytes 393224 | tf_op jit(solution)/shard_map/ppermute | solution.py:48
  23.9 1.6 %collective-permute-start.11 = (bf16[512,128]{1,0:T(8,128)(2,1)S(1)}, bf16[512,128]{1,0:T(8,128)(2,1)S(1)}, u32[]{:S(2)}, u32[]{:S(2)}) collective-permute-start(bf16[512,128]{1,0:T(8,128)(2,1)S(1)} %collective-permute-done.7), channel_id=1, source_target_pairs={{0,2},{4,0},{8,4},{12,8},{14,12},{10,14},{6,10},{2,6},{1,3},{5,1},... | collective-permute-start | bytes 393224 | tf_op jit(solution)/shard_map/ppermute | solution.py:48
  26.7 1.6 %collective-permute-done.8 = bf16[512,128]{1,0:T(8,128)(2,1)S(1)} collective-permute-done((bf16[512,128]{1,0:T(8,128)(2,1)S(1)}, bf16[512,128]{1,0:T(8,128)(2,1)S(1)}, u32[]{:S(2)}, u32[]{:S(2)}) %collective-permute-start.8) | collective-permute-done | bytes 131104 | tf_op jit(solution)/shard_map/ppermute | solution.py:48
  29.5 1.6 %collective-permute-start.13 = (bf16[512,128]{1,0:T(8,128)(2,1)S(1)}, bf16[512,128]{1,0:T(8,128)(2,1)S(1)}, u32[]{:S(2)}, u32[]{:S(2)}) collective-permute-start(bf16[512,128]{1,0:T(8,128)(2,1)S(1)} %collective-permute-done.11), channel_id=1, source_target_pairs={{0,2},{4,0},{8,4},{12,8},{14,12},{10,14},{6,10},{2,6},{1,3},{5,1},... | collective-permute-start | bytes 393224 | tf_op jit(solution)/shard_map/ppermute | solution.py:48
  31.8 1.4 %collective-permute-done.12 = bf16[512,128]{1,0:T(8,128)(2,1)S(1)} collective-permute-done((bf16[512,128]{1,0:T(8,128)(2,1)S(1)}, bf16[512,128]{1,0:T(8,128)(2,1)S(1)}, u32[]{:S(2)}, u32[]{:S(2)}) %collective-permute-start.12) | collective-permute-done | bytes 131104 | tf_op jit(solution)/shard_map/ppermute | solution.py:48
  33.3 1.1 collective-permute-done.13
  35.4 1.7 %collective-permute-start.14 = (bf16[512,128]{1,0:T(8,128)(2,1)S(1)}, bf16[512,128]{1,0:T(8,128)(2,1)S(1)}, u32[]{:S(2)}, u32[]{:S(2)}) collective-permute-start(bf16[512,128]{1,0:T(8,128)(2,1)S(1)} %shard_map.89), channel_id=1, source_target_pairs={{0,4},{4,8},{8,12},{12,14},{14,10},{10,6},{6,2},{2,0},{1,5},{5,9},... | collective-permute-start | bytes 393224 | tf_op jit(solution)/shard_map/ppermute | solution.py:48
  38.3 1.7 %collective-permute-start.18 = (bf16[512,128]{1,0:T(8,128)(2,1)S(1)}, bf16[512,128]{1,0:T(8,128)(2,1)S(1)}, u32[]{:S(2)}, u32[]{:S(2)}) collective-permute-start(bf16[512,128]{1,0:T(8,128)(2,1)S(1)} %shard_map.93), channel_id=1, source_target_pairs={{0,4},{4,8},{8,12},{12,14},{14,10},{10,6},{6,2},{2,0},{1,5},{5,9},... | collective-permute-start | bytes 393224 | tf_op jit(solution)/shard_map/ppermute | solution.py:48
  41.1 1.6 %collective-permute-start.15 = (bf16[512,128]{1,0:T(8,128)(2,1)S(1)}, bf16[512,128]{1,0:T(8,128)(2,1)S(1)}, u32[]{:S(2)}, u32[]{:S(2)}) collective-permute-start(bf16[512,128]{1,0:T(8,128)(2,1)S(1)} %shard_map.90), channel_id=1, source_target_pairs={{0,4},{4,8},{8,12},{12,14},{14,10},{10,6},{6,2},{2,0},{1,5},{5,9},... | collective-permute-start | bytes 393224 | tf_op jit(solution)/shard_map/ppermute | solution.py:48
  44.7 1.8 %collective-permute-start.19 = (bf16[512,128]{1,0:T(8,128)(2,1)S(1)}, bf16[512,128]{1,0:T(8,128)(2,1)S(1)}, u32[]{:S(2)}, u32[]{:S(2)}) collective-permute-start(bf16[512,128]{1,0:T(8,128)(2,1)S(1)} %shard_map.94), channel_id=1, source_target_pairs={{0,4},{4,8},{8,12},{12,14},{14,10},{10,6},{6,2},{2,0},{1,5},{5,9},... | collective-permute-start | bytes 393224 | tf_op jit(solution)/shard_map/ppermute | solution.py:48
  47.5 1.8 %collective-permute-start.16 = (bf16[512,128]{1,0:T(8,128)(2,1)S(1)}, bf16[512,128]{1,0:T(8,128)(2,1)S(1)}, u32[]{:S(2)}, u32[]{:S(2)}) collective-permute-start(bf16[512,128]{1,0:T(8,128)(2,1)S(1)} %shard_map.91), channel_id=1, source_target_pairs={{0,4},{4,8},{8,12},{12,14},{14,10},{10,6},{6,2},{2,0},{1,5},{5,9},... | collective-permute-start | bytes 393224 | tf_op jit(solution)/shard_map/ppermute | solution.py:48
  50.9 1.6 %collective-permute-start.20 = (bf16[512,128]{1,0:T(8,128)(2,1)S(1)}, bf16[512,128]{1,0:T(8,128)(2,1)S(1)}, u32[]{:S(2)}, u32[]{:S(2)}) collective-permute-start(bf16[512,128]{1,0:T(8,128)(2,1)S(1)} %shard_map.95), channel_id=1, source_target_pairs={{0,4},{4,8},{8,12},{12,14},{14,10},{10,6},{6,2},{2,0},{1,5},{5,9},... | collective-permute-start | bytes 393224 | tf_op jit(solution)/shard_map/ppermute | solution.py:48
  53.1 1.6 %collective-permute-start.17 = (bf16[512,128]{1,0:T(8,128)(2,1)S(1)}, bf16[512,128]{1,0:T(8,128)(2,1)S(1)}, u32[]{:S(2)}, u32[]{:S(2)}) collective-permute-start(bf16[512,128]{1,0:T(8,128)(2,1)S(1)} %shard_map.92), channel_id=1, source_target_pairs={{0,4},{4,8},{8,12},{12,14},{14,10},{10,6},{6,2},{2,0},{1,5},{5,9},... | collective-permute-start | bytes 393224 | tf_op jit(solution)/shard_map/ppermute | solution.py:48
  55.4 1.7 %collective-permute-done.20.refs_1_ = bf16[512,128]{1,0:T(8,128)(2,1)S(1)} collective-permute-done((bf16[512,128]{1,0:T(8,128)(2,1)S(1)}, bf16[512,128]{1,0:T(8,128)(2,1)S(1)}, u32[]{:S(2)}, u32[]{:S(2)}) %collective-permute-start.20) | collective-permute-done | bytes 131104 | tf_op jit(solution)/shard_map/ppermute | solution.py:48
  57.1 1.6 %collective-permute-done.23.refs_2_ = bf16[512,128]{1,0:T(8,128)(2,1)S(1)} collective-permute-done((bf16[512,128]{1,0:T(8,128)(2,1)S(1)}, bf16[512,128]{1,0:T(8,128)(2,1)S(1)}, u32[]{:S(2)}, u32[]{:S(2)}) %collective-permute-start.23) | collective-permute-done | bytes 131104 | tf_op jit(solution)/shard_map/ppermute | solution.py:48
  58.7 1.2 %collective-permute-done.17.refs_0_ = bf16[512,128]{1,0:T(8,128)(2,1)S(1)} collective-permute-done((bf16[512,128]{1,0:T(8,128)(2,1)S(1)}, bf16[512,128]{1,0:T(8,128)(2,1)S(1)}, u32[]{:S(2)}, u32[]{:S(2)}) %collective-permute-start.17) | collective-permute-done | bytes 131104 | tf_op jit(solution)/shard_map/ppermute | solution.py:48
  59.9 1.6 %collective-permute-done.27.refs_3_ = bf16[512,128]{1,0:T(8,128)(2,1)S(1)} collective-permute-done((bf16[512,128]{1,0:T(8,128)(2,1)S(1)}, bf16[512,128]{1,0:T(8,128)(2,1)S(1)}, u32[]{:S(2)}, u32[]{:S(2)}) %collective-permute-start.27) | collective-permute-done | bytes 131104 | tf_op jit(solution)/shard_map/ppermute | solution.py:48
  62.5 1.2 %collective-permute-start.28 = (bf16[512,128]{1,0:T(8,128)(2,1)S(1)}, bf16[512,128]{1,0:T(8,128)(2,1)S(1)}, u32[]{:S(2)}, u32[]{:S(2)}) collective-permute-start(bf16[512,128]{1,0:T(8,128)(2,1)S(1)} %get-tuple-element.12), channel_id=1, source_target_pairs={{0,4},{4,8},{8,12},{12,14},{14,10},{10,6},{6,2},{2,0},{1,5},{5,9},... | collective-permute-start | bytes 393224 | tf_op jit(solution)/shard_map/ppermute | solution.py:48
  64.5 1.2 %collective-permute-start.29 = (bf16[512,128]{1,0:T(8,128)(2,1)S(1)}, bf16[512,128]{1,0:T(8,128)(2,1)S(1)}, u32[]{:S(2)}, u32[]{:S(2)}) collective-permute-start(bf16[512,128]{1,0:T(8,128)(2,1)S(1)} %get-tuple-element.13), channel_id=1, source_target_pairs={{0,4},{4,8},{8,12},{12,14},{14,10},{10,6},{6,2},{2,0},{1,5},{5,9},... | collective-permute-start | bytes 393224 | tf_op jit(solution)/shard_map/ppermute | solution.py:48
  65.8 2.3 %collective-permute-done.30 = bf16[512,128]{1,0:T(8,128)(2,1)S(1)} collective-permute-done((bf16[512,128]{1,0:T(8,128)(2,1)S(1)}, bf16[512,128]{1,0:T(8,128)(2,1)S(1)}, u32[]{:S(2)}, u32[]{:S(2)}) %collective-permute-start.30) | collective-permute-done | bytes 131104 | tf_op jit(solution)/shard_map/ppermute | solution.py:48
  68.9 1.2 %collective-permute-start.32 = (bf16[512,128]{1,0:T(8,128)(2,1)S(1)}, bf16[512,128]{1,0:T(8,128)(2,1)S(1)}, u32[]{:S(2)}, u32[]{:S(2)}) collective-permute-start(bf16[512,128]{1,0:T(8,128)(2,1)S(1)} %collective-permute-done.28), channel_id=1, source_target_pairs={{0,4},{4,8},{8,12},{12,14},{14,10},{10,6},{6,2},{2,0},{1,5},{5,9},... | collective-permute-start | bytes 393224 | tf_op jit(solution)/shard_map/ppermute | solution.py:48
  70.1 1.3 %collective-permute-start.35 = (bf16[512,128]{1,0:T(8,128)(2,1)S(1)}, bf16[512,128]{1,0:T(8,128)(2,1)S(1)}, u32[]{:S(2)}, u32[]{:S(2)}) collective-permute-start(bf16[512,128]{1,0:T(8,128)(2,1)S(1)} %collective-permute-done.31), channel_id=1, source_target_pairs={{0,2},{4,0},{8,4},{12,8},{14,12},{10,14},{6,10},{2,6},{1,3},{5,1},... | collective-permute-start | bytes 393224 | tf_op jit(solution)/shard_map/ppermute | solution.py:48
  74.8 1.4 %collective-permute-start.36 = (bf16[512,128]{1,0:T(8,128)(2,1)S(1)}, bf16[512,128]{1,0:T(8,128)(2,1)S(1)}, u32[]{:S(2)}, u32[]{:S(2)}) collective-permute-start(bf16[512,128]{1,0:T(8,128)(2,1)S(1)} %collective-permute-done.32), channel_id=1, source_target_pairs={{0,4},{4,8},{8,12},{12,14},{14,10},{10,6},{6,2},{2,0},{1,5},{5,9},... | collective-permute-start | bytes 393224 | tf_op jit(solution)/shard_map/ppermute | solution.py:48
  76.9 1.4 %collective-permute-start.37 = (bf16[512,128]{1,0:T(8,128)(2,1)S(1)}, bf16[512,128]{1,0:T(8,128)(2,1)S(1)}, u32[]{:S(2)}, u32[]{:S(2)}) collective-permute-start(bf16[512,128]{1,0:T(8,128)(2,1)S(1)} %collective-permute-done.33), channel_id=1, source_target_pairs={{0,4},{4,8},{8,12},{12,14},{14,10},{10,6},{6,2},{2,0},{1,5},{5,9},... | collective-permute-start | bytes 393224 | tf_op jit(solution)/shard_map/ppermute | solution.py:48
  79.0 1.6 %collective-permute-done.36 = bf16[512,128]{1,0:T(8,128)(2,1)S(1)} collective-permute-done((bf16[512,128]{1,0:T(8,128)(2,1)S(1)}, bf16[512,128]{1,0:T(8,128)(2,1)S(1)}, u32[]{:S(2)}, u32[]{:S(2)}) %collective-permute-start.36) | collective-permute-done | bytes 131104 | tf_op jit(solution)/shard_map/ppermute | solution.py:48
  80.5 1.6 %collective-permute-start.40 = (bf16[512,128]{1,0:T(8,128)(2,1)S(1)}, bf16[512,128]{1,0:T(8,128)(2,1)S(1)}, u32[]{:S(2)}, u32[]{:S(2)}) collective-permute-start(bf16[512,128]{1,0:T(8,128)(2,1)S(1)} %collective-permute-done.36), channel_id=1, source_target_pairs={{0,4},{4,8},{8,12},{12,14},{14,10},{10,6},{6,2},{2,0},{1,5},{5,9},... | collective-permute-start | bytes 393224 | tf_op jit(solution)/shard_map/ppermute | solution.py:48
  84.1 2.1 %collective-permute-done.40 = bf16[512,128]{1,0:T(8,128)(2,1)S(1)} collective-permute-done((bf16[512,128]{1,0:T(8,128)(2,1)S(1)}, bf16[512,128]{1,0:T(8,128)(2,1)S(1)}, u32[]{:S(2)}, u32[]{:S(2)}) %collective-permute-start.40) | collective-permute-done | bytes 131104 | tf_op jit(solution)/shard_map/ppermute | solution.py:48
  88.8 1.4 %collective-permute-start.42 = (bf16[528,128]{1,0:T(8,128)(2,1)S(1)}, bf16[528,128]{1,0:T(8,128)(2,1)S(1)}, u32[]{:S(2)}, u32[]{:S(2)}) collective-permute-start(bf16[528,128]{1,0:T(8,128)(2,1)S(1)} %shard_map.107), channel_id=1, source_target_pairs={{0,4},{4,8},{8,12},{12,14},{14,10},{10,6},{6,2},{2,0},{1,5},{5,9},... | collective-permute-start | bytes 405512 | tf_op jit(solution)/shard_map/ppermute | solution.py:48
  91.0 1.6 %collective-permute-start.46 = (bf16[512,128]{1,0:T(8,128)(2,1)S(1)}, bf16[512,128]{1,0:T(8,128)(2,1)S(1)}, u32[]{:S(2)}, u32[]{:S(2)}) collective-permute-start(bf16[512,128]{1,0:T(8,128)(2,1)S(1)} %shard_map.111), channel_id=1, source_target_pairs={{0,4},{4,8},{8,12},{12,14},{14,10},{10,6},{6,2},{2,0},{1,5},{5,9},... | collective-permute-start | bytes 393224 | tf_op jit(solution)/shard_map/ppermute | solution.py:48
  93.1 1.1 collective-permute-done.52.arrived_ref
  94.9 1.5 %collective-permute-start.43 = (bf16[528,128]{1,0:T(8,128)(2,1)S(1)}, bf16[528,128]{1,0:T(8,128)(2,1)S(1)}, u32[]{:S(2)}, u32[]{:S(2)}) collective-permute-start(bf16[528,128]{1,0:T(8,128)(2,1)S(1)} %shard_map.108), channel_id=1, source_target_pairs={{0,4},{4,8},{8,12},{12,14},{14,10},{10,6},{6,2},{2,0},{1,5},{5,9},... | collective-permute-start | bytes 405512 | tf_op jit(solution)/shard_map/ppermute | solution.py:48
  97.5 1.6 %collective-permute-start.47 = (bf16[512,128]{1,0:T(8,128)(2,1)S(1)}, bf16[512,128]{1,0:T(8,128)(2,1)S(1)}, u32[]{:S(2)}, u32[]{:S(2)}) collective-permute-start(bf16[512,128]{1,0:T(8,128)(2,1)S(1)} %shard_map.112), channel_id=1, source_target_pairs={{0,4},{4,8},{8,12},{12,14},{14,10},{10,6},{6,2},{2,0},{1,5},{5,9},... | collective-permute-start | bytes 393224 | tf_op jit(solution)/shard_map/ppermute | solution.py:48
  101.1 1.6 %collective-permute-start.44 = (bf16[528,128]{1,0:T(8,128)(2,1)S(1)}, bf16[528,128]{1,0:T(8,128)(2,1)S(1)}, u32[]{:S(2)}, u32[]{:S(2)}) collective-permute-start(bf16[528,128]{1,0:T(8,128)(2,1)S(1)} %shard_map.109), channel_id=1, source_target_pairs={{0,4},{4,8},{8,12},{12,14},{14,10},{10,6},{6,2},{2,0},{1,5},{5,9},... | collective-permute-start | bytes 405512 | tf_op jit(solution)/shard_map/ppermute | solution.py:48
  104.8 1.6 %collective-permute-done.44.arrived_ref.refs_4_ = bf16[528,128]{1,0:T(8,128)(2,1)S(1)} collective-permute-done((bf16[528,128]{1,0:T(8,128)(2,1)S(1)}, bf16[528,128]{1,0:T(8,128)(2,1)S(1)}, u32[]{:S(2)}, u32[]{:S(2)}) %collective-permute-start.44) | collective-permute-done | bytes 135200 | tf_op jit(solution)/shard_map/ppermute | solution.py:48
  106.4 1.4 %collective-permute-start.45 = (bf16[528,128]{1,0:T(8,128)(2,1)S(1)}, bf16[528,128]{1,0:T(8,128)(2,1)S(1)}, u32[]{:S(2)}, u32[]{:S(2)}) collective-permute-start(bf16[528,128]{1,0:T(8,128)(2,1)S(1)} %shard_map.110), channel_id=1, source_target_pairs={{0,4},{4,8},{8,12},{12,14},{14,10},{10,6},{6,2},{2,0},{1,5},{5,9},... | collective-permute-start | bytes 405512 | tf_op jit(solution)/shard_map/ppermute | solution.py:48
  107.8 1.8 %collective-permute-start.48 = (bf16[512,128]{1,0:T(8,128)(2,1)S(1)}, bf16[512,128]{1,0:T(8,128)(2,1)S(1)}, u32[]{:S(2)}, u32[]{:S(2)}) collective-permute-start(bf16[512,128]{1,0:T(8,128)(2,1)S(1)} %shard_map.113), channel_id=1, source_target_pairs={{0,4},{4,8},{8,12},{12,14},{14,10},{10,6},{6,2},{2,0},{1,5},{5,9},... | collective-permute-start | bytes 393224 | tf_op jit(solution)/shard_map/ppermute | solution.py:48
  109.9 1.5 %collective-permute-done.45.refs_1_.refs_6_ = bf16[528,128]{1,0:T(8,128)(2,1)S(1)} collective-permute-done((bf16[528,128]{1,0:T(8,128)(2,1)S(1)}, bf16[528,128]{1,0:T(8,128)(2,1)S(1)}, u32[]{:S(2)}, u32[]{:S(2)}) %collective-permute-start.45) | collective-permute-done | bytes 135200 | tf_op jit(solution)/shard_map/ppermute | solution.py:48
  111.5 1.3 %collective-permute-done.48.refs_2_ = bf16[512,128]{1,0:T(8,128)(2,1)S(1)} collective-permute-done((bf16[512,128]{1,0:T(8,128)(2,1)S(1)}, bf16[512,128]{1,0:T(8,128)(2,1)S(1)}, u32[]{:S(2)}, u32[]{:S(2)}) %collective-permute-start.48) | collective-permute-done | bytes 131104 | tf_op jit(solution)/shard_map/ppermute | solution.py:48
  112.8 1.7 %collective-permute-done.55.refs_4_ = bf16[512,128]{1,0:T(8,128)(2,1)S(1)} collective-permute-done((bf16[512,128]{1,0:T(8,128)(2,1)S(1)}, bf16[512,128]{1,0:T(8,128)(2,1)S(1)}, u32[]{:S(2)}, u32[]{:S(2)}) %collective-permute-start.55) | collective-permute-done | bytes 131104 | tf_op jit(solution)/shard_map/ppermute | solution.py:48
  117.5 1.5 %shard_map.123 = f32[1024,128]{1,0:T(8,128)} custom-call(s32[2]{0:T(128)S(1)} %pad_add_fusion.here_ref, f32[1024,128]{1,0:T(8,128)S(1)} %shard_map.122.inner_ref, f32[1024,1]{1,0:T(8,128)S(1)} %get-tuple-element.16.mine_ref, f32[1024,1]{1,0:T(8,128)S(1)} %collective-permute-done.56.other_ref, f32[1024,128]{1,0:T(8,128)S(1)} %broadcast_in_dim.24.bound_ref), custom_call_target="tpu_custom_call" | custom-call | bytes 1048576 | tf_op jit(solution)/shard_map/pallas_call | solution.py:238
  (150 shorter events, 40.1 us)
Async XLA Ops:
  1.7 13.3 %collective-permute-start.2 = (bf16[512,128]{1,0:T(8,128)(2,1)S(1)}, bf16[512,128]{1,0:T(8,128)(2,1)S(1)}, u32[]{:S(2)}, u32[]{:S(2)}) collective-permute-start(bf16[512,128]{1,0:T(8,128)(2,1)S(1)} %get-tuple-element.10), channel_id=1, source_target_pairs={{0,2},{4,0},{8,4},{12,8},{14,12},{10,14},{6,10},{2,6},{1,3},{5,1},... | collective-permute-start | bytes 393224 | tf_op jit(solution)/shard_map/ppermute | solution.py:48
  4.8 12.2 %collective-permute-start = (bf16[512,128]{1,0:T(8,128)(2,1)S(1)}, bf16[512,128]{1,0:T(8,128)(2,1)S(1)}, u32[]{:S(2)}, u32[]{:S(2)}) collective-permute-start(bf16[512,128]{1,0:T(8,128)(2,1)S(1)} %get-tuple-element.10), channel_id=1, source_target_pairs={{0,4},{4,8},{8,12},{12,14},{14,10},{10,6},{6,2},{2,0},{1,5},{5,9},... | collective-permute-start | bytes 393224 | tf_op jit(solution)/shard_map/ppermute | solution.py:48
  4.9 12.3 %collective-permute-start.3 = (bf16[512,128]{1,0:T(8,128)(2,1)S(1)}, bf16[512,128]{1,0:T(8,128)(2,1)S(1)}, u32[]{:S(2)}, u32[]{:S(2)}) collective-permute-start(bf16[512,128]{1,0:T(8,128)(2,1)S(1)} %get-tuple-element.11), channel_id=1, source_target_pairs={{0,2},{4,0},{8,4},{12,8},{14,12},{10,14},{6,10},{2,6},{1,3},{5,1},... | collective-permute-start | bytes 393224 | tf_op jit(solution)/shard_map/ppermute | solution.py:48
  6.8 12.3 %collective-permute-start.1 = (bf16[512,128]{1,0:T(8,128)(2,1)S(1)}, bf16[512,128]{1,0:T(8,128)(2,1)S(1)}, u32[]{:S(2)}, u32[]{:S(2)}) collective-permute-start(bf16[512,128]{1,0:T(8,128)(2,1)S(1)} %get-tuple-element.11), channel_id=1, source_target_pairs={{0,4},{4,8},{8,12},{12,14},{14,10},{10,6},{6,2},{2,0},{1,5},{5,9},... | collective-permute-start | bytes 393224 | tf_op jit(solution)/shard_map/ppermute | solution.py:48
  15.0 6.1 %collective-permute-start.6 = (bf16[512,128]{1,0:T(8,128)(2,1)S(1)}, bf16[512,128]{1,0:T(8,128)(2,1)S(1)}, u32[]{:S(2)}, u32[]{:S(2)}) collective-permute-start(bf16[512,128]{1,0:T(8,128)(2,1)S(1)} %collective-permute-done.2), channel_id=1, source_target_pairs={{0,2},{4,0},{8,4},{12,8},{14,12},{10,14},{6,10},{2,6},{1,3},{5,1},... | collective-permute-start | bytes 393224 | tf_op jit(solution)/shard_map/ppermute | solution.py:48
  17.0 5.8 %collective-permute-start.4 = (bf16[512,128]{1,0:T(8,128)(2,1)S(1)}, bf16[512,128]{1,0:T(8,128)(2,1)S(1)}, u32[]{:S(2)}, u32[]{:S(2)}) collective-permute-start(bf16[512,128]{1,0:T(8,128)(2,1)S(1)} %collective-permute-done), channel_id=1, source_target_pairs={{0,4},{4,8},{8,12},{12,14},{14,10},{10,6},{6,2},{2,0},{1,5},{5,9},... | collective-permute-start | bytes 393224 | tf_op jit(solution)/shard_map/ppermute | solution.py:48
  17.1 6.8 %collective-permute-start.7 = (bf16[512,128]{1,0:T(8,128)(2,1)S(1)}, bf16[512,128]{1,0:T(8,128)(2,1)S(1)}, u32[]{:S(2)}, u32[]{:S(2)}) collective-permute-start(bf16[512,128]{1,0:T(8,128)(2,1)S(1)} %collective-permute-done.3), channel_id=1, source_target_pairs={{0,2},{4,0},{8,4},{12,8},{14,12},{10,14},{6,10},{2,6},{1,3},{5,1},... | collective-permute-start | bytes 393224 | tf_op jit(solution)/shard_map/ppermute | solution.py:48
  19.0 6.5 %collective-permute-start.5 = (bf16[512,128]{1,0:T(8,128)(2,1)S(1)}, bf16[512,128]{1,0:T(8,128)(2,1)S(1)}, u32[]{:S(2)}, u32[]{:S(2)}) collective-permute-start(bf16[512,128]{1,0:T(8,128)(2,1)S(1)} %collective-permute-done.1), channel_id=1, source_target_pairs={{0,4},{4,8},{8,12},{12,14},{14,10},{10,6},{6,2},{2,0},{1,5},{5,9},... | collective-permute-start | bytes 393224 | tf_op jit(solution)/shard_map/ppermute | solution.py:48
  21.1 10.0 %collective-permute-start.10 = (bf16[512,128]{1,0:T(8,128)(2,1)S(1)}, bf16[512,128]{1,0:T(8,128)(2,1)S(1)}, u32[]{:S(2)}, u32[]{:S(2)}) collective-permute-start(bf16[512,128]{1,0:T(8,128)(2,1)S(1)} %collective-permute-done.6), channel_id=1, source_target_pairs={{0,2},{4,0},{8,4},{12,8},{14,12},{10,14},{6,10},{2,6},{1,3},{5,1},... | collective-permute-start | bytes 393224 | tf_op jit(solution)/shard_map/ppermute | solution.py:48
  22.8 5.6 %collective-permute-start.8 = (bf16[512,128]{1,0:T(8,128)(2,1)S(1)}, bf16[512,128]{1,0:T(8,128)(2,1)S(1)}, u32[]{:S(2)}, u32[]{:S(2)}) collective-permute-start(bf16[512,128]{1,0:T(8,128)(2,1)S(1)} %collective-permute-done.4), channel_id=1, source_target_pairs={{0,4},{4,8},{8,12},{12,14},{14,10},{10,6},{6,2},{2,0},{1,5},{5,9},... | collective-permute-start | bytes 393224 | tf_op jit(solution)/shard_map/ppermute | solution.py:48
  23.9 5.5 %collective-permute-start.11 = (bf16[512,128]{1,0:T(8,128)(2,1)S(1)}, bf16[512,128]{1,0:T(8,128)(2,1)S(1)}, u32[]{:S(2)}, u32[]{:S(2)}) collective-permute-start(bf16[512,128]{1,0:T(8,128)(2,1)S(1)} %collective-permute-done.7), channel_id=1, source_target_pairs={{0,2},{4,0},{8,4},{12,8},{14,12},{10,14},{6,10},{2,6},{1,3},{5,1},... | collective-permute-start | bytes 393224 | tf_op jit(solution)/shard_map/ppermute | solution.py:48
  25.6 5.5 %collective-permute-start.9 = (bf16[512,128]{1,0:T(8,128)(2,1)S(1)}, bf16[512,128]{1,0:T(8,128)(2,1)S(1)}, u32[]{:S(2)}, u32[]{:S(2)}) collective-permute-start(bf16[512,128]{1,0:T(8,128)(2,1)S(1)} %collective-permute-done.5), channel_id=1, source_target_pairs={{0,4},{4,8},{8,12},{12,14},{14,10},{10,6},{6,2},{2,0},{1,5},{5,9},... | collective-permute-start | bytes 393224 | tf_op jit(solution)/shard_map/ppermute | solution.py:48
  35.4 5.6 %collective-permute-start.14 = (bf16[512,128]{1,0:T(8,128)(2,1)S(1)}, bf16[512,128]{1,0:T(8,128)(2,1)S(1)}, u32[]{:S(2)}, u32[]{:S(2)}) collective-permute-start(bf16[512,128]{1,0:T(8,128)(2,1)S(1)} %shard_map.89), channel_id=1, source_target_pairs={{0,4},{4,8},{8,12},{12,14},{14,10},{10,6},{6,2},{2,0},{1,5},{5,9},... | collective-permute-start | bytes 393224 | tf_op jit(solution)/shard_map/ppermute | solution.py:48
  37.2 5.5 %collective-permute-start.24 = (bf16[512,128]{1,0:T(8,128)(2,1)S(1)}, bf16[512,128]{1,0:T(8,128)(2,1)S(1)}, u32[]{:S(2)}, u32[]{:S(2)}) collective-permute-start(bf16[512,128]{1,0:T(8,128)(2,1)S(1)} %shard_map.99), channel_id=1, source_target_pairs={{0,2},{4,0},{8,4},{12,8},{14,12},{10,14},{6,10},{2,6},{1,3},{5,1},... | collective-permute-start | bytes 393224 | tf_op jit(solution)/shard_map/ppermute | solution.py:48
  38.3 6.4 %collective-permute-start.18 = (bf16[512,128]{1,0:T(8,128)(2,1)S(1)}, bf16[512,128]{1,0:T(8,128)(2,1)S(1)}, u32[]{:S(2)}, u32[]{:S(2)}) collective-permute-start(bf16[512,128]{1,0:T(8,128)(2,1)S(1)} %shard_map.93), channel_id=1, source_target_pairs={{0,4},{4,8},{8,12},{12,14},{14,10},{10,6},{6,2},{2,0},{1,5},{5,9},... | collective-permute-start | bytes 393224 | tf_op jit(solution)/shard_map/ppermute | solution.py:48
  40.0 6.5 %collective-permute-start.21 = (bf16[512,128]{1,0:T(8,128)(2,1)S(1)}, bf16[512,128]{1,0:T(8,128)(2,1)S(1)}, u32[]{:S(2)}, u32[]{:S(2)}) collective-permute-start(bf16[512,128]{1,0:T(8,128)(2,1)S(1)} %shard_map.96), channel_id=1, source_target_pairs={{0,2},{4,0},{8,4},{12,8},{14,12},{10,14},{6,10},{2,6},{1,3},{5,1},... | collective-permute-start | bytes 393224 | tf_op jit(solution)/shard_map/ppermute | solution.py:48
  41.1 6.4 %collective-permute-start.15 = (bf16[512,128]{1,0:T(8,128)(2,1)S(1)}, bf16[512,128]{1,0:T(8,128)(2,1)S(1)}, u32[]{:S(2)}, u32[]{:S(2)}) collective-permute-start(bf16[512,128]{1,0:T(8,128)(2,1)S(1)} %shard_map.90), channel_id=1, source_target_pairs={{0,4},{4,8},{8,12},{12,14},{14,10},{10,6},{6,2},{2,0},{1,5},{5,9},... | collective-permute-start | bytes 393224 | tf_op jit(solution)/shard_map/ppermute | solution.py:48
  42.7 6.6 %collective-permute-start.25 = (bf16[512,128]{1,0:T(8,128)(2,1)S(1)}, bf16[512,128]{1,0:T(8,128)(2,1)S(1)}, u32[]{:S(2)}, u32[]{:S(2)}) collective-permute-start(bf16[512,128]{1,0:T(8,128)(2,1)S(1)} %shard_map.100), channel_id=1, source_target_pairs={{0,2},{4,0},{8,4},{12,8},{14,12},{10,14},{6,10},{2,6},{1,3},{5,1},... | collective-permute-start | bytes 393224 | tf_op jit(solution)/shard_map/ppermute | solution.py:48
  44.7 6.2 %collective-permute-start.19 = (bf16[512,128]{1,0:T(8,128)(2,1)S(1)}, bf16[512,128]{1,0:T(8,128)(2,1)S(1)}, u32[]{:S(2)}, u32[]{:S(2)}) collective-permute-start(bf16[512,128]{1,0:T(8,128)(2,1)S(1)} %shard_map.94), channel_id=1, source_target_pairs={{0,4},{4,8},{8,12},{12,14},{14,10},{10,6},{6,2},{2,0},{1,5},{5,9},... | collective-permute-start | bytes 393224 | tf_op jit(solution)/shard_map/ppermute | solution.py:48
  46.5 6.0 %collective-permute-start.22 = (bf16[512,128]{1,0:T(8,128)(2,1)S(1)}, bf16[512,128]{1,0:T(8,128)(2,1)S(1)}, u32[]{:S(2)}, u32[]{:S(2)}) collective-permute-start(bf16[512,128]{1,0:T(8,128)(2,1)S(1)} %shard_map.97), channel_id=1, source_target_pairs={{0,2},{4,0},{8,4},{12,8},{14,12},{10,14},{6,10},{2,6},{1,3},{5,1},... | collective-permute-start | bytes 393224 | tf_op jit(solution)/shard_map/ppermute | solution.py:48
  47.5 5.6 %collective-permute-start.16 = (bf16[512,128]{1,0:T(8,128)(2,1)S(1)}, bf16[512,128]{1,0:T(8,128)(2,1)S(1)}, u32[]{:S(2)}, u32[]{:S(2)}) collective-permute-start(bf16[512,128]{1,0:T(8,128)(2,1)S(1)} %shard_map.91), channel_id=1, source_target_pairs={{0,4},{4,8},{8,12},{12,14},{14,10},{10,6},{6,2},{2,0},{1,5},{5,9},... | collective-permute-start | bytes 393224 | tf_op jit(solution)/shard_map/ppermute | solution.py:48
  49.3 5.5 %collective-permute-start.26 = (bf16[512,128]{1,0:T(8,128)(2,1)S(1)}, bf16[512,128]{1,0:T(8,128)(2,1)S(1)}, u32[]{:S(2)}, u32[]{:S(2)}) collective-permute-start(bf16[512,128]{1,0:T(8,128)(2,1)S(1)} %shard_map.101), channel_id=1, source_target_pairs={{0,2},{4,0},{8,4},{12,8},{14,12},{10,14},{6,10},{2,6},{1,3},{5,1},... | collective-permute-start | bytes 393224 | tf_op jit(solution)/shard_map/ppermute | solution.py:48
  50.9 6.1 %collective-permute-start.20 = (bf16[512,128]{1,0:T(8,128)(2,1)S(1)}, bf16[512,128]{1,0:T(8,128)(2,1)S(1)}, u32[]{:S(2)}, u32[]{:S(2)}) collective-permute-start(bf16[512,128]{1,0:T(8,128)(2,1)S(1)} %shard_map.95), channel_id=1, source_target_pairs={{0,4},{4,8},{8,12},{12,14},{14,10},{10,6},{6,2},{2,0},{1,5},{5,9},... | collective-permute-start | bytes 393224 | tf_op jit(solution)/shard_map/ppermute | solution.py:48
  52.6 6.1 %collective-permute-start.23 = (bf16[512,128]{1,0:T(8,128)(2,1)S(1)}, bf16[512,128]{1,0:T(8,128)(2,1)S(1)}, u32[]{:S(2)}, u32[]{:S(2)}) collective-permute-start(bf16[512,128]{1,0:T(8,128)(2,1)S(1)} %shard_map.98), channel_id=1, source_target_pairs={{0,2},{4,0},{8,4},{12,8},{14,12},{10,14},{6,10},{2,6},{1,3},{5,1},... | collective-permute-start | bytes 393224 | tf_op jit(solution)/shard_map/ppermute | solution.py:48
  53.1 6.7 %collective-permute-start.17 = (bf16[512,128]{1,0:T(8,128)(2,1)S(1)}, bf16[512,128]{1,0:T(8,128)(2,1)S(1)}, u32[]{:S(2)}, u32[]{:S(2)}) collective-permute-start(bf16[512,128]{1,0:T(8,128)(2,1)S(1)} %shard_map.92), channel_id=1, source_target_pairs={{0,4},{4,8},{8,12},{12,14},{14,10},{10,6},{6,2},{2,0},{1,5},{5,9},... | collective-permute-start | bytes 393224 | tf_op jit(solution)/shard_map/ppermute | solution.py:48
  54.8 6.6 %collective-permute-start.27 = (bf16[512,128]{1,0:T(8,128)(2,1)S(1)}, bf16[512,128]{1,0:T(8,128)(2,1)S(1)}, u32[]{:S(2)}, u32[]{:S(2)}) collective-permute-start(bf16[512,128]{1,0:T(8,128)(2,1)S(1)} %shard_map.102), channel_id=1, source_target_pairs={{0,2},{4,0},{8,4},{12,8},{14,12},{10,14},{6,10},{2,6},{1,3},{5,1},... | collective-permute-start | bytes 393224 | tf_op jit(solution)/shard_map/ppermute | solution.py:48
  61.6 6.4 %collective-permute-start.30 = (bf16[512,128]{1,0:T(8,128)(2,1)S(1)}, bf16[512,128]{1,0:T(8,128)(2,1)S(1)}, u32[]{:S(2)}, u32[]{:S(2)}) collective-permute-start(bf16[512,128]{1,0:T(8,128)(2,1)S(1)} %get-tuple-element.12), channel_id=1, source_target_pairs={{0,2},{4,0},{8,4},{12,8},{14,12},{10,14},{6,10},{2,6},{1,3},{5,1},... | collective-permute-start | bytes 393224 | tf_op jit(solution)/shard_map/ppermute | solution.py:48
  62.5 6.4 %collective-permute-start.28 = (bf16[512,128]{1,0:T(8,128)(2,1)S(1)}, bf16[512,128]{1,0:T(8,128)(2,1)S(1)}, u32[]{:S(2)}, u32[]{:S(2)}) collective-permute-start(bf16[512,128]{1,0:T(8,128)(2,1)S(1)} %get-tuple-element.12), channel_id=1, source_target_pairs={{0,4},{4,8},{8,12},{12,14},{14,10},{10,6},{6,2},{2,0},{1,5},{5,9},... | collective-permute-start | bytes 393224 | tf_op jit(solution)/shard_map/ppermute | solution.py:48
  63.7 6.4 %collective-permute-start.31 = (bf16[512,128]{1,0:T(8,128)(2,1)S(1)}, bf16[512,128]{1,0:T(8,128)(2,1)S(1)}, u32[]{:S(2)}, u32[]{:S(2)}) collective-permute-start(bf16[512,128]{1,0:T(8,128)(2,1)S(1)} %get-tuple-element.13), channel_id=1, source_target_pairs={{0,2},{4,0},{8,4},{12,8},{14,12},{10,14},{6,10},{2,6},{1,3},{5,1},... | collective-permute-start | bytes 393224 | tf_op jit(solution)/shard_map/ppermute | solution.py:48
  64.5 7.2 %collective-permute-start.29 = (bf16[512,128]{1,0:T(8,128)(2,1)S(1)}, bf16[512,128]{1,0:T(8,128)(2,1)S(1)}, u32[]{:S(2)}, u32[]{:S(2)}) collective-permute-start(bf16[512,128]{1,0:T(8,128)(2,1)S(1)} %get-tuple-element.13), channel_id=1, source_target_pairs={{0,4},{4,8},{8,12},{12,14},{14,10},{10,6},{6,2},{2,0},{1,5},{5,9},... | collective-permute-start | bytes 393224 | tf_op jit(solution)/shard_map/ppermute | solution.py:48
  68.0 6.1 %collective-permute-start.34 = (bf16[512,128]{1,0:T(8,128)(2,1)S(1)}, bf16[512,128]{1,0:T(8,128)(2,1)S(1)}, u32[]{:S(2)}, u32[]{:S(2)}) collective-permute-start(bf16[512,128]{1,0:T(8,128)(2,1)S(1)} %collective-permute-done.30), channel_id=1, source_target_pairs={{0,2},{4,0},{8,4},{12,8},{14,12},{10,14},{6,10},{2,6},{1,3},{5,1},... | collective-permute-start | bytes 393224 | tf_op jit(solution)/shard_map/ppermute | solution.py:48
  68.9 6.0 %collective-permute-start.32 = (bf16[512,128]{1,0:T(8,128)(2,1)S(1)}, bf16[512,128]{1,0:T(8,128)(2,1)S(1)}, u32[]{:S(2)}, u32[]{:S(2)}) collective-permute-start(bf16[512,128]{1,0:T(8,128)(2,1)S(1)} %collective-permute-done.28), channel_id=1, source_target_pairs={{0,4},{4,8},{8,12},{12,14},{14,10},{10,6},{6,2},{2,0},{1,5},{5,9},... | collective-permute-start | bytes 393224 | tf_op jit(solution)/shard_map/ppermute | solution.py:48
  70.1 6.1 %collective-permute-start.35 = (bf16[512,128]{1,0:T(8,128)(2,1)S(1)}, bf16[512,128]{1,0:T(8,128)(2,1)S(1)}, u32[]{:S(2)}, u32[]{:S(2)}) collective-permute-start(bf16[512,128]{1,0:T(8,128)(2,1)S(1)} %collective-permute-done.31), channel_id=1, source_target_pairs={{0,2},{4,0},{8,4},{12,8},{14,12},{10,14},{6,10},{2,6},{1,3},{5,1},... | collective-permute-start | bytes 393224 | tf_op jit(solution)/shard_map/ppermute | solution.py:48
  74.2 8.6 %collective-permute-start.38 = (bf16[512,128]{1,0:T(8,128)(2,1)S(1)}, bf16[512,128]{1,0:T(8,128)(2,1)S(1)}, u32[]{:S(2)}, u32[]{:S(2)}) collective-permute-start(bf16[512,128]{1,0:T(8,128)(2,1)S(1)} %collective-permute-done.34), channel_id=1, source_target_pairs={{0,2},{4,0},{8,4},{12,8},{14,12},{10,14},{6,10},{2,6},{1,3},{5,1},... | collective-permute-start | bytes 393224 | tf_op jit(solution)/shard_map/ppermute | solution.py:48
  74.8 5.7 %collective-permute-start.36 = (bf16[512,128]{1,0:T(8,128)(2,1)S(1)}, bf16[512,128]{1,0:T(8,128)(2,1)S(1)}, u32[]{:S(2)}, u32[]{:S(2)}) collective-permute-start(bf16[512,128]{1,0:T(8,128)(2,1)S(1)} %collective-permute-done.32), channel_id=1, source_target_pairs={{0,4},{4,8},{8,12},{12,14},{14,10},{10,6},{6,2},{2,0},{1,5},{5,9},... | collective-permute-start | bytes 393224 | tf_op jit(solution)/shard_map/ppermute | solution.py:48
  76.2 5.9 %collective-permute-start.39 = (bf16[512,128]{1,0:T(8,128)(2,1)S(1)}, bf16[512,128]{1,0:T(8,128)(2,1)S(1)}, u32[]{:S(2)}, u32[]{:S(2)}) collective-permute-start(bf16[512,128]{1,0:T(8,128)(2,1)S(1)} %collective-permute-done.35), channel_id=1, source_target_pairs={{0,2},{4,0},{8,4},{12,8},{14,12},{10,14},{6,10},{2,6},{1,3},{5,1},... | collective-permute-start | bytes 393224 | tf_op jit(solution)/shard_map/ppermute | solution.py:48
  76.9 6.5 %collective-permute-start.37 = (bf16[512,128]{1,0:T(8,128)(2,1)S(1)}, bf16[512,128]{1,0:T(8,128)(2,1)S(1)}, u32[]{:S(2)}, u32[]{:S(2)}) collective-permute-start(bf16[512,128]{1,0:T(8,128)(2,1)S(1)} %collective-permute-done.33), channel_id=1, source_target_pairs={{0,4},{4,8},{8,12},{12,14},{14,10},{10,6},{6,2},{2,0},{1,5},{5,9},... | collective-permute-start | bytes 393224 | tf_op jit(solution)/shard_map/ppermute | solution.py:48
  80.5 5.7 %collective-permute-start.40 = (bf16[512,128]{1,0:T(8,128)(2,1)S(1)}, bf16[512,128]{1,0:T(8,128)(2,1)S(1)}, u32[]{:S(2)}, u32[]{:S(2)}) collective-permute-start(bf16[512,128]{1,0:T(8,128)(2,1)S(1)} %collective-permute-done.36), channel_id=1, source_target_pairs={{0,4},{4,8},{8,12},{12,14},{14,10},{10,6},{6,2},{2,0},{1,5},{5,9},... | collective-permute-start | bytes 393224 | tf_op jit(solution)/shard_map/ppermute | solution.py:48
  88.2 6.0 %collective-permute-start.52 = (bf16[512,128]{1,0:T(8,128)(2,1)S(1)}, bf16[512,128]{1,0:T(8,128)(2,1)S(1)}, u32[]{:S(2)}, u32[]{:S(2)}) collective-permute-start(bf16[512,128]{1,0:T(8,128)(2,1)S(1)} %shard_map.117), channel_id=1, source_target_pairs={{0,2},{4,0},{8,4},{12,8},{14,12},{10,14},{6,10},{2,6},{1,3},{5,1},... | collective-permute-start | bytes 393224 | tf_op jit(solution)/shard_map/ppermute | solution.py:48
  88.8 6.1 %collective-permute-start.42 = (bf16[528,128]{1,0:T(8,128)(2,1)S(1)}, bf16[528,128]{1,0:T(8,128)(2,1)S(1)}, u32[]{:S(2)}, u32[]{:S(2)}) collective-permute-start(bf16[528,128]{1,0:T(8,128)(2,1)S(1)} %shard_map.107), channel_id=1, source_target_pairs={{0,4},{4,8},{8,12},{12,14},{14,10},{10,6},{6,2},{2,0},{1,5},{5,9},... | collective-permute-start | bytes 405512 | tf_op jit(solution)/shard_map/ppermute | solution.py:48
  91.0 6.4 %collective-permute-start.46 = (bf16[512,128]{1,0:T(8,128)(2,1)S(1)}, bf16[512,128]{1,0:T(8,128)(2,1)S(1)}, u32[]{:S(2)}, u32[]{:S(2)}) collective-permute-start(bf16[512,128]{1,0:T(8,128)(2,1)S(1)} %shard_map.111), channel_id=1, source_target_pairs={{0,4},{4,8},{8,12},{12,14},{14,10},{10,6},{6,2},{2,0},{1,5},{5,9},... | collective-permute-start | bytes 393224 | tf_op jit(solution)/shard_map/ppermute | solution.py:48
  92.6 6.5 %collective-permute-start.49 = (bf16[528,128]{1,0:T(8,128)(2,1)S(1)}, bf16[528,128]{1,0:T(8,128)(2,1)S(1)}, u32[]{:S(2)}, u32[]{:S(2)}) collective-permute-start(bf16[528,128]{1,0:T(8,128)(2,1)S(1)} %shard_map.114), channel_id=1, source_target_pairs={{0,2},{4,0},{8,4},{12,8},{14,12},{10,14},{6,10},{2,6},{1,3},{5,1},... | collective-permute-start | bytes 405512 | tf_op jit(solution)/shard_map/ppermute | solution.py:48
  94.2 6.2 %collective-permute-start.53 = (bf16[512,128]{1,0:T(8,128)(2,1)S(1)}, bf16[512,128]{1,0:T(8,128)(2,1)S(1)}, u32[]{:S(2)}, u32[]{:S(2)}) collective-permute-start(bf16[512,128]{1,0:T(8,128)(2,1)S(1)} %shard_map.118), channel_id=1, source_target_pairs={{0,2},{4,0},{8,4},{12,8},{14,12},{10,14},{6,10},{2,6},{1,3},{5,1},... | collective-permute-start | bytes 393224 | tf_op jit(solution)/shard_map/ppermute | solution.py:48
  94.9 6.1 %collective-permute-start.43 = (bf16[528,128]{1,0:T(8,128)(2,1)S(1)}, bf16[528,128]{1,0:T(8,128)(2,1)S(1)}, u32[]{:S(2)}, u32[]{:S(2)}) collective-permute-start(bf16[528,128]{1,0:T(8,128)(2,1)S(1)} %shard_map.108), channel_id=1, source_target_pairs={{0,4},{4,8},{8,12},{12,14},{14,10},{10,6},{6,2},{2,0},{1,5},{5,9},... | collective-permute-start | bytes 405512 | tf_op jit(solution)/shard_map/ppermute | solution.py:48
  97.5 10.2 %collective-permute-start.47 = (bf16[512,128]{1,0:T(8,128)(2,1)S(1)}, bf16[512,128]{1,0:T(8,128)(2,1)S(1)}, u32[]{:S(2)}, u32[]{:S(2)}) collective-permute-start(bf16[512,128]{1,0:T(8,128)(2,1)S(1)} %shard_map.112), channel_id=1, source_target_pairs={{0,4},{4,8},{8,12},{12,14},{14,10},{10,6},{6,2},{2,0},{1,5},{5,9},... | collective-permute-start | bytes 393224 | tf_op jit(solution)/shard_map/ppermute | solution.py:48
  100.4 9.1 %collective-permute-start.54 = (bf16[512,128]{1,0:T(8,128)(2,1)S(1)}, bf16[512,128]{1,0:T(8,128)(2,1)S(1)}, u32[]{:S(2)}, u32[]{:S(2)}) collective-permute-start(bf16[512,128]{1,0:T(8,128)(2,1)S(1)} %shard_map.119), channel_id=1, source_target_pairs={{0,2},{4,0},{8,4},{12,8},{14,12},{10,14},{6,10},{2,6},{1,3},{5,1},... | collective-permute-start | bytes 393224 | tf_op jit(solution)/shard_map/ppermute | solution.py:48
  104.2 5.8 %collective-permute-start.51 = (bf16[528,128]{1,0:T(8,128)(2,1)S(1)}, bf16[528,128]{1,0:T(8,128)(2,1)S(1)}, u32[]{:S(2)}, u32[]{:S(2)}) collective-permute-start(bf16[528,128]{1,0:T(8,128)(2,1)S(1)} %shard_map.116), channel_id=1, source_target_pairs={{0,2},{4,0},{8,4},{12,8},{14,12},{10,14},{6,10},{2,6},{1,3},{5,1},... | collective-permute-start | bytes 405512 | tf_op jit(solution)/shard_map/ppermute | solution.py:48
  111.4 7.5 %collective-permute-start.57 = (f32[16,128]{1,0:T(8,128)S(1)}, f32[16,128]{1,0:T(8,128)S(1)}, u32[]{:S(2)}, u32[]{:S(2)}) collective-permute-start(f32[16,128]{1,0:T(8,128)S(1)} %shard_map.125.left_ref), channel_id=1, source_target_pairs={{0,1},{1,0},{2,3},{3,2},{4,5},{5,4},{6,7},{7,6},{8,9},{9,8},{10,11... | collective-permute-start | bytes 24584 | tf_op jit(solution)/shard_map/ppermute | solution.py:431
  (14 other events, 75.4 us)

commit v5 on v4

--- a/solution.py
+++ b/solution.py
@@ -82,7 +82,7 @@
     return pl.pallas_call(
         kernel,
         out_shape=out_shape,
-        in_specs=[pl.BlockSpec(memory_space=pltpu.SMEM if x.dtype == jnp.int32 else pltpu.VMEM) for x in operands],
+        in_specs=[pl.BlockSpec(memory_space=pltpu.VMEM)] * len(operands),
         out_specs=jax.tree.map(lambda x: pl.BlockSpec(memory_space=pltpu.VMEM if x.ndim > 1 else pltpu.SMEM), out_shape),
         compiler_params=pltpu.CompilerParams(vmem_limit_bytes=16 << 20),
         cost_estimate=pl.CostEstimate(flops=0, transcendentals=0, bytes_accessed=touched),
@@ -126,7 +126,7 @@
     for send in scatter_sends(count):
         chunk, way, hop = send
         spread, low = part(chunk, (way * hop) % count)
-        more = extra is not None and chunk == 0
+        more = extra is not None and chunk == chunks - 1
         rows = height + (extra.shape[0] if more else 0)
         shape = jax.ShapeDtypeStruct((rows, spread.shape[1]), jnp.bfloat16)
         if (chunk, way) in held:
@@ -148,9 +148,9 @@
     return jnp.where(place < count // 2, 2 * place, 2 * (count - place) - 1)
 
 
-def reorder_kernel(distances, count, here_ref, factors_ref, out_ref, sems):
+def reorder_kernel(distances, count, _, factors_ref, out_ref, sems):
     width = factors_ref.shape[1] // count
-    mine = place_of(here_ref[0], count)
+    mine = place_of(lax.axis_index("net"), count)
     copies = []
     for j, distance in enumerate(distances):
         source = at_place((mine + distance) % count, count) * width
@@ -167,17 +167,17 @@
         copy.wait()
 
 
-def reorder(here, factors, distances, count):
+def reorder(factors, distances, count):
     rows, width = factors.shape[0], factors.shape[1] // count * len(distances)
     return pl.pallas_call(
         functools.partial(reorder_kernel, tuple(distances), count),
         out_shape=jax.ShapeDtypeStruct((rows, width), factors.dtype),
-        in_specs=[pl.BlockSpec(memory_space=pltpu.SMEM), pl.BlockSpec(memory_space=pltpu.HBM)],
+        in_specs=[pl.BlockSpec(memory_space=pl.ANY), pl.BlockSpec(memory_space=pltpu.HBM)],
         out_specs=pl.BlockSpec(memory_space=pltpu.VMEM),
         scratch_shapes=[pltpu.SemaphoreType.DMA((len(distances),))],
         compiler_params=pltpu.CompilerParams(vmem_limit_bytes=50 << 20),
         cost_estimate=pl.CostEstimate(flops=0, transcendentals=0, bytes_accessed=rows * width * factors.dtype.itemsize),
-    )(here, factors)
+    )(lax.axis_index("net").reshape(1), factors)
 
 
 def narrow_kernel(wide_ref, *out_refs):
@@ -186,64 +186,51 @@
         ref[...] = wide_ref[pl.ds(c * height, height), :].astype(ref.dtype)
 
 
-def last_update_kernel(lows, here_ref, *refs):
-    spread_ref, ahead, behind = refs[0], refs[1 : chunks + 1], refs[chunks + 1 : 2 * chunks + 1]
-    inject_ref, out_ref, edge_ref = refs[2 * chunks + 1 :]
-    height, top = inject_ref.shape[0] // chunks, pl.ds(0, inject_ref.shape[0] // chunks)
-    first = here_ref[1] == 0
-    for c, low in enumerate(lows):
-        rows = pl.ds(c * height, height)
-        total = spread_ref[pl.ds(low, height), :]
-        total = total + ahead[c][top, :].astype(jnp.float32) + behind[c][top, :].astype(jnp.float32)
-        inject = inject_ref[rows, :] - relax_step * total
-        out_ref[rows, :] = inject
-        edge_ref[rows, :] = jnp.where(first, inject[:, -1:], inject[:, :1])
+def last_update_kernel(low, chunk, spread_ref, ahead_ref, behind_ref, inject_ref, out_ref):
+    height = out_ref.shape[0]
+    top = pl.ds(0, height)
+    total = spread_ref[pl.ds(low, height), :]
+    total = total + ahead_ref[top, :].astype(jnp.float32) + behind_ref[top, :].astype(jnp.float32)
+    out_ref[...] = inject_ref[pl.ds(chunk * height, height), :] - relax_step * total
 
 
 def excess_of(step, bound):
     return step - jnp.clip(step, -bound, bound)
 
 
-def inner_ramp_kernel(inject_ref, bound_ref, out_ref):
-    inject, bound = inject_ref[...], bound_ref[...]
-    periods = inject.shape[1]
-    lane = lax.broadcasted_iota(jnp.int32, inject.shape, 1)
-    low = jnp.where(lane == 0, 0.0, excess_of(inject - pltpu.roll(inject, 1, 1), bound))
-    high = jnp.where(lane == periods - 1, 0.0, pltpu.roll(low, periods - 1, 1))
-    out_ref[...] = inject - 0.5 * low + 0.5 * high
-
-
-def edge_ramp_kernel(here_ref, inner_ref, mine_ref, other_ref, bound_ref, out_ref, whole, sems):
-    first = here_ref[1] == 0
-    parts = sems.shape[0]
-    rows, periods = whole.shape[0] // parts, whole.shape[1]
-    edge = jnp.where(first, periods - 1, 0)
-    copies = []
-    for p in range(parts):
-        at = pl.ds(p * rows, rows)
-        mine, other, inner = mine_ref[at, :], other_ref[at, :], inner_ref[at, :]
-        excess = excess_of(jnp.where(first, other - mine, mine - other), bound_ref[at, :1])
-        share = jnp.where(first, 0.5 * excess, -0.5 * excess)
-        lane = lax.broadcasted_iota(jnp.int32, inner.shape, 1)
-        whole[at, :] = jnp.where(lane == edge, inner + share, inner)
-        copy = pltpu.make_async_copy(whole.at[at, :], out_ref.at[at, :], sems.at[p])
-        copy.start()
-        copies.append(copy)
-    for copy in copies:
-        copy.wait()
-
-
-def edge_ramp(here, inner, mine, other, bound):
-    parts = 4
-    return pl.pallas_call(
-        edge_ramp_kernel,
-        out_shape=jax.ShapeDtypeStruct(inner.shape, inner.dtype),
-        in_specs=[pl.BlockSpec(memory_space=pltpu.SMEM)] + [pl.BlockSpec(memory_space=pltpu.VMEM)] * 4,
-        out_specs=pl.BlockSpec(memory_space=pltpu.HBM),
-        scratch_shapes=[pltpu.VMEM(inner.shape, inner.dtype), pltpu.SemaphoreType.DMA((parts,))],
-        compiler_params=pltpu.CompilerParams(vmem_limit_bytes=16 << 20),
-        cost_estimate=pl.CostEstimate(flops=0, transcendentals=0, bytes_accessed=2 * inner.size * inner.dtype.itemsize),
-    )(here, inner, mine, other, bound)
+def inner_ramp_kernel(*refs):
+    *parts, bound_ref, out_ref = refs
+    for c, ref in enumerate(parts):
+        inject = ref[...]
+        rows, periods = inject.shape
+        at = pl.ds(c * rows, rows)
+        lane = lax.broadcasted_iota(jnp.int32, inject.shape, 1)
+        low = jnp.where(lane == 0, 0.0, excess_of(inject - pltpu.roll(inject, 1, 1), bound_ref[at, :]))
+        high = jnp.where(lane == periods - 1, 0.0, pltpu.roll(low, periods - 1, 1))
+        out_ref[at, :] = inject - 0.5 * low + 0.5 * high
+
+
+def edge_kernel(*refs):
+    mine_refs, other_refs, (bound_ref, out_ref) = refs[:chunks], refs[chunks : 2 * chunks], refs[2 * chunks :]
+    first = lax.axis_index("tm") == 0
+    rows, periods = mine_refs[0].shape
+    lane = lax.broadcasted_iota(jnp.int32, (rows, periods), 1)
+    at_edge = lane == jnp.where(first, periods - 1, 0)
+    sign = jnp.where(first, 0.5, -0.5)
+    for c in range(chunks):
+        at = pl.ds(c * rows, rows)
+        mine, other = mine_refs[c][...], other_refs[c][...]
+        other = jnp.where(first, pltpu.roll(other, periods - 1, 1), pltpu.roll(other, 1, 1))
+        excess = excess_of(jnp.where(first, other - mine, mine - other), bound_ref[at, :])
+        out_ref[at, :] = jnp.where(at_edge, sign * excess, 0.0)
+
+
+def norms_kernel(entries, left_ref, right_ref, out_ref):
+    total = left_ref[...] + right_ref[...]
+    row = lax.broadcasted_iota(jnp.int32, total.shape, 0)
+    for k in range(passes):
+        square = jnp.sum(jnp.where((row >= 3 * k) & (row < 3 * k + 3), total, 0.0), axis=0, keepdims=True)
+        out_ref[k] = jnp.sum(jnp.sqrt(jnp.sum(square, axis=1, keepdims=True) / entries))
 
 
 def squares_kernel(misfit_ref, out_ref):
@@ -275,15 +262,6 @@
     out_ref[...] = total
 
 
-def norms_kernel(entries, left_ref, right_ref, out_ref):
-    total = left_ref[...] + right_ref[...]
-    row = lax.broadcasted_iota(jnp.int32, total.shape, 0)
-    for k in range(passes):
-        square = jnp.sum(jnp.where((row >= 3 * k) & (row < 3 * k + 3), total, 0.0), axis=0, keepdims=True)
-        norm = jnp.sqrt(jnp.sum(square, axis=1, keepdims=True) / entries)
-        out_ref[k] = jnp.sum(norm)
-
-
 def limits_of(outage_line, ratings):
     levels = lax.broadcasted_iota(jnp.int32, (outage_line.shape[0], ratings.shape[0]), 1)
     return jnp.sum(jnp.where(outage_line[:, None] == levels, ratings[None, :], 0.0), axis=1)
@@ -335,13 +313,12 @@
     count = lax.axis_size("net")
     ring = is_ring(count, lax.axis_size("tm"))
     height = owned // chunks
-    here = jnp.stack([lax.axis_index("net"), lax.axis_index("tm")]).astype(jnp.int32)
     if ring:
         order = ring_order(count)
         groups = ring_groups(count)
         factors = []
         for part in reorder_parts(groups):
-            side = reorder(here, shift_factors, [d for g in part for d in g], count)
+            side = reorder(shift_factors, [d for g in part for d in g], count)
             low = 0
             for g in part:
                 factors.append(side[:, low : low + len(g) * owned])
@@ -392,7 +369,6 @@
     chunk_shape = jax.ShapeDtypeStruct((height, periods), jnp.bfloat16)
     whole_shape = jax.ShapeDtypeStruct((owned, periods), jnp.float32)
     slim = small_call(narrow_kernel, [chunk_shape] * chunks, proposal)
-    bound = jnp.broadcast_to(ramp_limit[:, None], (owned, periods))
     inject = proposal
     for stage in range(passes):
         misfit, _ = project(forward(slim), dual, limits)
@@ -415,24 +391,20 @@
                 *arrived,
                 inject,
             )
-        else:
-            inject, edge = small_call(
-                functools.partial(last_update_kernel, lows),
-                [whole_shape, jax.ShapeDtypeStruct((owned, 1), jnp.float32)],
-                here,
-                own[0][0],
-                *arrived,
-                inject,
-            )
-    other = lax.ppermute(edge, "tm", [(0, 1), (1, 0)])
-    inner = small_call(inner_ramp_kernel, whole_shape, inject, bound)
+    last, other = [], []
+    for c in range(chunks):
+        shape = jax.ShapeDtypeStruct((height, periods), jnp.float32)
+        kernel = functools.partial(last_update_kernel, own[c][1], c)
+        last.append(small_call(kernel, shape, own[c][0], held[c, 1], held[c, -1], inject))
+        other.append(lax.ppermute(last[c], "tm", [(0, 1), (1, 0)]))
+    bound = jnp.broadcast_to(ramp_limit[:, None], (owned, periods))
+    inner = small_call(inner_ramp_kernel, whole_shape, *last, bound)
     wide = jax.ShapeDtypeStruct(extra.shape, jnp.float32)
     sums = small_call(unpack_kernel, wide, extra, *tiles)
     others = lax.ppermute(sums, "tm", [(0, 1), (1, 0)])
-    norms = small_call(
-        functools.partial(norms_kernel, entries), jax.ShapeDtypeStruct((passes,), jnp.float32), sums, others
-    )
-    dispatch = edge_ramp(here, inner, edge, other, bound)
+    shape = jax.ShapeDtypeStruct((passes,), jnp.float32)
+    norms = small_call(functools.partial(norms_kernel, entries), shape, sums, others)
+    dispatch = inner + small_call(edge_kernel, whole_shape, *last, *other, bound)
     return (dispatch, dual, norms)
 
 

time: 120 us -> 119 us (level)
  Pallas kernels: 12.2 us -> 8.69 us
    ppermute x56, waiting for transfers between devices: 32 us -> 33.6 us  [hop_to(): return lax.ppermute(block, 'net', pairs)]
    pallas_call x3, Pallas kernels: 7.03 us -> 5.43 us  [reorder(): pl.pallas_call(functools.partial(reorder_kernel, tuple(distances), count)...]
    pallas_call x1 -> x0, Pallas kernels: 1.5 us -> none  [edge_ramp(): pl.pallas_call(edge_ramp_kernel, out_shape=jax.ShapeDtypeStruct(inner.sha...]
    pallas_call x38 -> x40, Pallas kernels: 3.7 us -> 3.27 us  [small_call(): pl.pallas_call(kernel, out_shape=out_shape, in_specs=[pl.BlockSpec(memory...]
  transfers between devices with their start and end apart: 58 -> 59, of which waited for: 31 -> 29; matrix products, arithmetic and copies ran while one was open for 9% -> 9% of each run, Pallas kernels for 9% -> 7%
where the time goes in v5:
time: 119 us; the launch traced here: 118 us
  starting transfers between devices  60 us (50%)
  waiting for transfers between devices  33.6 us (28%)
  matrix products  11.7 us (10%)
  Pallas kernels  8.69 us (7%)
  other arithmetic  1.8 us (2%)
  local copies, waits for them, and re-layouts  1.45 us (1%)
    ppermute x56, starting transfers between devices, hop_to(): return lax.ppermute(block, 'net', pairs)  59.3 us
    ppermute x56, waiting for transfers between devices, hop_to(): return lax.ppermute(block, 'net', pairs)  33.6 us
    dot_general x8, matrix products, backward(): lax.dot_general(cols, narrow, (((0,), (0,)), ((), ())), preferred_element...  5.93 us
    dot_general x8, matrix products, forward(): share = jnp.dot(cols, blocks, preferred_element_type=jnp.float32)  5.78 us
    pallas_call x3, Pallas kernels, reorder(): pl.pallas_call(functools.partial(reorder_kernel, tuple(distances), count)...  5.43 us
    pallas_call x40, Pallas kernels, small_call(): pl.pallas_call(kernel, out_shape=out_shape, in_specs=[pl.BlockSpec(memory...  3.27 us
  transfers between devices with their start and end apart: 59, of which 29 were waited for; matrix products, arithmetic and copies ran while one was open for 9% of the time, Pallas kernels for 7%

profile of v5, /device:TPU:0, one launch (start us, length us, event | category | flops | bytes accessed | tf_op | source)
XLA Modules:
  0.0 118.4 jit_solution(15203671322631219475)
XLA Ops:
  0.6 1.0 copy-done
  1.7 3.0 %collective-permute-start.2 = (bf16[512,128]{1,0:T(8,128)(2,1)S(1)}, bf16[512,128]{1,0:T(8,128)(2,1)S(1)}, u32[]{:S(2)}, u32[]{:S(2)}) collective-permute-start(bf16[512,128]{1,0:T(8,128)(2,1)S(1)} %get-tuple-element.8), channel_id=1, source_target_pairs={{0,2},{4,0},{8,4},{12,8},{14,12},{10,14},{6,10},{2,6},{1,3},{5,1},... | collective-permute-start | bytes 393224 | tf_op jit(solution)/shard_map/ppermute | solution.py:48
  4.9 1.9 %collective-permute-start.3 = (bf16[512,128]{1,0:T(8,128)(2,1)S(1)}, bf16[512,128]{1,0:T(8,128)(2,1)S(1)}, u32[]{:S(2)}, u32[]{:S(2)}) collective-permute-start(bf16[512,128]{1,0:T(8,128)(2,1)S(1)} %get-tuple-element.9), channel_id=1, source_target_pairs={{0,2},{4,0},{8,4},{12,8},{14,12},{10,14},{6,10},{2,6},{1,3},{5,1},... | collective-permute-start | bytes 393224 | tf_op jit(solution)/shard_map/ppermute | solution.py:48
  7.9 1.6 %shard_map.87 = bf16[512,2048]{1,0:T(8,128)(2,1)S(1)} custom-call(s32[1]{0:T(128)} %bitcast._, bf16[512,8192]{1,0:T(8,128)(2,1)} %factors_ref.5), custom_call_target="tpu_custom_call" | custom-call | bytes 2097152 | tf_op jit(solution)/shard_map/pallas_call | solution.py:172
  9.5 1.9 %shard_map.88 = bf16[512,3072]{1,0:T(8,128)(2,1)S(1)} custom-call(s32[1]{0:T(128)} %bitcast._, bf16[512,8192]{1,0:T(8,128)(2,1)} %factors_ref.5), custom_call_target="tpu_custom_call" | custom-call | bytes 3145728 | tf_op jit(solution)/shard_map/pallas_call | solution.py:172
  11.4 1.9 %shard_map.85 = bf16[512,3072]{1,0:T(8,128)(2,1)S(1)} custom-call(s32[1]{0:T(128)} %bitcast._, bf16[512,8192]{1,0:T(8,128)(2,1)} %factors_ref.5), custom_call_target="tpu_custom_call" | custom-call | bytes 3145728 | tf_op jit(solution)/shard_map/pallas_call | solution.py:172
  13.4 2.0 %collective-permute-start.6 = (bf16[512,128]{1,0:T(8,128)(2,1)S(1)}, bf16[512,128]{1,0:T(8,128)(2,1)S(1)}, u32[]{:S(2)}, u32[]{:S(2)}) collective-permute-start(bf16[512,128]{1,0:T(8,128)(2,1)S(1)} %collective-permute-done.2), channel_id=1, source_target_pairs={{0,2},{4,0},{8,4},{12,8},{14,12},{10,14},{6,10},{2,6},{1,3},{5,1},... | collective-permute-start | bytes 393224 | tf_op jit(solution)/shard_map/ppermute | solution.py:48
  15.5 1.9 %collective-permute-start.7 = (bf16[512,128]{1,0:T(8,128)(2,1)S(1)}, bf16[512,128]{1,0:T(8,128)(2,1)S(1)}, u32[]{:S(2)}, u32[]{:S(2)}) collective-permute-start(bf16[512,128]{1,0:T(8,128)(2,1)S(1)} %collective-permute-done.3), channel_id=1, source_target_pairs={{0,2},{4,0},{8,4},{12,8},{14,12},{10,14},{6,10},{2,6},{1,3},{5,1},... | collective-permute-start | bytes 393224 | tf_op jit(solution)/shard_map/ppermute | solution.py:48
  19.5 1.6 %collective-permute-start.10 = (bf16[512,128]{1,0:T(8,128)(2,1)S(1)}, bf16[512,128]{1,0:T(8,128)(2,1)S(1)}, u32[]{:S(2)}, u32[]{:S(2)}) collective-permute-start(bf16[512,128]{1,0:T(8,128)(2,1)S(1)} %collective-permute-done.6), channel_id=1, source_target_pairs={{0,2},{4,0},{8,4},{12,8},{14,12},{10,14},{6,10},{2,6},{1,3},{5,1},... | collective-permute-start | bytes 393224 | tf_op jit(solution)/shard_map/ppermute | solution.py:48
  22.3 1.6 %collective-permute-start.11 = (bf16[512,128]{1,0:T(8,128)(2,1)S(1)}, bf16[512,128]{1,0:T(8,128)(2,1)S(1)}, u32[]{:S(2)}, u32[]{:S(2)}) collective-permute-start(bf16[512,128]{1,0:T(8,128)(2,1)S(1)} %collective-permute-done.7), channel_id=1, source_target_pairs={{0,2},{4,0},{8,4},{12,8},{14,12},{10,14},{6,10},{2,6},{1,3},{5,1},... | collective-permute-start | bytes 393224 | tf_op jit(solution)/shard_map/ppermute | solution.py:48
  25.1 1.6 %collective-permute-done.8 = bf16[512,128]{1,0:T(8,128)(2,1)S(1)} collective-permute-done((bf16[512,128]{1,0:T(8,128)(2,1)S(1)}, bf16[512,128]{1,0:T(8,128)(2,1)S(1)}, u32[]{:S(2)}, u32[]{:S(2)}) %collective-permute-start.8) | collective-permute-done | bytes 131104 | tf_op jit(solution)/shard_map/ppermute | solution.py:48
  27.8 1.6 %collective-permute-start.13 = (bf16[512,128]{1,0:T(8,128)(2,1)S(1)}, bf16[512,128]{1,0:T(8,128)(2,1)S(1)}, u32[]{:S(2)}, u32[]{:S(2)}) collective-permute-start(bf16[512,128]{1,0:T(8,128)(2,1)S(1)} %collective-permute-done.11), channel_id=1, source_target_pairs={{0,2},{4,0},{8,4},{12,8},{14,12},{10,14},{6,10},{2,6},{1,3},{5,1},... | collective-permute-start | bytes 393224 | tf_op jit(solution)/shard_map/ppermute | solution.py:48
  30.2 1.5 %collective-permute-done.12 = bf16[512,128]{1,0:T(8,128)(2,1)S(1)} collective-permute-done((bf16[512,128]{1,0:T(8,128)(2,1)S(1)}, bf16[512,128]{1,0:T(8,128)(2,1)S(1)}, u32[]{:S(2)}, u32[]{:S(2)}) %collective-permute-start.12) | collective-permute-done | bytes 131104 | tf_op jit(solution)/shard_map/ppermute | solution.py:48
  31.6 1.2 collective-permute-done.13
  33.7 1.7 %collective-permute-start.14 = (bf16[512,128]{1,0:T(8,128)(2,1)S(1)}, bf16[512,128]{1,0:T(8,128)(2,1)S(1)}, u32[]{:S(2)}, u32[]{:S(2)}) collective-permute-start(bf16[512,128]{1,0:T(8,128)(2,1)S(1)} %shard_map.89), channel_id=1, source_target_pairs={{0,4},{4,8},{8,12},{12,14},{14,10},{10,6},{6,2},{2,0},{1,5},{5,9},... | collective-permute-start | bytes 393224 | tf_op jit(solution)/shard_map/ppermute | solution.py:48
  36.6 1.7 %collective-permute-start.18 = (bf16[512,128]{1,0:T(8,128)(2,1)S(1)}, bf16[512,128]{1,0:T(8,128)(2,1)S(1)}, u32[]{:S(2)}, u32[]{:S(2)}) collective-permute-start(bf16[512,128]{1,0:T(8,128)(2,1)S(1)} %shard_map.93), channel_id=1, source_target_pairs={{0,4},{4,8},{8,12},{12,14},{14,10},{10,6},{6,2},{2,0},{1,5},{5,9},... | collective-permute-start | bytes 393224 | tf_op jit(solution)/shard_map/ppermute | solution.py:48
  39.4 1.6 %collective-permute-start.15 = (bf16[512,128]{1,0:T(8,128)(2,1)S(1)}, bf16[512,128]{1,0:T(8,128)(2,1)S(1)}, u32[]{:S(2)}, u32[]{:S(2)}) collective-permute-start(bf16[512,128]{1,0:T(8,128)(2,1)S(1)} %shard_map.90), channel_id=1, source_target_pairs={{0,4},{4,8},{8,12},{12,14},{14,10},{10,6},{6,2},{2,0},{1,5},{5,9},... | collective-permute-start | bytes 393224 | tf_op jit(solution)/shard_map/ppermute | solution.py:48
  43.0 1.7 %collective-permute-start.19 = (bf16[512,128]{1,0:T(8,128)(2,1)S(1)}, bf16[512,128]{1,0:T(8,128)(2,1)S(1)}, u32[]{:S(2)}, u32[]{:S(2)}) collective-permute-start(bf16[512,128]{1,0:T(8,128)(2,1)S(1)} %shard_map.94), channel_id=1, source_target_pairs={{0,4},{4,8},{8,12},{12,14},{14,10},{10,6},{6,2},{2,0},{1,5},{5,9},... | collective-permute-start | bytes 393224 | tf_op jit(solution)/shard_map/ppermute | solution.py:48
  45.8 1.7 %collective-permute-start.16 = (bf16[512,128]{1,0:T(8,128)(2,1)S(1)}, bf16[512,128]{1,0:T(8,128)(2,1)S(1)}, u32[]{:S(2)}, u32[]{:S(2)}) collective-permute-start(bf16[512,128]{1,0:T(8,128)(2,1)S(1)} %shard_map.91), channel_id=1, source_target_pairs={{0,4},{4,8},{8,12},{12,14},{14,10},{10,6},{6,2},{2,0},{1,5},{5,9},... | collective-permute-start | bytes 393224 | tf_op jit(solution)/shard_map/ppermute | solution.py:48
  48.0 1.0 fusion.71.spread_ref
  49.3 1.6 %collective-permute-start.20 = (bf16[512,128]{1,0:T(8,128)(2,1)S(1)}, bf16[512,128]{1,0:T(8,128)(2,1)S(1)}, u32[]{:S(2)}, u32[]{:S(2)}) collective-permute-start(bf16[512,128]{1,0:T(8,128)(2,1)S(1)} %shard_map.95), channel_id=1, source_target_pairs={{0,4},{4,8},{8,12},{12,14},{14,10},{10,6},{6,2},{2,0},{1,5},{5,9},... | collective-permute-start | bytes 393224 | tf_op jit(solution)/shard_map/ppermute | solution.py:48
  51.5 1.6 %collective-permute-start.17 = (bf16[512,128]{1,0:T(8,128)(2,1)S(1)}, bf16[512,128]{1,0:T(8,128)(2,1)S(1)}, u32[]{:S(2)}, u32[]{:S(2)}) collective-permute-start(bf16[512,128]{1,0:T(8,128)(2,1)S(1)} %shard_map.92), channel_id=1, source_target_pairs={{0,4},{4,8},{8,12},{12,14},{14,10},{10,6},{6,2},{2,0},{1,5},{5,9},... | collective-permute-start | bytes 393224 | tf_op jit(solution)/shard_map/ppermute | solution.py:48
  53.7 1.7 %collective-permute-done.20.refs_1_ = bf16[512,128]{1,0:T(8,128)(2,1)S(1)} collective-permute-done((bf16[512,128]{1,0:T(8,128)(2,1)S(1)}, bf16[512,128]{1,0:T(8,128)(2,1)S(1)}, u32[]{:S(2)}, u32[]{:S(2)}) %collective-permute-start.20) | collective-permute-done | bytes 131104 | tf_op jit(solution)/shard_map/ppermute | solution.py:48
  55.4 1.5 %collective-permute-done.23.refs_2_ = bf16[512,128]{1,0:T(8,128)(2,1)S(1)} collective-permute-done((bf16[512,128]{1,0:T(8,128)(2,1)S(1)}, bf16[512,128]{1,0:T(8,128)(2,1)S(1)}, u32[]{:S(2)}, u32[]{:S(2)}) %collective-permute-start.23) | collective-permute-done | bytes 131104 | tf_op jit(solution)/shard_map/ppermute | solution.py:48
  56.9 1.3 %collective-permute-done.17.refs_0_ = bf16[512,128]{1,0:T(8,128)(2,1)S(1)} collective-permute-done((bf16[512,128]{1,0:T(8,128)(2,1)S(1)}, bf16[512,128]{1,0:T(8,128)(2,1)S(1)}, u32[]{:S(2)}, u32[]{:S(2)}) %collective-permute-start.17) | collective-permute-done | bytes 131104 | tf_op jit(solution)/shard_map/ppermute | solution.py:48
  58.2 1.5 %collective-permute-done.27.refs_3_ = bf16[512,128]{1,0:T(8,128)(2,1)S(1)} collective-permute-done((bf16[512,128]{1,0:T(8,128)(2,1)S(1)}, bf16[512,128]{1,0:T(8,128)(2,1)S(1)}, u32[]{:S(2)}, u32[]{:S(2)}) %collective-permute-start.27) | collective-permute-done | bytes 131104 | tf_op jit(solution)/shard_map/ppermute | solution.py:48
  60.8 1.2 collective-permute-start.28
  62.8 1.2 collective-permute-start.29
  64.0 2.3 %collective-permute-done.30 = bf16[512,128]{1,0:T(8,128)(2,1)S(1)} collective-permute-done((bf16[512,128]{1,0:T(8,128)(2,1)S(1)}, bf16[512,128]{1,0:T(8,128)(2,1)S(1)}, u32[]{:S(2)}, u32[]{:S(2)}) %collective-permute-start.30) | collective-permute-done | bytes 131104 | tf_op jit(solution)/shard_map/ppermute | solution.py:48
  67.1 1.2 collective-permute-start.32
  68.3 1.4 %collective-permute-start.35 = (bf16[512,128]{1,0:T(8,128)(2,1)S(1)}, bf16[512,128]{1,0:T(8,128)(2,1)S(1)}, u32[]{:S(2)}, u32[]{:S(2)}) collective-permute-start(bf16[512,128]{1,0:T(8,128)(2,1)S(1)} %collective-permute-done.31), channel_id=1, source_target_pairs={{0,2},{4,0},{8,4},{12,8},{14,12},{10,14},{6,10},{2,6},{1,3},{5,1},... | collective-permute-start | bytes 393224 | tf_op jit(solution)/shard_map/ppermute | solution.py:48
  69.9 1.0 collective-permute-start.33
  73.1 1.3 %collective-permute-start.36 = (bf16[512,128]{1,0:T(8,128)(2,1)S(1)}, bf16[512,128]{1,0:T(8,128)(2,1)S(1)}, u32[]{:S(2)}, u32[]{:S(2)}) collective-permute-start(bf16[512,128]{1,0:T(8,128)(2,1)S(1)} %collective-permute-done.32), channel_id=1, source_target_pairs={{0,4},{4,8},{8,12},{12,14},{14,10},{10,6},{6,2},{2,0},{1,5},{5,9},... | collective-permute-start | bytes 393224 | tf_op jit(solution)/shard_map/ppermute | solution.py:48
  75.2 1.3 %collective-permute-start.37 = (bf16[512,128]{1,0:T(8,128)(2,1)S(1)}, bf16[512,128]{1,0:T(8,128)(2,1)S(1)}, u32[]{:S(2)}, u32[]{:S(2)}) collective-permute-start(bf16[512,128]{1,0:T(8,128)(2,1)S(1)} %collective-permute-done.33), channel_id=1, source_target_pairs={{0,4},{4,8},{8,12},{12,14},{14,10},{10,6},{6,2},{2,0},{1,5},{5,9},... | collective-permute-start | bytes 393224 | tf_op jit(solution)/shard_map/ppermute | solution.py:48
  77.2 2.3 %collective-permute-done.36 = bf16[512,128]{1,0:T(8,128)(2,1)S(1)} collective-permute-done((bf16[512,128]{1,0:T(8,128)(2,1)S(1)}, bf16[512,128]{1,0:T(8,128)(2,1)S(1)}, u32[]{:S(2)}, u32[]{:S(2)}) %collective-permute-start.36) | collective-permute-done | bytes 131104 | tf_op jit(solution)/shard_map/ppermute | solution.py:48
  82.8 2.4 %collective-permute-done.40 = bf16[512,128]{1,0:T(8,128)(2,1)S(1)} collective-permute-done((bf16[512,128]{1,0:T(8,128)(2,1)S(1)}, bf16[512,128]{1,0:T(8,128)(2,1)S(1)}, u32[]{:S(2)}, u32[]{:S(2)}) %collective-permute-start.40) | collective-permute-done | bytes 131104 | tf_op jit(solution)/shard_map/ppermute | solution.py:48
  85.2 1.8 %collective-permute-done.41 = bf16[512,128]{1,0:T(8,128)(2,1)S(1)} collective-permute-done((bf16[512,128]{1,0:T(8,128)(2,1)S(1)}, bf16[512,128]{1,0:T(8,128)(2,1)S(1)}, u32[]{:S(2)}, u32[]{:S(2)}) %collective-permute-start.41) | collective-permute-done | bytes 131104 | tf_op jit(solution)/shard_map/ppermute | solution.py:48
  88.0 1.5 %collective-permute-start.42 = (bf16[512,128]{1,0:T(8,128)(2,1)S(1)}, bf16[512,128]{1,0:T(8,128)(2,1)S(1)}, u32[]{:S(2)}, u32[]{:S(2)}) collective-permute-start(bf16[512,128]{1,0:T(8,128)(2,1)S(1)} %shard_map.105), channel_id=1, source_target_pairs={{0,4},{4,8},{8,12},{12,14},{14,10},{10,6},{6,2},{2,0},{1,5},{5,9},... | collective-permute-start | bytes 393224 | tf_op jit(solution)/shard_map/ppermute | solution.py:48
  91.9 1.1 collective-permute-start.49
  93.3 1.8 %collective-permute-start.43 = (bf16[512,128]{1,0:T(8,128)(2,1)S(1)}, bf16[512,128]{1,0:T(8,128)(2,1)S(1)}, u32[]{:S(2)}, u32[]{:S(2)}) collective-permute-start(bf16[512,128]{1,0:T(8,128)(2,1)S(1)} %shard_map.106), channel_id=1, source_target_pairs={{0,4},{4,8},{8,12},{12,14},{14,10},{10,6},{6,2},{2,0},{1,5},{5,9},... | collective-permute-start | bytes 393224 | tf_op jit(solution)/shard_map/ppermute | solution.py:48
  97.4 1.3 %collective-permute-done.46.arrived_ref = bf16[512,128]{1,0:T(8,128)(2,1)S(1)} collective-permute-done((bf16[512,128]{1,0:T(8,128)(2,1)S(1)}, bf16[512,128]{1,0:T(8,128)(2,1)S(1)}, u32[]{:S(2)}, u32[]{:S(2)}) %collective-permute-start.46) | collective-permute-done | bytes 131104 | tf_op jit(solution)/shard_map/ppermute | solution.py:48
  99.4 1.5 %collective-permute-start.50 = (bf16[528,128]{1,0:T(8,128)(2,1)S(1)}, bf16[528,128]{1,0:T(8,128)(2,1)S(1)}, u32[]{:S(2)}, u32[]{:S(2)}) collective-permute-start(bf16[528,128]{1,0:T(8,128)(2,1)S(1)} %shard_map.116), channel_id=1, source_target_pairs={{0,4},{4,8},{8,12},{12,14},{14,10},{10,6},{6,2},{2,0},{1,5},{5,9},... | collective-permute-start | bytes 405512 | tf_op jit(solution)/shard_map/ppermute | solution.py:48
  100.9 1.8 %collective-permute-start.44 = (bf16[512,128]{1,0:T(8,128)(2,1)S(1)}, bf16[512,128]{1,0:T(8,128)(2,1)S(1)}, u32[]{:S(2)}, u32[]{:S(2)}) collective-permute-start(bf16[512,128]{1,0:T(8,128)(2,1)S(1)} %shard_map.107), channel_id=1, source_target_pairs={{0,4},{4,8},{8,12},{12,14},{14,10},{10,6},{6,2},{2,0},{1,5},{5,9},... | collective-permute-start | bytes 393224 | tf_op jit(solution)/shard_map/ppermute | solution.py:48
  103.1 1.0 fusion.74.spread_ref
  104.4 1.5 %collective-permute-start.51 = (bf16[528,128]{1,0:T(8,128)(2,1)S(1)}, bf16[528,128]{1,0:T(8,128)(2,1)S(1)}, u32[]{:S(2)}, u32[]{:S(2)}) collective-permute-start(bf16[528,128]{1,0:T(8,128)(2,1)S(1)} %shard_map.117), channel_id=1, source_target_pairs={{0,4},{4,8},{8,12},{12,14},{14,10},{10,6},{6,2},{2,0},{1,5},{5,9},... | collective-permute-start | bytes 405512 | tf_op jit(solution)/shard_map/ppermute | solution.py:48
  105.9 1.8 %collective-permute-done.54.arrived_ref.refs_4_ = bf16[528,128]{1,0:T(8,128)(2,1)S(1)} collective-permute-done((bf16[528,128]{1,0:T(8,128)(2,1)S(1)}, bf16[528,128]{1,0:T(8,128)(2,1)S(1)}, u32[]{:S(2)}, u32[]{:S(2)}) %collective-permute-start.54) | collective-permute-done | bytes 135200 | tf_op jit(solution)/shard_map/ppermute | solution.py:48
  108.8 1.5 %collective-permute-start.45 = (bf16[512,128]{1,0:T(8,128)(2,1)S(1)}, bf16[512,128]{1,0:T(8,128)(2,1)S(1)}, u32[]{:S(2)}, u32[]{:S(2)}) collective-permute-start(bf16[512,128]{1,0:T(8,128)(2,1)S(1)} %shard_map.108), channel_id=1, source_target_pairs={{0,4},{4,8},{8,12},{12,14},{14,10},{10,6},{6,2},{2,0},{1,5},{5,9},... | collective-permute-start | bytes 393224 | tf_op jit(solution)/shard_map/ppermute | solution.py:48
  110.3 3.9 %collective-permute-done.48.behind_ref = bf16[512,128]{1,0:T(8,128)(2,1)S(1)} collective-permute-done((bf16[512,128]{1,0:T(8,128)(2,1)S(1)}, bf16[512,128]{1,0:T(8,128)(2,1)S(1)}, u32[]{:S(2)}, u32[]{:S(2)}) %collective-permute-start.48) | collective-permute-done | bytes 131104 | tf_op jit(solution)/shard_map/ppermute | solution.py:48
  (153 shorter events, 38.5 us)
Async XLA Ops:
  1.7 11.7 %collective-permute-start.2 = (bf16[512,128]{1,0:T(8,128)(2,1)S(1)}, bf16[512,128]{1,0:T(8,128)(2,1)S(1)}, u32[]{:S(2)}, u32[]{:S(2)}) collective-permute-start(bf16[512,128]{1,0:T(8,128)(2,1)S(1)} %get-tuple-element.8), channel_id=1, source_target_pairs={{0,2},{4,0},{8,4},{12,8},{14,12},{10,14},{6,10},{2,6},{1,3},{5,1},... | collective-permute-start | bytes 393224 | tf_op jit(solution)/shard_map/ppermute | solution.py:48
  4.8 10.6 %collective-permute-start = (bf16[512,128]{1,0:T(8,128)(2,1)S(1)}, bf16[512,128]{1,0:T(8,128)(2,1)S(1)}, u32[]{:S(2)}, u32[]{:S(2)}) collective-permute-start(bf16[512,128]{1,0:T(8,128)(2,1)S(1)} %get-tuple-element.8), channel_id=1, source_target_pairs={{0,4},{4,8},{8,12},{12,14},{14,10},{10,6},{6,2},{2,0},{1,5},{5,9},... | collective-permute-start | bytes 393224 | tf_op jit(solution)/shard_map/ppermute | solution.py:48
  4.9 10.6 %collective-permute-start.3 = (bf16[512,128]{1,0:T(8,128)(2,1)S(1)}, bf16[512,128]{1,0:T(8,128)(2,1)S(1)}, u32[]{:S(2)}, u32[]{:S(2)}) collective-permute-start(bf16[512,128]{1,0:T(8,128)(2,1)S(1)} %get-tuple-element.9), channel_id=1, source_target_pairs={{0,2},{4,0},{8,4},{12,8},{14,12},{10,14},{6,10},{2,6},{1,3},{5,1},... | collective-permute-start | bytes 393224 | tf_op jit(solution)/shard_map/ppermute | solution.py:48
  6.8 10.6 %collective-permute-start.1 = (bf16[512,128]{1,0:T(8,128)(2,1)S(1)}, bf16[512,128]{1,0:T(8,128)(2,1)S(1)}, u32[]{:S(2)}, u32[]{:S(2)}) collective-permute-start(bf16[512,128]{1,0:T(8,128)(2,1)S(1)} %get-tuple-element.9), channel_id=1, source_target_pairs={{0,4},{4,8},{8,12},{12,14},{14,10},{10,6},{6,2},{2,0},{1,5},{5,9},... | collective-permute-start | bytes 393224 | tf_op jit(solution)/shard_map/ppermute | solution.py:48
  13.4 6.1 %collective-permute-start.6 = (bf16[512,128]{1,0:T(8,128)(2,1)S(1)}, bf16[512,128]{1,0:T(8,128)(2,1)S(1)}, u32[]{:S(2)}, u32[]{:S(2)}) collective-permute-start(bf16[512,128]{1,0:T(8,128)(2,1)S(1)} %collective-permute-done.2), channel_id=1, source_target_pairs={{0,2},{4,0},{8,4},{12,8},{14,12},{10,14},{6,10},{2,6},{1,3},{5,1},... | collective-permute-start | bytes 393224 | tf_op jit(solution)/shard_map/ppermute | solution.py:48
  15.3 5.8 %collective-permute-start.4 = (bf16[512,128]{1,0:T(8,128)(2,1)S(1)}, bf16[512,128]{1,0:T(8,128)(2,1)S(1)}, u32[]{:S(2)}, u32[]{:S(2)}) collective-permute-start(bf16[512,128]{1,0:T(8,128)(2,1)S(1)} %collective-permute-done), channel_id=1, source_target_pairs={{0,4},{4,8},{8,12},{12,14},{14,10},{10,6},{6,2},{2,0},{1,5},{5,9},... | collective-permute-start | bytes 393224 | tf_op jit(solution)/shard_map/ppermute | solution.py:48
  15.5 6.8 %collective-permute-start.7 = (bf16[512,128]{1,0:T(8,128)(2,1)S(1)}, bf16[512,128]{1,0:T(8,128)(2,1)S(1)}, u32[]{:S(2)}, u32[]{:S(2)}) collective-permute-start(bf16[512,128]{1,0:T(8,128)(2,1)S(1)} %collective-permute-done.3), channel_id=1, source_target_pairs={{0,2},{4,0},{8,4},{12,8},{14,12},{10,14},{6,10},{2,6},{1,3},{5,1},... | collective-permute-start | bytes 393224 | tf_op jit(solution)/shard_map/ppermute | solution.py:48
  17.4 6.5 %collective-permute-start.5 = (bf16[512,128]{1,0:T(8,128)(2,1)S(1)}, bf16[512,128]{1,0:T(8,128)(2,1)S(1)}, u32[]{:S(2)}, u32[]{:S(2)}) collective-permute-start(bf16[512,128]{1,0:T(8,128)(2,1)S(1)} %collective-permute-done.1), channel_id=1, source_target_pairs={{0,4},{4,8},{8,12},{12,14},{14,10},{10,6},{6,2},{2,0},{1,5},{5,9},... | collective-permute-start | bytes 393224 | tf_op jit(solution)/shard_map/ppermute | solution.py:48
  19.5 9.9 %collective-permute-start.10 = (bf16[512,128]{1,0:T(8,128)(2,1)S(1)}, bf16[512,128]{1,0:T(8,128)(2,1)S(1)}, u32[]{:S(2)}, u32[]{:S(2)}) collective-permute-start(bf16[512,128]{1,0:T(8,128)(2,1)S(1)} %collective-permute-done.6), channel_id=1, source_target_pairs={{0,2},{4,0},{8,4},{12,8},{14,12},{10,14},{6,10},{2,6},{1,3},{5,1},... | collective-permute-start | bytes 393224 | tf_op jit(solution)/shard_map/ppermute | solution.py:48
  21.1 5.6 %collective-permute-start.8 = (bf16[512,128]{1,0:T(8,128)(2,1)S(1)}, bf16[512,128]{1,0:T(8,128)(2,1)S(1)}, u32[]{:S(2)}, u32[]{:S(2)}) collective-permute-start(bf16[512,128]{1,0:T(8,128)(2,1)S(1)} %collective-permute-done.4), channel_id=1, source_target_pairs={{0,4},{4,8},{8,12},{12,14},{14,10},{10,6},{6,2},{2,0},{1,5},{5,9},... | collective-permute-start | bytes 393224 | tf_op jit(solution)/shard_map/ppermute | solution.py:48
  22.3 5.5 %collective-permute-start.11 = (bf16[512,128]{1,0:T(8,128)(2,1)S(1)}, bf16[512,128]{1,0:T(8,128)(2,1)S(1)}, u32[]{:S(2)}, u32[]{:S(2)}) collective-permute-start(bf16[512,128]{1,0:T(8,128)(2,1)S(1)} %collective-permute-done.7), channel_id=1, source_target_pairs={{0,2},{4,0},{8,4},{12,8},{14,12},{10,14},{6,10},{2,6},{1,3},{5,1},... | collective-permute-start | bytes 393224 | tf_op jit(solution)/shard_map/ppermute | solution.py:48
  23.9 5.5 %collective-permute-start.9 = (bf16[512,128]{1,0:T(8,128)(2,1)S(1)}, bf16[512,128]{1,0:T(8,128)(2,1)S(1)}, u32[]{:S(2)}, u32[]{:S(2)}) collective-permute-start(bf16[512,128]{1,0:T(8,128)(2,1)S(1)} %collective-permute-done.5), channel_id=1, source_target_pairs={{0,4},{4,8},{8,12},{12,14},{14,10},{10,6},{6,2},{2,0},{1,5},{5,9},... | collective-permute-start | bytes 393224 | tf_op jit(solution)/shard_map/ppermute | solution.py:48
  33.7 5.6 %collective-permute-start.14 = (bf16[512,128]{1,0:T(8,128)(2,1)S(1)}, bf16[512,128]{1,0:T(8,128)(2,1)S(1)}, u32[]{:S(2)}, u32[]{:S(2)}) collective-permute-start(bf16[512,128]{1,0:T(8,128)(2,1)S(1)} %shard_map.89), channel_id=1, source_target_pairs={{0,4},{4,8},{8,12},{12,14},{14,10},{10,6},{6,2},{2,0},{1,5},{5,9},... | collective-permute-start | bytes 393224 | tf_op jit(solution)/shard_map/ppermute | solution.py:48
  35.5 5.5 %collective-permute-start.24 = (bf16[512,128]{1,0:T(8,128)(2,1)S(1)}, bf16[512,128]{1,0:T(8,128)(2,1)S(1)}, u32[]{:S(2)}, u32[]{:S(2)}) collective-permute-start(bf16[512,128]{1,0:T(8,128)(2,1)S(1)} %shard_map.99), channel_id=1, source_target_pairs={{0,2},{4,0},{8,4},{12,8},{14,12},{10,14},{6,10},{2,6},{1,3},{5,1},... | collective-permute-start | bytes 393224 | tf_op jit(solution)/shard_map/ppermute | solution.py:48
  36.6 6.4 %collective-permute-start.18 = (bf16[512,128]{1,0:T(8,128)(2,1)S(1)}, bf16[512,128]{1,0:T(8,128)(2,1)S(1)}, u32[]{:S(2)}, u32[]{:S(2)}) collective-permute-start(bf16[512,128]{1,0:T(8,128)(2,1)S(1)} %shard_map.93), channel_id=1, source_target_pairs={{0,4},{4,8},{8,12},{12,14},{14,10},{10,6},{6,2},{2,0},{1,5},{5,9},... | collective-permute-start | bytes 393224 | tf_op jit(solution)/shard_map/ppermute | solution.py:48
  38.3 6.4 %collective-permute-start.21 = (bf16[512,128]{1,0:T(8,128)(2,1)S(1)}, bf16[512,128]{1,0:T(8,128)(2,1)S(1)}, u32[]{:S(2)}, u32[]{:S(2)}) collective-permute-start(bf16[512,128]{1,0:T(8,128)(2,1)S(1)} %shard_map.96), channel_id=1, source_target_pairs={{0,2},{4,0},{8,4},{12,8},{14,12},{10,14},{6,10},{2,6},{1,3},{5,1},... | collective-permute-start | bytes 393224 | tf_op jit(solution)/shard_map/ppermute | solution.py:48
  39.4 6.4 %collective-permute-start.15 = (bf16[512,128]{1,0:T(8,128)(2,1)S(1)}, bf16[512,128]{1,0:T(8,128)(2,1)S(1)}, u32[]{:S(2)}, u32[]{:S(2)}) collective-permute-start(bf16[512,128]{1,0:T(8,128)(2,1)S(1)} %shard_map.90), channel_id=1, source_target_pairs={{0,4},{4,8},{8,12},{12,14},{14,10},{10,6},{6,2},{2,0},{1,5},{5,9},... | collective-permute-start | bytes 393224 | tf_op jit(solution)/shard_map/ppermute | solution.py:48
  41.0 6.6 %collective-permute-start.25 = (bf16[512,128]{1,0:T(8,128)(2,1)S(1)}, bf16[512,128]{1,0:T(8,128)(2,1)S(1)}, u32[]{:S(2)}, u32[]{:S(2)}) collective-permute-start(bf16[512,128]{1,0:T(8,128)(2,1)S(1)} %shard_map.100), channel_id=1, source_target_pairs={{0,2},{4,0},{8,4},{12,8},{14,12},{10,14},{6,10},{2,6},{1,3},{5,1},... | collective-permute-start | bytes 393224 | tf_op jit(solution)/shard_map/ppermute | solution.py:48
  43.0 6.2 %collective-permute-start.19 = (bf16[512,128]{1,0:T(8,128)(2,1)S(1)}, bf16[512,128]{1,0:T(8,128)(2,1)S(1)}, u32[]{:S(2)}, u32[]{:S(2)}) collective-permute-start(bf16[512,128]{1,0:T(8,128)(2,1)S(1)} %shard_map.94), channel_id=1, source_target_pairs={{0,4},{4,8},{8,12},{12,14},{14,10},{10,6},{6,2},{2,0},{1,5},{5,9},... | collective-permute-start | bytes 393224 | tf_op jit(solution)/shard_map/ppermute | solution.py:48
  44.8 6.0 %collective-permute-start.22 = (bf16[512,128]{1,0:T(8,128)(2,1)S(1)}, bf16[512,128]{1,0:T(8,128)(2,1)S(1)}, u32[]{:S(2)}, u32[]{:S(2)}) collective-permute-start(bf16[512,128]{1,0:T(8,128)(2,1)S(1)} %shard_map.97), channel_id=1, source_target_pairs={{0,2},{4,0},{8,4},{12,8},{14,12},{10,14},{6,10},{2,6},{1,3},{5,1},... | collective-permute-start | bytes 393224 | tf_op jit(solution)/shard_map/ppermute | solution.py:48
  45.8 5.6 %collective-permute-start.16 = (bf16[512,128]{1,0:T(8,128)(2,1)S(1)}, bf16[512,128]{1,0:T(8,128)(2,1)S(1)}, u32[]{:S(2)}, u32[]{:S(2)}) collective-permute-start(bf16[512,128]{1,0:T(8,128)(2,1)S(1)} %shard_map.91), channel_id=1, source_target_pairs={{0,4},{4,8},{8,12},{12,14},{14,10},{10,6},{6,2},{2,0},{1,5},{5,9},... | collective-permute-start | bytes 393224 | tf_op jit(solution)/shard_map/ppermute | solution.py:48
  49.3 6.2 %collective-permute-start.20 = (bf16[512,128]{1,0:T(8,128)(2,1)S(1)}, bf16[512,128]{1,0:T(8,128)(2,1)S(1)}, u32[]{:S(2)}, u32[]{:S(2)}) collective-permute-start(bf16[512,128]{1,0:T(8,128)(2,1)S(1)} %shard_map.95), channel_id=1, source_target_pairs={{0,4},{4,8},{8,12},{12,14},{14,10},{10,6},{6,2},{2,0},{1,5},{5,9},... | collective-permute-start | bytes 393224 | tf_op jit(solution)/shard_map/ppermute | solution.py:48
  50.8 6.1 %collective-permute-start.23 = (bf16[512,128]{1,0:T(8,128)(2,1)S(1)}, bf16[512,128]{1,0:T(8,128)(2,1)S(1)}, u32[]{:S(2)}, u32[]{:S(2)}) collective-permute-start(bf16[512,128]{1,0:T(8,128)(2,1)S(1)} %shard_map.98), channel_id=1, source_target_pairs={{0,2},{4,0},{8,4},{12,8},{14,12},{10,14},{6,10},{2,6},{1,3},{5,1},... | collective-permute-start | bytes 393224 | tf_op jit(solution)/shard_map/ppermute | solution.py:48
  51.5 6.8 %collective-permute-start.17 = (bf16[512,128]{1,0:T(8,128)(2,1)S(1)}, bf16[512,128]{1,0:T(8,128)(2,1)S(1)}, u32[]{:S(2)}, u32[]{:S(2)}) collective-permute-start(bf16[512,128]{1,0:T(8,128)(2,1)S(1)} %shard_map.92), channel_id=1, source_target_pairs={{0,4},{4,8},{8,12},{12,14},{14,10},{10,6},{6,2},{2,0},{1,5},{5,9},... | collective-permute-start | bytes 393224 | tf_op jit(solution)/shard_map/ppermute | solution.py:48
  53.1 6.6 %collective-permute-start.27 = (bf16[512,128]{1,0:T(8,128)(2,1)S(1)}, bf16[512,128]{1,0:T(8,128)(2,1)S(1)}, u32[]{:S(2)}, u32[]{:S(2)}) collective-permute-start(bf16[512,128]{1,0:T(8,128)(2,1)S(1)} %shard_map.102), channel_id=1, source_target_pairs={{0,2},{4,0},{8,4},{12,8},{14,12},{10,14},{6,10},{2,6},{1,3},{5,1},... | collective-permute-start | bytes 393224 | tf_op jit(solution)/shard_map/ppermute | solution.py:48
  59.9 6.4 %collective-permute-start.30 = (bf16[512,128]{1,0:T(8,128)(2,1)S(1)}, bf16[512,128]{1,0:T(8,128)(2,1)S(1)}, u32[]{:S(2)}, u32[]{:S(2)}) collective-permute-start(bf16[512,128]{1,0:T(8,128)(2,1)S(1)} %get-tuple-element.10), channel_id=1, source_target_pairs={{0,2},{4,0},{8,4},{12,8},{14,12},{10,14},{6,10},{2,6},{1,3},{5,1},... | collective-permute-start | bytes 393224 | tf_op jit(solution)/shard_map/ppermute | solution.py:48
  60.8 6.4 %collective-permute-start.28 = (bf16[512,128]{1,0:T(8,128)(2,1)S(1)}, bf16[512,128]{1,0:T(8,128)(2,1)S(1)}, u32[]{:S(2)}, u32[]{:S(2)}) collective-permute-start(bf16[512,128]{1,0:T(8,128)(2,1)S(1)} %get-tuple-element.10), channel_id=1, source_target_pairs={{0,4},{4,8},{8,12},{12,14},{14,10},{10,6},{6,2},{2,0},{1,5},{5,9},... | collective-permute-start | bytes 393224 | tf_op jit(solution)/shard_map/ppermute | solution.py:48
  62.0 6.4 %collective-permute-start.31 = (bf16[512,128]{1,0:T(8,128)(2,1)S(1)}, bf16[512,128]{1,0:T(8,128)(2,1)S(1)}, u32[]{:S(2)}, u32[]{:S(2)}) collective-permute-start(bf16[512,128]{1,0:T(8,128)(2,1)S(1)} %get-tuple-element.11), channel_id=1, source_target_pairs={{0,2},{4,0},{8,4},{12,8},{14,12},{10,14},{6,10},{2,6},{1,3},{5,1},... | collective-permute-start | bytes 393224 | tf_op jit(solution)/shard_map/ppermute | solution.py:48
  62.8 7.1 %collective-permute-start.29 = (bf16[512,128]{1,0:T(8,128)(2,1)S(1)}, bf16[512,128]{1,0:T(8,128)(2,1)S(1)}, u32[]{:S(2)}, u32[]{:S(2)}) collective-permute-start(bf16[512,128]{1,0:T(8,128)(2,1)S(1)} %get-tuple-element.11), channel_id=1, source_target_pairs={{0,4},{4,8},{8,12},{12,14},{14,10},{10,6},{6,2},{2,0},{1,5},{5,9},... | collective-permute-start | bytes 393224 | tf_op jit(solution)/shard_map/ppermute | solution.py:48
  66.3 6.1 %collective-permute-start.34 = (bf16[512,128]{1,0:T(8,128)(2,1)S(1)}, bf16[512,128]{1,0:T(8,128)(2,1)S(1)}, u32[]{:S(2)}, u32[]{:S(2)}) collective-permute-start(bf16[512,128]{1,0:T(8,128)(2,1)S(1)} %collective-permute-done.30), channel_id=1, source_target_pairs={{0,2},{4,0},{8,4},{12,8},{14,12},{10,14},{6,10},{2,6},{1,3},{5,1},... | collective-permute-start | bytes 393224 | tf_op jit(solution)/shard_map/ppermute | solution.py:48
  67.1 6.0 %collective-permute-start.32 = (bf16[512,128]{1,0:T(8,128)(2,1)S(1)}, bf16[512,128]{1,0:T(8,128)(2,1)S(1)}, u32[]{:S(2)}, u32[]{:S(2)}) collective-permute-start(bf16[512,128]{1,0:T(8,128)(2,1)S(1)} %collective-permute-done.28), channel_id=1, source_target_pairs={{0,4},{4,8},{8,12},{12,14},{14,10},{10,6},{6,2},{2,0},{1,5},{5,9},... | collective-permute-start | bytes 393224 | tf_op jit(solution)/shard_map/ppermute | solution.py:48
  68.3 6.1 %collective-permute-start.35 = (bf16[512,128]{1,0:T(8,128)(2,1)S(1)}, bf16[512,128]{1,0:T(8,128)(2,1)S(1)}, u32[]{:S(2)}, u32[]{:S(2)}) collective-permute-start(bf16[512,128]{1,0:T(8,128)(2,1)S(1)} %collective-permute-done.31), channel_id=1, source_target_pairs={{0,2},{4,0},{8,4},{12,8},{14,12},{10,14},{6,10},{2,6},{1,3},{5,1},... | collective-permute-start | bytes 393224 | tf_op jit(solution)/shard_map/ppermute | solution.py:48
  72.4 9.1 %collective-permute-start.38 = (bf16[512,128]{1,0:T(8,128)(2,1)S(1)}, bf16[512,128]{1,0:T(8,128)(2,1)S(1)}, u32[]{:S(2)}, u32[]{:S(2)}) collective-permute-start(bf16[512,128]{1,0:T(8,128)(2,1)S(1)} %collective-permute-done.34), channel_id=1, source_target_pairs={{0,2},{4,0},{8,4},{12,8},{14,12},{10,14},{6,10},{2,6},{1,3},{5,1},... | collective-permute-start | bytes 393224 | tf_op jit(solution)/shard_map/ppermute | solution.py:48
  73.1 6.3 %collective-permute-start.36 = (bf16[512,128]{1,0:T(8,128)(2,1)S(1)}, bf16[512,128]{1,0:T(8,128)(2,1)S(1)}, u32[]{:S(2)}, u32[]{:S(2)}) collective-permute-start(bf16[512,128]{1,0:T(8,128)(2,1)S(1)} %collective-permute-done.32), channel_id=1, source_target_pairs={{0,4},{4,8},{8,12},{12,14},{14,10},{10,6},{6,2},{2,0},{1,5},{5,9},... | collective-permute-start | bytes 393224 | tf_op jit(solution)/shard_map/ppermute | solution.py:48
  74.4 6.2 %collective-permute-start.39 = (bf16[512,128]{1,0:T(8,128)(2,1)S(1)}, bf16[512,128]{1,0:T(8,128)(2,1)S(1)}, u32[]{:S(2)}, u32[]{:S(2)}) collective-permute-start(bf16[512,128]{1,0:T(8,128)(2,1)S(1)} %collective-permute-done.35), channel_id=1, source_target_pairs={{0,2},{4,0},{8,4},{12,8},{14,12},{10,14},{6,10},{2,6},{1,3},{5,1},... | collective-permute-start | bytes 393224 | tf_op jit(solution)/shard_map/ppermute | solution.py:48
  75.2 6.9 %collective-permute-start.37 = (bf16[512,128]{1,0:T(8,128)(2,1)S(1)}, bf16[512,128]{1,0:T(8,128)(2,1)S(1)}, u32[]{:S(2)}, u32[]{:S(2)}) collective-permute-start(bf16[512,128]{1,0:T(8,128)(2,1)S(1)} %collective-permute-done.33), channel_id=1, source_target_pairs={{0,4},{4,8},{8,12},{12,14},{14,10},{10,6},{6,2},{2,0},{1,5},{5,9},... | collective-permute-start | bytes 393224 | tf_op jit(solution)/shard_map/ppermute | solution.py:48
  79.4 5.7 %collective-permute-start.40 = (bf16[512,128]{1,0:T(8,128)(2,1)S(1)}, bf16[512,128]{1,0:T(8,128)(2,1)S(1)}, u32[]{:S(2)}, u32[]{:S(2)}) collective-permute-start(bf16[512,128]{1,0:T(8,128)(2,1)S(1)} %collective-permute-done.36), channel_id=1, source_target_pairs={{0,4},{4,8},{8,12},{12,14},{14,10},{10,6},{6,2},{2,0},{1,5},{5,9},... | collective-permute-start | bytes 393224 | tf_op jit(solution)/shard_map/ppermute | solution.py:48
  80.6 6.4 %collective-permute-start.41 = (bf16[512,128]{1,0:T(8,128)(2,1)S(1)}, bf16[512,128]{1,0:T(8,128)(2,1)S(1)}, u32[]{:S(2)}, u32[]{:S(2)}) collective-permute-start(bf16[512,128]{1,0:T(8,128)(2,1)S(1)} %collective-permute-done.39), channel_id=1, source_target_pairs={{0,2},{4,0},{8,4},{12,8},{14,12},{10,14},{6,10},{2,6},{1,3},{5,1},... | collective-permute-start | bytes 393224 | tf_op jit(solution)/shard_map/ppermute | solution.py:48
  89.5 6.3 %collective-permute-start.52 = (bf16[528,128]{1,0:T(8,128)(2,1)S(1)}, bf16[528,128]{1,0:T(8,128)(2,1)S(1)}, u32[]{:S(2)}, u32[]{:S(2)}) collective-permute-start(bf16[528,128]{1,0:T(8,128)(2,1)S(1)} %shard_map.118), channel_id=1, source_target_pairs={{0,2},{4,0},{8,4},{12,8},{14,12},{10,14},{6,10},{2,6},{1,3},{5,1},... | collective-permute-start | bytes 405512 | tf_op jit(solution)/shard_map/ppermute | solution.py:48
  90.9 7.8 %collective-permute-start.46 = (bf16[512,128]{1,0:T(8,128)(2,1)S(1)}, bf16[512,128]{1,0:T(8,128)(2,1)S(1)}, u32[]{:S(2)}, u32[]{:S(2)}) collective-permute-start(bf16[512,128]{1,0:T(8,128)(2,1)S(1)} %shard_map.109), channel_id=1, source_target_pairs={{0,2},{4,0},{8,4},{12,8},{14,12},{10,14},{6,10},{2,6},{1,3},{5,1},... | collective-permute-start | bytes 393224 | tf_op jit(solution)/shard_map/ppermute | solution.py:48
  91.9 7.4 %collective-permute-start.49 = (bf16[528,128]{1,0:T(8,128)(2,1)S(1)}, bf16[528,128]{1,0:T(8,128)(2,1)S(1)}, u32[]{:S(2)}, u32[]{:S(2)}) collective-permute-start(bf16[528,128]{1,0:T(8,128)(2,1)S(1)} %shard_map.115), channel_id=1, source_target_pairs={{0,4},{4,8},{8,12},{12,14},{14,10},{10,6},{6,2},{2,0},{1,5},{5,9},... | collective-permute-start | bytes 405512 | tf_op jit(solution)/shard_map/ppermute | solution.py:48
  93.3 7.5 %collective-permute-start.43 = (bf16[512,128]{1,0:T(8,128)(2,1)S(1)}, bf16[512,128]{1,0:T(8,128)(2,1)S(1)}, u32[]{:S(2)}, u32[]{:S(2)}) collective-permute-start(bf16[512,128]{1,0:T(8,128)(2,1)S(1)} %shard_map.106), channel_id=1, source_target_pairs={{0,4},{4,8},{8,12},{12,14},{14,10},{10,6},{6,2},{2,0},{1,5},{5,9},... | collective-permute-start | bytes 393224 | tf_op jit(solution)/shard_map/ppermute | solution.py:48
  95.9 6.8 %collective-permute-start.53 = (bf16[528,128]{1,0:T(8,128)(2,1)S(1)}, bf16[528,128]{1,0:T(8,128)(2,1)S(1)}, u32[]{:S(2)}, u32[]{:S(2)}) collective-permute-start(bf16[528,128]{1,0:T(8,128)(2,1)S(1)} %shard_map.119), channel_id=1, source_target_pairs={{0,2},{4,0},{8,4},{12,8},{14,12},{10,14},{6,10},{2,6},{1,3},{5,1},... | collective-permute-start | bytes 405512 | tf_op jit(solution)/shard_map/ppermute | solution.py:48
  98.7 9.5 %collective-permute-start.47 = (bf16[512,128]{1,0:T(8,128)(2,1)S(1)}, bf16[512,128]{1,0:T(8,128)(2,1)S(1)}, u32[]{:S(2)}, u32[]{:S(2)}) collective-permute-start(bf16[512,128]{1,0:T(8,128)(2,1)S(1)} %shard_map.110), channel_id=1, source_target_pairs={{0,2},{4,0},{8,4},{12,8},{14,12},{10,14},{6,10},{2,6},{1,3},{5,1},... | collective-permute-start | bytes 393224 | tf_op jit(solution)/shard_map/ppermute | solution.py:48
  100.9 7.9 %collective-permute-start.44 = (bf16[512,128]{1,0:T(8,128)(2,1)S(1)}, bf16[512,128]{1,0:T(8,128)(2,1)S(1)}, u32[]{:S(2)}, u32[]{:S(2)}) collective-permute-start(bf16[512,128]{1,0:T(8,128)(2,1)S(1)} %shard_map.107), channel_id=1, source_target_pairs={{0,4},{4,8},{8,12},{12,14},{14,10},{10,6},{6,2},{2,0},{1,5},{5,9},... | collective-permute-start | bytes 393224 | tf_op jit(solution)/shard_map/ppermute | solution.py:48
  104.4 10.0 %collective-permute-start.51 = (bf16[528,128]{1,0:T(8,128)(2,1)S(1)}, bf16[528,128]{1,0:T(8,128)(2,1)S(1)}, u32[]{:S(2)}, u32[]{:S(2)}) collective-permute-start(bf16[528,128]{1,0:T(8,128)(2,1)S(1)} %shard_map.117), channel_id=1, source_target_pairs={{0,4},{4,8},{8,12},{12,14},{14,10},{10,6},{6,2},{2,0},{1,5},{5,9},... | collective-permute-start | bytes 405512 | tf_op jit(solution)/shard_map/ppermute | solution.py:48
  107.8 6.6 %collective-permute-start.55 = (bf16[528,128]{1,0:T(8,128)(2,1)S(1)}, bf16[528,128]{1,0:T(8,128)(2,1)S(1)}, u32[]{:S(2)}, u32[]{:S(2)}) collective-permute-start(bf16[528,128]{1,0:T(8,128)(2,1)S(1)} %shard_map.121), channel_id=1, source_target_pairs={{0,2},{4,0},{8,4},{12,8},{14,12},{10,14},{6,10},{2,6},{1,3},{5,1},... | collective-permute-start | bytes 405512 | tf_op jit(solution)/shard_map/ppermute | solution.py:48
  108.2 6.1 %collective-permute-start.48 = (bf16[512,128]{1,0:T(8,128)(2,1)S(1)}, bf16[512,128]{1,0:T(8,128)(2,1)S(1)}, u32[]{:S(2)}, u32[]{:S(2)}) collective-permute-start(bf16[512,128]{1,0:T(8,128)(2,1)S(1)} %shard_map.111), channel_id=1, source_target_pairs={{0,2},{4,0},{8,4},{12,8},{14,12},{10,14},{6,10},{2,6},{1,3},{5,1},... | collective-permute-start | bytes 393224 | tf_op jit(solution)/shard_map/ppermute | solution.py:48
  (15 other events, 69.2 us)

commit v6 on v5

--- a/solution.py
+++ b/solution.py
@@ -43,9 +43,12 @@
 
 
 def hop_to(block, send, order):
-    count = len(order)
-    pairs = [(order[i], order[(i + send[1]) % count]) for i in range(count)]
-    return lax.ppermute(block, "net", pairs)
+    count, split = len(order), lax.axis_size("tm")
+    pairs = []
+    for t in range(split):
+        way = send[1] if t % 2 == 0 else -send[1]
+        pairs += [(order[i] * split + t, order[(i + way) % count] * split + t) for i in range(count)]
+    return lax.ppermute(block, ("net", "tm"), pairs)
 
 
 def by_distance(count):
@@ -151,9 +154,10 @@
 def reorder_kernel(distances, count, _, factors_ref, out_ref, sems):
     width = factors_ref.shape[1] // count
     mine = place_of(lax.axis_index("net"), count)
+    way = jnp.where(lax.axis_index("tm") % 2 == 0, 1, count - 1)
     copies = []
     for j, distance in enumerate(distances):
-        source = at_place((mine + distance) % count, count) * width
+        source = at_place((mine + way * distance) % count, count) * width
         copies.append(
             pltpu.make_async_copy(
                 factors_ref.at[:, pl.ds(pl.multiple_of(source, width), width)],

time: 119 us -> 119 us (level)
  transfers between devices with their start and end apart: 59 -> 59, of which waited for: 29 -> 31; matrix products, arithmetic and copies ran while one was open for 9% -> 9% of each run, Pallas kernels for 7% -> 7%
where the time goes in v6:
time: 119 us
  starting transfers between devices  60.4 us (51%)
  waiting for transfers between devices  33.4 us (28%)
  matrix products  11.7 us (10%)
  Pallas kernels  8.71 us (7%)
  other arithmetic  1.8 us (2%)
  local copies, waits for them, and re-layouts  1.45 us (1%)
  between operations  1.21 us (1%)
    ppermute x56, starting transfers between devices, hop_to(): return lax.ppermute(block, ('net', 'tm'), pairs)  59.7 us
    ppermute x56, waiting for transfers between devices, hop_to(): return lax.ppermute(block, ('net', 'tm'), pairs)  33.4 us
    dot_general x8, matrix products, backward(): lax.dot_general(cols, narrow, (((0,), (0,)), ((), ())), preferred_element...  5.93 us
    dot_general x8, matrix products, forward(): share = jnp.dot(cols, blocks, preferred_element_type=jnp.float32)  5.77 us
    pallas_call x3, Pallas kernels, reorder(): pl.pallas_call(functools.partial(reorder_kernel, tuple(distances), count)...  5.43 us
    pallas_call x40, Pallas kernels, small_call(): pl.pallas_call(kernel, out_shape=out_shape, in_specs=[pl.BlockSpec(memory...  3.28 us
  transfers between devices with their start and end apart: 59, of which 31 were waited for; matrix products, arithmetic and copies ran while one was open for 9% of the time, Pallas kernels for 7%

profile of v6, /device:TPU:0, one launch (start us, length us, event | category | flops | bytes accessed | tf_op | source)
XLA Modules:
  0.0 118.6 jit_solution(15712906579618430809)
XLA Ops:
  0.6 1.0 copy-done
  1.7 3.0 %collective-permute-start.2 = (bf16[512,128]{1,0:T(8,128)(2,1)S(1)}, bf16[512,128]{1,0:T(8,128)(2,1)S(1)}, u32[]{:S(2)}, u32[]{:S(2)}) collective-permute-start(bf16[512,128]{1,0:T(8,128)(2,1)S(1)} %get-tuple-element.8), channel_id=1, source_target_pairs={{0,2},{4,0},{8,4},{12,8},{14,12},{10,14},{6,10},{2,6},{1,5},{5,9},... | collective-permute-start | bytes 393224 | tf_op jit(solution)/shard_map/ppermute | solution.py:51
  4.9 1.9 %collective-permute-start.3 = (bf16[512,128]{1,0:T(8,128)(2,1)S(1)}, bf16[512,128]{1,0:T(8,128)(2,1)S(1)}, u32[]{:S(2)}, u32[]{:S(2)}) collective-permute-start(bf16[512,128]{1,0:T(8,128)(2,1)S(1)} %get-tuple-element.9), channel_id=1, source_target_pairs={{0,2},{4,0},{8,4},{12,8},{14,12},{10,14},{6,10},{2,6},{1,5},{5,9},... | collective-permute-start | bytes 393224 | tf_op jit(solution)/shard_map/ppermute | solution.py:51
  7.9 1.6 %shard_map.87 = bf16[512,2048]{1,0:T(8,128)(2,1)S(1)} custom-call(s32[1]{0:T(128)} %bitcast._, bf16[512,8192]{1,0:T(8,128)(2,1)} %factors_ref.5), custom_call_target="tpu_custom_call" | custom-call | bytes 2097152 | tf_op jit(solution)/shard_map/pallas_call | solution.py:176
  9.5 1.9 %shard_map.88 = bf16[512,3072]{1,0:T(8,128)(2,1)S(1)} custom-call(s32[1]{0:T(128)} %bitcast._, bf16[512,8192]{1,0:T(8,128)(2,1)} %factors_ref.5), custom_call_target="tpu_custom_call" | custom-call | bytes 3145728 | tf_op jit(solution)/shard_map/pallas_call | solution.py:176
  11.4 1.9 %shard_map.85 = bf16[512,3072]{1,0:T(8,128)(2,1)S(1)} custom-call(s32[1]{0:T(128)} %bitcast._, bf16[512,8192]{1,0:T(8,128)(2,1)} %factors_ref.5), custom_call_target="tpu_custom_call" | custom-call | bytes 3145728 | tf_op jit(solution)/shard_map/pallas_call | solution.py:176
  13.4 2.0 %collective-permute-start.6 = (bf16[512,128]{1,0:T(8,128)(2,1)S(1)}, bf16[512,128]{1,0:T(8,128)(2,1)S(1)}, u32[]{:S(2)}, u32[]{:S(2)}) collective-permute-start(bf16[512,128]{1,0:T(8,128)(2,1)S(1)} %collective-permute-done.2), channel_id=1, source_target_pairs={{0,2},{4,0},{8,4},{12,8},{14,12},{10,14},{6,10},{2,6},{1,5},{5,9},... | collective-permute-start | bytes 393224 | tf_op jit(solution)/shard_map/ppermute | solution.py:51
  15.5 1.9 %collective-permute-start.7 = (bf16[512,128]{1,0:T(8,128)(2,1)S(1)}, bf16[512,128]{1,0:T(8,128)(2,1)S(1)}, u32[]{:S(2)}, u32[]{:S(2)}) collective-permute-start(bf16[512,128]{1,0:T(8,128)(2,1)S(1)} %collective-permute-done.3), channel_id=1, source_target_pairs={{0,2},{4,0},{8,4},{12,8},{14,12},{10,14},{6,10},{2,6},{1,5},{5,9},... | collective-permute-start | bytes 393224 | tf_op jit(solution)/shard_map/ppermute | solution.py:51
  17.6 1.0 fusion.70
  18.6 1.2 %collective-permute-done.6 = bf16[512,128]{1,0:T(8,128)(2,1)S(1)} collective-permute-done((bf16[512,128]{1,0:T(8,128)(2,1)S(1)}, bf16[512,128]{1,0:T(8,128)(2,1)S(1)}, u32[]{:S(2)}, u32[]{:S(2)}) %collective-permute-start.6) | collective-permute-done | bytes 131104 | tf_op jit(solution)/shard_map/ppermute | solution.py:51
  19.8 1.2 %collective-permute-start.10 = (bf16[512,128]{1,0:T(8,128)(2,1)S(1)}, bf16[512,128]{1,0:T(8,128)(2,1)S(1)}, u32[]{:S(2)}, u32[]{:S(2)}) collective-permute-start(bf16[512,128]{1,0:T(8,128)(2,1)S(1)} %collective-permute-done.6), channel_id=1, source_target_pairs={{0,2},{4,0},{8,4},{12,8},{14,12},{10,14},{6,10},{2,6},{1,5},{5,9},... | collective-permute-start | bytes 393224 | tf_op jit(solution)/shard_map/ppermute | solution.py:51
  25.4 1.1 collective-permute-done.8
  27.4 1.6 %collective-permute-done.11 = bf16[512,128]{1,0:T(8,128)(2,1)S(1)} collective-permute-done((bf16[512,128]{1,0:T(8,128)(2,1)S(1)}, bf16[512,128]{1,0:T(8,128)(2,1)S(1)}, u32[]{:S(2)}, u32[]{:S(2)}) %collective-permute-start.11) | collective-permute-done | bytes 131104 | tf_op jit(solution)/shard_map/ppermute | solution.py:51
  29.0 1.1 collective-permute-start.13
  31.4 3.3 %collective-permute-done.13 = bf16[512,128]{1,0:T(8,128)(2,1)S(1)} collective-permute-done((bf16[512,128]{1,0:T(8,128)(2,1)S(1)}, bf16[512,128]{1,0:T(8,128)(2,1)S(1)}, u32[]{:S(2)}, u32[]{:S(2)}) %collective-permute-start.13) | collective-permute-done | bytes 131104 | tf_op jit(solution)/shard_map/ppermute | solution.py:51
  35.7 2.4 %collective-permute-start.14 = (bf16[512,128]{1,0:T(8,128)(2,1)S(1)}, bf16[512,128]{1,0:T(8,128)(2,1)S(1)}, u32[]{:S(2)}, u32[]{:S(2)}) collective-permute-start(bf16[512,128]{1,0:T(8,128)(2,1)S(1)} %shard_map.89), channel_id=1, source_target_pairs={{0,4},{4,8},{8,12},{12,14},{14,10},{10,6},{6,2},{2,0},{1,3},{5,1},... | collective-permute-start | bytes 393224 | tf_op jit(solution)/shard_map/ppermute | solution.py:51
  38.9 2.1 %collective-permute-start.18 = (bf16[512,128]{1,0:T(8,128)(2,1)S(1)}, bf16[512,128]{1,0:T(8,128)(2,1)S(1)}, u32[]{:S(2)}, u32[]{:S(2)}) collective-permute-start(bf16[512,128]{1,0:T(8,128)(2,1)S(1)} %shard_map.93), channel_id=1, source_target_pairs={{0,4},{4,8},{8,12},{12,14},{14,10},{10,6},{6,2},{2,0},{1,3},{5,1},... | collective-permute-start | bytes 393224 | tf_op jit(solution)/shard_map/ppermute | solution.py:51
  42.0 1.9 %collective-permute-start.15 = (bf16[512,128]{1,0:T(8,128)(2,1)S(1)}, bf16[512,128]{1,0:T(8,128)(2,1)S(1)}, u32[]{:S(2)}, u32[]{:S(2)}) collective-permute-start(bf16[512,128]{1,0:T(8,128)(2,1)S(1)} %shard_map.90), channel_id=1, source_target_pairs={{0,4},{4,8},{8,12},{12,14},{14,10},{10,6},{6,2},{2,0},{1,3},{5,1},... | collective-permute-start | bytes 393224 | tf_op jit(solution)/shard_map/ppermute | solution.py:51
  45.4 2.0 %collective-permute-start.19 = (bf16[512,128]{1,0:T(8,128)(2,1)S(1)}, bf16[512,128]{1,0:T(8,128)(2,1)S(1)}, u32[]{:S(2)}, u32[]{:S(2)}) collective-permute-start(bf16[512,128]{1,0:T(8,128)(2,1)S(1)} %shard_map.94), channel_id=1, source_target_pairs={{0,4},{4,8},{8,12},{12,14},{14,10},{10,6},{6,2},{2,0},{1,3},{5,1},... | collective-permute-start | bytes 393224 | tf_op jit(solution)/shard_map/ppermute | solution.py:51
  47.8 2.5 %collective-permute-start.16 = (bf16[512,128]{1,0:T(8,128)(2,1)S(1)}, bf16[512,128]{1,0:T(8,128)(2,1)S(1)}, u32[]{:S(2)}, u32[]{:S(2)}) collective-permute-start(bf16[512,128]{1,0:T(8,128)(2,1)S(1)} %shard_map.91), channel_id=1, source_target_pairs={{0,4},{4,8},{8,12},{12,14},{14,10},{10,6},{6,2},{2,0},{1,3},{5,1},... | collective-permute-start | bytes 393224 | tf_op jit(solution)/shard_map/ppermute | solution.py:51
  50.8 1.0 fusion.71.spread_ref
  51.9 2.1 %collective-permute-start.20 = (bf16[512,128]{1,0:T(8,128)(2,1)S(1)}, bf16[512,128]{1,0:T(8,128)(2,1)S(1)}, u32[]{:S(2)}, u32[]{:S(2)}) collective-permute-start(bf16[512,128]{1,0:T(8,128)(2,1)S(1)} %shard_map.95), channel_id=1, source_target_pairs={{0,4},{4,8},{8,12},{12,14},{14,10},{10,6},{6,2},{2,0},{1,3},{5,1},... | collective-permute-start | bytes 393224 | tf_op jit(solution)/shard_map/ppermute | solution.py:51
  54.1 2.1 %collective-permute-start.17 = (bf16[512,128]{1,0:T(8,128)(2,1)S(1)}, bf16[512,128]{1,0:T(8,128)(2,1)S(1)}, u32[]{:S(2)}, u32[]{:S(2)}) collective-permute-start(bf16[512,128]{1,0:T(8,128)(2,1)S(1)} %shard_map.92), channel_id=1, source_target_pairs={{0,4},{4,8},{8,12},{12,14},{14,10},{10,6},{6,2},{2,0},{1,3},{5,1},... | collective-permute-start | bytes 393224 | tf_op jit(solution)/shard_map/ppermute | solution.py:51
  56.7 1.6 %collective-permute-done.20.refs_1_ = bf16[512,128]{1,0:T(8,128)(2,1)S(1)} collective-permute-done((bf16[512,128]{1,0:T(8,128)(2,1)S(1)}, bf16[512,128]{1,0:T(8,128)(2,1)S(1)}, u32[]{:S(2)}, u32[]{:S(2)}) %collective-permute-start.20) | collective-permute-done | bytes 131104 | tf_op jit(solution)/shard_map/ppermute | solution.py:51
  58.3 1.9 %collective-permute-done.23.refs_2_ = bf16[512,128]{1,0:T(8,128)(2,1)S(1)} collective-permute-done((bf16[512,128]{1,0:T(8,128)(2,1)S(1)}, bf16[512,128]{1,0:T(8,128)(2,1)S(1)}, u32[]{:S(2)}, u32[]{:S(2)}) %collective-permute-start.23) | collective-permute-done | bytes 131104 | tf_op jit(solution)/shard_map/ppermute | solution.py:51
  61.1 1.9 %collective-permute-done.27.refs_3_ = bf16[512,128]{1,0:T(8,128)(2,1)S(1)} collective-permute-done((bf16[512,128]{1,0:T(8,128)(2,1)S(1)}, bf16[512,128]{1,0:T(8,128)(2,1)S(1)}, u32[]{:S(2)}, u32[]{:S(2)}) %collective-permute-start.27) | collective-permute-done | bytes 131104 | tf_op jit(solution)/shard_map/ppermute | solution.py:51
  63.2 2.0 %collective-permute-start.28 = (bf16[512,128]{1,0:T(8,128)(2,1)S(1)}, bf16[512,128]{1,0:T(8,128)(2,1)S(1)}, u32[]{:S(2)}, u32[]{:S(2)}) collective-permute-start(bf16[512,128]{1,0:T(8,128)(2,1)S(1)} %get-tuple-element.10), channel_id=1, source_target_pairs={{0,4},{4,8},{8,12},{12,14},{14,10},{10,6},{6,2},{2,0},{1,3},{5,1},... | collective-permute-start | bytes 393224 | tf_op jit(solution)/shard_map/ppermute | solution.py:51
  65.2 2.0 %collective-permute-start.29 = (bf16[512,128]{1,0:T(8,128)(2,1)S(1)}, bf16[512,128]{1,0:T(8,128)(2,1)S(1)}, u32[]{:S(2)}, u32[]{:S(2)}) collective-permute-start(bf16[512,128]{1,0:T(8,128)(2,1)S(1)} %get-tuple-element.11), channel_id=1, source_target_pairs={{0,4},{4,8},{8,12},{12,14},{14,10},{10,6},{6,2},{2,0},{1,3},{5,1},... | collective-permute-start | bytes 393224 | tf_op jit(solution)/shard_map/ppermute | solution.py:51
  67.2 1.9 %collective-permute-done.30 = bf16[512,128]{1,0:T(8,128)(2,1)S(1)} collective-permute-done((bf16[512,128]{1,0:T(8,128)(2,1)S(1)}, bf16[512,128]{1,0:T(8,128)(2,1)S(1)}, u32[]{:S(2)}, u32[]{:S(2)}) %collective-permute-start.30) | collective-permute-done | bytes 131104 | tf_op jit(solution)/shard_map/ppermute | solution.py:51
  69.5 1.7 %collective-permute-start.32 = (bf16[512,128]{1,0:T(8,128)(2,1)S(1)}, bf16[512,128]{1,0:T(8,128)(2,1)S(1)}, u32[]{:S(2)}, u32[]{:S(2)}) collective-permute-start(bf16[512,128]{1,0:T(8,128)(2,1)S(1)} %collective-permute-done.28), channel_id=1, source_target_pairs={{0,4},{4,8},{8,12},{12,14},{14,10},{10,6},{6,2},{2,0},{1,3},{5,1},... | collective-permute-start | bytes 393224 | tf_op jit(solution)/shard_map/ppermute | solution.py:51
  72.0 1.6 %collective-permute-start.33 = (bf16[512,128]{1,0:T(8,128)(2,1)S(1)}, bf16[512,128]{1,0:T(8,128)(2,1)S(1)}, u32[]{:S(2)}, u32[]{:S(2)}) collective-permute-start(bf16[512,128]{1,0:T(8,128)(2,1)S(1)} %collective-permute-done.29), channel_id=1, source_target_pairs={{0,4},{4,8},{8,12},{12,14},{14,10},{10,6},{6,2},{2,0},{1,3},{5,1},... | collective-permute-start | bytes 393224 | tf_op jit(solution)/shard_map/ppermute | solution.py:51
  76.8 1.1 collective-permute-start.39
  77.9 1.1 collective-permute-start.37
  79.7 1.7 %collective-permute-done.36 = bf16[512,128]{1,0:T(8,128)(2,1)S(1)} collective-permute-done((bf16[512,128]{1,0:T(8,128)(2,1)S(1)}, bf16[512,128]{1,0:T(8,128)(2,1)S(1)}, u32[]{:S(2)}, u32[]{:S(2)}) %collective-permute-start.36) | collective-permute-done | bytes 131104 | tf_op jit(solution)/shard_map/ppermute | solution.py:51
  81.4 1.2 %collective-permute-start.40 = (bf16[512,128]{1,0:T(8,128)(2,1)S(1)}, bf16[512,128]{1,0:T(8,128)(2,1)S(1)}, u32[]{:S(2)}, u32[]{:S(2)}) collective-permute-start(bf16[512,128]{1,0:T(8,128)(2,1)S(1)} %collective-permute-done.36), channel_id=1, source_target_pairs={{0,4},{4,8},{8,12},{12,14},{14,10},{10,6},{6,2},{2,0},{1,3},{5,1},... | collective-permute-start | bytes 393224 | tf_op jit(solution)/shard_map/ppermute | solution.py:51
  85.0 2.1 %collective-permute-done.40 = bf16[512,128]{1,0:T(8,128)(2,1)S(1)} collective-permute-done((bf16[512,128]{1,0:T(8,128)(2,1)S(1)}, bf16[512,128]{1,0:T(8,128)(2,1)S(1)}, u32[]{:S(2)}, u32[]{:S(2)}) %collective-permute-start.40) | collective-permute-done | bytes 131104 | tf_op jit(solution)/shard_map/ppermute | solution.py:51
  89.1 2.2 %collective-permute-start.42 = (bf16[512,128]{1,0:T(8,128)(2,1)S(1)}, bf16[512,128]{1,0:T(8,128)(2,1)S(1)}, u32[]{:S(2)}, u32[]{:S(2)}) collective-permute-start(bf16[512,128]{1,0:T(8,128)(2,1)S(1)} %shard_map.105), channel_id=1, source_target_pairs={{0,4},{4,8},{8,12},{12,14},{14,10},{10,6},{6,2},{2,0},{1,3},{5,1},... | collective-permute-start | bytes 393224 | tf_op jit(solution)/shard_map/ppermute | solution.py:51
  92.4 1.8 %collective-permute-start.49 = (bf16[528,128]{1,0:T(8,128)(2,1)S(1)}, bf16[528,128]{1,0:T(8,128)(2,1)S(1)}, u32[]{:S(2)}, u32[]{:S(2)}) collective-permute-start(bf16[528,128]{1,0:T(8,128)(2,1)S(1)} %shard_map.115), channel_id=1, source_target_pairs={{0,4},{4,8},{8,12},{12,14},{14,10},{10,6},{6,2},{2,0},{1,3},{5,1},... | collective-permute-start | bytes 405512 | tf_op jit(solution)/shard_map/ppermute | solution.py:51
  94.5 1.9 %collective-permute-start.43 = (bf16[512,128]{1,0:T(8,128)(2,1)S(1)}, bf16[512,128]{1,0:T(8,128)(2,1)S(1)}, u32[]{:S(2)}, u32[]{:S(2)}) collective-permute-start(bf16[512,128]{1,0:T(8,128)(2,1)S(1)} %shard_map.106), channel_id=1, source_target_pairs={{0,4},{4,8},{8,12},{12,14},{14,10},{10,6},{6,2},{2,0},{1,3},{5,1},... | collective-permute-start | bytes 393224 | tf_op jit(solution)/shard_map/ppermute | solution.py:51
  96.4 1.1 collective-permute-start.53
  99.4 1.4 %collective-permute-start.50 = (bf16[528,128]{1,0:T(8,128)(2,1)S(1)}, bf16[528,128]{1,0:T(8,128)(2,1)S(1)}, u32[]{:S(2)}, u32[]{:S(2)}) collective-permute-start(bf16[528,128]{1,0:T(8,128)(2,1)S(1)} %shard_map.116), channel_id=1, source_target_pairs={{0,4},{4,8},{8,12},{12,14},{14,10},{10,6},{6,2},{2,0},{1,3},{5,1},... | collective-permute-start | bytes 405512 | tf_op jit(solution)/shard_map/ppermute | solution.py:51
  102.3 1.3 %collective-permute-start.54 = (bf16[528,128]{1,0:T(8,128)(2,1)S(1)}, bf16[528,128]{1,0:T(8,128)(2,1)S(1)}, u32[]{:S(2)}, u32[]{:S(2)}) collective-permute-start(bf16[528,128]{1,0:T(8,128)(2,1)S(1)} %shard_map.120), channel_id=1, source_target_pairs={{0,2},{4,0},{8,4},{12,8},{14,12},{10,14},{6,10},{2,6},{1,5},{5,9},... | collective-permute-start | bytes 405512 | tf_op jit(solution)/shard_map/ppermute | solution.py:51
  103.6 1.0 fusion.74.spread_ref
  104.6 1.3 %collective-permute-start.51 = (bf16[528,128]{1,0:T(8,128)(2,1)S(1)}, bf16[528,128]{1,0:T(8,128)(2,1)S(1)}, u32[]{:S(2)}, u32[]{:S(2)}) collective-permute-start(bf16[528,128]{1,0:T(8,128)(2,1)S(1)} %shard_map.117), channel_id=1, source_target_pairs={{0,4},{4,8},{8,12},{12,14},{14,10},{10,6},{6,2},{2,0},{1,3},{5,1},... | collective-permute-start | bytes 405512 | tf_op jit(solution)/shard_map/ppermute | solution.py:51
  105.9 1.5 %collective-permute-done.54.arrived_ref.refs_4_ = bf16[528,128]{1,0:T(8,128)(2,1)S(1)} collective-permute-done((bf16[528,128]{1,0:T(8,128)(2,1)S(1)}, bf16[528,128]{1,0:T(8,128)(2,1)S(1)}, u32[]{:S(2)}, u32[]{:S(2)}) %collective-permute-start.54) | collective-permute-done | bytes 135200 | tf_op jit(solution)/shard_map/ppermute | solution.py:51
  107.4 1.3 %collective-permute-start.55 = (bf16[528,128]{1,0:T(8,128)(2,1)S(1)}, bf16[528,128]{1,0:T(8,128)(2,1)S(1)}, u32[]{:S(2)}, u32[]{:S(2)}) collective-permute-start(bf16[528,128]{1,0:T(8,128)(2,1)S(1)} %shard_map.121), channel_id=1, source_target_pairs={{0,2},{4,0},{8,4},{12,8},{14,12},{10,14},{6,10},{2,6},{1,5},{5,9},... | collective-permute-start | bytes 405512 | tf_op jit(solution)/shard_map/ppermute | solution.py:51
  109.5 1.4 %collective-permute-start.45 = (bf16[512,128]{1,0:T(8,128)(2,1)S(1)}, bf16[512,128]{1,0:T(8,128)(2,1)S(1)}, u32[]{:S(2)}, u32[]{:S(2)}) collective-permute-start(bf16[512,128]{1,0:T(8,128)(2,1)S(1)} %shard_map.108), channel_id=1, source_target_pairs={{0,4},{4,8},{8,12},{12,14},{14,10},{10,6},{6,2},{2,0},{1,3},{5,1},... | collective-permute-start | bytes 393224 | tf_op jit(solution)/shard_map/ppermute | solution.py:51
  110.9 3.0 %collective-permute-done.48.behind_ref = bf16[512,128]{1,0:T(8,128)(2,1)S(1)} collective-permute-done((bf16[512,128]{1,0:T(8,128)(2,1)S(1)}, bf16[512,128]{1,0:T(8,128)(2,1)S(1)}, u32[]{:S(2)}, u32[]{:S(2)}) %collective-permute-start.48) | collective-permute-done | bytes 131104 | tf_op jit(solution)/shard_map/ppermute | solution.py:51
  (153 shorter events, 34.8 us)
Async XLA Ops:
  1.7 11.7 %collective-permute-start.2 = (bf16[512,128]{1,0:T(8,128)(2,1)S(1)}, bf16[512,128]{1,0:T(8,128)(2,1)S(1)}, u32[]{:S(2)}, u32[]{:S(2)}) collective-permute-start(bf16[512,128]{1,0:T(8,128)(2,1)S(1)} %get-tuple-element.8), channel_id=1, source_target_pairs={{0,2},{4,0},{8,4},{12,8},{14,12},{10,14},{6,10},{2,6},{1,5},{5,9},... | collective-permute-start | bytes 393224 | tf_op jit(solution)/shard_map/ppermute | solution.py:51
  4.8 10.6 %collective-permute-start = (bf16[512,128]{1,0:T(8,128)(2,1)S(1)}, bf16[512,128]{1,0:T(8,128)(2,1)S(1)}, u32[]{:S(2)}, u32[]{:S(2)}) collective-permute-start(bf16[512,128]{1,0:T(8,128)(2,1)S(1)} %get-tuple-element.8), channel_id=1, source_target_pairs={{0,4},{4,8},{8,12},{12,14},{14,10},{10,6},{6,2},{2,0},{1,3},{5,1},... | collective-permute-start | bytes 393224 | tf_op jit(solution)/shard_map/ppermute | solution.py:51
  4.9 10.6 %collective-permute-start.3 = (bf16[512,128]{1,0:T(8,128)(2,1)S(1)}, bf16[512,128]{1,0:T(8,128)(2,1)S(1)}, u32[]{:S(2)}, u32[]{:S(2)}) collective-permute-start(bf16[512,128]{1,0:T(8,128)(2,1)S(1)} %get-tuple-element.9), channel_id=1, source_target_pairs={{0,2},{4,0},{8,4},{12,8},{14,12},{10,14},{6,10},{2,6},{1,5},{5,9},... | collective-permute-start | bytes 393224 | tf_op jit(solution)/shard_map/ppermute | solution.py:51
  6.8 10.6 %collective-permute-start.1 = (bf16[512,128]{1,0:T(8,128)(2,1)S(1)}, bf16[512,128]{1,0:T(8,128)(2,1)S(1)}, u32[]{:S(2)}, u32[]{:S(2)}) collective-permute-start(bf16[512,128]{1,0:T(8,128)(2,1)S(1)} %get-tuple-element.9), channel_id=1, source_target_pairs={{0,4},{4,8},{8,12},{12,14},{14,10},{10,6},{6,2},{2,0},{1,3},{5,1},... | collective-permute-start | bytes 393224 | tf_op jit(solution)/shard_map/ppermute | solution.py:51
  13.4 6.4 %collective-permute-start.6 = (bf16[512,128]{1,0:T(8,128)(2,1)S(1)}, bf16[512,128]{1,0:T(8,128)(2,1)S(1)}, u32[]{:S(2)}, u32[]{:S(2)}) collective-permute-start(bf16[512,128]{1,0:T(8,128)(2,1)S(1)} %collective-permute-done.2), channel_id=1, source_target_pairs={{0,2},{4,0},{8,4},{12,8},{14,12},{10,14},{6,10},{2,6},{1,5},{5,9},... | collective-permute-start | bytes 393224 | tf_op jit(solution)/shard_map/ppermute | solution.py:51
  15.3 6.2 %collective-permute-start.4 = (bf16[512,128]{1,0:T(8,128)(2,1)S(1)}, bf16[512,128]{1,0:T(8,128)(2,1)S(1)}, u32[]{:S(2)}, u32[]{:S(2)}) collective-permute-start(bf16[512,128]{1,0:T(8,128)(2,1)S(1)} %collective-permute-done), channel_id=1, source_target_pairs={{0,4},{4,8},{8,12},{12,14},{14,10},{10,6},{6,2},{2,0},{1,3},{5,1},... | collective-permute-start | bytes 393224 | tf_op jit(solution)/shard_map/ppermute | solution.py:51
  15.5 7.1 %collective-permute-start.7 = (bf16[512,128]{1,0:T(8,128)(2,1)S(1)}, bf16[512,128]{1,0:T(8,128)(2,1)S(1)}, u32[]{:S(2)}, u32[]{:S(2)}) collective-permute-start(bf16[512,128]{1,0:T(8,128)(2,1)S(1)} %collective-permute-done.3), channel_id=1, source_target_pairs={{0,2},{4,0},{8,4},{12,8},{14,12},{10,14},{6,10},{2,6},{1,5},{5,9},... | collective-permute-start | bytes 393224 | tf_op jit(solution)/shard_map/ppermute | solution.py:51
  17.4 6.9 %collective-permute-start.5 = (bf16[512,128]{1,0:T(8,128)(2,1)S(1)}, bf16[512,128]{1,0:T(8,128)(2,1)S(1)}, u32[]{:S(2)}, u32[]{:S(2)}) collective-permute-start(bf16[512,128]{1,0:T(8,128)(2,1)S(1)} %collective-permute-done.1), channel_id=1, source_target_pairs={{0,4},{4,8},{8,12},{12,14},{14,10},{10,6},{6,2},{2,0},{1,3},{5,1},... | collective-permute-start | bytes 393224 | tf_op jit(solution)/shard_map/ppermute | solution.py:51
  19.8 10.3 %collective-permute-start.10 = (bf16[512,128]{1,0:T(8,128)(2,1)S(1)}, bf16[512,128]{1,0:T(8,128)(2,1)S(1)}, u32[]{:S(2)}, u32[]{:S(2)}) collective-permute-start(bf16[512,128]{1,0:T(8,128)(2,1)S(1)} %collective-permute-done.6), channel_id=1, source_target_pairs={{0,2},{4,0},{8,4},{12,8},{14,12},{10,14},{6,10},{2,6},{1,5},{5,9},... | collective-permute-start | bytes 393224 | tf_op jit(solution)/shard_map/ppermute | solution.py:51
  22.6 6.4 %collective-permute-start.11 = (bf16[512,128]{1,0:T(8,128)(2,1)S(1)}, bf16[512,128]{1,0:T(8,128)(2,1)S(1)}, u32[]{:S(2)}, u32[]{:S(2)}) collective-permute-start(bf16[512,128]{1,0:T(8,128)(2,1)S(1)} %collective-permute-done.7), channel_id=1, source_target_pairs={{0,2},{4,0},{8,4},{12,8},{14,12},{10,14},{6,10},{2,6},{1,5},{5,9},... | collective-permute-start | bytes 393224 | tf_op jit(solution)/shard_map/ppermute | solution.py:51
  24.3 5.8 %collective-permute-start.9 = (bf16[512,128]{1,0:T(8,128)(2,1)S(1)}, bf16[512,128]{1,0:T(8,128)(2,1)S(1)}, u32[]{:S(2)}, u32[]{:S(2)}) collective-permute-start(bf16[512,128]{1,0:T(8,128)(2,1)S(1)} %collective-permute-done.5), channel_id=1, source_target_pairs={{0,4},{4,8},{8,12},{12,14},{14,10},{10,6},{6,2},{2,0},{1,3},{5,1},... | collective-permute-start | bytes 393224 | tf_op jit(solution)/shard_map/ppermute | solution.py:51
  29.0 5.8 %collective-permute-start.13 = (bf16[512,128]{1,0:T(8,128)(2,1)S(1)}, bf16[512,128]{1,0:T(8,128)(2,1)S(1)}, u32[]{:S(2)}, u32[]{:S(2)}) collective-permute-start(bf16[512,128]{1,0:T(8,128)(2,1)S(1)} %collective-permute-done.11), channel_id=1, source_target_pairs={{0,2},{4,0},{8,4},{12,8},{14,12},{10,14},{6,10},{2,6},{1,5},{5,9},... | collective-permute-start | bytes 393224 | tf_op jit(solution)/shard_map/ppermute | solution.py:51
  35.7 6.2 %collective-permute-start.14 = (bf16[512,128]{1,0:T(8,128)(2,1)S(1)}, bf16[512,128]{1,0:T(8,128)(2,1)S(1)}, u32[]{:S(2)}, u32[]{:S(2)}) collective-permute-start(bf16[512,128]{1,0:T(8,128)(2,1)S(1)} %shard_map.89), channel_id=1, source_target_pairs={{0,4},{4,8},{8,12},{12,14},{14,10},{10,6},{6,2},{2,0},{1,3},{5,1},... | collective-permute-start | bytes 393224 | tf_op jit(solution)/shard_map/ppermute | solution.py:51
  38.1 6.3 %collective-permute-start.24 = (bf16[512,128]{1,0:T(8,128)(2,1)S(1)}, bf16[512,128]{1,0:T(8,128)(2,1)S(1)}, u32[]{:S(2)}, u32[]{:S(2)}) collective-permute-start(bf16[512,128]{1,0:T(8,128)(2,1)S(1)} %shard_map.99), channel_id=1, source_target_pairs={{0,2},{4,0},{8,4},{12,8},{14,12},{10,14},{6,10},{2,6},{1,5},{5,9},... | collective-permute-start | bytes 393224 | tf_op jit(solution)/shard_map/ppermute | solution.py:51
  38.9 6.4 %collective-permute-start.18 = (bf16[512,128]{1,0:T(8,128)(2,1)S(1)}, bf16[512,128]{1,0:T(8,128)(2,1)S(1)}, u32[]{:S(2)}, u32[]{:S(2)}) collective-permute-start(bf16[512,128]{1,0:T(8,128)(2,1)S(1)} %shard_map.93), channel_id=1, source_target_pairs={{0,4},{4,8},{8,12},{12,14},{14,10},{10,6},{6,2},{2,0},{1,3},{5,1},... | collective-permute-start | bytes 393224 | tf_op jit(solution)/shard_map/ppermute | solution.py:51
  41.0 6.4 %collective-permute-start.21 = (bf16[512,128]{1,0:T(8,128)(2,1)S(1)}, bf16[512,128]{1,0:T(8,128)(2,1)S(1)}, u32[]{:S(2)}, u32[]{:S(2)}) collective-permute-start(bf16[512,128]{1,0:T(8,128)(2,1)S(1)} %shard_map.96), channel_id=1, source_target_pairs={{0,2},{4,0},{8,4},{12,8},{14,12},{10,14},{6,10},{2,6},{1,5},{5,9},... | collective-permute-start | bytes 393224 | tf_op jit(solution)/shard_map/ppermute | solution.py:51
  42.0 5.7 %collective-permute-start.15 = (bf16[512,128]{1,0:T(8,128)(2,1)S(1)}, bf16[512,128]{1,0:T(8,128)(2,1)S(1)}, u32[]{:S(2)}, u32[]{:S(2)}) collective-permute-start(bf16[512,128]{1,0:T(8,128)(2,1)S(1)} %shard_map.90), channel_id=1, source_target_pairs={{0,4},{4,8},{8,12},{12,14},{14,10},{10,6},{6,2},{2,0},{1,3},{5,1},... | collective-permute-start | bytes 393224 | tf_op jit(solution)/shard_map/ppermute | solution.py:51
  44.5 6.3 %collective-permute-start.25 = (bf16[512,128]{1,0:T(8,128)(2,1)S(1)}, bf16[512,128]{1,0:T(8,128)(2,1)S(1)}, u32[]{:S(2)}, u32[]{:S(2)}) collective-permute-start(bf16[512,128]{1,0:T(8,128)(2,1)S(1)} %shard_map.100), channel_id=1, source_target_pairs={{0,2},{4,0},{8,4},{12,8},{14,12},{10,14},{6,10},{2,6},{1,5},{5,9},... | collective-permute-start | bytes 393224 | tf_op jit(solution)/shard_map/ppermute | solution.py:51
  45.4 6.4 %collective-permute-start.19 = (bf16[512,128]{1,0:T(8,128)(2,1)S(1)}, bf16[512,128]{1,0:T(8,128)(2,1)S(1)}, u32[]{:S(2)}, u32[]{:S(2)}) collective-permute-start(bf16[512,128]{1,0:T(8,128)(2,1)S(1)} %shard_map.94), channel_id=1, source_target_pairs={{0,4},{4,8},{8,12},{12,14},{14,10},{10,6},{6,2},{2,0},{1,3},{5,1},... | collective-permute-start | bytes 393224 | tf_op jit(solution)/shard_map/ppermute | solution.py:51
  47.5 6.5 %collective-permute-start.22 = (bf16[512,128]{1,0:T(8,128)(2,1)S(1)}, bf16[512,128]{1,0:T(8,128)(2,1)S(1)}, u32[]{:S(2)}, u32[]{:S(2)}) collective-permute-start(bf16[512,128]{1,0:T(8,128)(2,1)S(1)} %shard_map.97), channel_id=1, source_target_pairs={{0,2},{4,0},{8,4},{12,8},{14,12},{10,14},{6,10},{2,6},{1,5},{5,9},... | collective-permute-start | bytes 393224 | tf_op jit(solution)/shard_map/ppermute | solution.py:51
  47.8 6.3 %collective-permute-start.16 = (bf16[512,128]{1,0:T(8,128)(2,1)S(1)}, bf16[512,128]{1,0:T(8,128)(2,1)S(1)}, u32[]{:S(2)}, u32[]{:S(2)}) collective-permute-start(bf16[512,128]{1,0:T(8,128)(2,1)S(1)} %shard_map.91), channel_id=1, source_target_pairs={{0,4},{4,8},{8,12},{12,14},{14,10},{10,6},{6,2},{2,0},{1,3},{5,1},... | collective-permute-start | bytes 393224 | tf_op jit(solution)/shard_map/ppermute | solution.py:51
  50.7 5.8 %collective-permute-start.26 = (bf16[512,128]{1,0:T(8,128)(2,1)S(1)}, bf16[512,128]{1,0:T(8,128)(2,1)S(1)}, u32[]{:S(2)}, u32[]{:S(2)}) collective-permute-start(bf16[512,128]{1,0:T(8,128)(2,1)S(1)} %shard_map.101), channel_id=1, source_target_pairs={{0,2},{4,0},{8,4},{12,8},{14,12},{10,14},{6,10},{2,6},{1,5},{5,9},... | collective-permute-start | bytes 393224 | tf_op jit(solution)/shard_map/ppermute | solution.py:51
  51.9 6.4 %collective-permute-start.20 = (bf16[512,128]{1,0:T(8,128)(2,1)S(1)}, bf16[512,128]{1,0:T(8,128)(2,1)S(1)}, u32[]{:S(2)}, u32[]{:S(2)}) collective-permute-start(bf16[512,128]{1,0:T(8,128)(2,1)S(1)} %shard_map.95), channel_id=1, source_target_pairs={{0,4},{4,8},{8,12},{12,14},{14,10},{10,6},{6,2},{2,0},{1,3},{5,1},... | collective-permute-start | bytes 393224 | tf_op jit(solution)/shard_map/ppermute | solution.py:51
  54.0 6.2 %collective-permute-start.23 = (bf16[512,128]{1,0:T(8,128)(2,1)S(1)}, bf16[512,128]{1,0:T(8,128)(2,1)S(1)}, u32[]{:S(2)}, u32[]{:S(2)}) collective-permute-start(bf16[512,128]{1,0:T(8,128)(2,1)S(1)} %shard_map.98), channel_id=1, source_target_pairs={{0,2},{4,0},{8,4},{12,8},{14,12},{10,14},{6,10},{2,6},{1,5},{5,9},... | collective-permute-start | bytes 393224 | tf_op jit(solution)/shard_map/ppermute | solution.py:51
  54.1 7.0 %collective-permute-start.17 = (bf16[512,128]{1,0:T(8,128)(2,1)S(1)}, bf16[512,128]{1,0:T(8,128)(2,1)S(1)}, u32[]{:S(2)}, u32[]{:S(2)}) collective-permute-start(bf16[512,128]{1,0:T(8,128)(2,1)S(1)} %shard_map.92), channel_id=1, source_target_pairs={{0,4},{4,8},{8,12},{12,14},{14,10},{10,6},{6,2},{2,0},{1,3},{5,1},... | collective-permute-start | bytes 393224 | tf_op jit(solution)/shard_map/ppermute | solution.py:51
  56.5 6.5 %collective-permute-start.27 = (bf16[512,128]{1,0:T(8,128)(2,1)S(1)}, bf16[512,128]{1,0:T(8,128)(2,1)S(1)}, u32[]{:S(2)}, u32[]{:S(2)}) collective-permute-start(bf16[512,128]{1,0:T(8,128)(2,1)S(1)} %shard_map.102), channel_id=1, source_target_pairs={{0,2},{4,0},{8,4},{12,8},{14,12},{10,14},{6,10},{2,6},{1,5},{5,9},... | collective-permute-start | bytes 393224 | tf_op jit(solution)/shard_map/ppermute | solution.py:51
  63.1 6.1 %collective-permute-start.30 = (bf16[512,128]{1,0:T(8,128)(2,1)S(1)}, bf16[512,128]{1,0:T(8,128)(2,1)S(1)}, u32[]{:S(2)}, u32[]{:S(2)}) collective-permute-start(bf16[512,128]{1,0:T(8,128)(2,1)S(1)} %get-tuple-element.10), channel_id=1, source_target_pairs={{0,2},{4,0},{8,4},{12,8},{14,12},{10,14},{6,10},{2,6},{1,5},{5,9},... | collective-permute-start | bytes 393224 | tf_op jit(solution)/shard_map/ppermute | solution.py:51
  63.2 6.4 %collective-permute-start.28 = (bf16[512,128]{1,0:T(8,128)(2,1)S(1)}, bf16[512,128]{1,0:T(8,128)(2,1)S(1)}, u32[]{:S(2)}, u32[]{:S(2)}) collective-permute-start(bf16[512,128]{1,0:T(8,128)(2,1)S(1)} %get-tuple-element.10), channel_id=1, source_target_pairs={{0,4},{4,8},{8,12},{12,14},{14,10},{10,6},{6,2},{2,0},{1,3},{5,1},... | collective-permute-start | bytes 393224 | tf_op jit(solution)/shard_map/ppermute | solution.py:51
  65.2 6.1 %collective-permute-start.31 = (bf16[512,128]{1,0:T(8,128)(2,1)S(1)}, bf16[512,128]{1,0:T(8,128)(2,1)S(1)}, u32[]{:S(2)}, u32[]{:S(2)}) collective-permute-start(bf16[512,128]{1,0:T(8,128)(2,1)S(1)} %get-tuple-element.11), channel_id=1, source_target_pairs={{0,2},{4,0},{8,4},{12,8},{14,12},{10,14},{6,10},{2,6},{1,5},{5,9},... | collective-permute-start | bytes 393224 | tf_op jit(solution)/shard_map/ppermute | solution.py:51
  65.2 6.7 %collective-permute-start.29 = (bf16[512,128]{1,0:T(8,128)(2,1)S(1)}, bf16[512,128]{1,0:T(8,128)(2,1)S(1)}, u32[]{:S(2)}, u32[]{:S(2)}) collective-permute-start(bf16[512,128]{1,0:T(8,128)(2,1)S(1)} %get-tuple-element.11), channel_id=1, source_target_pairs={{0,4},{4,8},{8,12},{12,14},{14,10},{10,6},{6,2},{2,0},{1,3},{5,1},... | collective-permute-start | bytes 393224 | tf_op jit(solution)/shard_map/ppermute | solution.py:51
  69.2 5.5 %collective-permute-start.34 = (bf16[512,128]{1,0:T(8,128)(2,1)S(1)}, bf16[512,128]{1,0:T(8,128)(2,1)S(1)}, u32[]{:S(2)}, u32[]{:S(2)}) collective-permute-start(bf16[512,128]{1,0:T(8,128)(2,1)S(1)} %collective-permute-done.30), channel_id=1, source_target_pairs={{0,2},{4,0},{8,4},{12,8},{14,12},{10,14},{6,10},{2,6},{1,5},{5,9},... | collective-permute-start | bytes 393224 | tf_op jit(solution)/shard_map/ppermute | solution.py:51
  69.5 6.3 %collective-permute-start.32 = (bf16[512,128]{1,0:T(8,128)(2,1)S(1)}, bf16[512,128]{1,0:T(8,128)(2,1)S(1)}, u32[]{:S(2)}, u32[]{:S(2)}) collective-permute-start(bf16[512,128]{1,0:T(8,128)(2,1)S(1)} %collective-permute-done.28), channel_id=1, source_target_pairs={{0,4},{4,8},{8,12},{12,14},{14,10},{10,6},{6,2},{2,0},{1,3},{5,1},... | collective-permute-start | bytes 393224 | tf_op jit(solution)/shard_map/ppermute | solution.py:51
  71.2 5.6 %collective-permute-start.35 = (bf16[512,128]{1,0:T(8,128)(2,1)S(1)}, bf16[512,128]{1,0:T(8,128)(2,1)S(1)}, u32[]{:S(2)}, u32[]{:S(2)}) collective-permute-start(bf16[512,128]{1,0:T(8,128)(2,1)S(1)} %collective-permute-done.31), channel_id=1, source_target_pairs={{0,2},{4,0},{8,4},{12,8},{14,12},{10,14},{6,10},{2,6},{1,5},{5,9},... | collective-permute-start | bytes 393224 | tf_op jit(solution)/shard_map/ppermute | solution.py:51
  72.0 6.0 %collective-permute-start.33 = (bf16[512,128]{1,0:T(8,128)(2,1)S(1)}, bf16[512,128]{1,0:T(8,128)(2,1)S(1)}, u32[]{:S(2)}, u32[]{:S(2)}) collective-permute-start(bf16[512,128]{1,0:T(8,128)(2,1)S(1)} %collective-permute-done.29), channel_id=1, source_target_pairs={{0,4},{4,8},{8,12},{12,14},{14,10},{10,6},{6,2},{2,0},{1,3},{5,1},... | collective-permute-start | bytes 393224 | tf_op jit(solution)/shard_map/ppermute | solution.py:51
  74.7 8.8 %collective-permute-start.38 = (bf16[512,128]{1,0:T(8,128)(2,1)S(1)}, bf16[512,128]{1,0:T(8,128)(2,1)S(1)}, u32[]{:S(2)}, u32[]{:S(2)}) collective-permute-start(bf16[512,128]{1,0:T(8,128)(2,1)S(1)} %collective-permute-done.34), channel_id=1, source_target_pairs={{0,2},{4,0},{8,4},{12,8},{14,12},{10,14},{6,10},{2,6},{1,5},{5,9},... | collective-permute-start | bytes 393224 | tf_op jit(solution)/shard_map/ppermute | solution.py:51
  75.9 5.6 %collective-permute-start.36 = (bf16[512,128]{1,0:T(8,128)(2,1)S(1)}, bf16[512,128]{1,0:T(8,128)(2,1)S(1)}, u32[]{:S(2)}, u32[]{:S(2)}) collective-permute-start(bf16[512,128]{1,0:T(8,128)(2,1)S(1)} %collective-permute-done.32), channel_id=1, source_target_pairs={{0,4},{4,8},{8,12},{12,14},{14,10},{10,6},{6,2},{2,0},{1,3},{5,1},... | collective-permute-start | bytes 393224 | tf_op jit(solution)/shard_map/ppermute | solution.py:51
  76.8 6.2 %collective-permute-start.39 = (bf16[512,128]{1,0:T(8,128)(2,1)S(1)}, bf16[512,128]{1,0:T(8,128)(2,1)S(1)}, u32[]{:S(2)}, u32[]{:S(2)}) collective-permute-start(bf16[512,128]{1,0:T(8,128)(2,1)S(1)} %collective-permute-done.35), channel_id=1, source_target_pairs={{0,2},{4,0},{8,4},{12,8},{14,12},{10,14},{6,10},{2,6},{1,5},{5,9},... | collective-permute-start | bytes 393224 | tf_op jit(solution)/shard_map/ppermute | solution.py:51
  77.9 6.4 %collective-permute-start.37 = (bf16[512,128]{1,0:T(8,128)(2,1)S(1)}, bf16[512,128]{1,0:T(8,128)(2,1)S(1)}, u32[]{:S(2)}, u32[]{:S(2)}) collective-permute-start(bf16[512,128]{1,0:T(8,128)(2,1)S(1)} %collective-permute-done.33), channel_id=1, source_target_pairs={{0,4},{4,8},{8,12},{12,14},{14,10},{10,6},{6,2},{2,0},{1,3},{5,1},... | collective-permute-start | bytes 393224 | tf_op jit(solution)/shard_map/ppermute | solution.py:51
  81.4 5.7 %collective-permute-start.40 = (bf16[512,128]{1,0:T(8,128)(2,1)S(1)}, bf16[512,128]{1,0:T(8,128)(2,1)S(1)}, u32[]{:S(2)}, u32[]{:S(2)}) collective-permute-start(bf16[512,128]{1,0:T(8,128)(2,1)S(1)} %collective-permute-done.36), channel_id=1, source_target_pairs={{0,4},{4,8},{8,12},{12,14},{14,10},{10,6},{6,2},{2,0},{1,3},{5,1},... | collective-permute-start | bytes 393224 | tf_op jit(solution)/shard_map/ppermute | solution.py:51
  89.1 5.3 %collective-permute-start.42 = (bf16[512,128]{1,0:T(8,128)(2,1)S(1)}, bf16[512,128]{1,0:T(8,128)(2,1)S(1)}, u32[]{:S(2)}, u32[]{:S(2)}) collective-permute-start(bf16[512,128]{1,0:T(8,128)(2,1)S(1)} %shard_map.105), channel_id=1, source_target_pairs={{0,4},{4,8},{8,12},{12,14},{14,10},{10,6},{6,2},{2,0},{1,3},{5,1},... | collective-permute-start | bytes 393224 | tf_op jit(solution)/shard_map/ppermute | solution.py:51
  92.1 6.4 %collective-permute-start.46 = (bf16[512,128]{1,0:T(8,128)(2,1)S(1)}, bf16[512,128]{1,0:T(8,128)(2,1)S(1)}, u32[]{:S(2)}, u32[]{:S(2)}) collective-permute-start(bf16[512,128]{1,0:T(8,128)(2,1)S(1)} %shard_map.109), channel_id=1, source_target_pairs={{0,2},{4,0},{8,4},{12,8},{14,12},{10,14},{6,10},{2,6},{1,5},{5,9},... | collective-permute-start | bytes 393224 | tf_op jit(solution)/shard_map/ppermute | solution.py:51
  92.4 7.0 %collective-permute-start.49 = (bf16[528,128]{1,0:T(8,128)(2,1)S(1)}, bf16[528,128]{1,0:T(8,128)(2,1)S(1)}, u32[]{:S(2)}, u32[]{:S(2)}) collective-permute-start(bf16[528,128]{1,0:T(8,128)(2,1)S(1)} %shard_map.115), channel_id=1, source_target_pairs={{0,4},{4,8},{8,12},{12,14},{14,10},{10,6},{6,2},{2,0},{1,3},{5,1},... | collective-permute-start | bytes 405512 | tf_op jit(solution)/shard_map/ppermute | solution.py:51
  94.5 6.8 %collective-permute-start.43 = (bf16[512,128]{1,0:T(8,128)(2,1)S(1)}, bf16[512,128]{1,0:T(8,128)(2,1)S(1)}, u32[]{:S(2)}, u32[]{:S(2)}) collective-permute-start(bf16[512,128]{1,0:T(8,128)(2,1)S(1)} %shard_map.106), channel_id=1, source_target_pairs={{0,4},{4,8},{8,12},{12,14},{14,10},{10,6},{6,2},{2,0},{1,3},{5,1},... | collective-permute-start | bytes 393224 | tf_op jit(solution)/shard_map/ppermute | solution.py:51
  96.4 5.8 %collective-permute-start.53 = (bf16[528,128]{1,0:T(8,128)(2,1)S(1)}, bf16[528,128]{1,0:T(8,128)(2,1)S(1)}, u32[]{:S(2)}, u32[]{:S(2)}) collective-permute-start(bf16[528,128]{1,0:T(8,128)(2,1)S(1)} %shard_map.119), channel_id=1, source_target_pairs={{0,2},{4,0},{8,4},{12,8},{14,12},{10,14},{6,10},{2,6},{1,5},{5,9},... | collective-permute-start | bytes 405512 | tf_op jit(solution)/shard_map/ppermute | solution.py:51
  98.5 10.1 %collective-permute-start.47 = (bf16[512,128]{1,0:T(8,128)(2,1)S(1)}, bf16[512,128]{1,0:T(8,128)(2,1)S(1)}, u32[]{:S(2)}, u32[]{:S(2)}) collective-permute-start(bf16[512,128]{1,0:T(8,128)(2,1)S(1)} %shard_map.110), channel_id=1, source_target_pairs={{0,2},{4,0},{8,4},{12,8},{14,12},{10,14},{6,10},{2,6},{1,5},{5,9},... | collective-permute-start | bytes 393224 | tf_op jit(solution)/shard_map/ppermute | solution.py:51
  101.4 8.0 %collective-permute-start.44 = (bf16[512,128]{1,0:T(8,128)(2,1)S(1)}, bf16[512,128]{1,0:T(8,128)(2,1)S(1)}, u32[]{:S(2)}, u32[]{:S(2)}) collective-permute-start(bf16[512,128]{1,0:T(8,128)(2,1)S(1)} %shard_map.107), channel_id=1, source_target_pairs={{0,4},{4,8},{8,12},{12,14},{14,10},{10,6},{6,2},{2,0},{1,3},{5,1},... | collective-permute-start | bytes 393224 | tf_op jit(solution)/shard_map/ppermute | solution.py:51
  104.6 10.0 %collective-permute-start.51 = (bf16[528,128]{1,0:T(8,128)(2,1)S(1)}, bf16[528,128]{1,0:T(8,128)(2,1)S(1)}, u32[]{:S(2)}, u32[]{:S(2)}) collective-permute-start(bf16[528,128]{1,0:T(8,128)(2,1)S(1)} %shard_map.117), channel_id=1, source_target_pairs={{0,4},{4,8},{8,12},{12,14},{14,10},{10,6},{6,2},{2,0},{1,3},{5,1},... | collective-permute-start | bytes 405512 | tf_op jit(solution)/shard_map/ppermute | solution.py:51
  107.4 7.3 %collective-permute-start.55 = (bf16[528,128]{1,0:T(8,128)(2,1)S(1)}, bf16[528,128]{1,0:T(8,128)(2,1)S(1)}, u32[]{:S(2)}, u32[]{:S(2)}) collective-permute-start(bf16[528,128]{1,0:T(8,128)(2,1)S(1)} %shard_map.121), channel_id=1, source_target_pairs={{0,2},{4,0},{8,4},{12,8},{14,12},{10,14},{6,10},{2,6},{1,5},{5,9},... | collective-permute-start | bytes 405512 | tf_op jit(solution)/shard_map/ppermute | solution.py:51
  (15 other events, 70.5 us)

commit v7 on v6

--- a/solution.py
+++ b/solution.py
@@ -26,20 +26,21 @@
     return (near, far) if chunk % 2 else (far, near)
 
 
-def gather_sends(count):
+def hop_order(count, first):
     sends = []
     for hop in range(1, count // 2 + 1):
-        for flip in (0, 1):
-            for chunk in range(chunks):
-                for way in (1, -1):
-                    limit = hop_counts(count, chunk)[0 if way == 1 else 1]
-                    if hop <= limit and (chunk % 2 == (way == -1)) == (flip == 0):
-                        sends.append((chunk, way, hop))
+        for chunk, way in first:
+            if hop <= hop_counts(count, chunk)[0 if way == 1 else 1]:
+                sends.append((chunk, way, hop))
     return sends
 
 
+def gather_sends(count):
+    return hop_order(count, [(0, 1), (1, -1), (0, -1), (1, 1)])
+
+
 def scatter_sends(count):
-    return gather_sends(count)[::-1]
+    return hop_order(count, [(0, 1), (1, -1), (1, 1), (0, -1)])[::-1]
 
 
 def hop_to(block, send, order):

time: 119 us -> 119 us (level)
  no operation moved by 1% of the time
where the time goes in v7:
time: 119 us
  starting transfers between devices  60.4 us (51%)
  waiting for transfers between devices  33.4 us (28%)
  matrix products  11.7 us (10%)
  Pallas kernels  8.71 us (7%)
  other arithmetic  1.8 us (2%)
  local copies, waits for them, and re-layouts  1.45 us (1%)
  between operations  1.21 us (1%)
    ppermute x56, starting transfers between devices, hop_to(): return lax.ppermute(block, ('net', 'tm'), pairs)  59.7 us
    ppermute x56, waiting for transfers between devices, hop_to(): return lax.ppermute(block, ('net', 'tm'), pairs)  33.4 us
    dot_general x8, matrix products, backward(): lax.dot_general(cols, narrow, (((0,), (0,)), ((), ())), preferred_element...  5.93 us
    dot_general x8, matrix products, forward(): share = jnp.dot(cols, blocks, preferred_element_type=jnp.float32)  5.77 us
    pallas_call x3, Pallas kernels, reorder(): pl.pallas_call(functools.partial(reorder_kernel, tuple(distances), count)...  5.43 us
    pallas_call x40, Pallas kernels, small_call(): pl.pallas_call(kernel, out_shape=out_shape, in_specs=[pl.BlockSpec(memory...  3.28 us
  transfers between devices with their start and end apart: 59, of which 31 were waited for; matrix products, arithmetic and copies ran while one was open for 9% of the time, Pallas kernels for 7%

profile of v7, /device:TPU:0, one launch (start us, length us, event | category | flops | bytes accessed | tf_op | source)
XLA Modules:
  0.0 118.6 jit_solution(15712906579618430809)
XLA Ops:
  0.6 1.0 copy-done
  1.7 3.0 %collective-permute-start.2 = (bf16[512,128]{1,0:T(8,128)(2,1)S(1)}, bf16[512,128]{1,0:T(8,128)(2,1)S(1)}, u32[]{:S(2)}, u32[]{:S(2)}) collective-permute-start(bf16[512,128]{1,0:T(8,128)(2,1)S(1)} %get-tuple-element.8), channel_id=1, source_target_pairs={{0,2},{4,0},{8,4},{12,8},{14,12},{10,14},{6,10},{2,6},{1,5},{5,9},... | collective-permute-start | bytes 393224 | tf_op jit(solution)/shard_map/ppermute | solution.py:52
  4.9 1.9 %collective-permute-start.3 = (bf16[512,128]{1,0:T(8,128)(2,1)S(1)}, bf16[512,128]{1,0:T(8,128)(2,1)S(1)}, u32[]{:S(2)}, u32[]{:S(2)}) collective-permute-start(bf16[512,128]{1,0:T(8,128)(2,1)S(1)} %get-tuple-element.9), channel_id=1, source_target_pairs={{0,2},{4,0},{8,4},{12,8},{14,12},{10,14},{6,10},{2,6},{1,5},{5,9},... | collective-permute-start | bytes 393224 | tf_op jit(solution)/shard_map/ppermute | solution.py:52
  7.9 1.6 %shard_map.87 = bf16[512,2048]{1,0:T(8,128)(2,1)S(1)} custom-call(s32[1]{0:T(128)} %bitcast._, bf16[512,8192]{1,0:T(8,128)(2,1)} %factors_ref.5), custom_call_target="tpu_custom_call" | custom-call | bytes 2097152 | tf_op jit(solution)/shard_map/pallas_call | solution.py:177
  9.5 1.9 %shard_map.88 = bf16[512,3072]{1,0:T(8,128)(2,1)S(1)} custom-call(s32[1]{0:T(128)} %bitcast._, bf16[512,8192]{1,0:T(8,128)(2,1)} %factors_ref.5), custom_call_target="tpu_custom_call" | custom-call | bytes 3145728 | tf_op jit(solution)/shard_map/pallas_call | solution.py:177
  11.4 1.9 %shard_map.85 = bf16[512,3072]{1,0:T(8,128)(2,1)S(1)} custom-call(s32[1]{0:T(128)} %bitcast._, bf16[512,8192]{1,0:T(8,128)(2,1)} %factors_ref.5), custom_call_target="tpu_custom_call" | custom-call | bytes 3145728 | tf_op jit(solution)/shard_map/pallas_call | solution.py:177
  13.4 2.0 %collective-permute-start.6 = (bf16[512,128]{1,0:T(8,128)(2,1)S(1)}, bf16[512,128]{1,0:T(8,128)(2,1)S(1)}, u32[]{:S(2)}, u32[]{:S(2)}) collective-permute-start(bf16[512,128]{1,0:T(8,128)(2,1)S(1)} %collective-permute-done.2), channel_id=1, source_target_pairs={{0,2},{4,0},{8,4},{12,8},{14,12},{10,14},{6,10},{2,6},{1,5},{5,9},... | collective-permute-start | bytes 393224 | tf_op jit(solution)/shard_map/ppermute | solution.py:52
  15.5 1.9 %collective-permute-start.7 = (bf16[512,128]{1,0:T(8,128)(2,1)S(1)}, bf16[512,128]{1,0:T(8,128)(2,1)S(1)}, u32[]{:S(2)}, u32[]{:S(2)}) collective-permute-start(bf16[512,128]{1,0:T(8,128)(2,1)S(1)} %collective-permute-done.3), channel_id=1, source_target_pairs={{0,2},{4,0},{8,4},{12,8},{14,12},{10,14},{6,10},{2,6},{1,5},{5,9},... | collective-permute-start | bytes 393224 | tf_op jit(solution)/shard_map/ppermute | solution.py:52
  17.6 1.0 fusion.70
  18.6 1.2 %collective-permute-done.6 = bf16[512,128]{1,0:T(8,128)(2,1)S(1)} collective-permute-done((bf16[512,128]{1,0:T(8,128)(2,1)S(1)}, bf16[512,128]{1,0:T(8,128)(2,1)S(1)}, u32[]{:S(2)}, u32[]{:S(2)}) %collective-permute-start.6) | collective-permute-done | bytes 131104 | tf_op jit(solution)/shard_map/ppermute | solution.py:52
  19.8 1.2 %collective-permute-start.10 = (bf16[512,128]{1,0:T(8,128)(2,1)S(1)}, bf16[512,128]{1,0:T(8,128)(2,1)S(1)}, u32[]{:S(2)}, u32[]{:S(2)}) collective-permute-start(bf16[512,128]{1,0:T(8,128)(2,1)S(1)} %collective-permute-done.6), channel_id=1, source_target_pairs={{0,2},{4,0},{8,4},{12,8},{14,12},{10,14},{6,10},{2,6},{1,5},{5,9},... | collective-permute-start | bytes 393224 | tf_op jit(solution)/shard_map/ppermute | solution.py:52
  25.4 1.1 collective-permute-done.8
  27.4 1.6 %collective-permute-done.11 = bf16[512,128]{1,0:T(8,128)(2,1)S(1)} collective-permute-done((bf16[512,128]{1,0:T(8,128)(2,1)S(1)}, bf16[512,128]{1,0:T(8,128)(2,1)S(1)}, u32[]{:S(2)}, u32[]{:S(2)}) %collective-permute-start.11) | collective-permute-done | bytes 131104 | tf_op jit(solution)/shard_map/ppermute | solution.py:52
  29.0 1.1 collective-permute-start.13
  31.4 3.3 %collective-permute-done.13 = bf16[512,128]{1,0:T(8,128)(2,1)S(1)} collective-permute-done((bf16[512,128]{1,0:T(8,128)(2,1)S(1)}, bf16[512,128]{1,0:T(8,128)(2,1)S(1)}, u32[]{:S(2)}, u32[]{:S(2)}) %collective-permute-start.13) | collective-permute-done | bytes 131104 | tf_op jit(solution)/shard_map/ppermute | solution.py:52
  35.7 2.4 %collective-permute-start.14 = (bf16[512,128]{1,0:T(8,128)(2,1)S(1)}, bf16[512,128]{1,0:T(8,128)(2,1)S(1)}, u32[]{:S(2)}, u32[]{:S(2)}) collective-permute-start(bf16[512,128]{1,0:T(8,128)(2,1)S(1)} %shard_map.89), channel_id=1, source_target_pairs={{0,4},{4,8},{8,12},{12,14},{14,10},{10,6},{6,2},{2,0},{1,3},{5,1},... | collective-permute-start | bytes 393224 | tf_op jit(solution)/shard_map/ppermute | solution.py:52
  38.9 2.1 %collective-permute-start.18 = (bf16[512,128]{1,0:T(8,128)(2,1)S(1)}, bf16[512,128]{1,0:T(8,128)(2,1)S(1)}, u32[]{:S(2)}, u32[]{:S(2)}) collective-permute-start(bf16[512,128]{1,0:T(8,128)(2,1)S(1)} %shard_map.93), channel_id=1, source_target_pairs={{0,4},{4,8},{8,12},{12,14},{14,10},{10,6},{6,2},{2,0},{1,3},{5,1},... | collective-permute-start | bytes 393224 | tf_op jit(solution)/shard_map/ppermute | solution.py:52
  42.0 1.9 %collective-permute-start.15 = (bf16[512,128]{1,0:T(8,128)(2,1)S(1)}, bf16[512,128]{1,0:T(8,128)(2,1)S(1)}, u32[]{:S(2)}, u32[]{:S(2)}) collective-permute-start(bf16[512,128]{1,0:T(8,128)(2,1)S(1)} %shard_map.90), channel_id=1, source_target_pairs={{0,4},{4,8},{8,12},{12,14},{14,10},{10,6},{6,2},{2,0},{1,3},{5,1},... | collective-permute-start | bytes 393224 | tf_op jit(solution)/shard_map/ppermute | solution.py:52
  45.4 2.0 %collective-permute-start.19 = (bf16[512,128]{1,0:T(8,128)(2,1)S(1)}, bf16[512,128]{1,0:T(8,128)(2,1)S(1)}, u32[]{:S(2)}, u32[]{:S(2)}) collective-permute-start(bf16[512,128]{1,0:T(8,128)(2,1)S(1)} %shard_map.94), channel_id=1, source_target_pairs={{0,4},{4,8},{8,12},{12,14},{14,10},{10,6},{6,2},{2,0},{1,3},{5,1},... | collective-permute-start | bytes 393224 | tf_op jit(solution)/shard_map/ppermute | solution.py:52
  47.8 2.5 %collective-permute-start.16 = (bf16[512,128]{1,0:T(8,128)(2,1)S(1)}, bf16[512,128]{1,0:T(8,128)(2,1)S(1)}, u32[]{:S(2)}, u32[]{:S(2)}) collective-permute-start(bf16[512,128]{1,0:T(8,128)(2,1)S(1)} %shard_map.91), channel_id=1, source_target_pairs={{0,4},{4,8},{8,12},{12,14},{14,10},{10,6},{6,2},{2,0},{1,3},{5,1},... | collective-permute-start | bytes 393224 | tf_op jit(solution)/shard_map/ppermute | solution.py:52
  50.8 1.0 fusion.71.spread_ref
  51.9 2.1 %collective-permute-start.20 = (bf16[512,128]{1,0:T(8,128)(2,1)S(1)}, bf16[512,128]{1,0:T(8,128)(2,1)S(1)}, u32[]{:S(2)}, u32[]{:S(2)}) collective-permute-start(bf16[512,128]{1,0:T(8,128)(2,1)S(1)} %shard_map.95), channel_id=1, source_target_pairs={{0,4},{4,8},{8,12},{12,14},{14,10},{10,6},{6,2},{2,0},{1,3},{5,1},... | collective-permute-start | bytes 393224 | tf_op jit(solution)/shard_map/ppermute | solution.py:52
  54.1 2.1 %collective-permute-start.17 = (bf16[512,128]{1,0:T(8,128)(2,1)S(1)}, bf16[512,128]{1,0:T(8,128)(2,1)S(1)}, u32[]{:S(2)}, u32[]{:S(2)}) collective-permute-start(bf16[512,128]{1,0:T(8,128)(2,1)S(1)} %shard_map.92), channel_id=1, source_target_pairs={{0,4},{4,8},{8,12},{12,14},{14,10},{10,6},{6,2},{2,0},{1,3},{5,1},... | collective-permute-start | bytes 393224 | tf_op jit(solution)/shard_map/ppermute | solution.py:52
  56.7 1.6 %collective-permute-done.20.refs_1_ = bf16[512,128]{1,0:T(8,128)(2,1)S(1)} collective-permute-done((bf16[512,128]{1,0:T(8,128)(2,1)S(1)}, bf16[512,128]{1,0:T(8,128)(2,1)S(1)}, u32[]{:S(2)}, u32[]{:S(2)}) %collective-permute-start.20) | collective-permute-done | bytes 131104 | tf_op jit(solution)/shard_map/ppermute | solution.py:52
  58.3 1.9 %collective-permute-done.23.refs_2_ = bf16[512,128]{1,0:T(8,128)(2,1)S(1)} collective-permute-done((bf16[512,128]{1,0:T(8,128)(2,1)S(1)}, bf16[512,128]{1,0:T(8,128)(2,1)S(1)}, u32[]{:S(2)}, u32[]{:S(2)}) %collective-permute-start.23) | collective-permute-done | bytes 131104 | tf_op jit(solution)/shard_map/ppermute | solution.py:52
  61.1 1.9 %collective-permute-done.27.refs_3_ = bf16[512,128]{1,0:T(8,128)(2,1)S(1)} collective-permute-done((bf16[512,128]{1,0:T(8,128)(2,1)S(1)}, bf16[512,128]{1,0:T(8,128)(2,1)S(1)}, u32[]{:S(2)}, u32[]{:S(2)}) %collective-permute-start.27) | collective-permute-done | bytes 131104 | tf_op jit(solution)/shard_map/ppermute | solution.py:52
  63.2 2.0 %collective-permute-start.28 = (bf16[512,128]{1,0:T(8,128)(2,1)S(1)}, bf16[512,128]{1,0:T(8,128)(2,1)S(1)}, u32[]{:S(2)}, u32[]{:S(2)}) collective-permute-start(bf16[512,128]{1,0:T(8,128)(2,1)S(1)} %get-tuple-element.10), channel_id=1, source_target_pairs={{0,4},{4,8},{8,12},{12,14},{14,10},{10,6},{6,2},{2,0},{1,3},{5,1},... | collective-permute-start | bytes 393224 | tf_op jit(solution)/shard_map/ppermute | solution.py:52
  65.2 2.0 %collective-permute-start.29 = (bf16[512,128]{1,0:T(8,128)(2,1)S(1)}, bf16[512,128]{1,0:T(8,128)(2,1)S(1)}, u32[]{:S(2)}, u32[]{:S(2)}) collective-permute-start(bf16[512,128]{1,0:T(8,128)(2,1)S(1)} %get-tuple-element.11), channel_id=1, source_target_pairs={{0,4},{4,8},{8,12},{12,14},{14,10},{10,6},{6,2},{2,0},{1,3},{5,1},... | collective-permute-start | bytes 393224 | tf_op jit(solution)/shard_map/ppermute | solution.py:52
  67.2 1.9 %collective-permute-done.30 = bf16[512,128]{1,0:T(8,128)(2,1)S(1)} collective-permute-done((bf16[512,128]{1,0:T(8,128)(2,1)S(1)}, bf16[512,128]{1,0:T(8,128)(2,1)S(1)}, u32[]{:S(2)}, u32[]{:S(2)}) %collective-permute-start.30) | collective-permute-done | bytes 131104 | tf_op jit(solution)/shard_map/ppermute | solution.py:52
  69.5 1.7 %collective-permute-start.32 = (bf16[512,128]{1,0:T(8,128)(2,1)S(1)}, bf16[512,128]{1,0:T(8,128)(2,1)S(1)}, u32[]{:S(2)}, u32[]{:S(2)}) collective-permute-start(bf16[512,128]{1,0:T(8,128)(2,1)S(1)} %collective-permute-done.28), channel_id=1, source_target_pairs={{0,4},{4,8},{8,12},{12,14},{14,10},{10,6},{6,2},{2,0},{1,3},{5,1},... | collective-permute-start | bytes 393224 | tf_op jit(solution)/shard_map/ppermute | solution.py:52
  72.0 1.6 %collective-permute-start.33 = (bf16[512,128]{1,0:T(8,128)(2,1)S(1)}, bf16[512,128]{1,0:T(8,128)(2,1)S(1)}, u32[]{:S(2)}, u32[]{:S(2)}) collective-permute-start(bf16[512,128]{1,0:T(8,128)(2,1)S(1)} %collective-permute-done.29), channel_id=1, source_target_pairs={{0,4},{4,8},{8,12},{12,14},{14,10},{10,6},{6,2},{2,0},{1,3},{5,1},... | collective-permute-start | bytes 393224 | tf_op jit(solution)/shard_map/ppermute | solution.py:52
  76.8 1.1 collective-permute-start.39
  77.9 1.1 collective-permute-start.37
  79.7 1.7 %collective-permute-done.36 = bf16[512,128]{1,0:T(8,128)(2,1)S(1)} collective-permute-done((bf16[512,128]{1,0:T(8,128)(2,1)S(1)}, bf16[512,128]{1,0:T(8,128)(2,1)S(1)}, u32[]{:S(2)}, u32[]{:S(2)}) %collective-permute-start.36) | collective-permute-done | bytes 131104 | tf_op jit(solution)/shard_map/ppermute | solution.py:52
  81.4 1.2 %collective-permute-start.40 = (bf16[512,128]{1,0:T(8,128)(2,1)S(1)}, bf16[512,128]{1,0:T(8,128)(2,1)S(1)}, u32[]{:S(2)}, u32[]{:S(2)}) collective-permute-start(bf16[512,128]{1,0:T(8,128)(2,1)S(1)} %collective-permute-done.36), channel_id=1, source_target_pairs={{0,4},{4,8},{8,12},{12,14},{14,10},{10,6},{6,2},{2,0},{1,3},{5,1},... | collective-permute-start | bytes 393224 | tf_op jit(solution)/shard_map/ppermute | solution.py:52
  85.0 2.1 %collective-permute-done.40 = bf16[512,128]{1,0:T(8,128)(2,1)S(1)} collective-permute-done((bf16[512,128]{1,0:T(8,128)(2,1)S(1)}, bf16[512,128]{1,0:T(8,128)(2,1)S(1)}, u32[]{:S(2)}, u32[]{:S(2)}) %collective-permute-start.40) | collective-permute-done | bytes 131104 | tf_op jit(solution)/shard_map/ppermute | solution.py:52
  89.1 2.2 %collective-permute-start.42 = (bf16[512,128]{1,0:T(8,128)(2,1)S(1)}, bf16[512,128]{1,0:T(8,128)(2,1)S(1)}, u32[]{:S(2)}, u32[]{:S(2)}) collective-permute-start(bf16[512,128]{1,0:T(8,128)(2,1)S(1)} %shard_map.105), channel_id=1, source_target_pairs={{0,4},{4,8},{8,12},{12,14},{14,10},{10,6},{6,2},{2,0},{1,3},{5,1},... | collective-permute-start | bytes 393224 | tf_op jit(solution)/shard_map/ppermute | solution.py:52
  92.4 1.8 %collective-permute-start.49 = (bf16[528,128]{1,0:T(8,128)(2,1)S(1)}, bf16[528,128]{1,0:T(8,128)(2,1)S(1)}, u32[]{:S(2)}, u32[]{:S(2)}) collective-permute-start(bf16[528,128]{1,0:T(8,128)(2,1)S(1)} %shard_map.115), channel_id=1, source_target_pairs={{0,4},{4,8},{8,12},{12,14},{14,10},{10,6},{6,2},{2,0},{1,3},{5,1},... | collective-permute-start | bytes 405512 | tf_op jit(solution)/shard_map/ppermute | solution.py:52
  94.5 1.9 %collective-permute-start.43 = (bf16[512,128]{1,0:T(8,128)(2,1)S(1)}, bf16[512,128]{1,0:T(8,128)(2,1)S(1)}, u32[]{:S(2)}, u32[]{:S(2)}) collective-permute-start(bf16[512,128]{1,0:T(8,128)(2,1)S(1)} %shard_map.106), channel_id=1, source_target_pairs={{0,4},{4,8},{8,12},{12,14},{14,10},{10,6},{6,2},{2,0},{1,3},{5,1},... | collective-permute-start | bytes 393224 | tf_op jit(solution)/shard_map/ppermute | solution.py:52
  96.4 1.1 collective-permute-start.53
  99.4 1.4 %collective-permute-start.50 = (bf16[528,128]{1,0:T(8,128)(2,1)S(1)}, bf16[528,128]{1,0:T(8,128)(2,1)S(1)}, u32[]{:S(2)}, u32[]{:S(2)}) collective-permute-start(bf16[528,128]{1,0:T(8,128)(2,1)S(1)} %shard_map.116), channel_id=1, source_target_pairs={{0,4},{4,8},{8,12},{12,14},{14,10},{10,6},{6,2},{2,0},{1,3},{5,1},... | collective-permute-start | bytes 405512 | tf_op jit(solution)/shard_map/ppermute | solution.py:52
  102.3 1.3 %collective-permute-start.54 = (bf16[528,128]{1,0:T(8,128)(2,1)S(1)}, bf16[528,128]{1,0:T(8,128)(2,1)S(1)}, u32[]{:S(2)}, u32[]{:S(2)}) collective-permute-start(bf16[528,128]{1,0:T(8,128)(2,1)S(1)} %shard_map.120), channel_id=1, source_target_pairs={{0,2},{4,0},{8,4},{12,8},{14,12},{10,14},{6,10},{2,6},{1,5},{5,9},... | collective-permute-start | bytes 405512 | tf_op jit(solution)/shard_map/ppermute | solution.py:52
  103.6 1.0 fusion.74.spread_ref
  104.6 1.3 %collective-permute-start.51 = (bf16[528,128]{1,0:T(8,128)(2,1)S(1)}, bf16[528,128]{1,0:T(8,128)(2,1)S(1)}, u32[]{:S(2)}, u32[]{:S(2)}) collective-permute-start(bf16[528,128]{1,0:T(8,128)(2,1)S(1)} %shard_map.117), channel_id=1, source_target_pairs={{0,4},{4,8},{8,12},{12,14},{14,10},{10,6},{6,2},{2,0},{1,3},{5,1},... | collective-permute-start | bytes 405512 | tf_op jit(solution)/shard_map/ppermute | solution.py:52
  105.9 1.5 %collective-permute-done.54.arrived_ref.refs_4_ = bf16[528,128]{1,0:T(8,128)(2,1)S(1)} collective-permute-done((bf16[528,128]{1,0:T(8,128)(2,1)S(1)}, bf16[528,128]{1,0:T(8,128)(2,1)S(1)}, u32[]{:S(2)}, u32[]{:S(2)}) %collective-permute-start.54) | collective-permute-done | bytes 135200 | tf_op jit(solution)/shard_map/ppermute | solution.py:52
  107.4 1.3 %collective-permute-start.55 = (bf16[528,128]{1,0:T(8,128)(2,1)S(1)}, bf16[528,128]{1,0:T(8,128)(2,1)S(1)}, u32[]{:S(2)}, u32[]{:S(2)}) collective-permute-start(bf16[528,128]{1,0:T(8,128)(2,1)S(1)} %shard_map.121), channel_id=1, source_target_pairs={{0,2},{4,0},{8,4},{12,8},{14,12},{10,14},{6,10},{2,6},{1,5},{5,9},... | collective-permute-start | bytes 405512 | tf_op jit(solution)/shard_map/ppermute | solution.py:52
  109.5 1.4 %collective-permute-start.45 = (bf16[512,128]{1,0:T(8,128)(2,1)S(1)}, bf16[512,128]{1,0:T(8,128)(2,1)S(1)}, u32[]{:S(2)}, u32[]{:S(2)}) collective-permute-start(bf16[512,128]{1,0:T(8,128)(2,1)S(1)} %shard_map.108), channel_id=1, source_target_pairs={{0,4},{4,8},{8,12},{12,14},{14,10},{10,6},{6,2},{2,0},{1,3},{5,1},... | collective-permute-start | bytes 393224 | tf_op jit(solution)/shard_map/ppermute | solution.py:52
  110.9 3.0 %collective-permute-done.48.behind_ref = bf16[512,128]{1,0:T(8,128)(2,1)S(1)} collective-permute-done((bf16[512,128]{1,0:T(8,128)(2,1)S(1)}, bf16[512,128]{1,0:T(8,128)(2,1)S(1)}, u32[]{:S(2)}, u32[]{:S(2)}) %collective-permute-start.48) | collective-permute-done | bytes 131104 | tf_op jit(solution)/shard_map/ppermute | solution.py:52
  (153 shorter events, 34.8 us)
Async XLA Ops:
  1.7 11.7 %collective-permute-start.2 = (bf16[512,128]{1,0:T(8,128)(2,1)S(1)}, bf16[512,128]{1,0:T(8,128)(2,1)S(1)}, u32[]{:S(2)}, u32[]{:S(2)}) collective-permute-start(bf16[512,128]{1,0:T(8,128)(2,1)S(1)} %get-tuple-element.8), channel_id=1, source_target_pairs={{0,2},{4,0},{8,4},{12,8},{14,12},{10,14},{6,10},{2,6},{1,5},{5,9},... | collective-permute-start | bytes 393224 | tf_op jit(solution)/shard_map/ppermute | solution.py:52
  4.8 10.6 %collective-permute-start = (bf16[512,128]{1,0:T(8,128)(2,1)S(1)}, bf16[512,128]{1,0:T(8,128)(2,1)S(1)}, u32[]{:S(2)}, u32[]{:S(2)}) collective-permute-start(bf16[512,128]{1,0:T(8,128)(2,1)S(1)} %get-tuple-element.8), channel_id=1, source_target_pairs={{0,4},{4,8},{8,12},{12,14},{14,10},{10,6},{6,2},{2,0},{1,3},{5,1},... | collective-permute-start | bytes 393224 | tf_op jit(solution)/shard_map/ppermute | solution.py:52
  4.9 10.6 %collective-permute-start.3 = (bf16[512,128]{1,0:T(8,128)(2,1)S(1)}, bf16[512,128]{1,0:T(8,128)(2,1)S(1)}, u32[]{:S(2)}, u32[]{:S(2)}) collective-permute-start(bf16[512,128]{1,0:T(8,128)(2,1)S(1)} %get-tuple-element.9), channel_id=1, source_target_pairs={{0,2},{4,0},{8,4},{12,8},{14,12},{10,14},{6,10},{2,6},{1,5},{5,9},... | collective-permute-start | bytes 393224 | tf_op jit(solution)/shard_map/ppermute | solution.py:52
  6.8 10.6 %collective-permute-start.1 = (bf16[512,128]{1,0:T(8,128)(2,1)S(1)}, bf16[512,128]{1,0:T(8,128)(2,1)S(1)}, u32[]{:S(2)}, u32[]{:S(2)}) collective-permute-start(bf16[512,128]{1,0:T(8,128)(2,1)S(1)} %get-tuple-element.9), channel_id=1, source_target_pairs={{0,4},{4,8},{8,12},{12,14},{14,10},{10,6},{6,2},{2,0},{1,3},{5,1},... | collective-permute-start | bytes 393224 | tf_op jit(solution)/shard_map/ppermute | solution.py:52
  13.4 6.4 %collective-permute-start.6 = (bf16[512,128]{1,0:T(8,128)(2,1)S(1)}, bf16[512,128]{1,0:T(8,128)(2,1)S(1)}, u32[]{:S(2)}, u32[]{:S(2)}) collective-permute-start(bf16[512,128]{1,0:T(8,128)(2,1)S(1)} %collective-permute-done.2), channel_id=1, source_target_pairs={{0,2},{4,0},{8,4},{12,8},{14,12},{10,14},{6,10},{2,6},{1,5},{5,9},... | collective-permute-start | bytes 393224 | tf_op jit(solution)/shard_map/ppermute | solution.py:52
  15.3 6.2 %collective-permute-start.4 = (bf16[512,128]{1,0:T(8,128)(2,1)S(1)}, bf16[512,128]{1,0:T(8,128)(2,1)S(1)}, u32[]{:S(2)}, u32[]{:S(2)}) collective-permute-start(bf16[512,128]{1,0:T(8,128)(2,1)S(1)} %collective-permute-done), channel_id=1, source_target_pairs={{0,4},{4,8},{8,12},{12,14},{14,10},{10,6},{6,2},{2,0},{1,3},{5,1},... | collective-permute-start | bytes 393224 | tf_op jit(solution)/shard_map/ppermute | solution.py:52
  15.5 7.1 %collective-permute-start.7 = (bf16[512,128]{1,0:T(8,128)(2,1)S(1)}, bf16[512,128]{1,0:T(8,128)(2,1)S(1)}, u32[]{:S(2)}, u32[]{:S(2)}) collective-permute-start(bf16[512,128]{1,0:T(8,128)(2,1)S(1)} %collective-permute-done.3), channel_id=1, source_target_pairs={{0,2},{4,0},{8,4},{12,8},{14,12},{10,14},{6,10},{2,6},{1,5},{5,9},... | collective-permute-start | bytes 393224 | tf_op jit(solution)/shard_map/ppermute | solution.py:52
  17.4 6.9 %collective-permute-start.5 = (bf16[512,128]{1,0:T(8,128)(2,1)S(1)}, bf16[512,128]{1,0:T(8,128)(2,1)S(1)}, u32[]{:S(2)}, u32[]{:S(2)}) collective-permute-start(bf16[512,128]{1,0:T(8,128)(2,1)S(1)} %collective-permute-done.1), channel_id=1, source_target_pairs={{0,4},{4,8},{8,12},{12,14},{14,10},{10,6},{6,2},{2,0},{1,3},{5,1},... | collective-permute-start | bytes 393224 | tf_op jit(solution)/shard_map/ppermute | solution.py:52
  19.8 10.3 %collective-permute-start.10 = (bf16[512,128]{1,0:T(8,128)(2,1)S(1)}, bf16[512,128]{1,0:T(8,128)(2,1)S(1)}, u32[]{:S(2)}, u32[]{:S(2)}) collective-permute-start(bf16[512,128]{1,0:T(8,128)(2,1)S(1)} %collective-permute-done.6), channel_id=1, source_target_pairs={{0,2},{4,0},{8,4},{12,8},{14,12},{10,14},{6,10},{2,6},{1,5},{5,9},... | collective-permute-start | bytes 393224 | tf_op jit(solution)/shard_map/ppermute | solution.py:52
  22.6 6.4 %collective-permute-start.11 = (bf16[512,128]{1,0:T(8,128)(2,1)S(1)}, bf16[512,128]{1,0:T(8,128)(2,1)S(1)}, u32[]{:S(2)}, u32[]{:S(2)}) collective-permute-start(bf16[512,128]{1,0:T(8,128)(2,1)S(1)} %collective-permute-done.7), channel_id=1, source_target_pairs={{0,2},{4,0},{8,4},{12,8},{14,12},{10,14},{6,10},{2,6},{1,5},{5,9},... | collective-permute-start | bytes 393224 | tf_op jit(solution)/shard_map/ppermute | solution.py:52
  24.3 5.8 %collective-permute-start.9 = (bf16[512,128]{1,0:T(8,128)(2,1)S(1)}, bf16[512,128]{1,0:T(8,128)(2,1)S(1)}, u32[]{:S(2)}, u32[]{:S(2)}) collective-permute-start(bf16[512,128]{1,0:T(8,128)(2,1)S(1)} %collective-permute-done.5), channel_id=1, source_target_pairs={{0,4},{4,8},{8,12},{12,14},{14,10},{10,6},{6,2},{2,0},{1,3},{5,1},... | collective-permute-start | bytes 393224 | tf_op jit(solution)/shard_map/ppermute | solution.py:52
  29.0 5.8 %collective-permute-start.13 = (bf16[512,128]{1,0:T(8,128)(2,1)S(1)}, bf16[512,128]{1,0:T(8,128)(2,1)S(1)}, u32[]{:S(2)}, u32[]{:S(2)}) collective-permute-start(bf16[512,128]{1,0:T(8,128)(2,1)S(1)} %collective-permute-done.11), channel_id=1, source_target_pairs={{0,2},{4,0},{8,4},{12,8},{14,12},{10,14},{6,10},{2,6},{1,5},{5,9},... | collective-permute-start | bytes 393224 | tf_op jit(solution)/shard_map/ppermute | solution.py:52
  35.7 6.2 %collective-permute-start.14 = (bf16[512,128]{1,0:T(8,128)(2,1)S(1)}, bf16[512,128]{1,0:T(8,128)(2,1)S(1)}, u32[]{:S(2)}, u32[]{:S(2)}) collective-permute-start(bf16[512,128]{1,0:T(8,128)(2,1)S(1)} %shard_map.89), channel_id=1, source_target_pairs={{0,4},{4,8},{8,12},{12,14},{14,10},{10,6},{6,2},{2,0},{1,3},{5,1},... | collective-permute-start | bytes 393224 | tf_op jit(solution)/shard_map/ppermute | solution.py:52
  38.1 6.3 %collective-permute-start.24 = (bf16[512,128]{1,0:T(8,128)(2,1)S(1)}, bf16[512,128]{1,0:T(8,128)(2,1)S(1)}, u32[]{:S(2)}, u32[]{:S(2)}) collective-permute-start(bf16[512,128]{1,0:T(8,128)(2,1)S(1)} %shard_map.99), channel_id=1, source_target_pairs={{0,2},{4,0},{8,4},{12,8},{14,12},{10,14},{6,10},{2,6},{1,5},{5,9},... | collective-permute-start | bytes 393224 | tf_op jit(solution)/shard_map/ppermute | solution.py:52
  38.9 6.4 %collective-permute-start.18 = (bf16[512,128]{1,0:T(8,128)(2,1)S(1)}, bf16[512,128]{1,0:T(8,128)(2,1)S(1)}, u32[]{:S(2)}, u32[]{:S(2)}) collective-permute-start(bf16[512,128]{1,0:T(8,128)(2,1)S(1)} %shard_map.93), channel_id=1, source_target_pairs={{0,4},{4,8},{8,12},{12,14},{14,10},{10,6},{6,2},{2,0},{1,3},{5,1},... | collective-permute-start | bytes 393224 | tf_op jit(solution)/shard_map/ppermute | solution.py:52
  41.0 6.4 %collective-permute-start.21 = (bf16[512,128]{1,0:T(8,128)(2,1)S(1)}, bf16[512,128]{1,0:T(8,128)(2,1)S(1)}, u32[]{:S(2)}, u32[]{:S(2)}) collective-permute-start(bf16[512,128]{1,0:T(8,128)(2,1)S(1)} %shard_map.96), channel_id=1, source_target_pairs={{0,2},{4,0},{8,4},{12,8},{14,12},{10,14},{6,10},{2,6},{1,5},{5,9},... | collective-permute-start | bytes 393224 | tf_op jit(solution)/shard_map/ppermute | solution.py:52
  42.0 5.7 %collective-permute-start.15 = (bf16[512,128]{1,0:T(8,128)(2,1)S(1)}, bf16[512,128]{1,0:T(8,128)(2,1)S(1)}, u32[]{:S(2)}, u32[]{:S(2)}) collective-permute-start(bf16[512,128]{1,0:T(8,128)(2,1)S(1)} %shard_map.90), channel_id=1, source_target_pairs={{0,4},{4,8},{8,12},{12,14},{14,10},{10,6},{6,2},{2,0},{1,3},{5,1},... | collective-permute-start | bytes 393224 | tf_op jit(solution)/shard_map/ppermute | solution.py:52
  44.5 6.3 %collective-permute-start.25 = (bf16[512,128]{1,0:T(8,128)(2,1)S(1)}, bf16[512,128]{1,0:T(8,128)(2,1)S(1)}, u32[]{:S(2)}, u32[]{:S(2)}) collective-permute-start(bf16[512,128]{1,0:T(8,128)(2,1)S(1)} %shard_map.100), channel_id=1, source_target_pairs={{0,2},{4,0},{8,4},{12,8},{14,12},{10,14},{6,10},{2,6},{1,5},{5,9},... | collective-permute-start | bytes 393224 | tf_op jit(solution)/shard_map/ppermute | solution.py:52
  45.4 6.4 %collective-permute-start.19 = (bf16[512,128]{1,0:T(8,128)(2,1)S(1)}, bf16[512,128]{1,0:T(8,128)(2,1)S(1)}, u32[]{:S(2)}, u32[]{:S(2)}) collective-permute-start(bf16[512,128]{1,0:T(8,128)(2,1)S(1)} %shard_map.94), channel_id=1, source_target_pairs={{0,4},{4,8},{8,12},{12,14},{14,10},{10,6},{6,2},{2,0},{1,3},{5,1},... | collective-permute-start | bytes 393224 | tf_op jit(solution)/shard_map/ppermute | solution.py:52
  47.5 6.5 %collective-permute-start.22 = (bf16[512,128]{1,0:T(8,128)(2,1)S(1)}, bf16[512,128]{1,0:T(8,128)(2,1)S(1)}, u32[]{:S(2)}, u32[]{:S(2)}) collective-permute-start(bf16[512,128]{1,0:T(8,128)(2,1)S(1)} %shard_map.97), channel_id=1, source_target_pairs={{0,2},{4,0},{8,4},{12,8},{14,12},{10,14},{6,10},{2,6},{1,5},{5,9},... | collective-permute-start | bytes 393224 | tf_op jit(solution)/shard_map/ppermute | solution.py:52
  47.8 6.3 %collective-permute-start.16 = (bf16[512,128]{1,0:T(8,128)(2,1)S(1)}, bf16[512,128]{1,0:T(8,128)(2,1)S(1)}, u32[]{:S(2)}, u32[]{:S(2)}) collective-permute-start(bf16[512,128]{1,0:T(8,128)(2,1)S(1)} %shard_map.91), channel_id=1, source_target_pairs={{0,4},{4,8},{8,12},{12,14},{14,10},{10,6},{6,2},{2,0},{1,3},{5,1},... | collective-permute-start | bytes 393224 | tf_op jit(solution)/shard_map/ppermute | solution.py:52
  50.7 5.8 %collective-permute-start.26 = (bf16[512,128]{1,0:T(8,128)(2,1)S(1)}, bf16[512,128]{1,0:T(8,128)(2,1)S(1)}, u32[]{:S(2)}, u32[]{:S(2)}) collective-permute-start(bf16[512,128]{1,0:T(8,128)(2,1)S(1)} %shard_map.101), channel_id=1, source_target_pairs={{0,2},{4,0},{8,4},{12,8},{14,12},{10,14},{6,10},{2,6},{1,5},{5,9},... | collective-permute-start | bytes 393224 | tf_op jit(solution)/shard_map/ppermute | solution.py:52
  51.9 6.4 %collective-permute-start.20 = (bf16[512,128]{1,0:T(8,128)(2,1)S(1)}, bf16[512,128]{1,0:T(8,128)(2,1)S(1)}, u32[]{:S(2)}, u32[]{:S(2)}) collective-permute-start(bf16[512,128]{1,0:T(8,128)(2,1)S(1)} %shard_map.95), channel_id=1, source_target_pairs={{0,4},{4,8},{8,12},{12,14},{14,10},{10,6},{6,2},{2,0},{1,3},{5,1},... | collective-permute-start | bytes 393224 | tf_op jit(solution)/shard_map/ppermute | solution.py:52
  54.0 6.2 %collective-permute-start.23 = (bf16[512,128]{1,0:T(8,128)(2,1)S(1)}, bf16[512,128]{1,0:T(8,128)(2,1)S(1)}, u32[]{:S(2)}, u32[]{:S(2)}) collective-permute-start(bf16[512,128]{1,0:T(8,128)(2,1)S(1)} %shard_map.98), channel_id=1, source_target_pairs={{0,2},{4,0},{8,4},{12,8},{14,12},{10,14},{6,10},{2,6},{1,5},{5,9},... | collective-permute-start | bytes 393224 | tf_op jit(solution)/shard_map/ppermute | solution.py:52
  54.1 7.0 %collective-permute-start.17 = (bf16[512,128]{1,0:T(8,128)(2,1)S(1)}, bf16[512,128]{1,0:T(8,128)(2,1)S(1)}, u32[]{:S(2)}, u32[]{:S(2)}) collective-permute-start(bf16[512,128]{1,0:T(8,128)(2,1)S(1)} %shard_map.92), channel_id=1, source_target_pairs={{0,4},{4,8},{8,12},{12,14},{14,10},{10,6},{6,2},{2,0},{1,3},{5,1},... | collective-permute-start | bytes 393224 | tf_op jit(solution)/shard_map/ppermute | solution.py:52
  56.5 6.5 %collective-permute-start.27 = (bf16[512,128]{1,0:T(8,128)(2,1)S(1)}, bf16[512,128]{1,0:T(8,128)(2,1)S(1)}, u32[]{:S(2)}, u32[]{:S(2)}) collective-permute-start(bf16[512,128]{1,0:T(8,128)(2,1)S(1)} %shard_map.102), channel_id=1, source_target_pairs={{0,2},{4,0},{8,4},{12,8},{14,12},{10,14},{6,10},{2,6},{1,5},{5,9},... | collective-permute-start | bytes 393224 | tf_op jit(solution)/shard_map/ppermute | solution.py:52
  63.1 6.1 %collective-permute-start.30 = (bf16[512,128]{1,0:T(8,128)(2,1)S(1)}, bf16[512,128]{1,0:T(8,128)(2,1)S(1)}, u32[]{:S(2)}, u32[]{:S(2)}) collective-permute-start(bf16[512,128]{1,0:T(8,128)(2,1)S(1)} %get-tuple-element.10), channel_id=1, source_target_pairs={{0,2},{4,0},{8,4},{12,8},{14,12},{10,14},{6,10},{2,6},{1,5},{5,9},... | collective-permute-start | bytes 393224 | tf_op jit(solution)/shard_map/ppermute | solution.py:52
  63.2 6.4 %collective-permute-start.28 = (bf16[512,128]{1,0:T(8,128)(2,1)S(1)}, bf16[512,128]{1,0:T(8,128)(2,1)S(1)}, u32[]{:S(2)}, u32[]{:S(2)}) collective-permute-start(bf16[512,128]{1,0:T(8,128)(2,1)S(1)} %get-tuple-element.10), channel_id=1, source_target_pairs={{0,4},{4,8},{8,12},{12,14},{14,10},{10,6},{6,2},{2,0},{1,3},{5,1},... | collective-permute-start | bytes 393224 | tf_op jit(solution)/shard_map/ppermute | solution.py:52
  65.2 6.1 %collective-permute-start.31 = (bf16[512,128]{1,0:T(8,128)(2,1)S(1)}, bf16[512,128]{1,0:T(8,128)(2,1)S(1)}, u32[]{:S(2)}, u32[]{:S(2)}) collective-permute-start(bf16[512,128]{1,0:T(8,128)(2,1)S(1)} %get-tuple-element.11), channel_id=1, source_target_pairs={{0,2},{4,0},{8,4},{12,8},{14,12},{10,14},{6,10},{2,6},{1,5},{5,9},... | collective-permute-start | bytes 393224 | tf_op jit(solution)/shard_map/ppermute | solution.py:52
  65.2 6.7 %collective-permute-start.29 = (bf16[512,128]{1,0:T(8,128)(2,1)S(1)}, bf16[512,128]{1,0:T(8,128)(2,1)S(1)}, u32[]{:S(2)}, u32[]{:S(2)}) collective-permute-start(bf16[512,128]{1,0:T(8,128)(2,1)S(1)} %get-tuple-element.11), channel_id=1, source_target_pairs={{0,4},{4,8},{8,12},{12,14},{14,10},{10,6},{6,2},{2,0},{1,3},{5,1},... | collective-permute-start | bytes 393224 | tf_op jit(solution)/shard_map/ppermute | solution.py:52
  69.2 5.5 %collective-permute-start.34 = (bf16[512,128]{1,0:T(8,128)(2,1)S(1)}, bf16[512,128]{1,0:T(8,128)(2,1)S(1)}, u32[]{:S(2)}, u32[]{:S(2)}) collective-permute-start(bf16[512,128]{1,0:T(8,128)(2,1)S(1)} %collective-permute-done.30), channel_id=1, source_target_pairs={{0,2},{4,0},{8,4},{12,8},{14,12},{10,14},{6,10},{2,6},{1,5},{5,9},... | collective-permute-start | bytes 393224 | tf_op jit(solution)/shard_map/ppermute | solution.py:52
  69.5 6.3 %collective-permute-start.32 = (bf16[512,128]{1,0:T(8,128)(2,1)S(1)}, bf16[512,128]{1,0:T(8,128)(2,1)S(1)}, u32[]{:S(2)}, u32[]{:S(2)}) collective-permute-start(bf16[512,128]{1,0:T(8,128)(2,1)S(1)} %collective-permute-done.28), channel_id=1, source_target_pairs={{0,4},{4,8},{8,12},{12,14},{14,10},{10,6},{6,2},{2,0},{1,3},{5,1},... | collective-permute-start | bytes 393224 | tf_op jit(solution)/shard_map/ppermute | solution.py:52
  71.2 5.6 %collective-permute-start.35 = (bf16[512,128]{1,0:T(8,128)(2,1)S(1)}, bf16[512,128]{1,0:T(8,128)(2,1)S(1)}, u32[]{:S(2)}, u32[]{:S(2)}) collective-permute-start(bf16[512,128]{1,0:T(8,128)(2,1)S(1)} %collective-permute-done.31), channel_id=1, source_target_pairs={{0,2},{4,0},{8,4},{12,8},{14,12},{10,14},{6,10},{2,6},{1,5},{5,9},... | collective-permute-start | bytes 393224 | tf_op jit(solution)/shard_map/ppermute | solution.py:52
  72.0 6.0 %collective-permute-start.33 = (bf16[512,128]{1,0:T(8,128)(2,1)S(1)}, bf16[512,128]{1,0:T(8,128)(2,1)S(1)}, u32[]{:S(2)}, u32[]{:S(2)}) collective-permute-start(bf16[512,128]{1,0:T(8,128)(2,1)S(1)} %collective-permute-done.29), channel_id=1, source_target_pairs={{0,4},{4,8},{8,12},{12,14},{14,10},{10,6},{6,2},{2,0},{1,3},{5,1},... | collective-permute-start | bytes 393224 | tf_op jit(solution)/shard_map/ppermute | solution.py:52
  74.7 8.8 %collective-permute-start.38 = (bf16[512,128]{1,0:T(8,128)(2,1)S(1)}, bf16[512,128]{1,0:T(8,128)(2,1)S(1)}, u32[]{:S(2)}, u32[]{:S(2)}) collective-permute-start(bf16[512,128]{1,0:T(8,128)(2,1)S(1)} %collective-permute-done.34), channel_id=1, source_target_pairs={{0,2},{4,0},{8,4},{12,8},{14,12},{10,14},{6,10},{2,6},{1,5},{5,9},... | collective-permute-start | bytes 393224 | tf_op jit(solution)/shard_map/ppermute | solution.py:52
  75.9 5.6 %collective-permute-start.36 = (bf16[512,128]{1,0:T(8,128)(2,1)S(1)}, bf16[512,128]{1,0:T(8,128)(2,1)S(1)}, u32[]{:S(2)}, u32[]{:S(2)}) collective-permute-start(bf16[512,128]{1,0:T(8,128)(2,1)S(1)} %collective-permute-done.32), channel_id=1, source_target_pairs={{0,4},{4,8},{8,12},{12,14},{14,10},{10,6},{6,2},{2,0},{1,3},{5,1},... | collective-permute-start | bytes 393224 | tf_op jit(solution)/shard_map/ppermute | solution.py:52
  76.8 6.2 %collective-permute-start.39 = (bf16[512,128]{1,0:T(8,128)(2,1)S(1)}, bf16[512,128]{1,0:T(8,128)(2,1)S(1)}, u32[]{:S(2)}, u32[]{:S(2)}) collective-permute-start(bf16[512,128]{1,0:T(8,128)(2,1)S(1)} %collective-permute-done.35), channel_id=1, source_target_pairs={{0,2},{4,0},{8,4},{12,8},{14,12},{10,14},{6,10},{2,6},{1,5},{5,9},... | collective-permute-start | bytes 393224 | tf_op jit(solution)/shard_map/ppermute | solution.py:52
  77.9 6.4 %collective-permute-start.37 = (bf16[512,128]{1,0:T(8,128)(2,1)S(1)}, bf16[512,128]{1,0:T(8,128)(2,1)S(1)}, u32[]{:S(2)}, u32[]{:S(2)}) collective-permute-start(bf16[512,128]{1,0:T(8,128)(2,1)S(1)} %collective-permute-done.33), channel_id=1, source_target_pairs={{0,4},{4,8},{8,12},{12,14},{14,10},{10,6},{6,2},{2,0},{1,3},{5,1},... | collective-permute-start | bytes 393224 | tf_op jit(solution)/shard_map/ppermute | solution.py:52
  81.4 5.7 %collective-permute-start.40 = (bf16[512,128]{1,0:T(8,128)(2,1)S(1)}, bf16[512,128]{1,0:T(8,128)(2,1)S(1)}, u32[]{:S(2)}, u32[]{:S(2)}) collective-permute-start(bf16[512,128]{1,0:T(8,128)(2,1)S(1)} %collective-permute-done.36), channel_id=1, source_target_pairs={{0,4},{4,8},{8,12},{12,14},{14,10},{10,6},{6,2},{2,0},{1,3},{5,1},... | collective-permute-start | bytes 393224 | tf_op jit(solution)/shard_map/ppermute | solution.py:52
  89.1 5.3 %collective-permute-start.42 = (bf16[512,128]{1,0:T(8,128)(2,1)S(1)}, bf16[512,128]{1,0:T(8,128)(2,1)S(1)}, u32[]{:S(2)}, u32[]{:S(2)}) collective-permute-start(bf16[512,128]{1,0:T(8,128)(2,1)S(1)} %shard_map.105), channel_id=1, source_target_pairs={{0,4},{4,8},{8,12},{12,14},{14,10},{10,6},{6,2},{2,0},{1,3},{5,1},... | collective-permute-start | bytes 393224 | tf_op jit(solution)/shard_map/ppermute | solution.py:52
  92.1 6.4 %collective-permute-start.46 = (bf16[512,128]{1,0:T(8,128)(2,1)S(1)}, bf16[512,128]{1,0:T(8,128)(2,1)S(1)}, u32[]{:S(2)}, u32[]{:S(2)}) collective-permute-start(bf16[512,128]{1,0:T(8,128)(2,1)S(1)} %shard_map.109), channel_id=1, source_target_pairs={{0,2},{4,0},{8,4},{12,8},{14,12},{10,14},{6,10},{2,6},{1,5},{5,9},... | collective-permute-start | bytes 393224 | tf_op jit(solution)/shard_map/ppermute | solution.py:52
  92.4 7.0 %collective-permute-start.49 = (bf16[528,128]{1,0:T(8,128)(2,1)S(1)}, bf16[528,128]{1,0:T(8,128)(2,1)S(1)}, u32[]{:S(2)}, u32[]{:S(2)}) collective-permute-start(bf16[528,128]{1,0:T(8,128)(2,1)S(1)} %shard_map.115), channel_id=1, source_target_pairs={{0,4},{4,8},{8,12},{12,14},{14,10},{10,6},{6,2},{2,0},{1,3},{5,1},... | collective-permute-start | bytes 405512 | tf_op jit(solution)/shard_map/ppermute | solution.py:52
  94.5 6.8 %collective-permute-start.43 = (bf16[512,128]{1,0:T(8,128)(2,1)S(1)}, bf16[512,128]{1,0:T(8,128)(2,1)S(1)}, u32[]{:S(2)}, u32[]{:S(2)}) collective-permute-start(bf16[512,128]{1,0:T(8,128)(2,1)S(1)} %shard_map.106), channel_id=1, source_target_pairs={{0,4},{4,8},{8,12},{12,14},{14,10},{10,6},{6,2},{2,0},{1,3},{5,1},... | collective-permute-start | bytes 393224 | tf_op jit(solution)/shard_map/ppermute | solution.py:52
  96.4 5.8 %collective-permute-start.53 = (bf16[528,128]{1,0:T(8,128)(2,1)S(1)}, bf16[528,128]{1,0:T(8,128)(2,1)S(1)}, u32[]{:S(2)}, u32[]{:S(2)}) collective-permute-start(bf16[528,128]{1,0:T(8,128)(2,1)S(1)} %shard_map.119), channel_id=1, source_target_pairs={{0,2},{4,0},{8,4},{12,8},{14,12},{10,14},{6,10},{2,6},{1,5},{5,9},... | collective-permute-start | bytes 405512 | tf_op jit(solution)/shard_map/ppermute | solution.py:52
  98.5 10.1 %collective-permute-start.47 = (bf16[512,128]{1,0:T(8,128)(2,1)S(1)}, bf16[512,128]{1,0:T(8,128)(2,1)S(1)}, u32[]{:S(2)}, u32[]{:S(2)}) collective-permute-start(bf16[512,128]{1,0:T(8,128)(2,1)S(1)} %shard_map.110), channel_id=1, source_target_pairs={{0,2},{4,0},{8,4},{12,8},{14,12},{10,14},{6,10},{2,6},{1,5},{5,9},... | collective-permute-start | bytes 393224 | tf_op jit(solution)/shard_map/ppermute | solution.py:52
  101.4 8.0 %collective-permute-start.44 = (bf16[512,128]{1,0:T(8,128)(2,1)S(1)}, bf16[512,128]{1,0:T(8,128)(2,1)S(1)}, u32[]{:S(2)}, u32[]{:S(2)}) collective-permute-start(bf16[512,128]{1,0:T(8,128)(2,1)S(1)} %shard_map.107), channel_id=1, source_target_pairs={{0,4},{4,8},{8,12},{12,14},{14,10},{10,6},{6,2},{2,0},{1,3},{5,1},... | collective-permute-start | bytes 393224 | tf_op jit(solution)/shard_map/ppermute | solution.py:52
  104.6 10.0 %collective-permute-start.51 = (bf16[528,128]{1,0:T(8,128)(2,1)S(1)}, bf16[528,128]{1,0:T(8,128)(2,1)S(1)}, u32[]{:S(2)}, u32[]{:S(2)}) collective-permute-start(bf16[528,128]{1,0:T(8,128)(2,1)S(1)} %shard_map.117), channel_id=1, source_target_pairs={{0,4},{4,8},{8,12},{12,14},{14,10},{10,6},{6,2},{2,0},{1,3},{5,1},... | collective-permute-start | bytes 405512 | tf_op jit(solution)/shard_map/ppermute | solution.py:52
  107.4 7.3 %collective-permute-start.55 = (bf16[528,128]{1,0:T(8,128)(2,1)S(1)}, bf16[528,128]{1,0:T(8,128)(2,1)S(1)}, u32[]{:S(2)}, u32[]{:S(2)}) collective-permute-start(bf16[528,128]{1,0:T(8,128)(2,1)S(1)} %shard_map.121), channel_id=1, source_target_pairs={{0,2},{4,0},{8,4},{12,8},{14,12},{10,14},{6,10},{2,6},{1,5},{5,9},... | collective-permute-start | bytes 405512 | tf_op jit(solution)/shard_map/ppermute | solution.py:52
  (15 other events, 70.5 us)
